TPU v7x, 128 devices: a whole 4x4x4 slice. The times are simulated.
128 devices in a mesh: batch: 8 (over y_lo, z), tensor: 16 (over y_hi, x, core).
Axes of the slice: x: 4, y: 4 (y_hi: 2, y_lo: 2; y = y_hi * 2 + y_lo), z: 4, core: 2. Of those that a mesh axis runs over, the one named last changes fastest.
Arguments:
- attn_values: bfloat16 [2048, 8192], P('batch', 'tensor'), may hold values from -6 to 6
- out_weight: bfloat16 [8192, 8192], P('tensor'), may hold values from -0.09375 to 0.09375
- residual_t: bfloat16 [8192, 2048], P('tensor', 'batch'), may hold values from -6 to 6
- projector: bfloat16 [8192, 4096], P('tensor'), may hold values from -0.0625 to 0.0625
- student_input: bfloat16 [2048, 4096], P('batch', 'tensor'), may hold values from -6 to 6
- norm_gain: float32 [4096], replicated, may hold values from 0.1 to 1.9
- w_gate: bfloat16 [4096, 8192], P('batch', 'tensor'), may hold values from -0.09375 to 0.09375
- w_up: bfloat16 [4096, 8192], P('batch', 'tensor'), may hold values from -0.09375 to 0.09375
- w_down: bfloat16 [4096, 8192], P('batch', 'tensor'), may hold values from -0.0625 to 0.0625
- route_index: int32 [8, 64], P('batch'), may hold values from -1 to 255, as said below
Outputs:
- teacher_hidden: bfloat16 [8192, 2048], P('tensor', 'batch')
- grad_gate: float32 [4096, 8192], P('batch', 'tensor')
- grad_up: float32 [4096, 8192], P('batch', 'tensor')
- grad_down: float32 [4096, 8192], P('batch', 'tensor')
Inputs may be any that keep to these rules, and one draw needn't show every extreme that they name: `route_index`: in each batch group the live slots come first, hold distinct positions in increasing order, and the empty slots after them hold -1. The batch groups hold 256 live slots together, and some batch group has all 64 slots live.
All inputs are finite; a program needn't handle non-finite values.
Results may differ from a plain program's by a relative error of at most 0.025.
Values may be sent and summed in bfloat16 or wider, within the bound.
No kernel may reach another device: no remote copies, remote signals or barrier semaphores. Data moves between devices by JAX's collectives and lax.ppermute only.
A program may use at most 128 MiB of HBM per device.

v0:
```python
import math

import jax
import jax.numpy as jnp
from jax import lax
from jax.sharding import Mesh
from jax.sharding import PartitionSpec as P

TENSOR = ("tensor_0", "tensor_1", "tensor_2")


epsilon = 1e-05


def from_everyone(value, axis):
    copies = jnp.broadcast_to(value, (lax.axis_size(axis), *value.shape))
    return lax.all_to_all(copies, axis, split_axis=0, concat_axis=0, tiled=True)


def joined_along(blocks, dim):
    lengths = list(blocks.shape[1:])
    lengths[dim] *= blocks.shape[0]
    return jnp.moveaxis(blocks, 0, dim).reshape(lengths)


def collect(value, axis, dim):
    blocks = from_everyone(value, axis)
    return joined_along(blocks, dim)


def side_by_side(arrays, axis, dim, along):
    ends, at = ([], 0)
    for a in arrays[:-1]:
        at += a.shape[along]
        ends.append(at)
    both = jnp.concatenate(arrays, axis=along)
    return tuple(jnp.split(lax.all_gather(both, axis, axis=dim, tiled=True), ends, axis=along))


def cut_along(value, dim, devices):
    lengths = value.shape
    blocks = value.reshape(*lengths[:dim], devices, lengths[dim] // devices, *lengths[dim + 1 :])
    return jnp.moveaxis(blocks, dim, 0)


def sent_and_summed(value, axis, dim):
    devices = lax.axis_size(axis)
    blocks = lax.all_to_all(cut_along(value, dim, devices), axis, 0, 0, tiled=True)
    return jnp.sum(blocks.astype(jnp.float32), axis=0)


def summed_rows(value, axes, dim):
    far, near = axes
    own = sent_and_summed(cut_along(value, dim, lax.axis_size(far)), near, dim + 1)
    return jnp.sum(
        lax.all_to_all(own.astype(jnp.bfloat16), far, 0, 0, tiled=True).astype(jnp.float32), axis=0
    )


def filled_up(lines, devices):
    spare = -len(lines) % devices
    return jnp.pad(lines, [(0, spare)] + [(0, 0)] * (lines.ndim - 1))


def gather_axes(value, axes, dim):
    far, near = axes
    blocks = from_everyone(from_everyone(value, far), near)
    return joined_along(blocks.swapaxes(0, 1).reshape(-1, *value.shape), dim)


def total_of(value, axes):
    lines = value.reshape(-1, value.shape[-1])
    own = summed_rows(filled_up(lines, lax.axis_size(axes[0]) * lax.axis_size(axes[1])), axes, 0)
    whole = gather_axes(own.astype(jnp.bfloat16), axes, 0)
    return whole[: len(lines)].reshape(value.shape).astype(jnp.float32)


def grouped_product(left, right):
    dims = (((1,), (1,)), ((0,), (0,)))
    full = lax.dot_general(left, right, dims, preferred_element_type=jnp.float32)
    rounded = lax.optimization_barrier(full.astype(jnp.bfloat16))
    return jnp.sum(rounded.astype(jnp.float32), axis=0)


def on_device(
    attn_values,
    out_weight,
    residual_t,
    projector,
    student_input,
    norm_gain,
    w_gate,
    w_up,
    w_down,
    route_index,
):
    summed = lax.psum_scatter(
        lax.dot_general(
            out_weight, attn_values, (((0,), (1,)), ((), ())), preferred_element_type=jnp.float32
        ).astype(jnp.bfloat16),
        TENSOR,
        scatter_dimension=0,
        tiled=True,
    ).astype(jnp.float32)
    teacher_hidden = (residual_t.astype(jnp.float32) + summed).astype(jnp.bfloat16)
    slot_pos = route_index[0]
    present = slot_pos >= 0
    safe_slot = jnp.maximum(slot_pos, 0)
    routed_teacher = jnp.where(present[None, :], jnp.take(teacher_hidden, safe_slot, axis=1), 0)
    target_part = lax.dot_general(
        routed_teacher, projector, (((0,), (0,)), ((), ())), preferred_element_type=jnp.float32
    )
    local_rows = jnp.where(present[:, None], jnp.take(student_input, safe_slot, axis=0), 0)
    routed_input = collect(local_rows, TENSOR, 1).astype(jnp.float32)
    mean_square = jnp.mean(routed_input * routed_input, axis=1, keepdims=True)
    normed = (routed_input * lax.rsqrt(mean_square + epsilon) * norm_gain[None, :]).astype(
        jnp.bfloat16
    )
    slot_total = normed.shape[0]
    local_units = w_gate.shape[1]
    gate_full, up_full, down_full = side_by_side((w_gate, w_up, w_down), "batch", 0, 1)
    gate_act = jnp.dot(normed, gate_full, preferred_element_type=jnp.float32)
    up_act = jnp.dot(normed, up_full, preferred_element_type=jnp.float32)
    sigma_gate = jax.nn.sigmoid(gate_act)
    hidden = (gate_act * sigma_gate * up_act).astype(jnp.bfloat16)
    out_part = lax.dot_general(
        hidden, down_full, (((1,), (1,)), ((), ())), preferred_element_type=jnp.float32
    )
    misfit = total_of(
        (out_part - target_part).astype(jnp.bfloat16), (("tensor_0", "tensor_1"), "tensor_2")
    )
    group_count = lax.axis_size("batch")
    mean_routed = student_input.shape[0] // 8
    loss_scale = 1.0 / math.sqrt(mean_routed * group_count)
    grad_out = (jnp.where(present[:, None], misfit, 0.0) * loss_scale).astype(jnp.bfloat16)
    grad_hidden = jnp.dot(grad_out, down_full, preferred_element_type=jnp.float32)
    grad_gate_act = (
        grad_hidden * up_act * sigma_gate * (1.0 + gate_act * (1.0 - sigma_gate))
    ).astype(jnp.bfloat16)
    grad_up_act = (grad_hidden * gate_act * sigma_gate).astype(jnp.bfloat16)
    rows_local = w_gate.shape[0]
    every_normed, every_grad = (
        lax.all_to_all(normed, "batch", split_axis=1, concat_axis=0, tiled=True),
        lax.all_to_all(grad_out, "batch", split_axis=1, concat_axis=0, tiled=True),
    )
    every_gate, every_up, every_hidden = side_by_side(
        (grad_gate_act, grad_up_act, hidden), "batch", 0, 1
    )
    normed_groups = every_normed.reshape(group_count, slot_total, rows_local)
    grad_groups = every_grad.reshape(group_count, slot_total, rows_local)
    gate_groups = every_gate.reshape(group_count, slot_total, local_units)
    up_groups = every_up.reshape(group_count, slot_total, local_units)
    hidden_groups = every_hidden.reshape(group_count, slot_total, local_units)
    grad_gate = grouped_product(normed_groups, gate_groups)
    grad_up = grouped_product(normed_groups, up_groups)
    grad_down = grouped_product(grad_groups, hidden_groups)
    return (teacher_hidden, grad_gate, grad_up, grad_down)


def solution(mesh):
    split = Mesh(
        mesh.devices.reshape(mesh.shape["batch"], 2, 4, 2),
        ("batch", "tensor_0", "tensor_1", "tensor_2"),
    )
    in_specs = (
        P("batch", TENSOR),
        P(TENSOR, None),
        P(TENSOR, "batch"),
        P(TENSOR, None),
        P("batch", TENSOR),
        P(),
        P("batch", TENSOR),
        P("batch", TENSOR),
        P("batch", TENSOR),
        P("batch", None),
    )
    out_specs = (P(TENSOR, "batch"), P("batch", TENSOR), P("batch", TENSOR), P("batch", TENSOR))
    return jax.shard_map(
        on_device, mesh=split, in_specs=in_specs, out_specs=out_specs, check_vma=False
    )
```

profile of v0, /device:TPU:0, one launch (start us, length us, event | category | flops | bytes accessed | tf_op | source)
XLA Modules:
  0.0 288.6 jit_solution(2432564171475395224)
XLA Ops:
  9.0 7.7 %convolution_convert_fusion = bf16[8192,256]{1,0:T(8,128)(2,1)} fusion(bf16[512,8192]{1,0:T(8,128)(2,1)} %param.11, bf16[256,512]{1,0:T(8,128)(2,1)S(1)} %copy-done), kind=kOutput, calls=%fused_computation.2 | convolution fusion | flops 2149580800 | bytes 12845056 | tf_op jit(solution)/shard_map/dot_general | solution.py:98
  20.3 19.3 %all_to_all.51 = bf16[16,64,256]{2,1,0:T(8,128)(2,1)S(1)} all-to-all(bf16[16,64,256]{2,1,0:T(8,128)(2,1)S(1)} %broadcast_in_dim.78), channel_id=1, replica_groups=mesh['batch'=8,'tensor_0'=2,'tensor_1'=4,'tensor_2'=2] {'tensor_0','tens..., dimensions={0} | all-to-all | bytes 1048576 | tf_op jit(solution)/shard_map/all_to_all | solution.py:17
  40.1 83.2 %reduce-scatter.2.cloned.1.call-done = bf16[512,256]{1,0:T(8,128)(2,1)} async-done(((bf16[8192,256]{1,0:T(8,128)(2,1)}), bf16[512,256]{1,0:T(8,128)(2,1)}) %reduce-scatter.2.cloned.1.call-update) | async-done | bytes 262160 | tf_op jit(solution)/shard_map/reduce_scatter | solution.py:97
  125.2 46.1 %all-gather.3.cloned.1.call-done = bf16[4096,1536]{1,0:T(8,128)(2,1)} async-done(((bf16[512,1536]{1,0:T(8,128)(2,1)}), bf16[4096,1536]{1,0:T(8,128)(2,1)}) %all-gather.3.cloned.1.call-update) | async-done | bytes 12582928 | tf_op jit(solution)/shard_map/all_gather | solution.py:37
  171.3 3.1 %fusion.3 = f32[64,512]{1,0:T(8,128)S(1)} fusion(bf16[4096,1536]{1,0:T(8,128)(2,1)} %all-gather.3.cloned.1.call-done, f32[64,4096]{1,0:T(8,128)S(1)} %bitcast.38, f32[4096]{0:T(1024)S(1)} %copy-done.11, f32[64]{0:T(128)S(1)} %add_rsqrt_fusion), kind=kOutput, calls=%fused_computation.10 | convolution fusion | flops 269221888 | bytes 5390592 | tf_op jit(solution)/shard_map/dot_general | solution.py:122
  174.3 3.7 %multiply_convert_fusion.5 = (bf16[64,512]{1,0:T(8,128)(2,1)S(1)}, f32[64,512]{1,0:T(8,128)}) fusion(f32[64,512]{1,0:T(8,128)S(1)} %fusion.3, bf16[4096,1536]{1,0:T(8,128)(2,1)} %all-gather.3.cloned.1.call-done, f32[64,4096]{1,0:T(8,128)S(1)} %bitcast.39, f32[4096]{0:T(1024)S(1)} %copy-done.11, f32[64]{0:T(128)S(1)} %add_rsqrt_fusion), kind=kOutput, calls=%fused_computation.44 | convolution fusion | flops 269418496 | bytes 5587200 | tf_op jit(solution)/shard_map/dot_general | solution.py:123
  178.1 3.7 %fusion.7 = f32[64,4096]{1,0:T(8,128)S(1)} fusion(bf16[64,512]{1,0:T(8,128)(2,1)S(1)} %get-tuple-element.13, bf16[4096,1536]{1,0:T(8,128)(2,1)} %all-gather.3.cloned.1.call-done), kind=kOutput, calls=%fused_computation.14 | convolution fusion | flops 268435456 | bytes 5308416 | tf_op jit(solution)/shard_map/dot_general | solution.py:126
  183.1 4.2 %all_to_all.52 = bf16[2,8,4,4096]{3,2,1,0:T(4,128)(2,1)S(1)} all-to-all(bf16[2,8,4,4096]{3,2,1,0:T(4,128)(2,1)S(1)} %bitcast.37), channel_id=1, replica_groups=mesh['batch'=8,'tensor_0'=2,'tensor_1'=4,'tensor_2'=2] {'tensor_2'}, dimensions={0} | all-to-all | bytes 1048576 | tf_op jit(solution)/shard_map/all_to_all | solution.py:48
  187.8 16.1 %all_to_all.53 = bf16[8,4,4096]{2,1,0:T(4,128)(2,1)S(1)} all-to-all(bf16[8,4,4096]{2,1,0:T(4,128)(2,1)S(1)} %reduce_sum.61), channel_id=1, replica_groups=mesh['batch'=8,'tensor_0'=2,'tensor_1'=4,'tensor_2'=2] {'tensor_0','tens..., dimensions={0} | all-to-all | bytes 524288 | tf_op jit(solution)/shard_map/all_to_all | solution.py:56
  204.1 11.3 %all_to_all.54 = bf16[8,4,4096]{2,1,0:T(4,128)(2,1)S(1)} all-to-all(bf16[8,4,4096]{2,1,0:T(4,128)(2,1)S(1)} %broadcast_in_dim.84), channel_id=1, replica_groups=mesh['batch'=8,'tensor_0'=2,'tensor_1'=4,'tensor_2'=2] {'tensor_0','tens..., dimensions={0} | all-to-all | bytes 524288 | tf_op jit(solution)/shard_map/all_to_all | solution.py:17
  215.6 4.2 %all_to_all.55 = bf16[2,8,4,4096]{3,2,1,0:T(4,128)(2,1)S(1)} all-to-all(bf16[2,8,4,4096]{3,2,1,0:T(4,128)(2,1)S(1)} %broadcast_in_dim.85), channel_id=1, replica_groups=mesh['batch'=8,'tensor_0'=2,'tensor_1'=4,'tensor_2'=2] {'tensor_2'}, dimensions={0} | all-to-all | bytes 1048576 | tf_op jit(solution)/shard_map/all_to_all | solution.py:17
  220.4 3.1 %multiply_convert_fusion.4 = (bf16[64,512]{1,0:T(8,128)(2,1)S(1)}, bf16[64,512]{1,0:T(8,128)(2,1)S(1)}) fusion(f32[64,512]{1,0:T(8,128)S(1)} %fusion.3, f32[64,512]{1,0:T(8,128)} %get-tuple-element.14, bf16[4096,1536]{1,0:T(8,128)(2,1)} %all-gather.3.cloned.1.call-done, f32[64,4096]{1,0:T(8,128)S(1)} %reshape.96, pred[64]{0:T(512)(128)(4,1)S(1)} %get-tuple-element.11), kind=kOutput, calls=%fused_computation.43 | convolution fusion | flops 269647872 | bytes 5636160 | tf_op jit(solution)/shard_map/dot_general | solution.py:136
  225.1 1.4 fusion.13
  226.5 3.7 %all-to-all-start.1 = ((bf16[64,8,512]{2,0,1:T(8,128)(2,1)}), bf16[64,8,512]{2,0,1:T(8,128)(2,1)S(1)}, u32[]{:S(2)}, u32[]{:S(2)}) async-start(bf16[64,8,512]{2,0,1:T(8,128)(2,1)} %fusion.13), calls=%async_computation.2 | async-start | bytes 1048576 | tf_op jit(solution)/shard_map/all_to_all | solution.py:143
  230.9 1.4 fusion.11
  232.3 28.5 %all-gather.5.cloned.1.call-done = bf16[512,1536]{1,0:T(8,128)(2,1)} async-done(((bf16[64,1536]{1,0:T(8,128)(2,1)}), bf16[512,1536]{1,0:T(8,128)(2,1)}) %all-gather.5.cloned.1.call-update) | async-done | bytes 1572880 | tf_op jit(solution)/shard_map/all_gather | solution.py:37
  260.9 1.5 fusion.30
  262.4 4.2 %all-to-all-start.6 = ((bf16[64,8,512]{2,0,1:T(8,128)(2,1)}), bf16[64,8,512]{2,0,1:T(8,128)(2,1)S(1)}, u32[]{:S(2)}, u32[]{:S(2)}) async-start(bf16[64,8,512]{2,0,1:T(8,128)(2,1)} %fusion.11), calls=%async_computation.7 | async-start | bytes 1048576 | tf_op jit(solution)/shard_map/all_to_all | solution.py:144
  266.6 3.3 %convolution_convert_fusion.2 = bf16[8,512,512]{2,1,0:T(8,128)(2,1)} fusion(bf16[8,64,512]{2,1,0:T(8,128)(2,1)S(1)} %bitcast.36, bf16[64,8,512]{2,0,1:T(8,128)(2,1)S(1)} %all-to-all-done.1), kind=kOutput, calls=%fused_computation.17 | convolution fusion | flops 270532608 | bytes 5242880 | tf_op jit(solution)/shard_map/dot_general | solution.py:80
  269.8 3.3 %convolution_convert_fusion.3 = bf16[8,512,512]{2,1,0:T(8,128)(2,1)} fusion(bf16[8,64,512]{2,1,0:T(8,128)(2,1)S(1)} %bitcast.35, bf16[64,8,512]{2,0,1:T(8,128)(2,1)S(1)} %all-to-all-done.1), kind=kOutput, calls=%fused_computation.18 | convolution fusion | flops 270532608 | bytes 5242880 | tf_op jit(solution)/shard_map/dot_general | solution.py:80
  273.1 1.8 all-to-all-done.6
  274.9 1.3 convolution_convert_fusion.1
  276.2 1.6 convert_reduce_fusion
  278.7 2.5 convert_reduce_fusion.1
  (62 shorter events, 12.9 us)
Async XLA Ops:
  8.0 1.0 copy-start
  8.0 115.3 %reduce-scatter.2.cloned.1.call-start = ((), (), s32[]{:S(2)}) async-start(), calls=%async_computation.8 | async-start | bytes 4456448 | tf_op jit(solution)/shard_map/reduce_scatter | solution.py:97
  16.7 1.0 copy-start.7
  16.7 1.2 copy-start.8
  16.7 1.4 copy-start.9
  16.7 2.7 copy-start.12
  16.7 2.7 copy-start.6
  16.7 154.5 %all-gather.3.cloned.1.call-start = ((), (), s32[]{:S(2)}) async-start(), calls=%async_computation.9 | async-start | bytes 14155776 | tf_op jit(solution)/shard_map/all_gather | solution.py:37
  19.3 104.0 %copy-start.10 = (bf16[512,256]{1,0:T(8,128)(2,1)S(1)}, bf16[512,256]{1,0:T(8,128)(2,1)}, u32[]{:S(2)}) copy-start(bf16[512,256]{1,0:T(8,128)(2,1)} %param.12) | copy-start | bytes 786436
  19.3 241.6 %all-gather.5.cloned.1.call-start = ((), (), s32[]{:S(2)}) async-start(), calls=%async_computation.10 | async-start | bytes 1769472 | tf_op jit(solution)/shard_map/all_gather | solution.py:37
  20.3 151.0 %copy-start.11 = (f32[4096]{0:T(1024)S(1)}, f32[4096]{0:T(1024)}, u32[]{:S(2)}) copy-start(f32[4096]{0:T(1024)} %param.15) | copy-start | bytes 49156
  124.3 53.7 %copy-start.5 = (bf16[512,256]{1,0:T(8,128)(2,1)}, bf16[512,256]{1,0:T(8,128)(2,1)S(1)}, u32[]{:S(2)}) copy-start(bf16[512,256]{1,0:T(8,128)(2,1)S(1)} %add_convert_fusion) | copy-start | bytes 786436
  178.1 3.7 %copy-start.4 = (bf16[512,4096]{1,0:T(8,128)(2,1)S(1)}, bf16[512,4096]{1,0:T(8,128)(2,1)}, u32[]{:S(2)}) copy-start(bf16[512,4096]{1,0:T(8,128)(2,1)} %param.13) | copy-start | bytes 12582916
  226.5 35.8 %all-to-all-start.1 = ((bf16[64,8,512]{2,0,1:T(8,128)(2,1)}), bf16[64,8,512]{2,0,1:T(8,128)(2,1)S(1)}, u32[]{:S(2)}, u32[]{:S(2)}) async-start(bf16[64,8,512]{2,0,1:T(8,128)(2,1)} %fusion.13), calls=%async_computation.2 | async-start | bytes 1048576 | tf_op jit(solution)/shard_map/all_to_all | solution.py:143
  262.4 12.5 %all-to-all-start.6 = ((bf16[64,8,512]{2,0,1:T(8,128)(2,1)}), bf16[64,8,512]{2,0,1:T(8,128)(2,1)S(1)}, u32[]{:S(2)}, u32[]{:S(2)}) async-start(bf16[64,8,512]{2,0,1:T(8,128)(2,1)} %fusion.11), calls=%async_computation.7 | async-start | bytes 1048576 | tf_op jit(solution)/shard_map/all_to_all | solution.py:144
  274.9 2.9 %copy-start.2 = (bf16[8,512,512]{2,1,0:T(8,128)(2,1)S(1)}, bf16[8,512,512]{2,1,0:T(8,128)(2,1)}, u32[]{:S(2)}) copy-start(bf16[8,512,512]{2,1,0:T(8,128)(2,1)} %convolution_convert_fusion.2) | copy-start | bytes 12582916
  274.9 3.8 %copy-start.3 = (bf16[8,512,512]{2,1,0:T(8,128)(2,1)S(1)}, bf16[8,512,512]{2,1,0:T(8,128)(2,1)}, u32[]{:S(2)}) copy-start(bf16[8,512,512]{2,1,0:T(8,128)(2,1)} %convolution_convert_fusion.3) | copy-start | bytes 12582916
  276.2 5.0 %copy-start.1 = (bf16[256,512]{1,0:T(8,128)(2,1)S(1)}, bf16[256,512]{1,0:T(8,128)(2,1)}, u32[]{:S(2)}) copy-start(bf16[256,512]{1,0:T(8,128)(2,1)} %param.10) | copy-start | bytes 786436
Sparse Core Ops, SparseCore 0:
  16.8 106.4 reduce-scatter.1
Sparse Core Ops, SparseCore 1:
  19.4 151.8 all-gather.2
  224.3 36.6 all-gather.4
where the time goes:
time: 289 us
  waiting for transfers between devices  160 us (55%)
  blocking collectives  55 us (19%)
  matrix products  30 us (10%)
  between operations  15.8 us (5%)
  other arithmetic  11.1 us (4%)
  local copies, waits for them, and re-layouts  9.04 us (3%)
  starting transfers between devices  8.01 us (3%)
    reduce_scatter x1, waiting for transfers between devices, on_device(): lax.psum_scatter(lax.dot_general(out_weight, attn_values, (((0,), (1,)),...  83.2 us
    all_gather x2, waiting for transfers between devices, side_by_side(): lax.all_gather(both, axis, axis=dim, tiled=True)  74.6 us
    all_to_all x3, blocking collectives, from_everyone(): return lax.all_to_all(copies, axis, split_axis=0, concat_axis=0, tiled=True)  34.8 us
    all_to_all x1, blocking collectives, summed_rows(): lax.all_to_all(own.astype(jnp.bfloat16), far, 0, 0, tiled=True)  16.1 us
    dot_general x3, matrix products, grouped_product(): lax.dot_general(left, right, dims, preferred_element_type=jnp.float32)  7.81 us
    dot_general x1, matrix products, on_device(): lax.dot_general(out_weight, attn_values, (((0,), (1,)), ((), ())), prefer...  7.72 us
  transfers between devices with their start and end apart: 5, of which 4 were waited for; matrix products, arithmetic and copies ran while one was open for 6% of the time, Pallas kernels for 0%

commit v1 on v0

v1 whole, which is shorter than its diff:
```python
import math

import jax
import jax.numpy as jnp
from jax import lax
from jax.experimental import pallas as pl
from jax.experimental.pallas import tpu as pltpu
from jax.sharding import PartitionSpec as P

EPS = 1e-05
BF = jnp.bfloat16
F32 = jnp.float32
MIB = 1 << 20


def params(mib):
    return pltpu.CompilerParams(vmem_limit_bytes=mib * MIB)


def cost(flops, nbytes):
    return pl.CostEstimate(flops=flops, bytes_accessed=nbytes, transcendentals=0)


def dot(a, b, ca=1, cb=0):
    return lax.dot_general(a, b, (((ca,), (cb,)), ((), ())), preferred_element_type=F32)


def whole(shape):
    return pl.BlockSpec(shape, lambda *_: (0,) * len(shape))


def slot_rows(route, tokens):
    slots = route.shape[1]
    grid = (slots, slots)
    diagonal = lax.broadcasted_iota(jnp.int32, grid, 0) == lax.broadcasted_iota(jnp.int32, grid, 1)
    spread = jnp.broadcast_to(route.astype(F32), grid)
    column = jnp.sum(jnp.where(diagonal, spread, 0.0), axis=1, keepdims=True)
    lane = lax.broadcasted_iota(jnp.int32, (slots, tokens), 1).astype(F32)
    return jnp.where(lane == column, 1.0, 0.0).astype(BF)


def rows_kernel(route_ref, x_ref, out_ref):
    route = route_ref[...]
    slots, wide = route.shape[1], x_ref.shape[1]
    rows = dot(slot_rows(route, x_ref.shape[0]), x_ref[...]).astype(BF)
    half = slots // 2
    out_ref[0:half, 0:wide] = rows[0:half]
    out_ref[0:half, wide : 2 * wide] = rows[half:]
    live = jnp.sum(jnp.where(route >= 0, 1.0, 0.0), axis=1, keepdims=True)
    out_ref[half : half + 8, :] = jnp.broadcast_to(live, (8, 2 * wide)).astype(BF)


def teacher_kernel(route_ref, attn_ref, weight_ref, full_ref, routed_ref, left_ref):
    tokens = attn_ref.shape[0]
    slots = route_ref.shape[1]

    @pl.when(pl.program_id(0) == 0)
    def _():
        left_ref[0:tokens, :] = attn_ref[...]
        left_ref[tokens:, :] = dot(slot_rows(route_ref[...], tokens), attn_ref[...]).astype(BF)

    product = dot(left_ref[...], weight_ref[...]).astype(BF)
    full_ref[...] = product[0:tokens]
    routed_ref[0, 0:slots, :] = product[tokens:]


def up_kernel(
    group_ref, route_ref, got_ref, residual_ref, gain_ref, gate_ref, up_ref,
    out_ref, rows_ref, padded_ref,
):
    group = group_ref[0]
    slots = route_ref.shape[1]
    sources, _, wide = got_ref.shape
    groups = sources // 2
    half, side = slots // 2, wide // 2
    total = groups * out_ref.shape[1]

    routed = dot(slot_rows(route_ref[...], residual_ref.shape[1]), residual_ref[...], 1, 1)
    for s in range(sources):
        routed = routed + got_ref[s, 0:slots, :].astype(F32)
        g, d = s // 2, s % 2
        block = got_ref[s, slots : slots + half, :]
        padded_ref[g * slots : g * slots + half, d * side : (d + 1) * side] = block[:, 0:side]
        padded_ref[g * slots + half : (g + 1) * slots, d * side : (d + 1) * side] = block[:, side:]
    at = slots + half
    counts = [got_ref[2 * g, at : at + 8, 0:128].astype(F32)[0:1] for g in range(groups)]
    zero = jnp.zeros_like(counts[0])
    starts, own_start, own_count, run = [], zero, zero, zero
    for g in range(groups):
        starts.append(run)
        own_start = jnp.where(group == g, run, own_start)
        own_count = jnp.where(group == g, counts[g], own_count)
        run = run + counts[g]

    row = lax.broadcasted_iota(jnp.int32, (total, 2 * slots), 0)
    lane = lax.broadcasted_iota(jnp.int32, (total, 2 * slots), 1)
    second = lane >= slots
    slot = jnp.where(second, lane - slots, lane)
    slot_f = slot.astype(F32)
    shift = (row - slot).astype(F32)
    x = jnp.zeros((total, wide), F32)
    for q in range(groups // 2):
        start = jnp.where(second, starts[2 * q + 1], starts[2 * q])
        count = jnp.where(second, counts[2 * q + 1], counts[2 * q])
        chosen = jnp.where((shift == start) & (slot_f < count), 1.0, 0.0).astype(BF)
        x = x + dot(chosen, padded_ref[2 * q * slots : 2 * (q + 1) * slots, :])
    chosen = jnp.where((shift == own_start) & (slot_f < own_count) & (lane < slots), 1.0, 0.0)
    routed = routed.astype(BF)
    target_rows = dot(chosen[:, 0:slots].astype(BF), routed).astype(BF)

    square = jnp.sum(x * x, axis=1, keepdims=True)
    high = square.astype(BF)
    low = (square - high.astype(F32)).astype(BF)
    lane128 = lax.broadcasted_iota(jnp.int32, (total, 128), 1)
    squares = jnp.where(lane128 < 64, high.astype(F32), low.astype(F32)).astype(BF)
    scaled = (x * gain_ref[...]).astype(BF)
    rows_ref[...] = scaled
    gate = dot(scaled, gate_ref[...]).astype(BF)
    up = dot(scaled, up_ref[...]).astype(BF)
    per = out_ref.shape[1]
    for g in range(groups):
        own = slice(g * per, (g + 1) * per)
        out_ref[g, :, 0:wide] = gate[own]
        out_ref[g, :, wide : 2 * wide] = up[own]
        out_ref[g, :, 2 * wide : 3 * wide] = target_rows[own]
        out_ref[g, :, 3 * wide :] = squares[own]


def down_kernel(
    features, got_ref, down_ref, projector_ref,
    out_ref, gate_ref, up_ref, hidden_ref, scale_ref, target_ref,
):
    wide = hidden_ref.shape[1]

    @pl.when(pl.program_id(0) == 0)
    def _():
        total = got_ref[0].astype(F32)
        for g in range(1, got_ref.shape[0]):
            total = total + got_ref[g].astype(F32)
        square = total[:, 3 * wide : 3 * wide + 1] + total[:, 3 * wide + 64 : 3 * wide + 65]
        scale = lax.rsqrt(square * (1.0 / features) + EPS)
        gate = total[:, 0:wide] * scale
        up = total[:, wide : 2 * wide] * scale
        gate_ref[...] = gate
        up_ref[...] = up
        scale_ref[...] = jnp.broadcast_to(scale, scale_ref.shape)
        target_ref[...] = total[:, 2 * wide : 3 * wide].astype(BF)
        hidden_ref[...] = (gate * jax.nn.sigmoid(gate) * up).astype(BF)

    part = dot(hidden_ref[...], down_ref[...], 1, 1) - dot(target_ref[...], projector_ref[...])
    part = part.astype(BF)
    chunk = out_ref.shape[2]
    for i in range(out_ref.shape[0]):
        out_ref[i] = part[:, i * chunk : (i + 1) * chunk]


def misfit_kernel(scale, got_ref, out_ref):
    total = got_ref[0].astype(F32)
    for s in range(1, got_ref.shape[0]):
        total = total + got_ref[s].astype(F32)
    grad = (total * scale).astype(BF)
    for s in range(out_ref.shape[0]):
        out_ref[s] = grad


def back_kernel(got_ref, down_ref, gate_ref, up_ref, hidden_ref, scale_ref, out_ref, total_ref):
    step, chunk = pl.program_id(0), got_ref.shape[2]
    wide = hidden_ref.shape[1]

    @pl.when(step == 0)
    def _():
        total_ref[...] = jnp.zeros_like(total_ref)

    part = total_ref[...]
    for i in range(got_ref.shape[0]):
        part = part + dot(got_ref[i], down_ref[i * chunk : (i + 1) * chunk, :])
        out_ref[step, :, 3 * wide + i * chunk : 3 * wide + (i + 1) * chunk] = got_ref[i]
    total_ref[...] = part

    @pl.when(step == pl.num_programs(0) - 1)
    def _():
        grad = total_ref[...] * scale_ref[:, 0:1]
        gate, up = gate_ref[...], up_ref[...]
        sigma = jax.nn.sigmoid(gate)
        grad_gate = (grad * up * sigma * (1.0 + gate * (1.0 - sigma))).astype(BF)
        grad_up = (grad * gate * sigma).astype(BF)
        for g in range(out_ref.shape[0]):
            out_ref[g, :, 0:wide] = grad_gate
            out_ref[g, :, wide : 2 * wide] = grad_up
            out_ref[g, :, 2 * wide : 3 * wide] = hidden_ref[...]


def weights_kernel(rows_ref, got_ref, grad_ref, gate_ref, up_ref, down_ref):
    wide = gate_ref.shape[1]
    groups, per, _ = got_ref.shape

    def columns(i):
        return got_ref[:, :, i * wide : (i + 1) * wide].reshape(groups * per, wide)

    rows = rows_ref[...]
    gate_ref[...] = dot(rows, columns(0), 0, 0)
    up_ref[...] = dot(rows, columns(1), 0, 0)
    grad = grad_ref[...].reshape(groups * per, grad_ref.shape[2])
    down_ref[...] = dot(grad, columns(2), 0, 0)


def on_device(
    attn_values,
    out_weight,
    residual_t,
    projector,
    student_input,
    norm_gain,
    w_gate,
    w_up,
    w_down,
    route_index,
):
    groups, parts = lax.axis_size("batch"), lax.axis_size("tensor")
    slots = route_index.shape[1]
    tokens, wide = attn_values.shape
    side = student_input.shape[1]
    features = norm_gain.shape[0]
    live = tokens * groups // 8
    per = live // groups
    units = w_gate.shape[1]
    extra = slots // 2 + 8
    down_full = lax.all_gather(w_down, "batch", axis=0, tiled=True)

    rows = pl.pallas_call(
        rows_kernel,
        out_shape=jax.ShapeDtypeStruct((extra, 2 * side), BF),
        name="rows",
    )(route_index, student_input)
    pairs = [
        (b * parts + t, (t // 2) * parts + 2 * b + t % 2)
        for b in range(groups)
        for t in range(parts)
    ]
    rows = lax.ppermute(rows, ("batch", "tensor"), pairs)

    full, routed = pl.pallas_call(
        teacher_kernel,
        grid=(parts,),
        in_specs=[
            whole(route_index.shape),
            whole(attn_values.shape),
            pl.BlockSpec((wide, wide), lambda j: (0, j)),
        ],
        out_specs=[
            pl.BlockSpec((tokens, wide), lambda j: (j, 0)),
            pl.BlockSpec((1, slots + extra, wide), lambda j: (j, 0, 0)),
        ],
        out_shape=[
            jax.ShapeDtypeStruct((parts * tokens, wide), BF),
            jax.ShapeDtypeStruct((parts, slots + extra, wide), BF),
        ],
        scratch_shapes=[pltpu.VMEM((tokens + slots, wide), BF)],
        compiler_params=params(16),
        cost_estimate=cost(2 * (tokens + slots) * wide * wide * parts, 14 * MIB),
        name="teacher",
    )(route_index, attn_values, out_weight)
    summed = lax.psum_scatter(full, "tensor", scatter_dimension=0, tiled=True)
    teacher_hidden = (residual_t.astype(F32) + summed.astype(F32).T).astype(BF)

    routed = routed.at[:, slots:, :].set(jnp.broadcast_to(rows[None], (parts, *rows.shape)))
    routed = lax.all_to_all(routed, "tensor", 0, 0, tiled=True)

    group = lax.axis_index("batch")
    gain = lax.dynamic_slice_in_dim(norm_gain, group * wide, wide)[None]
    sent, scaled = pl.pallas_call(
        up_kernel,
        in_specs=[pl.BlockSpec(memory_space=pltpu.SMEM)]
        + [pl.BlockSpec(memory_space=pltpu.VMEM)] * 6,
        out_shape=[
            jax.ShapeDtypeStruct((groups, per, 3 * wide + 128), BF),
            jax.ShapeDtypeStruct((live, wide), BF),
        ],
        scratch_shapes=[pltpu.VMEM((groups * slots, wide), BF)],
        compiler_params=params(24),
        name="up",
    )(group.reshape(1), route_index, routed, residual_t, gain, w_gate, w_up)
    got = lax.all_to_all(sent, "batch", 0, 0, tiled=True)

    steps = features // wide
    chunk = features // parts
    each = parts // steps
    flat = jax.ShapeDtypeStruct((per, units), F32)
    misfit, gate, up, hidden, scale = pl.pallas_call(
        lambda *refs: down_kernel(features, *refs),
        grid=(steps,),
        in_specs=[
            whole(got.shape),
            pl.BlockSpec((wide, units), lambda j: (j, 0)),
            pl.BlockSpec((wide, wide), lambda j: (0, j)),
        ],
        out_specs=[pl.BlockSpec((each, per, chunk), lambda j: (j, 0, 0))]
        + [whole((per, units))] * 3
        + [whole((per, 128))],
        out_shape=[
            jax.ShapeDtypeStruct((parts, per, chunk), BF),
            flat,
            flat,
            jax.ShapeDtypeStruct((per, units), BF),
            jax.ShapeDtypeStruct((per, 128), F32),
        ],
        scratch_shapes=[pltpu.VMEM((per, wide), BF)],
        compiler_params=params(16),
        name="down",
    )(got, down_full, projector)
    misfit = lax.all_to_all(misfit, "tensor", 0, 0, tiled=True)
    loss_scale = 1.0 / math.sqrt(live)
    grad_out = pl.pallas_call(
        lambda *refs: misfit_kernel(loss_scale, *refs),
        out_shape=jax.ShapeDtypeStruct(misfit.shape, BF),
        name="misfit",
    )(misfit)
    grad_out = lax.all_to_all(grad_out, "tensor", 0, 0, tiled=True)

    sent = pl.pallas_call(
        back_kernel,
        grid=(steps,),
        in_specs=[
            pl.BlockSpec((each, per, chunk), lambda j: (j, 0, 0)),
            pl.BlockSpec((wide, units), lambda j: (j, 0)),
        ]
        + [whole((per, units))] * 3
        + [whole((per, 128))],
        out_specs=whole((groups, per, 4 * wide)),
        out_shape=jax.ShapeDtypeStruct((groups, per, 4 * wide), BF),
        scratch_shapes=[pltpu.VMEM((per, units), F32)],
        compiler_params=params(16),
        name="back",
    )(grad_out, down_full, gate, up, hidden, scale)
    got = lax.all_to_all(sent, "batch", 0, 0, tiled=True)

    tile = wide // 4
    grads = pl.pallas_call(
        weights_kernel,
        grid=(4,),
        in_specs=[
            pl.BlockSpec((live, tile), lambda j: (0, j)),
            whole(got.shape),
            pl.BlockSpec((groups, per, tile), lambda j: (0, 0, 3 * wide // tile + j)),
        ],
        out_specs=[pl.BlockSpec((tile, units), lambda j: (j, 0))] * 3,
        out_shape=[jax.ShapeDtypeStruct((wide, units), F32)] * 3,
        compiler_params=params(16),
        name="weights",
    )(scaled, got, got)
    return (teacher_hidden, *grads)


def solution(mesh):
    in_specs = (
        P("batch", "tensor"),
        P("tensor", None),
        P("tensor", "batch"),
        P("tensor", None),
        P("batch", "tensor"),
        P(),
        P("batch", "tensor"),
        P("batch", "tensor"),
        P("batch", "tensor"),
        P("batch", None),
    )
    out_specs = (P("tensor", "batch"),) + (P("batch", "tensor"),) * 3
    return jax.shard_map(
        on_device, mesh=mesh, in_specs=in_specs, out_specs=out_specs, check_vma=False
    )
```

time: 289 us -> 179 us (0.62)
  waiting for transfers between devices: 160 us -> 43.1 us
  matrix products: 30 us -> 0 us
  Pallas kernels: 0 us -> 21.8 us
  starting transfers between devices: 8.01 us -> 22.5 us
  other arithmetic: 11.1 us -> 1.02 us
  local copies, waits for them, and re-layouts: 9.04 us -> 16.2 us
    reduce_scatter x1, waiting for transfers between devices: 83.2 us -> 0.03 us  [on_device(): summed = lax.psum_scatter(full, 'tensor', scatter_dimension=0, tiled=True)]
    all_gather x2 -> x1, waiting for transfers between devices: 74.6 us -> 3.12 us  [on_device(): down_full = lax.all_gather(w_down, 'batch', axis=0, tiled=True)]
    all_to_all x2, waiting for transfers between devices: 1.77 us -> 39.3 us  [the longest x1 26.5 us: on_device(): routed = lax.all_to_all(routed, 'tensor', 0, 0, tiled=True)]
    dot_general x9 -> x0, matrix products: 30 us -> none  [the longest x3 7.81 us: grouped_product(): lax.dot_general(left, right, dims, preferred_element_type=jnp.float32)]
    pallas_call x0 -> x7, Pallas kernels: none -> 21.8 us  [the longest x1 8.75 us: on_device(): pl.pallas_call(teacher_kernel, grid=(parts,), in_specs=[whole(route_index...]
    all_to_all x2, starting transfers between devices: 7.88 us -> 21 us  [the longest x1 17.4 us: on_device(): routed = lax.all_to_all(routed, 'tensor', 0, 0, tiled=True)]
    unnamed x26 -> x24, local copies, waits for them, and re-layouts: 3.15 us -> 14.5 us
    reduce_sum x5 -> x0, other arithmetic: 4.89 us -> none  [the longest x2 4.04 us: grouped_product(): return jnp.sum(rounded.astype(jnp.float32), axis=0)]
  transfers between devices with their start and end apart: 5 -> 5, of which waited for: 4 -> 3; matrix products, arithmetic and copies ran while one was open for 6% -> 2% of each run, Pallas kernels for 0% -> 11%
where the time goes in v1:
time: 179 us; the launch traced here: 177 us
  blocking collectives  57.1 us (32%)
  waiting for transfers between devices  43.1 us (24%)
  starting transfers between devices  22.5 us (13%)
  Pallas kernels  21.8 us (12%)
  local copies, waits for them, and re-layouts  16.2 us (9%)
  between operations  15.6 us (9%)
    all_to_all x1, blocking collectives, on_device(): got = lax.all_to_all(sent, 'batch', 0, 0, tiled=True)  27.2 us
    all_to_all x1, waiting for transfers between devices, on_device(): routed = lax.all_to_all(routed, 'tensor', 0, 0, tiled=True)  26.5 us
    all_to_all x1, starting transfers between devices, on_device(): routed = lax.all_to_all(routed, 'tensor', 0, 0, tiled=True)  17.4 us
    all_to_all x1, blocking collectives, on_device(): misfit = lax.all_to_all(misfit, 'tensor', 0, 0, tiled=True)  17 us
    unnamed x24, local copies, waits for them, and re-layouts  14.5 us
    all_to_all x1, blocking collectives, on_device(): grad_out = lax.all_to_all(grad_out, 'tensor', 0, 0, tiled=True)  12.9 us
    all_to_all x1, waiting for transfers between devices, on_device(): got = lax.all_to_all(sent, 'batch', 0, 0, tiled=True)  12.8 us
    pallas_call x1, Pallas kernels, on_device(): pl.pallas_call(teacher_kernel, grid=(parts,), in_specs=[whole(route_index...  8.75 us
  transfers between devices with their start and end apart: 5, of which 3 were waited for; matrix products, arithmetic and copies ran while one was open for 2% of the time, Pallas kernels for 11%

profile of v1, /device:TPU:0, one launch (start us, length us, event | category | flops | bytes accessed | tf_op | source)
XLA Modules:
  0.0 177.3 jit_solution(12918028619885740392)
XLA Ops:
  9.4 3.4 %copy-done.9 = bf16[512,8192]{1,0:T(8,128)(2,1)S(1)} copy-done((bf16[512,8192]{1,0:T(8,128)(2,1)S(1)}, bf16[512,8192]{1,0:T(8,128)(2,1)}, u32[]{:S(2)}) %copy-start.9) | copy-done | bytes 8388632
  12.8 0.9 copy-done.10
  13.8 8.8 %teacher.1 = (bf16[4096,512]{1,0:T(8,128)(2,1)S(1)}, bf16[16,104,512]{2,1,0:T(8,128)(2,1)}) custom-call(s32[1,64]{1,0:T(1,128)S(1)} %copy-done.7, bf16[256,512]{1,0:T(8,128)(2,1)S(1)} %copy-done.10, bf16[512,8192]{1,0:T(8,128)(2,1)S(1)} %copy-done.9), custom_call_target="tpu_custom_call" | custom-call | flops 2684354560 | bytes 14680064 | tf_op jit(solution)/shard_map/teacher/pallas_call | solution.py:242
  22.5 2.0 %copy-done.3 = bf16[4096,512]{1,0:T(8,128)(2,1)} copy-done((bf16[4096,512]{1,0:T(8,128)(2,1)}, bf16[4096,512]{1,0:T(8,128)(2,1)S(1)}, u32[]{:S(2)}) %copy-start.3) | copy-done | bytes 4194328
  24.6 1.7 rows.1
  26.3 1.4 collective-permute-start
  27.7 0.9 broadcast_dynamic-update-slice_fusion
  28.7 17.4 %all-to-all-start = ((bf16[16,104,512]{2,1,0:T(8,128)(2,1)}), bf16[16,104,512]{2,1,0:T(8,128)(2,1)S(1)}, u32[]{:S(2)}, u32[]{:S(2)}) async-start(bf16[16,104,512]{2,1,0:T(8,128)(2,1)} %broadcast_dynamic-update-slice_fusion), calls=%async_computation.1 | async-start | bytes 3407872 | tf_op jit(solution)/shard_map/all_to_all | solution.py:267
  46.9 26.5 %all-to-all-done.got_ref = bf16[16,104,512]{2,1,0:T(8,128)(2,1)S(1)} async-done(((bf16[16,104,512]{2,1,0:T(8,128)(2,1)}), bf16[16,104,512]{2,1,0:T(8,128)(2,1)S(1)}, u32[]{:S(2)}, u32[]{:S(2)}) %all-to-all-start) | async-done | bytes 1703968 | tf_op jit(solution)/shard_map/all_to_all | solution.py:267
  73.4 1.0 up.1
  74.3 27.2 %all_to_all.25.refs_0_ = bf16[8,32,1664]{2,1,0:T(8,128)(2,1)S(1)} all-to-all(bf16[8,32,1664]{2,1,0:T(8,128)(2,1)S(1)} %get-tuple-element.31), channel_id=1, replica_groups=mesh['batch'=8,'tensor'=16] {'batch'}, dimensions={0} | all-to-all | bytes 1703936 | tf_op jit(solution)/shard_map/all_to_all | solution.py:283
  101.5 3.1 %all-gather.2.cloned.1.call-done.refs_1_.down_ref = bf16[4096,512]{1,0:T(8,128)(2,1)} async-done(((bf16[512,512]{1,0:T(8,128)(2,1)}), bf16[4096,512]{1,0:T(8,128)(2,1)}) %all-gather.2.cloned.1.call-update) | async-done | bytes 4194320 | tf_op jit(solution)/shard_map/all_gather | solution.py:228
  104.6 2.2 %copy-done = bf16[4096,512]{1,0:T(8,128)(2,1)S(1)} copy-done((bf16[4096,512]{1,0:T(8,128)(2,1)S(1)}, bf16[4096,512]{1,0:T(8,128)(2,1)}, u32[]{:S(2)}) %copy-start) | copy-done | bytes 4194328
  106.8 2.2 %copy-done.2 = bf16[512,4096]{1,0:T(8,128)(2,1)S(1)} copy-done((bf16[512,4096]{1,0:T(8,128)(2,1)S(1)}, bf16[512,4096]{1,0:T(8,128)(2,1)}, u32[]{:S(2)}) %copy-start.2) | copy-done | bytes 4194328
  109.0 3.4 %down.1 = (bf16[16,32,256]{2,1,0:T(8,128)(2,1)S(1)}, f32[32,512]{1,0:T(8,128)S(1)}, f32[32,512]{1,0:T(8,128)S(1)}, bf16[32,512]{1,0:T(8,128)(2,1)S(1)}, f32[32,128]{1,0:T(8,128)S(1)}) custom-call(bf16[8,32,1664]{2,1,0:T(8,128)(2,1)S(1)} %all_to_all.25.refs_0_, bf16[4096,512]{1,0:T(8,128)(2,1)S(1)} %copy-done, bf16[512,4096]{1,0:T(8,128)(2,1)S(1)} %copy-done.2), custom_call_target="tpu_custom_call" | custom-call | tf_op jit(solution)/shard_map/down/pallas_call | solution.py:289
  112.4 17.0 %all_to_all.26.refs_0_ = bf16[16,32,256]{2,1,0:T(8,128)(2,1)} all-to-all(bf16[16,32,256]{2,1,0:T(8,128)(2,1)S(1)} %get-tuple-element.32), channel_id=1, replica_groups=mesh['batch'=8,'tensor'=16] {'tensor'}, dimensions={0} | all-to-all | bytes 524288 | tf_op jit(solution)/shard_map/all_to_all | solution.py:311
  129.4 1.7 misfit.1
  131.2 12.9 %all_to_all.27.got_ref = bf16[16,32,256]{2,1,0:T(8,128)(2,1)S(1)} all-to-all(bf16[16,32,256]{2,1,0:T(8,128)(2,1)} %misfit.1), channel_id=1, replica_groups=mesh['batch'=8,'tensor'=16] {'tensor'}, dimensions={0} | all-to-all | bytes 524288 | tf_op jit(solution)/shard_map/all_to_all | solution.py:318
  144.0 2.2 %copy-done.1 = bf16[4096,512]{1,0:T(8,128)(2,1)S(1)} copy-done((bf16[4096,512]{1,0:T(8,128)(2,1)S(1)}, bf16[4096,512]{1,0:T(8,128)(2,1)}, u32[]{:S(2)}) %copy-start.1) | copy-done | bytes 4194328
  146.2 2.7 %back.1 = bf16[8,32,2048]{2,1,0:T(8,128)(2,1)} custom-call(bf16[16,32,256]{2,1,0:T(8,128)(2,1)S(1)} %all_to_all.27.got_ref, bf16[4096,512]{1,0:T(8,128)(2,1)S(1)} %copy-done.1, f32[32,512]{1,0:T(8,128)S(1)} %get-tuple-element.33.gate_ref, f32[32,512]{1,0:T(8,128)S(1)} %get-tuple-element.34.up_ref, bf16[32,512]{1,0:T(8,128)(2,1)S(1)} %get-tuple-element.35.hidden_ref, ...), custom_call_target="tpu_custom_call" | custom-call | tf_op jit(solution)/shard_map/back/pallas_call | solution.py:320
  148.9 3.6 %all-to-all-start.4 = ((bf16[8,32,2048]{2,1,0:T(8,128)(2,1)}), bf16[8,32,2048]{2,1,0:T(8,128)(2,1)S(1)}, u32[]{:S(2)}, u32[]{:S(2)}) async-start(bf16[8,32,2048]{2,1,0:T(8,128)(2,1)} %back.1), calls=%async_computation.5 | async-start | bytes 2097152 | tf_op jit(solution)/shard_map/all_to_all | solution.py:335
  152.6 1.0 fusion
  154.5 12.8 %all-to-all-done.4.got_ref.grad_ref = bf16[8,32,2048]{2,1,0:T(8,128)(2,1)S(1)} async-done(((bf16[8,32,2048]{2,1,0:T(8,128)(2,1)}), bf16[8,32,2048]{2,1,0:T(8,128)(2,1)S(1)}, u32[]{:S(2)}, u32[]{:S(2)}) %all-to-all-start.4) | async-done | bytes 1048608 | tf_op jit(solution)/shard_map/all_to_all | solution.py:335
  167.3 2.6 %weights.1 = (f32[512,512]{1,0:T(8,128)}, f32[512,512]{1,0:T(8,128)}, f32[512,512]{1,0:T(8,128)}) custom-call(bf16[256,512]{1,0:T(8,128)(2,1)S(1)} %get-tuple-element.30.rows_ref, bf16[8,32,2048]{2,1,0:T(8,128)(2,1)S(1)} %all-to-all-done.4.got_ref.grad_ref, bf16[8,32,2048]{2,1,0:T(8,128)(2,1)S(1)} %all-to-all-done.4.got_ref.grad_ref), custom_call_target="tpu_custom_call" | custom-call | tf_op jit(solution)/shard_map/weights/pallas_call | solution.py:338
  (25 shorter events, 3.2 us)
Async XLA Ops:
  8.0 96.6 %all-gather.2.cloned.1.call-start = ((), (), s32[]{:S(2)}) async-start(), calls=%async_computation.7 | async-start | bytes 4718592 | tf_op jit(solution)/shard_map/all_gather | solution.py:228
  8.7 143.9 %reduce-scatter.2.cloned.1.call-start = ((), (), s32[]{:S(2)}) async-start(), calls=%async_computation.6 | async-start | bytes 4456448 | tf_op jit(solution)/shard_map/reduce_scatter | solution.py:263
  8.8 0.7 copy-start.7
  9.4 3.4 %copy-start.9 = (bf16[512,8192]{1,0:T(8,128)(2,1)S(1)}, bf16[512,8192]{1,0:T(8,128)(2,1)}, u32[]{:S(2)}) copy-start(bf16[512,8192]{1,0:T(8,128)(2,1)} %weight_ref.1) | copy-start | bytes 25165828
  12.8 0.9 copy-start.10
  22.5 2.0 %copy-start.3 = (bf16[4096,512]{1,0:T(8,128)(2,1)}, bf16[4096,512]{1,0:T(8,128)(2,1)S(1)}, u32[]{:S(2)}) copy-start(bf16[4096,512]{1,0:T(8,128)(2,1)S(1)} %get-tuple-element.28) | copy-start | bytes 12582916
  26.3 1.4 collective-permute-start
  28.6 44.7 %copy-start.4 = (bf16[512,256]{1,0:T(8,128)(2,1)S(1)}, bf16[512,256]{1,0:T(8,128)(2,1)}, u32[]{:S(2)}) copy-start(bf16[512,256]{1,0:T(8,128)(2,1)} %residual_ref.1) | copy-start | bytes 786436
  28.6 44.7 %copy-start.5 = (bf16[512,512]{1,0:T(8,128)(2,1)S(1)}, bf16[512,512]{1,0:T(8,128)(2,1)}, u32[]{:S(2)}) copy-start(bf16[512,512]{1,0:T(8,128)(2,1)} %gate_ref.1) | copy-start | bytes 1572868
  28.7 44.7 %copy-start.6 = (bf16[512,512]{1,0:T(8,128)(2,1)S(1)}, bf16[512,512]{1,0:T(8,128)(2,1)}, u32[]{:S(2)}) copy-start(bf16[512,512]{1,0:T(8,128)(2,1)} %up_ref.1) | copy-start | bytes 1572868
  28.7 44.7 %copy-start.8 = (s32[1,64]{1,0:T(1,128)S(1)}, s32[1,64]{1,0:T(1,128)}, u32[]{:S(2)}) copy-start(s32[1,64]{1,0:T(1,128)} %route_ref.5) | copy-start | bytes 772
  28.7 44.7 %all-to-all-start = ((bf16[16,104,512]{2,1,0:T(8,128)(2,1)}), bf16[16,104,512]{2,1,0:T(8,128)(2,1)S(1)}, u32[]{:S(2)}, u32[]{:S(2)}) async-start(bf16[16,104,512]{2,1,0:T(8,128)(2,1)} %broadcast_dynamic-update-slice_fusion), calls=%async_computation.1 | async-start | bytes 3407872 | tf_op jit(solution)/shard_map/all_to_all | solution.py:267
  104.6 2.2 %copy-start = (bf16[4096,512]{1,0:T(8,128)(2,1)S(1)}, bf16[4096,512]{1,0:T(8,128)(2,1)}, u32[]{:S(2)}) copy-start(bf16[4096,512]{1,0:T(8,128)(2,1)} %all-gather.2.cloned.1.call-done.refs_1_.down_ref) | copy-start | bytes 12582916
  106.8 2.2 %copy-start.2 = (bf16[512,4096]{1,0:T(8,128)(2,1)S(1)}, bf16[512,4096]{1,0:T(8,128)(2,1)}, u32[]{:S(2)}) copy-start(bf16[512,4096]{1,0:T(8,128)(2,1)} %refs_2_.1) | copy-start | bytes 12582916
  144.0 2.2 %copy-start.1 = (bf16[4096,512]{1,0:T(8,128)(2,1)S(1)}, bf16[4096,512]{1,0:T(8,128)(2,1)}, u32[]{:S(2)}) copy-start(bf16[4096,512]{1,0:T(8,128)(2,1)} %all-gather.2.cloned.1.call-done.refs_1_.down_ref) | copy-start | bytes 12582916
  148.9 18.4 %all-to-all-start.4 = ((bf16[8,32,2048]{2,1,0:T(8,128)(2,1)}), bf16[8,32,2048]{2,1,0:T(8,128)(2,1)S(1)}, u32[]{:S(2)}, u32[]{:S(2)}) async-start(bf16[8,32,2048]{2,1,0:T(8,128)(2,1)} %back.1), calls=%async_computation.5 | async-start | bytes 2097152 | tf_op jit(solution)/shard_map/all_to_all | solution.py:335
Sparse Core Ops, SparseCore 0:
  10.6 94.0 all-gather.1
Sparse Core Ops, SparseCore 1:
  24.6 102.8 reduce-scatter.1

commit v2 on v1

v2 whole, which is shorter than its diff:
```python
import math

import jax
import jax.numpy as jnp
from jax import lax
from jax.experimental import pallas as pl
from jax.experimental.pallas import tpu as pltpu
from jax.sharding import PartitionSpec as P

EPS = 1e-05
BF = jnp.bfloat16
F32 = jnp.float32
MIB = 1 << 20


def params(mib):
    return pltpu.CompilerParams(vmem_limit_bytes=mib * MIB)


def cost(flops, nbytes):
    return pl.CostEstimate(flops=flops, bytes_accessed=nbytes, transcendentals=0)


def dot(a, b, ca=1, cb=0):
    return lax.dot_general(a, b, (((ca,), (cb,)), ((), ())), preferred_element_type=F32)


def whole(shape):
    return pl.BlockSpec(shape, lambda *_: (0,) * len(shape))


def slot_rows(route, tokens):
    slots = route.shape[1]
    grid = (slots, slots)
    diagonal = lax.broadcasted_iota(jnp.int32, grid, 0) == lax.broadcasted_iota(jnp.int32, grid, 1)
    spread = jnp.broadcast_to(route.astype(F32), grid)
    column = jnp.sum(jnp.where(diagonal, spread, 0.0), axis=1, keepdims=True)
    lane = lax.broadcasted_iota(jnp.int32, (slots, tokens), 1).astype(F32)
    return jnp.where(lane == column, 1.0, 0.0).astype(BF)


def rows_kernel(route_ref, x_ref, out_ref):
    route = route_ref[...]
    slots, wide = route.shape[1], x_ref.shape[1]
    rows = dot(slot_rows(route, x_ref.shape[0]), x_ref[...]).astype(BF)
    half = slots // 2
    out_ref[0:half, 0:wide] = rows[0:half]
    out_ref[0:half, wide : 2 * wide] = rows[half:]
    live = jnp.sum(jnp.where(route >= 0, 1.0, 0.0), axis=1, keepdims=True)
    out_ref[half : half + 8, :] = jnp.broadcast_to(live, (8, 2 * wide)).astype(BF)


def teacher_kernel(
    core_ref, route_ref, attn_ref, weight_ref, keep_ref, send_ref, routed_ref, left_ref
):
    step = pl.program_id(0)
    tokens = attn_ref.shape[0]
    slots = route_ref.shape[1]

    @pl.when(step == 0)
    def _():
        left_ref[0:tokens, :] = attn_ref[...]
        left_ref[tokens:, :] = dot(slot_rows(route_ref[...], tokens), attn_ref[...]).astype(BF)

    product = dot(left_ref[...], weight_ref[...]).astype(BF)
    routed_ref[0, 0:slots, :] = product[tokens:]

    @pl.when(step % 2 == 0)
    def _():
        send_ref[...] = product[0:tokens]

    @pl.when(step % 2 == 1)
    def _():
        keep_ref[...] = product[0:tokens]


def core_sum_kernel(x_ref, keep_ref, got_ref, *out_refs):
    total = (keep_ref[...].astype(F32) + got_ref[...].astype(F32)).astype(BF)
    for j, out_ref in enumerate(out_refs):

        @pl.when(pl.program_id(0) // 2 == j)
        def _(out_ref=out_ref):
            out_ref[...] = total


def x_sum_kernel(y_ref, *refs):
    total = refs[0][...].astype(F32)
    for ref in refs[1:-2]:
        total = total + ref[...].astype(F32)
    for j, out_ref in enumerate(refs[-2:]):

        @pl.when(pl.program_id(0) == j)
        def _(out_ref=out_ref):
            out_ref[...] = total.astype(out_ref.dtype)


def residual_kernel(residual_ref, keep_ref, got_ref, out_ref):
    summed = keep_ref[...] + got_ref[...].astype(F32)
    out_ref[...] = (residual_ref[...].astype(F32) + summed.T).astype(BF)


def up_kernel(
    group_ref, route_ref, got_ref, residual_ref, gain_ref, gate_ref, up_ref,
    out_ref, rows_ref, chosen_ref, padded_ref,
):
    slots = route_ref.shape[1]
    sources, _, wide = got_ref.shape
    groups = sources // 2
    half, side = slots // 2, wide // 2
    per = out_ref.shape[1]
    total = groups * per

    routed = dot(slot_rows(route_ref[...], residual_ref.shape[1]), residual_ref[...], 1, 1)
    for s in range(sources):
        routed = routed + got_ref[s, 0:slots, :].astype(F32)
        g, d = s // 2, s % 2
        block = got_ref[s, slots : slots + half, :]
        padded_ref[g * slots : g * slots + half, d * side : (d + 1) * side] = block[:, 0:side]
        padded_ref[g * slots + half : (g + 1) * slots, d * side : (d + 1) * side] = block[:, side:]
    routed = routed.astype(BF)
    at = slots + half
    counts = [got_ref[2 * g, at : at + 8, 0 : 2 * slots].astype(F32)[0:1] for g in range(groups)]

    row = lax.broadcasted_iota(jnp.int32, (total, 2 * slots), 0)
    lane = lax.broadcasted_iota(jnp.int32, (total, 2 * slots), 1)
    second = lane >= slots
    slot = jnp.where(second, lane - slots, lane)
    slot_f = slot.astype(F32)
    shift = (row - slot).astype(F32)
    x = jnp.zeros((total, wide), F32)
    run = jnp.zeros_like(counts[0])
    for q in range(groups // 2):
        one, two = counts[2 * q], counts[2 * q + 1]
        start = jnp.where(second, run + one, run)
        count = jnp.where(second, two, one)
        run = run + one + two
        chosen = jnp.where((shift == start) & (slot_f < count), 1.0, 0.0).astype(BF)
        chosen_ref[:, 2 * q * slots : 2 * (q + 1) * slots] = chosen
        x = x + dot(chosen, padded_ref[2 * q * slots : 2 * (q + 1) * slots, :])

    square = jnp.sum(x * x, axis=1, keepdims=True)
    high = square.astype(BF)
    low = (square - high.astype(F32)).astype(BF)
    lane128 = lax.broadcasted_iota(jnp.int32, (total, 128), 1)
    squares = jnp.where(lane128 < 64, high.astype(F32), low.astype(F32)).astype(BF)
    scaled = (x * gain_ref[...]).astype(BF)
    rows_ref[...] = scaled
    gate = dot(scaled, gate_ref[...]).astype(BF)
    up = dot(scaled, up_ref[...]).astype(BF)
    at = 2 * wide + 128
    for g in range(groups):
        own = slice(g * per, (g + 1) * per)
        out_ref[g, :, 0:wide] = gate[own]
        out_ref[g, :, wide : 2 * wide] = up[own]
        out_ref[g, :, 2 * wide : at] = squares[own]
        for h in range(slots // per):
            out_ref[g, :, at + h * wide : at + (h + 1) * wide] = routed[h * per : (h + 1) * per]


def hidden_kernel(features, got_ref, out_ref, gate_ref, up_ref, scale_ref):
    wide = gate_ref.shape[1]
    at = 2 * wide + 128
    total = got_ref[0, :, 0:at].astype(F32)
    for g in range(1, got_ref.shape[0]):
        total = total + got_ref[g, :, 0:at].astype(F32)
    square = total[:, 2 * wide : 2 * wide + 1] + total[:, 2 * wide + 64 : 2 * wide + 65]
    scale = lax.rsqrt(square * (1.0 / features) + EPS)
    gate = total[:, 0:wide] * scale
    up = total[:, wide : 2 * wide] * scale
    gate_ref[...] = gate
    up_ref[...] = up
    scale_ref[...] = jnp.broadcast_to(scale, scale_ref.shape)
    hidden = (gate * jax.nn.sigmoid(gate) * up).astype(BF)
    for g in range(out_ref.shape[0]):
        out_ref[g] = hidden


def target_kernel(group_ref, got_ref, chosen_ref, projector_ref, out_ref, rows_ref):
    groups, per, _ = got_ref.shape
    wide = rows_ref.shape[1]
    parts = rows_ref.shape[0] // (groups * per)
    at = got_ref.shape[2] - parts * wide
    for g in range(groups):
        for h in range(parts):
            first = (g * parts + h) * per
            rows_ref[first : first + per, :] = got_ref[g, :, at + h * wide : at + (h + 1) * wide]
    rows = dot(chosen_ref[...], rows_ref[...]).astype(BF)
    out_ref[...] = dot(rows, projector_ref[...])


def down_kernel(got_ref, down_ref, target_ref, out_ref):
    rows, wide = target_ref.shape
    part = dot(got_ref[...].reshape(rows, wide), down_ref[...], 1, 1) - target_ref[...]
    out_ref[...] = part.astype(BF).reshape(out_ref.shape)


def misfit_kernel(scale, got_ref, out_ref):
    total = got_ref[0].astype(F32)
    for s in range(1, got_ref.shape[0]):
        total = total + got_ref[s].astype(F32)
    grad = (total * scale).astype(BF)
    for s in range(out_ref.shape[0]):
        out_ref[s] = grad


def back_kernel(got_ref, down_ref, out_ref):
    groups, per, wide = out_ref.shape
    part = dot(got_ref[...].reshape(groups * per, got_ref.shape[2]), down_ref[...])
    out_ref[...] = part.astype(BF).reshape(groups, per, wide)


def acts_kernel(got_ref, gate_ref, up_ref, scale_ref, out_ref):
    wide = gate_ref.shape[1]
    grad = got_ref[0].astype(F32)
    for g in range(1, got_ref.shape[0]):
        grad = grad + got_ref[g].astype(F32)
    grad = grad * scale_ref[:, 0:1]
    gate, up = gate_ref[...], up_ref[...]
    sigma = jax.nn.sigmoid(gate)
    grad_gate = (grad * up * sigma * (1.0 + gate * (1.0 - sigma))).astype(BF)
    grad_up = (grad * gate * sigma).astype(BF)
    for g in range(out_ref.shape[0]):
        out_ref[g, :, 0:wide] = grad_gate
        out_ref[g, :, wide : 2 * wide] = grad_up


def down_weights_kernel(grad_ref, hidden_ref, out_ref):
    rows = hidden_ref.shape[0] * hidden_ref.shape[1]
    wide = out_ref.shape[0]
    out_ref[...] = dot(grad_ref[...].reshape(rows, wide), hidden_ref[...].reshape(rows, -1), 0, 0)


def weights_kernel(rows_ref, got_ref, gate_ref, up_ref):
    wide = gate_ref.shape[1]
    acts = got_ref[...].reshape(got_ref.shape[0] * got_ref.shape[1], 2 * wide)
    gate_ref[...] = dot(rows_ref[...], acts[:, 0:wide], 0, 0)
    up_ref[...] = dot(rows_ref[...], acts[:, wide:], 0, 0)


def on_device(
    attn_values,
    out_weight,
    residual_t,
    projector,
    student_input,
    norm_gain,
    w_gate,
    w_up,
    w_down,
    route_index,
):
    groups, parts = lax.axis_size("batch"), lax.axis_size("tensor")
    slots = route_index.shape[1]
    tokens, wide = attn_values.shape
    side = student_input.shape[1]
    features = norm_gain.shape[0]
    live = tokens * groups // 8
    per = live // groups
    units = w_gate.shape[1]
    extra = slots // 2 + 8
    group, part = lax.axis_index("batch"), lax.axis_index("tensor")
    core, x_at, y_at = part & 1, (part >> 1) & 3, part >> 3
    shape = jax.ShapeDtypeStruct
    vmem = pl.BlockSpec(memory_space=pltpu.VMEM)

    rows = pl.pallas_call(
        rows_kernel,
        out_shape=shape((extra, 2 * side), BF),
        cost_estimate=cost(2 * slots * tokens * side, MIB // 4),
        name="rows",
    )(route_index, student_input)
    pairs = [
        (b * parts + t, (t // 2) * parts + 2 * b + t % 2)
        for b in range(groups)
        for t in range(parts)
    ]
    rows = lax.ppermute(rows, ("batch", "tensor"), pairs)

    def column(j, core):
        return 2 * (j >> 1) + jnp.where((j & 1) == 0, 1 - core[0], core[0])

    keep, send, routed = pl.pallas_call(
        teacher_kernel,
        grid_spec=pltpu.PrefetchScalarGridSpec(
            num_scalar_prefetch=1,
            grid=(parts,),
            in_specs=[
                pl.BlockSpec(route_index.shape, lambda j, core: (0, 0)),
                pl.BlockSpec(attn_values.shape, lambda j, core: (0, 0)),
                pl.BlockSpec((wide, wide), lambda j, core: (0, column(j, core))),
            ],
            out_specs=[
                pl.BlockSpec((tokens, wide), lambda j, core: (j >> 1, 0)),
                pl.BlockSpec((tokens, wide), lambda j, core: (j >> 1, 0)),
                pl.BlockSpec((1, slots + extra, wide), lambda j, core: (column(j, core), 0, 0)),
            ],
            scratch_shapes=[pltpu.VMEM((tokens + slots, wide), BF)],
        ),
        out_shape=[
            shape((parts // 2 * tokens, wide), BF),
            shape((parts // 2 * tokens, wide), BF),
            shape((parts, slots + extra, wide), BF),
        ],
        compiler_params=params(56),
        cost_estimate=cost(2 * (tokens + slots) * wide * wide * parts, 14 * MIB),
        name="teacher",
    )(core.reshape(1), route_index, attn_values, out_weight)

    routed = routed.at[:, slots:, :].set(jnp.broadcast_to(rows[None], (parts, *rows.shape)))
    routed = lax.all_to_all(routed, "tensor", 0, 0, tiled=True)

    def along(value, move):
        return lax.ppermute(value, "tensor", [(t, move(t // 8, (t // 2) % 4, t % 2)) for t in range(parts)])

    got = along(send, lambda y, x, c: y * 8 + x * 2 + 1 - c)
    block = shape((2 * tokens, wide), BF)
    sums = pl.pallas_call(
        core_sum_kernel,
        grid_spec=pltpu.PrefetchScalarGridSpec(
            num_scalar_prefetch=1,
            grid=(8,),
            in_specs=[
                pl.BlockSpec((tokens, wide), lambda g, x: ((g & 1) * 4 + ((x[0] + (g >> 1)) & 3), 0))
            ]
            * 2,
            out_specs=[
                pl.BlockSpec((tokens, wide), lambda g, x, j=j: (jnp.clip(g - 2 * j, 0, 1), 0))
                for j in range(4)
            ],
        ),
        out_shape=[block] * 4,
        compiler_params=params(16),
        cost_estimate=cost(MIB, 6 * MIB),
        name="core_sum",
    )(x_at.reshape(1), keep, got)
    others = [
        along(sums[j], lambda y, x, c, j=j: y * 8 + (x + j) % 4 * 2 + c) for j in range(1, 4)
    ]
    send, keep = pl.pallas_call(
        x_sum_kernel,
        grid_spec=pltpu.PrefetchScalarGridSpec(
            num_scalar_prefetch=1,
            grid=(2,),
            in_specs=[
                pl.BlockSpec((tokens, wide), lambda g, y: (jnp.where(g == 0, 1 - y[0], y[0]), 0))
            ]
            * 4,
            out_specs=[pl.BlockSpec((tokens, wide), lambda g, y: (0, 0))] * 2,
        ),
        out_shape=[shape((tokens, wide), BF), shape((tokens, wide), F32)],
        compiler_params=params(16),
        cost_estimate=cost(MIB, 3 * MIB),
        name="x_sum",
    )(y_at.reshape(1), sums[0], *others)
    got = along(send, lambda y, x, c: (1 - y) * 8 + x * 2 + c)
    teacher_hidden = pl.pallas_call(
        residual_kernel,
        out_shape=shape(residual_t.shape, BF),
        compiler_params=params(16),
        cost_estimate=cost(MIB, 2 * MIB),
        name="residual",
    )(residual_t, keep, got)

    packed = 2 * wide + 128 + slots // per * wide
    sent, scaled, chosen = pl.pallas_call(
        up_kernel,
        grid_spec=pltpu.PrefetchScalarGridSpec(
            num_scalar_prefetch=1,
            grid=(1,),
            in_specs=[
                vmem,
                vmem,
                vmem,
                pl.BlockSpec((1, wide), lambda i, group: (0, group[0])),
                vmem,
                vmem,
            ],
            out_specs=[vmem] * 3,
            scratch_shapes=[pltpu.VMEM((groups * slots, wide), BF)],
        ),
        out_shape=[
            shape((groups, per, packed), BF),
            shape((live, wide), BF),
            shape((live, groups * slots), BF),
        ],
        compiler_params=params(24),
        cost_estimate=cost(800 * MIB, 4 * MIB),
        name="up",
    )(group.reshape(1), route_index, routed, residual_t, norm_gain[None], w_gate, w_up)
    got = lax.all_to_all(sent, "batch", 0, 0, tiled=True)

    flat = shape((per, units), F32)
    hidden, gate, up, scale = pl.pallas_call(
        lambda *refs: hidden_kernel(features, *refs),
        out_shape=[shape((groups, per, units), BF), flat, flat, shape((per, 128), F32)],
        cost_estimate=cost(MIB, MIB),
        name="hidden",
    )(got)
    hidden = lax.all_to_all(hidden, "batch", 0, 0, tiled=True)
    target = pl.pallas_call(
        target_kernel,
        grid_spec=pltpu.PrefetchScalarGridSpec(
            num_scalar_prefetch=1,
            grid=(1,),
            in_specs=[vmem, vmem, pl.BlockSpec((wide, wide), lambda i, group: (0, group[0]))],
            out_specs=vmem,
            scratch_shapes=[pltpu.VMEM((groups * slots, wide), BF)],
        ),
        out_shape=shape((live, wide), F32),
        compiler_params=params(16),
        cost_estimate=cost(512 * MIB, 3 * MIB),
        name="target",
    )(group.reshape(1), got, chosen, projector)
    misfit = pl.pallas_call(
        down_kernel,
        out_shape=shape((parts, live // parts, wide), BF),
        compiler_params=params(16),
        cost_estimate=cost(256 * MIB, 2 * MIB),
        name="down",
    )(hidden, w_down, target)
    misfit = lax.all_to_all(misfit, "tensor", 0, 0, tiled=True)
    loss_scale = 1.0 / math.sqrt(live)
    grad_out = pl.pallas_call(
        lambda *refs: misfit_kernel(loss_scale, *refs),
        out_shape=shape(misfit.shape, BF),
        cost_estimate=cost(MIB, MIB),
        name="misfit",
    )(misfit)
    grad_out = lax.all_to_all(grad_out, "tensor", 0, 0, tiled=True)
    back = pl.pallas_call(
        back_kernel,
        out_shape=shape((groups, per, units), BF),
        compiler_params=params(16),
        cost_estimate=cost(256 * MIB, MIB),
        name="back",
    )(grad_out, w_down)
    back = lax.all_to_all(back, "batch", 0, 0, tiled=True)
    acts = pl.pallas_call(
        acts_kernel,
        out_shape=shape((groups, per, 2 * units), BF),
        cost_estimate=cost(MIB, MIB),
        name="acts",
    )(back, gate, up, scale)
    acts = lax.all_to_all(acts, "batch", 0, 0, tiled=True)
    grad_down = pl.pallas_call(
        down_weights_kernel,
        out_shape=shape((wide, units), F32),
        compiler_params=params(16),
        cost_estimate=cost(256 * MIB, 2 * MIB),
        name="down_weights",
    )(grad_out, hidden)
    grad_gate, grad_up = pl.pallas_call(
        weights_kernel,
        out_shape=[shape((wide, units), F32)] * 2,
        compiler_params=params(16),
        cost_estimate=cost(512 * MIB, 4 * MIB),
        name="weights",
    )(scaled, acts)
    return teacher_hidden, grad_gate, grad_up, grad_down


def solution(mesh):
    in_specs = (
        P("batch", "tensor"),
        P("tensor", None),
        P("tensor", "batch"),
        P("tensor", None),
        P("batch", "tensor"),
        P(),
        P("batch", "tensor"),
        P("batch", "tensor"),
        P("batch", "tensor"),
        P("batch", None),
    )
    out_specs = (P("tensor", "batch"),) + (P("batch", "tensor"),) * 3
    return jax.shard_map(
        on_device, mesh=mesh, in_specs=in_specs, out_specs=out_specs, check_vma=False
    )
```

time: 179 us -> 162 us (0.905)
  between operations: 15.6 us -> 0.81 us
  Pallas kernels: 21.8 us -> 35.9 us
  blocking collectives: 57.1 us -> 43.7 us
  starting transfers between devices: 22.5 us -> 32.9 us
  local copies, waits for them, and re-layouts: 16.2 us -> 6.47 us
  waiting for transfers between devices: 43.1 us -> 40.8 us
    pallas_call x6 -> x13, Pallas kernels: 20.1 us -> 34.2 us  [the longest x1 14.7 us: on_device(): pl.pallas_call(teacher_kernel, grid_spec=pltpu.PrefetchScalarGridSpec(num...]
    ppermute x0 -> x5, waiting for transfers between devices: none -> 11.8 us  [along(): lax.ppermute(value, 'tensor', [(t, move(t // 8, t // 2 % 4, t % 2)) for t...]
    ppermute x0 -> x5, starting transfers between devices: none -> 9.46 us  [along(): lax.ppermute(value, 'tensor', [(t, move(t // 8, t // 2 % 4, t % 2)) for t...]
    unnamed x24, local copies, waits for them, and re-layouts: 14.5 us -> 5.53 us
    all_to_all x1 -> x3, waiting for transfers between devices: 12.8 us -> 4.44 us  [the longest x1 4.44 us: on_device(): hidden = lax.all_to_all(hidden, 'batch', 0, 0, tiled=True)]
    all_to_all x1, blocking collectives: 27.2 us -> 20 us  [on_device(): got = lax.all_to_all(sent, 'batch', 0, 0, tiled=True)]
    all_to_all x1 -> x3, starting transfers between devices: 3.56 us -> 10.6 us  [the longest x1 3.62 us: on_device(): acts = lax.all_to_all(acts, 'batch', 0, 0, tiled=True)]
    all_to_all x1, starting transfers between devices: 17.4 us -> 11.5 us  [on_device(): routed = lax.all_to_all(routed, 'tensor', 0, 0, tiled=True)]
  transfers between devices with their start and end apart: 5 -> 10, of which waited for: 3 -> 4; matrix products, arithmetic and copies ran while one was open for 2% -> 0% of each run, Pallas kernels for 11% -> 20%
where the time goes in v2:
time: 162 us; the launch traced here: 161 us
  blocking collectives  43.7 us (27%)
  waiting for transfers between devices  40.8 us (25%)
  Pallas kernels  35.9 us (22%)
  starting transfers between devices  32.9 us (20%)
  local copies, waits for them, and re-layouts  6.47 us (4%)
    all_to_all x1, waiting for transfers between devices, on_device(): routed = lax.all_to_all(routed, 'tensor', 0, 0, tiled=True)  24.6 us
    all_to_all x1, blocking collectives, on_device(): got = lax.all_to_all(sent, 'batch', 0, 0, tiled=True)  20 us
    pallas_call x1, Pallas kernels, on_device(): pl.pallas_call(teacher_kernel, grid_spec=pltpu.PrefetchScalarGridSpec(num...  14.7 us
    all_to_all x1, blocking collectives, on_device(): misfit = lax.all_to_all(misfit, 'tensor', 0, 0, tiled=True)  13.4 us
    ppermute x5, waiting for transfers between devices, along(): lax.ppermute(value, 'tensor', [(t, move(t // 8, t // 2 % 4, t % 2)) for t...  11.8 us
    all_to_all x1, starting transfers between devices, on_device(): routed = lax.all_to_all(routed, 'tensor', 0, 0, tiled=True)  11.5 us
    all_to_all x1, blocking collectives, on_device(): back = lax.all_to_all(back, 'batch', 0, 0, tiled=True)  10.3 us
    ppermute x5, starting transfers between devices, along(): lax.ppermute(value, 'tensor', [(t, move(t // 8, t // 2 % 4, t % 2)) for t...  9.46 us
  transfers between devices with their start and end apart: 10, of which 4 were waited for; matrix products, arithmetic and copies ran while one was open for 0% of the time, Pallas kernels for 20%

profile of v2, /device:TPU:0, one launch (start us, length us, event | category | flops | bytes accessed | tf_op | source)
XLA Modules:
  0.0 160.6 jit_solution(15816189601889842538)
XLA Ops:
  0.6 1.7 %rows.1 = bf16[40,512]{1,0:T(8,128)(2,1)} custom-call(s32[1,64]{1,0:T(1,128)} %route_ref.5, bf16[256,256]{1,0:T(8,128)(2,1)} %x_ref.1), custom_call_target="tpu_custom_call" | custom-call | flops 8388608 | bytes 262144 | tf_op jit(solution)/shard_map/rows/pallas_call | solution.py:266
  3.8 14.7 %teacher.1 = (bf16[2048,512]{1,0:T(8,128)(2,1)}, bf16[2048,512]{1,0:T(8,128)(2,1)}, bf16[16,104,512]{2,1,0:T(8,128)(2,1)}) custom-call(s32[1]{0:T(128)} %bitcast.2.core_ref, s32[1,64]{1,0:T(1,128)} %route_ref.5, bf16[256,512]{1,0:T(8,128)(2,1)} %attn_ref.1, bf16[512,8192]{1,0:T(8,128)(2,1)} %weight_ref.1), custom_call_target="tpu_custom_call" | custom-call | flops 2684354560 | bytes 14680064 | tf_op jit(solution)/shard_map/teacher/pallas_call | solution.py:282
  19.5 11.5 %all-to-all-start = ((bf16[16,104,512]{2,1,0:T(8,128)(2,1)}), bf16[16,104,512]{2,1,0:T(8,128)(2,1)S(1)}, u32[]{:S(2)}, u32[]{:S(2)}) async-start(bf16[16,104,512]{2,1,0:T(8,128)(2,1)} %broadcast_dynamic-update-slice_fusion), calls=%async_computation | async-start | bytes 3407872 | tf_op jit(solution)/shard_map/all_to_all | solution.py:310
  31.4 24.6 %all-to-all-done.got_ref = bf16[16,104,512]{2,1,0:T(8,128)(2,1)S(1)} async-done(((bf16[16,104,512]{2,1,0:T(8,128)(2,1)}), bf16[16,104,512]{2,1,0:T(8,128)(2,1)S(1)}, u32[]{:S(2)}, u32[]{:S(2)}) %all-to-all-start) | async-done | bytes 1703968 | tf_op jit(solution)/shard_map/all_to_all | solution.py:310
  58.8 20.0 %all_to_all.35.refs_0_.got_ref = bf16[8,32,2176]{2,1,0:T(8,128)(2,1)} all-to-all(bf16[8,32,2176]{2,1,0:T(8,128)(2,1)S(1)} %get-tuple-element.44), channel_id=1, replica_groups=mesh['batch'=8,'tensor'=16] {'batch'}, dimensions={0} | all-to-all | bytes 2228224 | tf_op jit(solution)/shard_map/all_to_all | solution.py:390
  78.8 2.3 %hidden.1 = (bf16[8,32,512]{2,1,0:T(8,128)(2,1)}, f32[32,512]{1,0:T(8,128)}, f32[32,512]{1,0:T(8,128)}, f32[32,128]{1,0:T(8,128)}) custom-call(bf16[8,32,2176]{2,1,0:T(8,128)(2,1)} %all_to_all.35.refs_0_.got_ref), custom_call_target="tpu_custom_call" | custom-call | flops 1048576 | bytes 1048576 | tf_op jit(solution)/shard_map/hidden/pallas_call | solution.py:393
  81.0 3.4 %all-to-all-start.2 = ((bf16[8,32,512]{2,1,0:T(8,128)(2,1)}), bf16[8,32,512]{2,1,0:T(8,128)(2,1)S(1)}, u32[]{:S(2)}, u32[]{:S(2)}) async-start(bf16[8,32,512]{2,1,0:T(8,128)(2,1)} %get-tuple-element.45), calls=%async_computation.2 | async-start | bytes 524288 | tf_op jit(solution)/shard_map/all_to_all | solution.py:399
  84.5 2.2 %copy-done.1 = bf16[512,4096]{1,0:T(8,128)(2,1)S(1)} copy-done((bf16[512,4096]{1,0:T(8,128)(2,1)S(1)}, bf16[512,4096]{1,0:T(8,128)(2,1)}, u32[]{:S(2)}) %copy-start.1) | copy-done | bytes 4194328
  87.2 4.4 %all-to-all-done.2.got_ref.hidden_ref = bf16[8,32,512]{2,1,0:T(8,128)(2,1)S(1)} async-done(((bf16[8,32,512]{2,1,0:T(8,128)(2,1)}), bf16[8,32,512]{2,1,0:T(8,128)(2,1)S(1)}, u32[]{:S(2)}, u32[]{:S(2)}) %all-to-all-start.2) | async-done | bytes 262176 | tf_op jit(solution)/shard_map/all_to_all | solution.py:399
  92.0 13.4 %all_to_all.36.refs_0_ = bf16[16,16,512]{2,1,0:T(8,128)(2,1)} all-to-all(bf16[16,16,512]{2,1,0:T(8,128)(2,1)S(1)} %down.1), channel_id=1, replica_groups=mesh['batch'=8,'tensor'=16] {'tensor'}, dimensions={0} | all-to-all | bytes 524288 | tf_op jit(solution)/shard_map/all_to_all | solution.py:421
  105.3 1.7 %misfit.1 = bf16[16,16,512]{2,1,0:T(8,128)(2,1)} custom-call(bf16[16,16,512]{2,1,0:T(8,128)(2,1)} %all_to_all.36.refs_0_), custom_call_target="tpu_custom_call" | custom-call | flops 1048576 | bytes 1048576 | tf_op jit(solution)/shard_map/misfit/pallas_call | solution.py:423
  107.1 3.5 %all-to-all-start.4 = ((bf16[16,16,512]{2,1,0:T(8,128)(2,1)}), bf16[16,16,512]{2,1,0:T(8,128)(2,1)S(1)}, u32[]{:S(2)}, u32[]{:S(2)}) async-start(bf16[16,16,512]{2,1,0:T(8,128)(2,1)} %misfit.1), calls=%async_computation.4 | async-start | bytes 524288 | tf_op jit(solution)/shard_map/all_to_all | solution.py:429
  110.6 1.6 copy-done.3
  112.2 6.1 %core_sum.1 = (bf16[512,512]{1,0:T(8,128)(2,1)S(1)}, bf16[512,512]{1,0:T(8,128)(2,1)}, bf16[512,512]{1,0:T(8,128)(2,1)}, bf16[512,512]{1,0:T(8,128)(2,1)}) custom-call(s32[1]{0:T(128)} %bitcast.1.x_ref, bf16[2048,512]{1,0:T(8,128)(2,1)S(1)} %copy-done.3, bf16[2048,512]{1,0:T(8,128)(2,1)} %collective-permute-done.got_ref), custom_call_target="tpu_custom_call" | custom-call | flops 1048576 | bytes 6291456 | tf_op jit(solution)/shard_map/core_sum/pallas_call | solution.py:317
  118.3 1.8 %collective-permute-start.1 = (bf16[512,512]{1,0:T(8,128)(2,1)}, bf16[512,512]{1,0:T(8,128)(2,1)S(1)}, u32[]{:S(2)}, u32[]{:S(2)}) collective-permute-start(bf16[512,512]{1,0:T(8,128)(2,1)} %get-tuple-element.37), channel_id=1, source_target_pairs={{0,2},{1,3},{2,4},{3,5},{4,6},{5,7},{6,0},{7,1},{8,10},{9,11},{10,... | collective-permute-start | bytes 1572872 | tf_op jit(solution)/shard_map/ppermute | solution.py:313
  120.1 2.7 %collective-permute-start.2 = (bf16[512,512]{1,0:T(8,128)(2,1)}, bf16[512,512]{1,0:T(8,128)(2,1)S(1)}, u32[]{:S(2)}, u32[]{:S(2)}) collective-permute-start(bf16[512,512]{1,0:T(8,128)(2,1)} %get-tuple-element.38), channel_id=1, source_target_pairs={{0,4},{1,5},{2,6},{3,7},{4,0},{5,1},{6,2},{7,3},{8,12},{9,13},{10,... | collective-permute-start | bytes 1572872 | tf_op jit(solution)/shard_map/ppermute | solution.py:313
  124.6 10.3 %all_to_all.37.got_ref = bf16[8,32,512]{2,1,0:T(8,128)(2,1)} all-to-all(bf16[8,32,512]{2,1,0:T(8,128)(2,1)S(1)} %back.1), channel_id=1, replica_groups=mesh['batch'=8,'tensor'=16] {'batch'}, dimensions={0} | all-to-all | bytes 524288 | tf_op jit(solution)/shard_map/all_to_all | solution.py:437
  134.8 1.9 %acts.1 = bf16[8,32,1024]{2,1,0:T(8,128)(2,1)} custom-call(bf16[8,32,512]{2,1,0:T(8,128)(2,1)} %all_to_all.37.got_ref, f32[32,512]{1,0:T(8,128)} %get-tuple-element.47.gate_ref, f32[32,512]{1,0:T(8,128)} %get-tuple-element.48.up_ref, f32[32,128]{1,0:T(8,128)} %get-tuple-element.49.scale_ref), custom_call_target="tpu_custom_call" | custom-call | flops 1048576 | bytes 1048576 | tf_op jit(solution)/shard_map/acts/pallas_call | solution.py:438
  136.8 3.6 %all-to-all-start.6 = ((bf16[8,32,1024]{2,1,0:T(8,128)(2,1)}), bf16[8,32,1024]{2,1,0:T(8,128)(2,1)S(1)}, u32[]{:S(2)}, u32[]{:S(2)}) async-start(bf16[8,32,1024]{2,1,0:T(8,128)(2,1)} %acts.1), calls=%async_computation.6 | async-start | bytes 1048576 | tf_op jit(solution)/shard_map/all_to_all | solution.py:444
  140.4 5.8 %collective-permute-done.2.refs_2_ = bf16[512,512]{1,0:T(8,128)(2,1)S(1)} collective-permute-done((bf16[512,512]{1,0:T(8,128)(2,1)}, bf16[512,512]{1,0:T(8,128)(2,1)S(1)}, u32[]{:S(2)}, u32[]{:S(2)}) %collective-permute-start.2) | collective-permute-done | bytes 524320 | tf_op jit(solution)/shard_map/ppermute | solution.py:313
  146.2 1.5 x_sum.1
  147.7 3.1 %collective-permute-start.4 = (bf16[256,512]{1,0:T(8,128)(2,1)S(1)}, bf16[256,512]{1,0:T(8,128)(2,1)S(1)}, u32[]{:S(2)}, u32[]{:S(2)}) collective-permute-start(bf16[256,512]{1,0:T(8,128)(2,1)S(1)} %get-tuple-element.41), channel_id=1, source_target_pairs={{0,8},{1,9},{2,10},{3,11},{4,12},{5,13},{6,14},{7,15},{8,0},{9,1},... | collective-permute-start | bytes 786440 | tf_op jit(solution)/shard_map/ppermute | solution.py:313
  150.8 6.0 %collective-permute-done.4.got_ref = bf16[256,512]{1,0:T(8,128)(2,1)S(1)} collective-permute-done((bf16[256,512]{1,0:T(8,128)(2,1)S(1)}, bf16[256,512]{1,0:T(8,128)(2,1)S(1)}, u32[]{:S(2)}, u32[]{:S(2)}) %collective-permute-start.4) | collective-permute-done | bytes 262176 | tf_op jit(solution)/shard_map/ppermute | solution.py:313
  159.0 1.6 %weights.1 = (f32[512,512]{1,0:T(8,128)}, f32[512,512]{1,0:T(8,128)}) custom-call(bf16[256,512]{1,0:T(8,128)(2,1)S(1)} %copy-done.11, bf16[8,32,1024]{2,1,0:T(8,128)(2,1)S(1)} %all-to-all-done.6.got_ref), custom_call_target="tpu_custom_call" | custom-call | flops 536870912 | bytes 4194304 | tf_op jit(solution)/shard_map/weights/pallas_call | solution.py:452
  (38 shorter events, 10.4 us)
Async XLA Ops:
  2.4 16.2 %collective-permute-start.5 = (bf16[40,512]{1,0:T(8,128)(2,1)}, bf16[40,512]{1,0:T(8,128)(2,1)S(1)}, u32[]{:S(2)}, u32[]{:S(2)}) collective-permute-start(bf16[40,512]{1,0:T(8,128)(2,1)} %rows.1), channel_id=1, source_target_pairs={{0,0},{1,1},{2,16},{3,17},{4,32},{5,33},{6,48},{7,49},{8,64},{9,65... | collective-permute-start | bytes 122888 | tf_op jit(solution)/shard_map/ppermute | solution.py:277
  19.5 36.5 %copy-start.4 = (bf16[512,256]{1,0:T(8,128)(2,1)S(1)}, bf16[512,256]{1,0:T(8,128)(2,1)}, u32[]{:S(2)}) copy-start(bf16[512,256]{1,0:T(8,128)(2,1)} %residual_ref.3) | copy-start | bytes 786436
  19.5 36.5 %copy-start.6 = (s32[1,64]{1,0:T(1,128)S(1)}, s32[1,64]{1,0:T(1,128)}, u32[]{:S(2)}) copy-start(s32[1,64]{1,0:T(1,128)} %route_ref.5) | copy-start | bytes 772
  19.5 36.5 %copy-start.7 = (bf16[512,512]{1,0:T(8,128)(2,1)S(1)}, bf16[512,512]{1,0:T(8,128)(2,1)}, u32[]{:S(2)}) copy-start(bf16[512,512]{1,0:T(8,128)(2,1)} %gate_ref.1) | copy-start | bytes 1572868
  19.5 36.5 %copy-start.9 = (f32[4096]{0:T(1024)S(1)}, f32[4096]{0:T(1024)}, u32[]{:S(2)}) copy-start(f32[4096]{0:T(1024)} %param.17) | copy-start | bytes 49156
  19.5 36.5 %all-to-all-start = ((bf16[16,104,512]{2,1,0:T(8,128)(2,1)}), bf16[16,104,512]{2,1,0:T(8,128)(2,1)S(1)}, u32[]{:S(2)}, u32[]{:S(2)}) async-start(bf16[16,104,512]{2,1,0:T(8,128)(2,1)} %broadcast_dynamic-update-slice_fusion), calls=%async_computation | async-start | bytes 3407872 | tf_op jit(solution)/shard_map/all_to_all | solution.py:310
  31.0 79.6 %collective-permute-start = (bf16[2048,512]{1,0:T(8,128)(2,1)}, bf16[2048,512]{1,0:T(8,128)(2,1)}, u32[]{:S(2)}, u32[]{:S(2)}) collective-permute-start(bf16[2048,512]{1,0:T(8,128)(2,1)} %get-tuple-element.35), channel_id=1, source_target_pairs={{0,1},{1,0},{2,3},{3,2},{4,5},{5,4},{6,7},{7,6},{8,9},{9,8},{10,11... | collective-permute-start | bytes 6291464 | tf_op jit(solution)/shard_map/ppermute | solution.py:313
  56.0 1.0 copy-start.8
  58.1 0.7 copy-start.10
  78.8 5.7 %copy-start = (bf16[8,32,2176]{2,1,0:T(8,128)(2,1)S(1)}, bf16[8,32,2176]{2,1,0:T(8,128)(2,1)}, u32[]{:S(2)}) copy-start(bf16[8,32,2176]{2,1,0:T(8,128)(2,1)} %all_to_all.35.refs_0_.got_ref) | copy-start | bytes 3342340
  81.0 10.6 %all-to-all-start.2 = ((bf16[8,32,512]{2,1,0:T(8,128)(2,1)}), bf16[8,32,512]{2,1,0:T(8,128)(2,1)S(1)}, u32[]{:S(2)}, u32[]{:S(2)}) async-start(bf16[8,32,512]{2,1,0:T(8,128)(2,1)} %get-tuple-element.45), calls=%async_computation.2 | async-start | bytes 524288 | tf_op jit(solution)/shard_map/all_to_all | solution.py:399
  84.5 2.2 %copy-start.1 = (bf16[512,4096]{1,0:T(8,128)(2,1)S(1)}, bf16[512,4096]{1,0:T(8,128)(2,1)}, u32[]{:S(2)}) copy-start(bf16[512,4096]{1,0:T(8,128)(2,1)} %projector_ref.1) | copy-start | bytes 12582916
  86.7 5.0 %copy-start.2 = (bf16[512,512]{1,0:T(8,128)(2,1)S(1)}, bf16[512,512]{1,0:T(8,128)(2,1)}, u32[]{:S(2)}) copy-start(bf16[512,512]{1,0:T(8,128)(2,1)} %down_ref.3) | copy-start | bytes 1572868
  107.1 17.2 %all-to-all-start.4 = ((bf16[16,16,512]{2,1,0:T(8,128)(2,1)}), bf16[16,16,512]{2,1,0:T(8,128)(2,1)S(1)}, u32[]{:S(2)}, u32[]{:S(2)}) async-start(bf16[16,16,512]{2,1,0:T(8,128)(2,1)} %misfit.1), calls=%async_computation.4 | async-start | bytes 524288 | tf_op jit(solution)/shard_map/all_to_all | solution.py:429
  110.6 1.6 copy-start.3
  118.3 22.1 %collective-permute-start.1 = (bf16[512,512]{1,0:T(8,128)(2,1)}, bf16[512,512]{1,0:T(8,128)(2,1)S(1)}, u32[]{:S(2)}, u32[]{:S(2)}) collective-permute-start(bf16[512,512]{1,0:T(8,128)(2,1)} %get-tuple-element.37), channel_id=1, source_target_pairs={{0,2},{1,3},{2,4},{3,5},{4,6},{5,7},{6,0},{7,1},{8,10},{9,11},{10,... | collective-permute-start | bytes 1572872 | tf_op jit(solution)/shard_map/ppermute | solution.py:313
  120.1 26.1 %collective-permute-start.2 = (bf16[512,512]{1,0:T(8,128)(2,1)}, bf16[512,512]{1,0:T(8,128)(2,1)S(1)}, u32[]{:S(2)}, u32[]{:S(2)}) collective-permute-start(bf16[512,512]{1,0:T(8,128)(2,1)} %get-tuple-element.38), channel_id=1, source_target_pairs={{0,4},{1,5},{2,6},{3,7},{4,0},{5,1},{6,2},{7,3},{8,12},{9,13},{10,... | collective-permute-start | bytes 1572872 | tf_op jit(solution)/shard_map/ppermute | solution.py:313
  122.8 23.4 %collective-permute-start.3 = (bf16[512,512]{1,0:T(8,128)(2,1)}, bf16[512,512]{1,0:T(8,128)(2,1)}, u32[]{:S(2)}, u32[]{:S(2)}) collective-permute-start(bf16[512,512]{1,0:T(8,128)(2,1)} %get-tuple-element.39), channel_id=1, source_target_pairs={{0,6},{1,7},{2,0},{3,1},{4,2},{5,3},{6,4},{7,5},{8,14},{9,15},{10,... | collective-permute-start | bytes 1572872 | tf_op jit(solution)/shard_map/ppermute | solution.py:313
  136.8 20.0 %copy-start.5 = (bf16[512,256]{1,0:T(8,128)(2,1)S(1)}, bf16[512,256]{1,0:T(8,128)(2,1)}, u32[]{:S(2)}) copy-start(bf16[512,256]{1,0:T(8,128)(2,1)} %residual_ref.3) | copy-start | bytes 786436
  136.8 22.2 %all-to-all-start.6 = ((bf16[8,32,1024]{2,1,0:T(8,128)(2,1)}), bf16[8,32,1024]{2,1,0:T(8,128)(2,1)S(1)}, u32[]{:S(2)}, u32[]{:S(2)}) async-start(bf16[8,32,1024]{2,1,0:T(8,128)(2,1)} %acts.1), calls=%async_computation.6 | async-start | bytes 1048576 | tf_op jit(solution)/shard_map/all_to_all | solution.py:444
  147.7 11.3 %copy-start.11 = (bf16[256,512]{1,0:T(8,128)(2,1)S(1)}, bf16[256,512]{1,0:T(8,128)(2,1)}, u32[]{:S(2)}) copy-start(bf16[256,512]{1,0:T(8,128)(2,1)} %copy-done.10) | copy-start | bytes 786436
  147.7 9.1 %collective-permute-start.4 = (bf16[256,512]{1,0:T(8,128)(2,1)S(1)}, bf16[256,512]{1,0:T(8,128)(2,1)S(1)}, u32[]{:S(2)}, u32[]{:S(2)}) collective-permute-start(bf16[256,512]{1,0:T(8,128)(2,1)S(1)} %get-tuple-element.41), channel_id=1, source_target_pairs={{0,8},{1,9},{2,10},{3,11},{4,12},{5,13},{6,14},{7,15},{8,0},{9,1},... | collective-permute-start | bytes 786440 | tf_op jit(solution)/shard_map/ppermute | solution.py:313

commit v3 on v2

--- a/solution.py
+++ b/solution.py
@@ -51,58 +51,68 @@
 
 
 def teacher_kernel(
-    core_ref, route_ref, attn_ref, weight_ref, keep_ref, send_ref, routed_ref, left_ref
+    core_ref, route_ref, attn_ref, mine_ref, other_ref, keep_ref, send_ref, routed_ref, left_ref
 ):
-    step = pl.program_id(0)
     tokens = attn_ref.shape[0]
     slots = route_ref.shape[1]
 
-    @pl.when(step == 0)
+    @pl.when(pl.program_id(0) == 0)
     def _():
         left_ref[0:tokens, :] = attn_ref[...]
         left_ref[tokens:, :] = dot(slot_rows(route_ref[...], tokens), attn_ref[...]).astype(BF)
 
-    product = dot(left_ref[...], weight_ref[...]).astype(BF)
-    routed_ref[0, 0:slots, :] = product[tokens:]
-
-    @pl.when(step % 2 == 0)
-    def _():
-        send_ref[...] = product[0:tokens]
-
-    @pl.when(step % 2 == 1)
-    def _():
-        keep_ref[...] = product[0:tokens]
-
-
-def core_sum_kernel(x_ref, keep_ref, got_ref, *out_refs):
-    total = (keep_ref[...].astype(F32) + got_ref[...].astype(F32)).astype(BF)
-    for j, out_ref in enumerate(out_refs):
-
-        @pl.when(pl.program_id(0) // 2 == j)
-        def _(out_ref=out_ref):
-            out_ref[...] = total
+    core = core_ref[0]
+    for weight_ref, out_ref, place in ((other_ref, send_ref, 1 - core), (mine_ref, keep_ref, core)):
+        product = dot(left_ref[...], weight_ref[...]).astype(BF)
+        out_ref[0] = product[0:tokens]
+        routed_ref[place, 0:slots, :] = product[tokens:]
+
+
+def pack_kernel(rows_ref, routed_ref, send_ref, out_ref, same_ref, sems):
+    first = routed_ref.shape[1] - rows_ref.shape[0]
+    copies = [
+        pltpu.make_async_copy(
+            rows_ref, out_ref.at[s, first : routed_ref.shape[1], :], sems.at[s]
+        )
+        for s in range(routed_ref.shape[0])
+    ]
+    for copy in copies:
+        copy.start()
+    for copy in copies:
+        copy.wait()
+
+
+def core_sum_kernel(x_ref, *refs):
+    ways = len(refs) // 3
+    for j in range(ways):
+        total = refs[j][...].astype(F32) + refs[ways + j][...].astype(F32)
+        refs[2 * ways + j][...] = total.astype(BF).reshape(refs[2 * ways + j].shape)
 
 
 def x_sum_kernel(y_ref, *refs):
-    total = refs[0][...].astype(F32)
-    for ref in refs[1:-2]:
-        total = total + ref[...].astype(F32)
-    for j, out_ref in enumerate(refs[-2:]):
-
-        @pl.when(pl.program_id(0) == j)
-        def _(out_ref=out_ref):
-            out_ref[...] = total.astype(out_ref.dtype)
+    ways = len(refs) // 2 - 1
+    for i, out_ref in enumerate(refs[-2:]):
+        total = refs[i * ways][...].astype(F32)
+        for ref in refs[i * ways + 1 : (i + 1) * ways]:
+            total = total + ref[...].astype(F32)
+        out_ref[...] = total.astype(out_ref.dtype)
 
 
 def residual_kernel(residual_ref, keep_ref, got_ref, out_ref):
-    summed = keep_ref[...] + got_ref[...].astype(F32)
+    summed = keep_ref[0] + got_ref[0].astype(F32)
     out_ref[...] = (residual_ref[...].astype(F32) + summed.T).astype(BF)
 
 
 def up_kernel(
-    group_ref, route_ref, got_ref, residual_ref, gain_ref, gate_ref, up_ref,
-    out_ref, rows_ref, chosen_ref, padded_ref,
+    group_ref, route_ref, got_ref, residual_ref, gain_ref, gate_ref, up_ref, s1, s2, s3,
+    out_ref, rows_ref, chosen_ref, t1, t2, t3, padded_ref, weights_ref, sems,
 ):
+    loads = [
+        pltpu.make_async_copy(ref, weights_ref.at[i], sems.at[i])
+        for i, ref in enumerate((gate_ref, up_ref))
+    ]
+    for load in loads:
+        load.start()
     slots = route_ref.shape[1]
     sources, _, wide = got_ref.shape
     groups = sources // 2
@@ -145,8 +155,10 @@
     squares = jnp.where(lane128 < 64, high.astype(F32), low.astype(F32)).astype(BF)
     scaled = (x * gain_ref[...]).astype(BF)
     rows_ref[...] = scaled
-    gate = dot(scaled, gate_ref[...]).astype(BF)
-    up = dot(scaled, up_ref[...]).astype(BF)
+    for load in loads:
+        load.wait()
+    gate = dot(scaled, weights_ref[0]).astype(BF)
+    up = dot(scaled, weights_ref[1]).astype(BF)
     at = 2 * wide + 128
     for g in range(groups):
         own = slice(g * per, (g + 1) * per)
@@ -188,7 +200,7 @@
     out_ref[...] = dot(rows, projector_ref[...])
 
 
-def down_kernel(got_ref, down_ref, target_ref, out_ref):
+def down_kernel(got_ref, down_ref, target_ref, passed_ref, out_ref, same_ref):
     rows, wide = target_ref.shape
     part = dot(got_ref[...].reshape(rows, wide), down_ref[...], 1, 1) - target_ref[...]
     out_ref[...] = part.astype(BF).reshape(out_ref.shape)
@@ -203,7 +215,7 @@
         out_ref[s] = grad
 
 
-def back_kernel(got_ref, down_ref, out_ref):
+def back_kernel(got_ref, down_ref, passed_ref, out_ref, same_ref):
     groups, per, wide = out_ref.shape
     part = dot(got_ref[...].reshape(groups * per, got_ref.shape[2]), down_ref[...])
     out_ref[...] = part.astype(BF).reshape(groups, per, wide)
@@ -262,11 +274,16 @@
     core, x_at, y_at = part & 1, (part >> 1) & 3, part >> 3
     shape = jax.ShapeDtypeStruct
     vmem = pl.BlockSpec(memory_space=pltpu.VMEM)
+    anywhere = pl.BlockSpec(memory_space=pl.ANY)
+    w_gate, w_up, w_down, projector = (
+        pltpu.with_memory_space_constraint(w, pltpu.HBM) for w in (w_gate, w_up, w_down, projector)
+    )
 
     rows = pl.pallas_call(
         rows_kernel,
-        out_shape=shape((extra, 2 * side), BF),
+        out_shape=pltpu.HBM((extra, 2 * side), BF),
         cost_estimate=cost(2 * slots * tokens * side, MIB // 4),
+        compiler_params=params(4),
         name="rows",
     )(route_index, student_input)
     pairs = [
@@ -276,93 +293,72 @@
     ]
     rows = lax.ppermute(rows, ("batch", "tensor"), pairs)
 
-    def column(j, core):
-        return 2 * (j >> 1) + jnp.where((j & 1) == 0, 1 - core[0], core[0])
-
     keep, send, routed = pl.pallas_call(
         teacher_kernel,
         grid_spec=pltpu.PrefetchScalarGridSpec(
             num_scalar_prefetch=1,
-            grid=(parts,),
+            grid=(parts // 2,),
             in_specs=[
                 pl.BlockSpec(route_index.shape, lambda j, core: (0, 0)),
                 pl.BlockSpec(attn_values.shape, lambda j, core: (0, 0)),
-                pl.BlockSpec((wide, wide), lambda j, core: (0, column(j, core))),
+                pl.BlockSpec((wide, wide), lambda j, core: (0, 2 * j + core[0])),
+                pl.BlockSpec((wide, wide), lambda j, core: (0, 2 * j + 1 - core[0])),
             ],
             out_specs=[
-                pl.BlockSpec((tokens, wide), lambda j, core: (j >> 1, 0)),
-                pl.BlockSpec((tokens, wide), lambda j, core: (j >> 1, 0)),
-                pl.BlockSpec((1, slots + extra, wide), lambda j, core: (column(j, core), 0, 0)),
+                pl.BlockSpec((1, tokens, wide), lambda j, core: (j, 0, 0)),
+                pl.BlockSpec((1, tokens, wide), lambda j, core: (j, 0, 0)),
+                pl.BlockSpec((2, slots + extra, wide), lambda j, core: (j, 0, 0)),
             ],
             scratch_shapes=[pltpu.VMEM((tokens + slots, wide), BF)],
         ),
         out_shape=[
-            shape((parts // 2 * tokens, wide), BF),
-            shape((parts // 2 * tokens, wide), BF),
+            shape((parts // 2, tokens, wide), BF),
+            shape((parts // 2, tokens, wide), BF),
             shape((parts, slots + extra, wide), BF),
         ],
         compiler_params=params(56),
         cost_estimate=cost(2 * (tokens + slots) * wide * wide * parts, 14 * MIB),
         name="teacher",
-    )(core.reshape(1), route_index, attn_values, out_weight)
-
-    routed = routed.at[:, slots:, :].set(jnp.broadcast_to(rows[None], (parts, *rows.shape)))
+    )(core.reshape(1), route_index, attn_values, out_weight, out_weight)
+
+    routed, send = pl.pallas_call(
+        pack_kernel,
+        in_specs=[vmem, anywhere, anywhere],
+        out_specs=[anywhere] * 2,
+        out_shape=[pltpu.HBM(routed.shape, BF), pltpu.HBM(send.shape, BF)],
+        scratch_shapes=[pltpu.SemaphoreType.DMA((parts,))],
+        input_output_aliases={1: 0, 2: 1},
+        compiler_params=params(4),
+        cost_estimate=cost(0, MIB),
+        name="pack",
+    )(rows, routed, send)
     routed = lax.all_to_all(routed, "tensor", 0, 0, tiled=True)
 
     def along(value, move):
         return lax.ppermute(value, "tensor", [(t, move(t // 8, (t // 2) % 4, t % 2)) for t in range(parts)])
 
     got = along(send, lambda y, x, c: y * 8 + x * 2 + 1 - c)
-    block = shape((2 * tokens, wide), BF)
+    strip = tokens // 2
     sums = pl.pallas_call(
         core_sum_kernel,
         grid_spec=pltpu.PrefetchScalarGridSpec(
             num_scalar_prefetch=1,
-            grid=(8,),
+            grid=(2, tokens // strip),
             in_specs=[
-                pl.BlockSpec((tokens, wide), lambda g, x: ((g & 1) * 4 + ((x[0] + (g >> 1)) & 3), 0))
+                pl.BlockSpec((1, strip, wide), lambda y, i, x, j=j: (4 * y + ((x[0] + j) & 3), i, 0))
+                for j in range(4)
             ]
             * 2,
-            out_specs=[
-                pl.BlockSpec((tokens, wide), lambda g, x, j=j: (jnp.clip(g - 2 * j, 0, 1), 0))
-                for j in range(4)
-            ],
+            out_specs=[pl.BlockSpec((1, strip, wide), lambda y, i, x: (y, i, 0))] * 4,
         ),
-        out_shape=[block] * 4,
+        out_shape=[pltpu.HBM((2, tokens, wide), BF)] * 4,
         compiler_params=params(16),
         cost_estimate=cost(MIB, 6 * MIB),
         name="core_sum",
-    )(x_at.reshape(1), keep, got)
-    others = [
-        along(sums[j], lambda y, x, c, j=j: y * 8 + (x + j) % 4 * 2 + c) for j in range(1, 4)
-    ]
-    send, keep = pl.pallas_call(
-        x_sum_kernel,
-        grid_spec=pltpu.PrefetchScalarGridSpec(
-            num_scalar_prefetch=1,
-            grid=(2,),
-            in_specs=[
-                pl.BlockSpec((tokens, wide), lambda g, y: (jnp.where(g == 0, 1 - y[0], y[0]), 0))
-            ]
-            * 4,
-            out_specs=[pl.BlockSpec((tokens, wide), lambda g, y: (0, 0))] * 2,
-        ),
-        out_shape=[shape((tokens, wide), BF), shape((tokens, wide), F32)],
-        compiler_params=params(16),
-        cost_estimate=cost(MIB, 3 * MIB),
-        name="x_sum",
-    )(y_at.reshape(1), sums[0], *others)
-    got = along(send, lambda y, x, c: (1 - y) * 8 + x * 2 + c)
-    teacher_hidden = pl.pallas_call(
-        residual_kernel,
-        out_shape=shape(residual_t.shape, BF),
-        compiler_params=params(16),
-        cost_estimate=cost(MIB, 2 * MIB),
-        name="residual",
-    )(residual_t, keep, got)
+    )(x_at.reshape(1), *[keep] * 4, *[got] * 4)
 
     packed = 2 * wide + 128 + slots // per * wide
-    sent, scaled, chosen = pl.pallas_call(
+    sent, scaled, chosen, *moved = pl.pallas_call(
         up_kernel,
         grid_spec=pltpu.PrefetchScalarGridSpec(
             num_scalar_prefetch=1,
@@ -372,28 +368,52 @@
                 vmem,
                 vmem,
                 pl.BlockSpec((1, wide), lambda i, group: (0, group[0])),
-                vmem,
-                vmem,
+            ]
+            + [anywhere] * 5,
+            out_specs=[vmem] * 3 + [anywhere] * 3,
+            scratch_shapes=[
+                pltpu.VMEM((groups * slots, wide), BF),
+                pltpu.VMEM((2, wide, units), BF),
+                pltpu.SemaphoreType.DMA((2,)),
             ],
-            out_specs=[vmem] * 3,
-            scratch_shapes=[pltpu.VMEM((groups * slots, wide), BF)],
         ),
         out_shape=[
-            shape((groups, per, packed), BF),
-            shape((live, wide), BF),
-            shape((live, groups * slots), BF),
-        ],
-        compiler_params=params(24),
+            pltpu.HBM((groups, per, packed), BF),
+            pltpu.HBM((live, wide), BF),
+            pltpu.HBM((live, groups * slots), BF),
+        ]
+        + [pltpu.HBM((2, tokens, wide), BF)] * 3,
+        input_output_aliases={7: 3, 8: 4, 9: 5},
+        compiler_params=params(16),
         cost_estimate=cost(800 * MIB, 4 * MIB),
         name="up",
-    )(group.reshape(1), route_index, routed, residual_t, norm_gain[None], w_gate, w_up)
+    )(group.reshape(1), route_index, routed, residual_t, norm_gain[None], w_gate, w_up, *sums[1:])
+    others = [
+        along(moved[j - 1], lambda y, x, c, j=j: y * 8 + (x + j) % 4 * 2 + c) for j in range(1, 4)
+    ]
+    send, keep = pl.pallas_call(
+        x_sum_kernel,
+        grid_spec=pltpu.PrefetchScalarGridSpec(
+            num_scalar_prefetch=1,
+            grid=(tokens // strip,),
+            in_specs=[pl.BlockSpec((1, strip, wide), lambda i, y: (1 - y[0], i, 0))] * 4
+            + [pl.BlockSpec((1, strip, wide), lambda i, y: (y[0], i, 0))] * 4,
+            out_specs=[pl.BlockSpec((1, strip, wide), lambda i, y: (0, i, 0))] * 2,
+        ),
+        out_shape=[pltpu.HBM((1, tokens, wide), BF), pltpu.HBM((1, tokens, wide), F32)],
+        compiler_params=params(16),
+        cost_estimate=cost(MIB, 3 * MIB),
+        name="x_sum",
+    )(y_at.reshape(1), *[sums[0], *others] * 2)
+
     got = lax.all_to_all(sent, "batch", 0, 0, tiled=True)
 
     flat = shape((per, units), F32)
     hidden, gate, up, scale = pl.pallas_call(
         lambda *refs: hidden_kernel(features, *refs),
-        out_shape=[shape((groups, per, units), BF), flat, flat, shape((per, 128), F32)],
+        out_shape=[pltpu.HBM((groups, per, units), BF), flat, flat, shape((per, 128), F32)],
         cost_estimate=cost(MIB, MIB),
+        compiler_params=params(8),
         name="hidden",
     )(got)
     hidden = lax.all_to_all(hidden, "batch", 0, 0, tiled=True)
@@ -411,34 +431,50 @@
         cost_estimate=cost(512 * MIB, 3 * MIB),
         name="target",
     )(group.reshape(1), got, chosen, projector)
-    misfit = pl.pallas_call(
+    misfit, send = pl.pallas_call(
         down_kernel,
-        out_shape=shape((parts, live // parts, wide), BF),
+        in_specs=[vmem] * 3 + [anywhere],
+        out_specs=[vmem, anywhere],
+        out_shape=[shape((parts, live // parts, wide), BF), pltpu.HBM(send.shape, BF)],
+        input_output_aliases={3: 1},
         compiler_params=params(16),
         cost_estimate=cost(256 * MIB, 2 * MIB),
         name="down",
-    )(hidden, w_down, target)
+    )(hidden, w_down, target, send)
+    got = along(send, lambda y, x, c: (1 - y) * 8 + x * 2 + c)
+    teacher_hidden = pl.pallas_call(
+        residual_kernel,
+        out_shape=shape(residual_t.shape, BF),
+        compiler_params=params(16),
+        cost_estimate=cost(MIB, 2 * MIB),
+        name="residual",
+    )(residual_t, keep, got)
     misfit = lax.all_to_all(misfit, "tensor", 0, 0, tiled=True)
     loss_scale = 1.0 / math.sqrt(live)
     grad_out = pl.pallas_call(
         lambda *refs: misfit_kernel(loss_scale, *refs),
         out_shape=shape(misfit.shape, BF),
         cost_estimate=cost(MIB, MIB),
+        compiler_params=params(8),
         name="misfit",
     )(misfit)
     grad_out = lax.all_to_all(grad_out, "tensor", 0, 0, tiled=True)
-    back = pl.pallas_call(
+    back, teacher_hidden = pl.pallas_call(
         back_kernel,
-        out_shape=shape((groups, per, units), BF),
+        in_specs=[vmem] * 2 + [anywhere],
+        out_specs=[vmem, anywhere],
+        out_shape=[shape((groups, per, units), BF), shape(residual_t.shape, BF)],
+        input_output_aliases={2: 1},
         compiler_params=params(16),
         cost_estimate=cost(256 * MIB, MIB),
         name="back",
-    )(grad_out, w_down)
+    )(grad_out, w_down, teacher_hidden)
     back = lax.all_to_all(back, "batch", 0, 0, tiled=True)
     acts = pl.pallas_call(
         acts_kernel,
         out_shape=shape((groups, per, 2 * units), BF),
         cost_estimate=cost(MIB, MIB),
+        compiler_params=params(8),
         name="acts",
     )(back, gate, up, scale)
     acts = lax.all_to_all(acts, "batch", 0, 0, tiled=True)

time: 162 us -> 148 us (0.914)
  blocking collectives: 43.7 us -> 11.9 us
  waiting for transfers between devices: 40.8 us -> 60.9 us
  starting transfers between devices: 32.9 us -> 38.9 us
  local copies, waits for them, and re-layouts: 6.47 us -> 2.23 us
  Pallas kernels: 35.9 us -> 31.8 us
    all_to_all x2 -> x0, blocking collectives: 33.4 us -> none  [the longest x1 20 us: on_device(): got = lax.all_to_all(sent, 'batch', 0, 0, tiled=True)]
    all_to_all x0 -> x2, waiting for transfers between devices: none -> 18.1 us  [the longest x1 12.2 us: on_device(): got = lax.all_to_all(sent, 'batch', 0, 0, tiled=True)]
    all_to_all x1, waiting for transfers between devices: 0.01 us -> 8.4 us  [on_device(): grad_out = lax.all_to_all(grad_out, 'tensor', 0, 0, tiled=True)]
    all_to_all x0 -> x2, starting transfers between devices: none -> 8.26 us  [the longest x1 4.55 us: on_device(): misfit = lax.all_to_all(misfit, 'tensor', 0, 0, tiled=True)]
    all_to_all x1, waiting for transfers between devices: 0.01 us -> 7.07 us  [on_device(): acts = lax.all_to_all(acts, 'batch', 0, 0, tiled=True)]
    ppermute x5, waiting for transfers between devices: 11.8 us -> 6.2 us  [along(): lax.ppermute(value, 'tensor', [(t, move(t // 8, t // 2 % 4, t % 2)) for t...]
    pallas_call x1, Pallas kernels: 14.7 us -> 9.55 us  [on_device(): pl.pallas_call(teacher_kernel, grid_spec=pltpu.PrefetchScalarGridSpec(num...]
    all_to_all x1, waiting for transfers between devices: 4.44 us -> 0.01 us  [on_device(): hidden = lax.all_to_all(hidden, 'batch', 0, 0, tiled=True)]
  transfers between devices with their start and end apart: 10 -> 12, of which waited for: 4 -> 7; matrix products, arithmetic and copies ran while one was open for 0% -> 0% of each run, Pallas kernels for 20% -> 14%
where the time goes in v3:
time: 148 us; the launch traced here: 147 us
  waiting for transfers between devices  60.9 us (41%)
  starting transfers between devices  38.9 us (26%)
  Pallas kernels  31.8 us (21%)
  blocking collectives  11.9 us (8%)
  local copies, waits for them, and re-layouts  2.23 us (2%)
    all_to_all x1, waiting for transfers between devices, on_device(): routed = lax.all_to_all(routed, 'tensor', 0, 0, tiled=True)  21.1 us
    all_to_all x1, waiting for transfers between devices, on_device(): got = lax.all_to_all(sent, 'batch', 0, 0, tiled=True)  12.2 us
    all_to_all x1, blocking collectives, on_device(): back = lax.all_to_all(back, 'batch', 0, 0, tiled=True)  11.9 us
    all_to_all x1, starting transfers between devices, on_device(): routed = lax.all_to_all(routed, 'tensor', 0, 0, tiled=True)  11.5 us
    pallas_call x1, Pallas kernels, on_device(): pl.pallas_call(teacher_kernel, grid_spec=pltpu.PrefetchScalarGridSpec(num...  9.55 us
    all_to_all x1, waiting for transfers between devices, on_device(): grad_out = lax.all_to_all(grad_out, 'tensor', 0, 0, tiled=True)  8.4 us
    all_to_all x1, waiting for transfers between devices, on_device(): acts = lax.all_to_all(acts, 'batch', 0, 0, tiled=True)  7.07 us
    ppermute x5, starting transfers between devices, along(): lax.ppermute(value, 'tensor', [(t, move(t // 8, t // 2 % 4, t % 2)) for t...  7.02 us
  transfers between devices with their start and end apart: 12, of which 7 were waited for; matrix products, arithmetic and copies ran while one was open for 0% of the time, Pallas kernels for 14%

profile of v3, /device:TPU:0, one launch (start us, length us, event | category | flops | bytes accessed | tf_op | source)
XLA Modules:
  0.0 146.6 jit_solution(16608897503111747710)
XLA Ops:
  3.0 1.4 collective-permute-start
  4.4 9.6 %teacher.1 = (bf16[8,256,512]{2,1,0:T(8,128)(2,1)}, bf16[8,256,512]{2,1,0:T(8,128)(2,1)}, bf16[16,104,512]{2,1,0:T(8,128)(2,1)}) custom-call(s32[1]{0:T(128)} %bitcast.1.core_ref, s32[1,64]{1,0:T(1,128)} %route_ref.5, bf16[256,512]{1,0:T(8,128)(2,1)} %attn_ref.1, bf16[512,8192]{1,0:T(8,128)(2,1)} %other_ref.1, bf16[512,8192]{1,0:T(8,128)(2,1)} %other_ref.1), custom_call_target="tpu_custom_call" | custom-call | flops 2684354560 | bytes 14680064 | tf_op jit(solution)/shard_map/teacher/pallas_call | solution.py:296
  15.1 11.5 %all-to-all-start = ((bf16[16,104,512]{2,1,0:T(8,128)(2,1)}), bf16[16,104,512]{2,1,0:T(8,128)(2,1)}, u32[]{:S(2)}, u32[]{:S(2)}) async-start(bf16[16,104,512]{2,1,0:T(8,128)(2,1)} %get-tuple-element.33), calls=%async_computation | async-start | bytes 3407872 | tf_op jit(solution)/shard_map/all_to_all | solution.py:335
  26.8 3.9 %core_sum.1 = (bf16[2,256,512]{2,1,0:T(8,128)(2,1)}, bf16[2,256,512]{2,1,0:T(8,128)(2,1)}, bf16[2,256,512]{2,1,0:T(8,128)(2,1)}, bf16[2,256,512]{2,1,0:T(8,128)(2,1)}) custom-call(s32[1]{0:T(128)} %bitcast.3.x_ref, bf16[8,256,512]{2,1,0:T(8,128)(2,1)S(1)} %copy-done, bf16[8,256,512]{2,1,0:T(8,128)(2,1)S(1)} %copy-done, bf16[8,256,512]{2,1,0:T(8,128)(2,1)S(1)} %copy-done, ...), custom_call_target="tpu_custom_call" | custom-call | flops 1048576 | bytes 6291456 | tf_op jit(solution)/shard_map/core_sum/pallas_call | solution.py:342
  30.6 21.1 %all-to-all-done.got_ref = bf16[16,104,512]{2,1,0:T(8,128)(2,1)} async-done(((bf16[16,104,512]{2,1,0:T(8,128)(2,1)}), bf16[16,104,512]{2,1,0:T(8,128)(2,1)}, u32[]{:S(2)}, u32[]{:S(2)}) %all-to-all-start) | async-done | bytes 1703968 | tf_op jit(solution)/shard_map/all_to_all | solution.py:335
  51.8 4.1 %up.1 = (bf16[8,32,2176]{2,1,0:T(8,128)(2,1)}, bf16[256,512]{1,0:T(8,128)(2,1)}, bf16[256,512]{1,0:T(8,128)(2,1)}, bf16[2,256,512]{2,1,0:T(8,128)(2,1)}, bf16[2,...) custom-call(s32[1]{0:T(128)} %bitcast.group_ref, ...), custom_call_target="tpu_custom_call", output_to_operand_aliasing={{3}: (7, {}), {4}: (8, {}), {5}: (9, {})} | custom-call | flops 838860800 | bytes 4194304 | tf_op jit(solution)/shard_map/up/pallas_call | solution.py:361
  55.9 3.7 %all-to-all-start.1 = ((bf16[8,32,2176]{2,1,0:T(8,128)(2,1)}), bf16[8,32,2176]{2,1,0:T(8,128)(2,1)S(1)}, u32[]{:S(2)}, u32[]{:S(2)}) async-start(bf16[8,32,2176]{2,1,0:T(8,128)(2,1)} %get-tuple-element.39), calls=%async_computation.1 | async-start | bytes 2228224 | tf_op jit(solution)/shard_map/all_to_all | solution.py:409
  60.0 1.7 %collective-permute-start.3 = (bf16[2,256,512]{2,1,0:T(8,128)(2,1)}, bf16[2,256,512]{2,1,0:T(8,128)(2,1)S(1)}, u32[]{:S(2)}, u32[]{:S(2)}) collective-permute-start(bf16[2,256,512]{2,1,0:T(8,128)(2,1)} %get-tuple-element.44), channel_id=1, source_target_pairs={{0,4},{1,5},{2,6},{3,7},{4,0},{5,1},{6,2},{7,3},{8,12},{9,13},{10,... | collective-permute-start | bytes 1572872 | tf_op jit(solution)/shard_map/ppermute | solution.py:338
  61.7 1.3 collective-permute-start.4
  63.1 12.2 %all-to-all-done.1.refs_0_.got_ref = bf16[8,32,2176]{2,1,0:T(8,128)(2,1)S(1)} async-done(((bf16[8,32,2176]{2,1,0:T(8,128)(2,1)}), bf16[8,32,2176]{2,1,0:T(8,128)(2,1)S(1)}, u32[]{:S(2)}, u32[]{:S(2)}) %all-to-all-start.1) | async-done | bytes 1114144 | tf_op jit(solution)/shard_map/all_to_all | solution.py:409
  76.8 3.6 %all-to-all-start.2 = ((bf16[8,32,512]{2,1,0:T(8,128)(2,1)}), bf16[8,32,512]{2,1,0:T(8,128)(2,1)S(1)}, u32[]{:S(2)}, u32[]{:S(2)}) async-start(bf16[8,32,512]{2,1,0:T(8,128)(2,1)} %get-tuple-element.40), calls=%async_computation.2 | async-start | bytes 524288 | tf_op jit(solution)/shard_map/all_to_all | solution.py:419
  80.4 5.6 %collective-permute-done.2.refs_1_.refs_5_ = bf16[2,256,512]{2,1,0:T(8,128)(2,1)S(1)} collective-permute-done((bf16[2,256,512]{2,1,0:T(8,128)(2,1)}, bf16[2,256,512]{2,1,0:T(8,128)(2,1)S(1)}, u32[]{:S(2)}, u32[]{:S(2)}) %collective-permute-start.2) | collective-permute-done | bytes 524320 | tf_op jit(solution)/shard_map/ppermute | solution.py:338
  87.6 1.5 %target.1.target_ref = f32[256,512]{1,0:T(8,128)S(1)} custom-call(s32[1]{0:T(128)} %bitcast.group_ref, bf16[8,32,2176]{2,1,0:T(8,128)(2,1)S(1)} %all-to-all-done.1.refs_0_.got_ref, bf16[256,512]{1,0:T(8,128)(2,1)S(1)} %copy-done.5, bf16[512,4096]{1,0:T(8,128)(2,1)} %projector_ref.1), custom_call_target="tpu_custom_call" | custom-call | flops 536870912 | bytes 3145728 | tf_op jit(solution)/shard_map/target/pallas_call | solution.py:420
  89.2 2.1 %down.1 = (bf16[16,16,512]{2,1,0:T(8,128)(2,1)}, bf16[1,256,512]{2,1,0:T(8,128)(2,1)}) custom-call(bf16[8,32,512]{2,1,0:T(8,128)(2,1)S(1)} %all-to-all-done.2.got_ref.hidden_ref, bf16[512,512]{1,0:T(8,128)(2,1)} %down_ref.3, f32[256,512]{1,0:T(8,128)S(1)} %target.1.target_ref, ...), custom_call_target="tpu_custom_call", output_to_operand_aliasing={{1}: (3, {})} | custom-call | flops 268435456 | bytes 2097152 | tf_op jit(solution)/shard_map/down/pallas_call | solution.py:434
  91.3 4.6 %all-to-all-start.3 = ((bf16[16,16,512]{2,1,0:T(8,128)(2,1)}), bf16[16,16,512]{2,1,0:T(8,128)(2,1)S(1)}, u32[]{:S(2)}, u32[]{:S(2)}) async-start(bf16[16,16,512]{2,1,0:T(8,128)(2,1)} %get-tuple-element.47), calls=%async_computation.3 | async-start | bytes 524288 | tf_op jit(solution)/shard_map/all_to_all | solution.py:452
  95.9 3.5 %collective-permute-start.5 = (bf16[1,256,512]{2,1,0:T(8,128)(2,1)}, bf16[1,256,512]{2,1,0:T(8,128)(2,1)S(1)}, u32[]{:S(2)}, u32[]{:S(2)}) collective-permute-start(bf16[1,256,512]{2,1,0:T(8,128)(2,1)} %get-tuple-element.49), channel_id=1, source_target_pairs={{0,8},{1,9},{2,10},{3,11},{4,12},{5,13},{6,14},{7,15},{8,0},{9,1},... | collective-permute-start | bytes 786440 | tf_op jit(solution)/shard_map/ppermute | solution.py:338
  99.4 5.9 %all-to-all-done.3.refs_0_ = bf16[16,16,512]{2,1,0:T(8,128)(2,1)S(1)} async-done(((bf16[16,16,512]{2,1,0:T(8,128)(2,1)}), bf16[16,16,512]{2,1,0:T(8,128)(2,1)S(1)}, u32[]{:S(2)}, u32[]{:S(2)}) %all-to-all-start.3) | async-done | bytes 262176 | tf_op jit(solution)/shard_map/all_to_all | solution.py:452
  106.0 3.5 %all-to-all-start.4 = ((bf16[16,16,512]{2,1,0:T(8,128)(2,1)}), bf16[16,16,512]{2,1,0:T(8,128)(2,1)S(1)}, u32[]{:S(2)}, u32[]{:S(2)}) async-start(bf16[16,16,512]{2,1,0:T(8,128)(2,1)} %misfit.1), calls=%async_computation.4 | async-start | bytes 524288 | tf_op jit(solution)/shard_map/all_to_all | solution.py:461
  110.5 8.4 %all-to-all-done.4.got_ref.grad_ref = bf16[16,16,512]{2,1,0:T(8,128)(2,1)S(1)} async-done(((bf16[16,16,512]{2,1,0:T(8,128)(2,1)}), bf16[16,16,512]{2,1,0:T(8,128)(2,1)S(1)}, u32[]{:S(2)}, u32[]{:S(2)}) %all-to-all-start.4) | async-done | bytes 262176 | tf_op jit(solution)/shard_map/all_to_all | solution.py:461
  118.9 1.3 back.1
  120.3 11.9 %all_to_all.35.got_ref = bf16[8,32,512]{2,1,0:T(8,128)(2,1)S(1)} all-to-all(bf16[8,32,512]{2,1,0:T(8,128)(2,1)S(1)} %get-tuple-element.52), channel_id=1, replica_groups=mesh['batch'=8,'tensor'=16] {'batch'}, dimensions={0} | all-to-all | bytes 524288 | tf_op jit(solution)/shard_map/all_to_all | solution.py:472
  133.1 3.5 %all-to-all-start.6 = ((bf16[8,32,1024]{2,1,0:T(8,128)(2,1)}), bf16[8,32,1024]{2,1,0:T(8,128)(2,1)S(1)}, u32[]{:S(2)}, u32[]{:S(2)}) async-start(bf16[8,32,1024]{2,1,0:T(8,128)(2,1)} %acts.1), calls=%async_computation.6 | async-start | bytes 1048576 | tf_op jit(solution)/shard_map/all_to_all | solution.py:480
  137.9 7.1 %all-to-all-done.6.got_ref = bf16[8,32,1024]{2,1,0:T(8,128)(2,1)S(1)} async-done(((bf16[8,32,1024]{2,1,0:T(8,128)(2,1)}), bf16[8,32,1024]{2,1,0:T(8,128)(2,1)S(1)}, u32[]{:S(2)}, u32[]{:S(2)}) %all-to-all-start.6) | async-done | bytes 524320 | tf_op jit(solution)/shard_map/all_to_all | solution.py:480
  144.9 1.6 %weights.1 = (f32[512,512]{1,0:T(8,128)}, f32[512,512]{1,0:T(8,128)}) custom-call(bf16[256,512]{1,0:T(8,128)(2,1)S(1)} %copy-done.12, bf16[8,32,1024]{2,1,0:T(8,128)(2,1)S(1)} %all-to-all-done.6.got_ref), custom_call_target="tpu_custom_call" | custom-call | flops 536870912 | bytes 4194304 | tf_op jit(solution)/shard_map/weights/pallas_call | solution.py:488
  (42 shorter events, 10.9 us)
Async XLA Ops:
  0.6 0.9 copy-start.6
  1.5 0.7 copy-start.10
  3.0 11.0 %collective-permute-start = (bf16[40,512]{1,0:T(8,128)(2,1)}, bf16[40,512]{1,0:T(8,128)(2,1)S(1)}, u32[]{:S(2)}, u32[]{:S(2)}) collective-permute-start(bf16[40,512]{1,0:T(8,128)(2,1)} %rows.1), channel_id=1, source_target_pairs={{0,0},{1,1},{2,16},{3,17},{4,32},{5,33},{6,48},{7,49},{8,64},{9,65... | collective-permute-start | bytes 122888 | tf_op jit(solution)/shard_map/ppermute | solution.py:294
  15.0 11.7 %copy-start = (bf16[8,256,512]{2,1,0:T(8,128)(2,1)S(1)}, bf16[8,256,512]{2,1,0:T(8,128)(2,1)}, u32[]{:S(2)}) copy-start(bf16[8,256,512]{2,1,0:T(8,128)(2,1)} %get-tuple-element.34.refs_0_.refs_1_.refs_2_.refs_3_) | copy-start | bytes 6291460
  15.0 11.7 %collective-permute-start.1 = (bf16[8,256,512]{2,1,0:T(8,128)(2,1)}, bf16[8,256,512]{2,1,0:T(8,128)(2,1)}, u32[]{:S(2)}, u32[]{:S(2)}) collective-permute-start(bf16[8,256,512]{2,1,0:T(8,128)(2,1)} %get-tuple-element.35), channel_id=1, source_target_pairs={{0,1},{1,0},{2,3},{3,2},{4,5},{5,4},{6,7},{7,6},{8,9},{9,8},{10,11... | collective-permute-start | bytes 6291464 | tf_op jit(solution)/shard_map/ppermute | solution.py:338
  15.1 36.6 %all-to-all-start = ((bf16[16,104,512]{2,1,0:T(8,128)(2,1)}), bf16[16,104,512]{2,1,0:T(8,128)(2,1)}, u32[]{:S(2)}, u32[]{:S(2)}) async-start(bf16[16,104,512]{2,1,0:T(8,128)(2,1)} %get-tuple-element.33), calls=%async_computation | async-start | bytes 3407872 | tf_op jit(solution)/shard_map/all_to_all | solution.py:335
  26.7 25.0 %copy-start.2 = (bf16[512,256]{1,0:T(8,128)(2,1)S(1)}, bf16[512,256]{1,0:T(8,128)(2,1)}, u32[]{:S(2)}) copy-start(bf16[512,256]{1,0:T(8,128)(2,1)} %residual_ref.3) | copy-start | bytes 786436
  26.7 25.0 %copy-start.9 = (f32[4096]{0:T(1024)S(1)}, f32[4096]{0:T(1024)}, u32[]{:S(2)}) copy-start(f32[4096]{0:T(1024)} %param.15) | copy-start | bytes 49156
  26.7 25.0 %copy-start.11 = (s32[1,64]{1,0:T(1,128)S(1)}, s32[1,64]{1,0:T(1,128)}, u32[]{:S(2)}) copy-start(s32[1,64]{1,0:T(1,128)} %route_ref.5) | copy-start | bytes 772
  55.9 30.7 %copy-start.1 = (bf16[2,256,512]{2,1,0:T(8,128)(2,1)S(1)}, bf16[2,256,512]{2,1,0:T(8,128)(2,1)}, u32[]{:S(2)}) copy-start(bf16[2,256,512]{2,1,0:T(8,128)(2,1)} %get-tuple-element.42.refs_0_.refs_4_) | copy-start | bytes 1572868
  55.9 19.4 %all-to-all-start.1 = ((bf16[8,32,2176]{2,1,0:T(8,128)(2,1)}), bf16[8,32,2176]{2,1,0:T(8,128)(2,1)S(1)}, u32[]{:S(2)}, u32[]{:S(2)}) async-start(bf16[8,32,2176]{2,1,0:T(8,128)(2,1)} %get-tuple-element.39), calls=%async_computation.1 | async-start | bytes 2228224 | tf_op jit(solution)/shard_map/all_to_all | solution.py:409
  59.6 26.3 %collective-permute-start.2 = (bf16[2,256,512]{2,1,0:T(8,128)(2,1)}, bf16[2,256,512]{2,1,0:T(8,128)(2,1)S(1)}, u32[]{:S(2)}, u32[]{:S(2)}) collective-permute-start(bf16[2,256,512]{2,1,0:T(8,128)(2,1)} %get-tuple-element.43), channel_id=1, source_target_pairs={{0,2},{1,3},{2,4},{3,5},{4,6},{5,7},{6,0},{7,1},{8,10},{9,11},{10,... | collective-permute-start | bytes 1572872 | tf_op jit(solution)/shard_map/ppermute | solution.py:338
  60.0 26.0 %collective-permute-start.3 = (bf16[2,256,512]{2,1,0:T(8,128)(2,1)}, bf16[2,256,512]{2,1,0:T(8,128)(2,1)S(1)}, u32[]{:S(2)}, u32[]{:S(2)}) collective-permute-start(bf16[2,256,512]{2,1,0:T(8,128)(2,1)} %get-tuple-element.44), channel_id=1, source_target_pairs={{0,4},{1,5},{2,6},{3,7},{4,0},{5,1},{6,2},{7,3},{8,12},{9,13},{10,... | collective-permute-start | bytes 1572872 | tf_op jit(solution)/shard_map/ppermute | solution.py:338
  61.7 24.9 %collective-permute-start.4 = (bf16[2,256,512]{2,1,0:T(8,128)(2,1)}, bf16[2,256,512]{2,1,0:T(8,128)(2,1)S(1)}, u32[]{:S(2)}, u32[]{:S(2)}) collective-permute-start(bf16[2,256,512]{2,1,0:T(8,128)(2,1)} %get-tuple-element.45), channel_id=1, source_target_pairs={{0,6},{1,7},{2,0},{3,1},{4,2},{5,3},{6,4},{7,5},{8,14},{9,15},{10,... | collective-permute-start | bytes 1572872 | tf_op jit(solution)/shard_map/ppermute | solution.py:338
  76.8 12.4 %all-to-all-start.2 = ((bf16[8,32,512]{2,1,0:T(8,128)(2,1)}), bf16[8,32,512]{2,1,0:T(8,128)(2,1)S(1)}, u32[]{:S(2)}, u32[]{:S(2)}) async-start(bf16[8,32,512]{2,1,0:T(8,128)(2,1)} %get-tuple-element.40), calls=%async_computation.2 | async-start | bytes 524288 | tf_op jit(solution)/shard_map/all_to_all | solution.py:419
  86.6 1.0 copy-start.5
  89.1 20.4 %copy-start.3 = (bf16[512,256]{1,0:T(8,128)(2,1)S(1)}, bf16[512,256]{1,0:T(8,128)(2,1)}, u32[]{:S(2)}) copy-start(bf16[512,256]{1,0:T(8,128)(2,1)} %residual_ref.3) | copy-start | bytes 786436
  89.1 20.4 %copy-start.4 = (f32[1,256,512]{2,1,0:T(8,128)S(1)}, f32[1,256,512]{2,1,0:T(8,128)}, u32[]{:S(2)}) copy-start(f32[1,256,512]{2,1,0:T(8,128)} %get-tuple-element.48.keep_ref) | copy-start | bytes 1572868
  91.3 13.9 %all-to-all-start.3 = ((bf16[16,16,512]{2,1,0:T(8,128)(2,1)}), bf16[16,16,512]{2,1,0:T(8,128)(2,1)S(1)}, u32[]{:S(2)}, u32[]{:S(2)}) async-start(bf16[16,16,512]{2,1,0:T(8,128)(2,1)} %get-tuple-element.47), calls=%async_computation.3 | async-start | bytes 524288 | tf_op jit(solution)/shard_map/all_to_all | solution.py:452
  95.9 36.3 %copy-start.8 = (f32[32,512]{1,0:T(8,128)S(1)}, f32[32,512]{1,0:T(8,128)}, u32[]{:S(2)}) copy-start(f32[32,512]{1,0:T(8,128)} %copy-done.7) | copy-start | bytes 196612
  95.9 13.7 %collective-permute-start.5 = (bf16[1,256,512]{2,1,0:T(8,128)(2,1)}, bf16[1,256,512]{2,1,0:T(8,128)(2,1)S(1)}, u32[]{:S(2)}, u32[]{:S(2)}) collective-permute-start(bf16[1,256,512]{2,1,0:T(8,128)(2,1)} %get-tuple-element.49), channel_id=1, source_target_pairs={{0,8},{1,9},{2,10},{3,11},{4,12},{5,13},{6,14},{7,15},{8,0},{9,1},... | collective-permute-start | bytes 786440 | tf_op jit(solution)/shard_map/ppermute | solution.py:338
  106.0 12.9 %all-to-all-start.4 = ((bf16[16,16,512]{2,1,0:T(8,128)(2,1)}), bf16[16,16,512]{2,1,0:T(8,128)(2,1)S(1)}, u32[]{:S(2)}, u32[]{:S(2)}) async-start(bf16[16,16,512]{2,1,0:T(8,128)(2,1)} %misfit.1), calls=%async_computation.4 | async-start | bytes 524288 | tf_op jit(solution)/shard_map/all_to_all | solution.py:461
  120.2 24.7 %copy-start.12 = (bf16[256,512]{1,0:T(8,128)(2,1)S(1)}, bf16[256,512]{1,0:T(8,128)(2,1)}, u32[]{:S(2)}) copy-start(bf16[256,512]{1,0:T(8,128)(2,1)} %get-tuple-element.51.rows_ref) | copy-start | bytes 786436
  133.1 11.9 %all-to-all-start.6 = ((bf16[8,32,1024]{2,1,0:T(8,128)(2,1)}), bf16[8,32,1024]{2,1,0:T(8,128)(2,1)S(1)}, u32[]{:S(2)}, u32[]{:S(2)}) async-start(bf16[8,32,1024]{2,1,0:T(8,128)(2,1)} %acts.1), calls=%async_computation.6 | async-start | bytes 1048576 | tf_op jit(solution)/shard_map/all_to_all | solution.py:480
  (1 other events, 0.6 us)

commit v4 on v3

v4 whole, which is shorter than its diff:
```python
import math

import jax
import jax.numpy as jnp
from jax import lax
from jax.experimental import pallas as pl
from jax.experimental.pallas import tpu as pltpu
from jax.sharding import PartitionSpec as P

EPS = 1e-05
BF = jnp.bfloat16
F32 = jnp.float32
MIB = 1 << 20


def params(mib):
    return pltpu.CompilerParams(vmem_limit_bytes=mib * MIB)


def cost(flops, nbytes):
    return pl.CostEstimate(flops=flops // 1024, bytes_accessed=nbytes // 1024, transcendentals=0)


def dot(a, b, ca=1, cb=0):
    return lax.dot_general(a, b, (((ca,), (cb,)), ((), ())), preferred_element_type=F32)


def whole(shape):
    return pl.BlockSpec(shape, lambda *_: (0,) * len(shape))


def slot_rows(route, tokens):
    slots = route.shape[1]
    grid = (slots, slots)
    diagonal = lax.broadcasted_iota(jnp.int32, grid, 0) == lax.broadcasted_iota(jnp.int32, grid, 1)
    spread = jnp.broadcast_to(route.astype(F32), grid)
    column = jnp.sum(jnp.where(diagonal, spread, 0.0), axis=1, keepdims=True)
    lane = lax.broadcasted_iota(jnp.int32, (slots, tokens), 1).astype(F32)
    return jnp.where(lane == column, 1.0, 0.0).astype(BF)


def rows_kernel(route_ref, x_ref, out_ref):
    route = route_ref[...]
    slots, wide = route.shape[1], x_ref.shape[1]
    rows = dot(slot_rows(route, x_ref.shape[0]), x_ref[...]).astype(BF)
    half = slots // 2
    out_ref[0:half, 0:wide] = rows[0:half]
    out_ref[0:half, wide : 2 * wide] = rows[half:]
    live = jnp.sum(jnp.where(route >= 0, 1.0, 0.0), axis=1, keepdims=True)
    out_ref[half : half + 8, :] = jnp.broadcast_to(live, (8, 2 * wide)).astype(BF)


def teacher_kernel(
    core_ref, route_ref, attn_ref, mine_ref, other_ref, after_ref,
    keep_ref, send_ref, keep_routed_ref, send_routed_ref, left_ref,
):
    tokens = attn_ref.shape[0]

    @pl.when(pl.program_id(0) == 0)
    def _():
        left_ref[0:tokens, :] = attn_ref[...]
        left_ref[tokens:, :] = dot(slot_rows(route_ref[...], tokens), attn_ref[...]).astype(BF)

    for weight_ref, out_ref, routed_ref in (
        (other_ref, send_ref, send_routed_ref),
        (mine_ref, keep_ref, keep_routed_ref),
    ):
        product = dot(left_ref[...], weight_ref[...]).astype(BF)
        out_ref[0] = product[0:tokens]
        routed_ref[0] = product[tokens:]


def copies_kernel(rows_ref, out_ref, sems):
    copies = [
        pltpu.make_async_copy(rows_ref, out_ref.at[s], sems.at[s]) for s in range(out_ref.shape[0])
    ]
    for copy in copies:
        copy.start()
    for copy in copies:
        copy.wait()


def core_sum_kernel(x_ref, *refs):
    ways = len(refs) // 3
    for j in range(ways):
        total = refs[j][...].astype(F32) + refs[ways + j][...].astype(F32)
        refs[2 * ways + j][...] = total.astype(BF).reshape(refs[2 * ways + j].shape)


def x_sum_kernel(y_ref, *refs):
    ways = len(refs) // 2 - 1
    for i, out_ref in enumerate(refs[-2:]):
        total = refs[i * ways][...].astype(F32)
        for ref in refs[i * ways + 1 : (i + 1) * ways]:
            total = total + ref[...].astype(F32)
        out_ref[...] = total.astype(out_ref.dtype)


def routed_sum_kernel(y_ref, route_ref, residual_ref, *refs):
    x_sum_kernel(y_ref, *refs)
    hot = slot_rows(route_ref[...], residual_ref.shape[1])
    refs[-1][0] = refs[-1][0] + dot(hot, residual_ref[...], 1, 1)


def residual_kernel(residual_ref, keep_ref, got_ref, out_ref):
    summed = keep_ref[0] + got_ref[0].astype(F32)
    out_ref[...] = (residual_ref[...].astype(F32) + summed.T).astype(BF)


def up_kernel(
    group_ref, got_ref, gain_ref, gate_ref, up_ref, after_ref, passed_ref,
    out_ref, rows_ref, chosen_ref, same_ref, padded_ref, weights_ref, sems,
):
    loads = [
        pltpu.make_async_copy(ref, weights_ref.at[i], sems.at[i])
        for i, ref in enumerate((gate_ref, up_ref))
    ]
    for load in loads:
        load.start()
    sources, height, wide = got_ref.shape
    groups = sources // 2
    half, side = height - 8, wide // 2
    slots = 2 * half
    per = out_ref.shape[1]
    total = groups * per

    for s in range(sources):
        g, d = s // 2, s % 2
        block = got_ref[s, 0:half, :]
        padded_ref[g * slots : g * slots + half, d * side : (d + 1) * side] = block[:, 0:side]
        padded_ref[g * slots + half : (g + 1) * slots, d * side : (d + 1) * side] = block[:, side:]
    at = half
    counts = [got_ref[2 * g, at : at + 8, 0 : 2 * slots].astype(F32)[0:1] for g in range(groups)]

    row = lax.broadcasted_iota(jnp.int32, (total, 2 * slots), 0)
    lane = lax.broadcasted_iota(jnp.int32, (total, 2 * slots), 1)
    second = lane >= slots
    slot = jnp.where(second, lane - slots, lane)
    slot_f = slot.astype(F32)
    shift = (row - slot).astype(F32)
    x = jnp.zeros((total, wide), F32)
    run = jnp.zeros_like(counts[0])
    for q in range(groups // 2):
        one, two = counts[2 * q], counts[2 * q + 1]
        start = jnp.where(second, run + one, run)
        count = jnp.where(second, two, one)
        run = run + one + two
        chosen = jnp.where((shift == start) & (slot_f < count), 1.0, 0.0).astype(BF)
        chosen_ref[:, 2 * q * slots : 2 * (q + 1) * slots] = chosen
        x = x + dot(chosen, padded_ref[2 * q * slots : 2 * (q + 1) * slots, :])

    square = jnp.sum(x * x, axis=1, keepdims=True)
    high = square.astype(BF)
    low = (square - high.astype(F32)).astype(BF)
    lane128 = lax.broadcasted_iota(jnp.int32, (total, 128), 1)
    squares = jnp.where(lane128 < 64, high.astype(F32), low.astype(F32)).astype(BF)
    scaled = (x * gain_ref[...]).astype(BF)
    rows_ref[...] = scaled
    for load in loads:
        load.wait()
    gate = dot(scaled, weights_ref[0]).astype(BF)
    up = dot(scaled, weights_ref[1]).astype(BF)
    at = 2 * wide + 128
    for g in range(groups):
        own = slice(g * per, (g + 1) * per)
        out_ref[g, :, 0:wide] = gate[own]
        out_ref[g, :, wide : 2 * wide] = up[own]
        out_ref[g, :, 2 * wide : at] = squares[own]


def hidden_kernel(
    features, got_ref, keep_ref, other_ref, s1, s2, s3,
    out_ref, gate_ref, up_ref, scale_ref, t1, t2, t3,
):
    per, wide = gate_ref.shape
    at = got_ref.shape[2]
    total = got_ref[0, :, 0:at].astype(F32)
    for g in range(1, got_ref.shape[0]):
        total = total + got_ref[g, :, 0:at].astype(F32)
    square = total[:, 2 * wide : 2 * wide + 1] + total[:, 2 * wide + 64 : 2 * wide + 65]
    scale = lax.rsqrt(square * (1.0 / features) + EPS)
    gate = total[:, 0:wide] * scale
    up = total[:, wide : 2 * wide] * scale
    gate_ref[...] = gate
    up_ref[...] = up
    scale_ref[...] = jnp.broadcast_to(scale, scale_ref.shape)
    hidden = (gate * jax.nn.sigmoid(gate) * up).astype(BF)
    routed = (keep_ref[0] + other_ref[0].astype(F32)).astype(BF)
    for g in range(out_ref.shape[0]):
        out_ref[g, 0:per, :] = hidden
        out_ref[g, per:, :] = routed


def down_kernel(
    group_ref, got_ref, down_ref, chosen_ref, projector_ref, out_ref, hidden_ref, rows_ref
):
    groups = got_ref.shape[0]
    per = hidden_ref.shape[0] // groups
    slots = got_ref.shape[1] - per
    for g in range(groups):
        hidden_ref[g * per : (g + 1) * per, :] = got_ref[g, 0:per, :]
        rows_ref[g * slots : (g + 1) * slots, :] = got_ref[g, per:, :]
    rows = dot(chosen_ref[...], rows_ref[...]).astype(BF)
    part = dot(hidden_ref[...], down_ref[...], 1, 1) - dot(rows, projector_ref[...])
    out_ref[...] = part.astype(BF).reshape(out_ref.shape)


def misfit_kernel(scale, got_ref, passed_ref, out_ref, same_ref):
    total = got_ref[0].astype(F32)
    for s in range(1, got_ref.shape[0]):
        total = total + got_ref[s].astype(F32)
    grad = (total * scale).astype(BF)
    for s in range(out_ref.shape[0]):
        out_ref[s] = grad


def back_kernel(got_ref, down_ref, out_ref):
    groups, per, wide = out_ref.shape
    part = dot(got_ref[...].reshape(groups * per, got_ref.shape[2]), down_ref[...])
    out_ref[...] = part.astype(BF).reshape(groups, per, wide)


def acts_kernel(got_ref, gate_ref, up_ref, scale_ref, out_ref):
    wide = gate_ref.shape[1]
    grad = got_ref[0].astype(F32)
    for g in range(1, got_ref.shape[0]):
        grad = grad + got_ref[g].astype(F32)
    grad = grad * scale_ref[:, 0:1]
    gate, up = gate_ref[...], up_ref[...]
    sigma = jax.nn.sigmoid(gate)
    grad_gate = (grad * up * sigma * (1.0 + gate * (1.0 - sigma))).astype(BF)
    grad_up = (grad * gate * sigma).astype(BF)
    for g in range(out_ref.shape[0]):
        out_ref[g, :, 0:wide] = grad_gate
        out_ref[g, :, wide : 2 * wide] = grad_up


def down_weights_kernel(grad_ref, hidden_ref, out_ref):
    rows, units = hidden_ref.shape
    out_ref[...] = dot(grad_ref[...].reshape(rows, out_ref.shape[0]), hidden_ref[...], 0, 0)


def weights_kernel(rows_ref, got_ref, gate_ref, up_ref):
    wide = gate_ref.shape[1]
    acts = got_ref[...].reshape(got_ref.shape[0] * got_ref.shape[1], 2 * wide)
    gate_ref[...] = dot(rows_ref[...], acts[:, 0:wide], 0, 0)
    up_ref[...] = dot(rows_ref[...], acts[:, wide:], 0, 0)


def on_device(
    attn_values,
    out_weight,
    residual_t,
    projector,
    student_input,
    norm_gain,
    w_gate,
    w_up,
    w_down,
    route_index,
):
    groups, parts = lax.axis_size("batch"), lax.axis_size("tensor")
    slots = route_index.shape[1]
    tokens, wide = attn_values.shape
    side = student_input.shape[1]
    features = norm_gain.shape[0]
    live = tokens * groups // 8
    per = live // groups
    units = w_gate.shape[1]
    extra = slots // 2 + 8
    group, part = lax.axis_index("batch"), lax.axis_index("tensor")
    core, x_at, y_at = part & 1, (part >> 1) & 3, part >> 3
    shape = jax.ShapeDtypeStruct
    vmem = pl.BlockSpec(memory_space=pltpu.VMEM)
    anywhere = pl.BlockSpec(memory_space=pl.ANY)
    out_weight, w_gate, w_up, w_down, projector = (
        pltpu.with_memory_space_constraint(w, pltpu.HBM)
        for w in (out_weight, w_gate, w_up, w_down, projector)
    )

    rows = pl.pallas_call(
        rows_kernel,
        out_shape=pltpu.HBM((extra, 2 * side), BF),
        cost_estimate=cost(2 * slots * tokens * side, MIB // 4),
        compiler_params=params(4),
        name="rows",
    )(route_index, student_input)
    pairs = [
        (b * parts + t, (t // 2) * parts + 2 * b + t % 2)
        for b in range(groups)
        for t in range(parts)
    ]
    rows = lax.ppermute(rows, ("batch", "tensor"), pairs)

    copies = pl.pallas_call(
        copies_kernel,
        in_specs=[vmem],
        out_specs=anywhere,
        out_shape=pltpu.HBM((parts, *rows.shape), BF),
        scratch_shapes=[pltpu.SemaphoreType.DMA((parts,))],
        compiler_params=params(4),
        cost_estimate=cost(0, MIB // 2),
        name="copies",
    )(rows)
    every = lax.all_to_all(copies, "tensor", 0, 0, tiled=True)

    keep, send, keep_routed, send_routed = pl.pallas_call(
        teacher_kernel,
        grid_spec=pltpu.PrefetchScalarGridSpec(
            num_scalar_prefetch=1,
            grid=(parts // 2,),
            in_specs=[
                pl.BlockSpec(route_index.shape, lambda j, core: (0, 0)),
                pl.BlockSpec(attn_values.shape, lambda j, core: (0, 0)),
                pl.BlockSpec((wide, wide), lambda j, core: (0, 2 * j + core[0])),
                pl.BlockSpec((wide, wide), lambda j, core: (0, 2 * j + 1 - core[0])),
                anywhere,
            ],
            out_specs=[pl.BlockSpec((1, tokens, wide), lambda j, core: (j, 0, 0))] * 2
            + [pl.BlockSpec((1, slots, wide), lambda j, core: (j, 0, 0))] * 2,
            scratch_shapes=[pltpu.VMEM((tokens + slots, wide), BF)],
        ),
        out_shape=[pltpu.HBM((parts // 2, tokens, wide), BF)] * 2
        + [pltpu.HBM((parts // 2, slots, wide), BF)] * 2,
        compiler_params=params(16),
        cost_estimate=cost(2 * (tokens + slots) * wide * wide * parts, 14 * MIB),
        name="teacher",
    )(core.reshape(1), route_index, attn_values, out_weight, out_weight, copies)

    def along(value, move):
        return lax.ppermute(value, "tensor", [(t, move(t // 8, (t // 2) % 4, t % 2)) for t in range(parts)])

    def core_sum(keep, send, strip):
        got = along(send, lambda y, x, c: y * 8 + x * 2 + 1 - c)
        height = keep.shape[1]
        block = (1, strip, wide)
        return pl.pallas_call(
            core_sum_kernel,
            grid_spec=pltpu.PrefetchScalarGridSpec(
                num_scalar_prefetch=1,
                grid=(2, height // strip),
                in_specs=[
                    pl.BlockSpec(block, lambda y, i, x, j=j: (4 * y + ((x[0] + j) & 3), i, 0))
                    for j in range(4)
                ]
                * 2,
                out_specs=[pl.BlockSpec(block, lambda y, i, x: (y, i, 0))] * 4,
            ),
            out_shape=[pltpu.HBM((2, height, wide), BF)] * 4,
            compiler_params=params(16),
            cost_estimate=cost(MIB, 24 * height * wide * 2),
            name="core_sum",
        )(x_at.reshape(1), *[keep] * 4, *[got] * 4)

    def along_x(own, moved):
        return [own] + [
            along(moved[j - 1], lambda y, x, c, j=j: y * 8 + (x + j) % 4 * 2 + c)
            for j in range(1, 4)
        ]

    def along_y(send):
        return along(send, lambda y, x, c: (1 - y) * 8 + x * 2 + c)

    def y_blocks(strip):
        block = (1, strip, wide)
        return [pl.BlockSpec(block, lambda i, y: (1 - y[0], i, 0))] * 4 + [
            pl.BlockSpec(block, lambda i, y: (y[0], i, 0))
        ] * 4

    routed_sums = core_sum(keep_routed, send_routed, slots)
    own, *moved = routed_sums
    send_routed, keep_routed = pl.pallas_call(
        routed_sum_kernel,
        grid_spec=pltpu.PrefetchScalarGridSpec(
            num_scalar_prefetch=1,
            grid=(1,),
            in_specs=[vmem, vmem] + y_blocks(slots),
            out_specs=[pl.BlockSpec((1, slots, wide), lambda i, y: (0, 0, 0))] * 2,
        ),
        out_shape=[pltpu.HBM((1, slots, wide), BF), pltpu.HBM((1, slots, wide), F32)],
        compiler_params=params(8),
        cost_estimate=cost(MIB, MIB),
        name="routed_sum",
    )(y_at.reshape(1), route_index, residual_t, *along_x(own, moved) * 2)
    other_routed = along_y(send_routed)

    packed = 2 * wide + 128
    sent, scaled, chosen, send = pl.pallas_call(
        up_kernel,
        grid_spec=pltpu.PrefetchScalarGridSpec(
            num_scalar_prefetch=1,
            grid=(1,),
            in_specs=[vmem, pl.BlockSpec((1, wide), lambda i, group: (0, group[0]))]
            + [anywhere] * 4,
            out_specs=[vmem] * 3 + [anywhere],
            scratch_shapes=[
                pltpu.VMEM((groups * slots, wide), BF),
                pltpu.VMEM((2, wide, units), BF),
                pltpu.SemaphoreType.DMA((2,)),
            ],
        ),
        out_shape=[
            pltpu.HBM((groups, per, packed), BF),
            pltpu.HBM((live, wide), BF),
            pltpu.HBM((live, groups * slots), BF),
            pltpu.HBM(send.shape, BF),
        ],
        input_output_aliases={6: 3},
        compiler_params=params(16),
        cost_estimate=cost(800 * MIB, 4 * MIB),
        name="up",
    )(group.reshape(1), every, norm_gain[None], w_gate, w_up, routed_sums[0], send)
    got = lax.all_to_all(sent, "batch", 0, 0, tiled=True)

    strip = tokens // 2
    own, *moved = core_sum(keep, send, strip)
    flat = shape((per, units), F32)
    both, gate, up, scale, *moved = pl.pallas_call(
        lambda *refs: hidden_kernel(features, *refs),
        in_specs=[vmem] * 3 + [anywhere] * 3,
        out_specs=[vmem] * 4 + [anywhere] * 3,
        out_shape=[pltpu.HBM((groups, per + slots, units), BF), flat, flat, shape((per, 128), F32)]
        + [pltpu.HBM((2, tokens, wide), BF)] * 3,
        input_output_aliases={3: 4, 4: 5, 5: 6},
        compiler_params=params(8),
        cost_estimate=cost(MIB, MIB),
        name="hidden",
    )(got, keep_routed, other_routed, *moved)
    both = lax.all_to_all(both, "batch", 0, 0, tiled=True)
    misfit, hidden = pl.pallas_call(
        down_kernel,
        grid_spec=pltpu.PrefetchScalarGridSpec(
            num_scalar_prefetch=1,
            grid=(1,),
            in_specs=[vmem] * 3 + [pl.BlockSpec((wide, wide), lambda i, group: (0, group[0]))],
            out_specs=[vmem] * 2,
            scratch_shapes=[pltpu.VMEM((groups * slots, wide), BF)],
        ),
        out_shape=[
            pltpu.HBM((parts, live // parts, wide), BF),
            pltpu.HBM((live, units), BF),
        ],
        compiler_params=params(16),
        cost_estimate=cost(768 * MIB, 4 * MIB),
        name="down",
    )(group.reshape(1), both, w_down, chosen, projector)
    misfit = lax.all_to_all(misfit, "tensor", 0, 0, tiled=True)
    loss_scale = 1.0 / math.sqrt(live)
    send, keep = pl.pallas_call(
        x_sum_kernel,
        grid_spec=pltpu.PrefetchScalarGridSpec(
            num_scalar_prefetch=1,
            grid=(tokens // strip,),
            in_specs=y_blocks(strip),
            out_specs=[pl.BlockSpec((1, strip, wide), lambda i, y: (0, i, 0))] * 2,
        ),
        out_shape=[pltpu.HBM((1, tokens, wide), BF), pltpu.HBM((1, tokens, wide), F32)],
        compiler_params=params(16),
        cost_estimate=cost(MIB, 3 * MIB),
        name="x_sum",
    )(y_at.reshape(1), *along_x(own, moved) * 2)
    grad_out, send = pl.pallas_call(
        lambda *refs: misfit_kernel(loss_scale, *refs),
        in_specs=[vmem, anywhere],
        out_specs=[vmem, anywhere],
        out_shape=[pltpu.HBM(misfit.shape, BF), pltpu.HBM(send.shape, BF)],
        input_output_aliases={1: 1},
        compiler_params=params(8),
        cost_estimate=cost(MIB, MIB),
        name="misfit",
    )(misfit, send)
    other = along_y(send)
    grad_out = lax.all_to_all(grad_out, "tensor", 0, 0, tiled=True)

    back = pl.pallas_call(
        back_kernel,
        out_shape=pltpu.HBM((groups, per, units), BF),
        compiler_params=params(16),
        cost_estimate=cost(256 * MIB, MIB),
        name="back",
    )(grad_out, w_down)
    back = lax.all_to_all(back, "batch", 0, 0, tiled=True)
    acts = pl.pallas_call(
        acts_kernel,
        out_shape=pltpu.HBM((groups, per, 2 * units), BF),
        compiler_params=params(8),
        cost_estimate=cost(MIB, MIB),
        name="acts",
    )(back, gate, up, scale)
    acts = lax.all_to_all(acts, "batch", 0, 0, tiled=True)
    teacher_hidden = pl.pallas_call(
        residual_kernel,
        out_shape=shape(residual_t.shape, BF),
        compiler_params=params(8),
        cost_estimate=cost(MIB, 2 * MIB),
        name="residual",
    )(residual_t, keep, other)
    grad_down = pl.pallas_call(
        down_weights_kernel,
        out_shape=shape((wide, units), F32),
        compiler_params=params(16),
        cost_estimate=cost(256 * MIB, 2 * MIB),
        name="down_weights",
    )(grad_out, hidden)
    grad_gate, grad_up = pl.pallas_call(
        weights_kernel,
        out_shape=[shape((wide, units), F32)] * 2,
        compiler_params=params(16),
        cost_estimate=cost(512 * MIB, 4 * MIB),
        name="weights",
    )(scaled, acts)
    return teacher_hidden, grad_gate, grad_up, grad_down


def solution(mesh):
    in_specs = (
        P("batch", "tensor"),
        P("tensor", None),
        P("tensor", "batch"),
        P("tensor", None),
        P("batch", "tensor"),
        P(),
        P("batch", "tensor"),
        P("batch", "tensor"),
        P("batch", "tensor"),
        P("batch", None),
    )
    out_specs = (P("tensor", "batch"),) + (P("batch", "tensor"),) * 3
    return jax.shard_map(
        on_device, mesh=mesh, in_specs=in_specs, out_specs=out_specs, check_vma=False
    )
```

time: 148 us -> 150 us (1.014)
  waiting for transfers between devices: 60.9 us -> 32.3 us
  blocking collectives: 11.9 us -> 27.3 us
  starting transfers between devices: 38.9 us -> 52 us
  local copies, waits for them, and re-layouts: 2.23 us -> 4.7 us
    all_to_all x3 -> x2, waiting for transfers between devices: 29.5 us -> 5.98 us  [the longest x1 5.97 us: on_device(): both = lax.all_to_all(both, 'batch', 0, 0, tiled=True)]
    ppermute x5 -> x10, waiting for transfers between devices: 6.2 us -> 24.7 us  [along(): lax.ppermute(value, 'tensor', [(t, move(t // 8, t // 2 % 4, t % 2)) for t...]
    all_to_all x0 -> x1, blocking collectives: none -> 14.6 us  [on_device(): grad_out = lax.all_to_all(grad_out, 'tensor', 0, 0, tiled=True)]
    all_to_all x1, waiting for transfers between devices: 12.2 us -> 0.01 us  [on_device(): got = lax.all_to_all(sent, 'batch', 0, 0, tiled=True)]
    ppermute x5 -> x10, starting transfers between devices: 7.02 us -> 16.6 us  [along(): lax.ppermute(value, 'tensor', [(t, move(t // 8, t // 2 % 4, t % 2)) for t...]
    all_to_all x1, waiting for transfers between devices: 7.07 us -> 0.01 us  [on_device(): acts = lax.all_to_all(acts, 'batch', 0, 0, tiled=True)]
    all_to_all x1, waiting for transfers between devices: 5.87 us -> 1.62 us  [on_device(): misfit = lax.all_to_all(misfit, 'tensor', 0, 0, tiled=True)]
    all_to_all x3 -> x2, starting transfers between devices: 18.7 us -> 21.5 us  [the longest x1 16.9 us: on_device(): every = lax.all_to_all(copies, 'tensor', 0, 0, tiled=True)]
  transfers between devices with their start and end apart: 12 -> 16, of which waited for: 7 -> 7; matrix products, arithmetic and copies ran while one was open for 0% -> 0% of each run, Pallas kernels for 14% -> 14%
where the time goes in v4:
time: 150 us; the launch traced here: 148 us
  starting transfers between devices  52 us (35%)
  waiting for transfers between devices  32.3 us (22%)
  Pallas kernels  31.2 us (21%)
  blocking collectives  27.3 us (18%)
  local copies, waits for them, and re-layouts  4.7 us (3%)
    ppermute x10, waiting for transfers between devices, along(): lax.ppermute(value, 'tensor', [(t, move(t // 8, t // 2 % 4, t % 2)) for t...  24.7 us
    all_to_all x1, starting transfers between devices, on_device(): every = lax.all_to_all(copies, 'tensor', 0, 0, tiled=True)  16.9 us
    ppermute x10, starting transfers between devices, along(): lax.ppermute(value, 'tensor', [(t, move(t // 8, t // 2 % 4, t % 2)) for t...  16.6 us
    all_to_all x1, blocking collectives, on_device(): grad_out = lax.all_to_all(grad_out, 'tensor', 0, 0, tiled=True)  14.6 us
    all_to_all x1, blocking collectives, on_device(): back = lax.all_to_all(back, 'batch', 0, 0, tiled=True)  12.8 us
    pallas_call x1, Pallas kernels, on_device(): pl.pallas_call(teacher_kernel, grid_spec=pltpu.PrefetchScalarGridSpec(num...  9.1 us
    all_to_all x1, waiting for transfers between devices, on_device(): both = lax.all_to_all(both, 'batch', 0, 0, tiled=True)  5.97 us
    all_to_all x1, starting transfers between devices, on_device(): misfit = lax.all_to_all(misfit, 'tensor', 0, 0, tiled=True)  5.14 us
  transfers between devices with their start and end apart: 16, of which 7 were waited for; matrix products, arithmetic and copies ran while one was open for 0% of the time, Pallas kernels for 14%

profile of v4, /device:TPU:0, one launch (start us, length us, event | category | flops | bytes accessed | tf_op | source)
XLA Modules:
  0.0 148.3 jit_solution(15846365161392122852)
XLA Ops:
  5.5 16.9 %all-to-all-start = ((bf16[16,40,512]{2,1,0:T(8,128)(2,1)}), bf16[16,40,512]{2,1,0:T(8,128)(2,1)S(1)}, u32[]{:S(2)}, u32[]{:S(2)}) async-start(bf16[16,40,512]{2,1,0:T(8,128)(2,1)} %copies.1.after_ref), calls=%async_computation | async-start | bytes 1310720 | tf_op jit(solution)/shard_map/all_to_all | solution.py:305
  23.5 9.1 %teacher.1 = (bf16[8,256,512]{2,1,0:T(8,128)(2,1)}, bf16[8,256,512]{2,1,0:T(8,128)(2,1)}, bf16[8,64,512]{2,1,0:T(8,128)(2,1)}, bf16[8,64,512]{2,1,0:T(8,128)(2,1)}) custom-call(s32[1]{0:T(128)} %bitcast.2.core_ref, s32[1,64]{1,0:T(1,128)S(1)} %copy-done.16, bf16[256,512]{1,0:T(8,128)(2,1)S(1)} %copy-done.8, bf16[512,8192]{1,0:T(8,128)(2,1)} %other_ref.1, ...), custom_call_target="tpu_custom_call" | custom-call | flops 2621440 | bytes 14336 | tf_op jit(solution)/shard_map/teacher/pallas_call | solution.py:307
  33.0 1.7 %collective-permute-done.1.refs_4_.refs_5_.refs_6_.refs_7_ = bf16[8,64,512]{2,1,0:T(8,128)(2,1)S(1)} collective-permute-done((bf16[8,64,512]{2,1,0:T(8,128)(2,1)}, bf16[8,64,512]{2,1,0:T(8,128)(2,1)S(1)}, u32[]{:S(2)}, u32[]{:S(2)}) %collective-permute-start.1) | collective-permute-done | bytes 524320 | tf_op jit(solution)/shard_map/ppermute | solution.py:331
  37.5 2.6 %up.1 = (bf16[8,32,1152]{2,1,0:T(8,128)(2,1)}, bf16[256,512]{1,0:T(8,128)(2,1)}, bf16[256,512]{1,0:T(8,128)(2,1)}, bf16[8,256,512]{2,1,0:T(8,128)(2,1)}) custom-call(s32[1]{0:T(128)} %bitcast.3.group_ref, bf16[16,40,512]{2,1,0:T(8,128)(2,1)S(1)} %all-to-all-done.got_ref, f32[1,4096]{1,0:T(1,128)S(1)} %bitcast.5, ...), custom_call_target="tpu_custom_call", output_to_operand_aliasing={{3}: (6, {})} | custom-call | flops 819200 | bytes 4096 | tf_op jit(solution)/shard_map/up/pallas_call | solution.py:388
  40.6 3.7 %all-to-all-start.1 = ((bf16[8,32,1152]{2,1,0:T(8,128)(2,1)}), bf16[8,32,1152]{2,1,0:T(8,128)(2,1)S(1)}, u32[]{:S(2)}, u32[]{:S(2)}) async-start(bf16[8,32,1152]{2,1,0:T(8,128)(2,1)} %get-tuple-element.44), calls=%async_computation.1 | async-start | bytes 1179648 | tf_op jit(solution)/shard_map/all_to_all | solution.py:413
  44.3 1.7 %collective-permute-start.3 = (bf16[2,64,512]{2,1,0:T(8,128)(2,1)}, bf16[2,64,512]{2,1,0:T(8,128)(2,1)S(1)}, u32[]{:S(2)}, u32[]{:S(2)}) collective-permute-start(bf16[2,64,512]{2,1,0:T(8,128)(2,1)} %get-tuple-element.45), channel_id=1, source_target_pairs={{0,2},{1,3},{2,4},{3,5},{4,6},{5,7},{6,0},{7,1},{8,10},{9,11},{10,... | collective-permute-start | bytes 393224 | tf_op jit(solution)/shard_map/ppermute | solution.py:331
  46.0 2.7 %collective-permute-start.4 = (bf16[2,64,512]{2,1,0:T(8,128)(2,1)}, bf16[2,64,512]{2,1,0:T(8,128)(2,1)S(1)}, u32[]{:S(2)}, u32[]{:S(2)}) collective-permute-start(bf16[2,64,512]{2,1,0:T(8,128)(2,1)} %get-tuple-element.46), channel_id=1, source_target_pairs={{0,4},{1,5},{2,6},{3,7},{4,0},{5,1},{6,2},{7,3},{8,12},{9,13},{10,... | collective-permute-start | bytes 393224 | tf_op jit(solution)/shard_map/ppermute | solution.py:331
  51.4 4.0 %collective-permute-done.4.refs_2_.refs_6_ = bf16[2,64,512]{2,1,0:T(8,128)(2,1)S(1)} collective-permute-done((bf16[2,64,512]{2,1,0:T(8,128)(2,1)}, bf16[2,64,512]{2,1,0:T(8,128)(2,1)S(1)}, u32[]{:S(2)}, u32[]{:S(2)}) %collective-permute-start.4) | collective-permute-done | bytes 131104 | tf_op jit(solution)/shard_map/ppermute | solution.py:331
  56.3 3.0 %collective-permute-start.6 = (bf16[1,64,512]{2,1,0:T(8,128)(2,1)}, bf16[1,64,512]{2,1,0:T(8,128)(2,1)S(1)}, u32[]{:S(2)}, u32[]{:S(2)}) collective-permute-start(bf16[1,64,512]{2,1,0:T(8,128)(2,1)} %get-tuple-element.49), channel_id=1, source_target_pairs={{0,8},{1,9},{2,10},{3,11},{4,12},{5,13},{6,14},{7,15},{8,0},{9,1},... | collective-permute-start | bytes 196616 | tf_op jit(solution)/shard_map/ppermute | solution.py:331
  59.3 3.9 %core_sum.3 = (bf16[2,256,512]{2,1,0:T(8,128)(2,1)}, bf16[2,256,512]{2,1,0:T(8,128)(2,1)}, bf16[2,256,512]{2,1,0:T(8,128)(2,1)}, bf16[2,256,512]{2,1,0:T(8,128)(2,1)}) custom-call(s32[1]{0:T(128)} %bitcast.1.x_ref, bf16[8,256,512]{2,1,0:T(8,128)(2,1)S(1)} %copy-done, bf16[8,256,512]{2,1,0:T(8,128)(2,1)S(1)} %copy-done, bf16[8,256,512]{2,1,0:T(8,128)(2,1)S(1)} %copy-done, ...), custom_call_target="tpu_custom_call" | custom-call | flops 1024 | bytes 6144 | tf_op jit(solution)/shard_map/core_sum/pallas_call | solution.py:337
  64.3 4.7 %all-to-all-start.2 = ((bf16[8,96,512]{2,1,0:T(8,128)(2,1)}), bf16[8,96,512]{2,1,0:T(8,128)(2,1)S(1)}, u32[]{:S(2)}, u32[]{:S(2)}) async-start(bf16[8,96,512]{2,1,0:T(8,128)(2,1)} %get-tuple-element.57), calls=%async_computation.2 | async-start | bytes 1572864 | tf_op jit(solution)/shard_map/all_to_all | solution.py:429
  70.4 2.4 %collective-permute-start.8 = (bf16[2,256,512]{2,1,0:T(8,128)(2,1)}, bf16[2,256,512]{2,1,0:T(8,128)(2,1)S(1)}, u32[]{:S(2)}, u32[]{:S(2)}) collective-permute-start(bf16[2,256,512]{2,1,0:T(8,128)(2,1)} %get-tuple-element.54), channel_id=1, source_target_pairs={{0,4},{1,5},{2,6},{3,7},{4,0},{5,1},{6,2},{7,3},{8,12},{9,13},{10,... | collective-permute-start | bytes 1572872 | tf_op jit(solution)/shard_map/ppermute | solution.py:331
  74.3 6.0 %all-to-all-done.2.got_ref = bf16[8,96,512]{2,1,0:T(8,128)(2,1)S(1)} async-done(((bf16[8,96,512]{2,1,0:T(8,128)(2,1)}), bf16[8,96,512]{2,1,0:T(8,128)(2,1)S(1)}, u32[]{:S(2)}, u32[]{:S(2)}) %all-to-all-start.2) | async-done | bytes 786464 | tf_op jit(solution)/shard_map/all_to_all | solution.py:429
  80.3 2.5 %down.1 = (bf16[16,16,512]{2,1,0:T(8,128)(2,1)}, bf16[256,512]{1,0:T(8,128)(2,1)}) custom-call(s32[1]{0:T(128)} %bitcast.3.group_ref, bf16[8,96,512]{2,1,0:T(8,128)(2,1)S(1)} %all-to-all-done.2.got_ref, bf16[512,512]{1,0:T(8,128)(2,1)} %down_ref.3, bf16[256,512]{1,0:T(8,128)(2,1)S(1)} %copy-done.10, bf16[512,4096]{1,0:T(8,128)(2,1)} %projector_ref.1), custom_call_target="tpu_custom_call" | custom-call | flops 786432 | bytes 4096 | tf_op jit(solution)/shard_map/down/pallas_call | solution.py:430
  82.8 5.1 %all-to-all-start.3 = ((bf16[16,16,512]{2,1,0:T(8,128)(2,1)}), bf16[16,16,512]{2,1,0:T(8,128)(2,1)S(1)}, u32[]{:S(2)}, u32[]{:S(2)}) async-start(bf16[16,16,512]{2,1,0:T(8,128)(2,1)} %get-tuple-element.59), calls=%async_computation.3 | async-start | bytes 524288 | tf_op jit(solution)/shard_map/all_to_all | solution.py:447
  88.0 8.2 %collective-permute-done.8.refs_2_.refs_6_ = bf16[2,256,512]{2,1,0:T(8,128)(2,1)S(1)} collective-permute-done((bf16[2,256,512]{2,1,0:T(8,128)(2,1)}, bf16[2,256,512]{2,1,0:T(8,128)(2,1)S(1)}, u32[]{:S(2)}, u32[]{:S(2)}) %collective-permute-start.8) | collective-permute-done | bytes 524320 | tf_op jit(solution)/shard_map/ppermute | solution.py:331
  97.2 1.6 %all-to-all-done.3.refs_0_ = bf16[16,16,512]{2,1,0:T(8,128)(2,1)S(1)} async-done(((bf16[16,16,512]{2,1,0:T(8,128)(2,1)}), bf16[16,16,512]{2,1,0:T(8,128)(2,1)S(1)}, u32[]{:S(2)}, u32[]{:S(2)}) %all-to-all-start.3) | async-done | bytes 262176 | tf_op jit(solution)/shard_map/all_to_all | solution.py:447
  99.5 14.6 %all_to_all.35.got_ref.grad_ref = bf16[16,16,512]{2,1,0:T(8,128)(2,1)S(1)} all-to-all(bf16[16,16,512]{2,1,0:T(8,128)(2,1)} %get-tuple-element.63), channel_id=1, replica_groups=mesh['batch'=8,'tensor'=16] {'tensor'}, dimensions={0} | all-to-all | bytes 524288 | tf_op jit(solution)/shard_map/all_to_all | solution.py:473
  114.1 2.0 %back.1 = bf16[8,32,512]{2,1,0:T(8,128)(2,1)} custom-call(bf16[16,16,512]{2,1,0:T(8,128)(2,1)S(1)} %all_to_all.35.got_ref.grad_ref, bf16[512,512]{1,0:T(8,128)(2,1)} %down_ref.3), custom_call_target="tpu_custom_call" | custom-call | flops 262144 | bytes 1024 | tf_op jit(solution)/shard_map/back/pallas_call | solution.py:475
  116.2 12.8 %all_to_all.36.got_ref = bf16[8,32,512]{2,1,0:T(8,128)(2,1)S(1)} all-to-all(bf16[8,32,512]{2,1,0:T(8,128)(2,1)} %back.1), channel_id=1, replica_groups=mesh['batch'=8,'tensor'=16] {'batch'}, dimensions={0} | all-to-all | bytes 524288 | tf_op jit(solution)/shard_map/all_to_all | solution.py:482
  129.8 3.6 %all-to-all-start.6 = ((bf16[8,32,1024]{2,1,0:T(8,128)(2,1)}), bf16[8,32,1024]{2,1,0:T(8,128)(2,1)S(1)}, u32[]{:S(2)}, u32[]{:S(2)}) async-start(bf16[8,32,1024]{2,1,0:T(8,128)(2,1)} %acts.1), calls=%async_computation.6 | async-start | bytes 1048576 | tf_op jit(solution)/shard_map/all_to_all | solution.py:490
  133.5 1.5 %collective-permute-start.10 = (bf16[1,256,512]{2,1,0:T(8,128)(2,1)S(1)}, bf16[1,256,512]{2,1,0:T(8,128)(2,1)S(1)}, u32[]{:S(2)}, u32[]{:S(2)}) collective-permute-start(bf16[1,256,512]{2,1,0:T(8,128)(2,1)S(1)} %copy-done.17), channel_id=1, source_target_pairs={{0,8},{1,9},{2,10},{3,11},{4,12},{5,13},{6,14},{7,15},{8,0},{9,1},... | collective-permute-start | bytes 786440 | tf_op jit(solution)/shard_map/ppermute | solution.py:331
  136.3 9.4 %collective-permute-done.10.got_ref = bf16[1,256,512]{2,1,0:T(8,128)(2,1)S(1)} collective-permute-done((bf16[1,256,512]{2,1,0:T(8,128)(2,1)S(1)}, bf16[1,256,512]{2,1,0:T(8,128)(2,1)S(1)}, u32[]{:S(2)}, u32[]{:S(2)}) %collective-permute-start.10) | collective-permute-done | bytes 262176 | tf_op jit(solution)/shard_map/ppermute | solution.py:331
  146.7 1.6 %weights.1 = (f32[512,512]{1,0:T(8,128)}, f32[512,512]{1,0:T(8,128)}) custom-call(bf16[256,512]{1,0:T(8,128)(2,1)S(1)} %copy-done.9, bf16[8,32,1024]{2,1,0:T(8,128)(2,1)S(1)} %all-to-all-done.6.got_ref), custom_call_target="tpu_custom_call" | custom-call | flops 524288 | bytes 4096 | tf_op jit(solution)/shard_map/weights/pallas_call | solution.py:505
  (62 shorter events, 22.2 us)
Async XLA Ops:
  0.6 21.7 %copy-start.8 = (bf16[256,512]{1,0:T(8,128)(2,1)S(1)}, bf16[256,512]{1,0:T(8,128)(2,1)}, u32[]{:S(2)}) copy-start(bf16[256,512]{1,0:T(8,128)(2,1)} %attn_ref.1) | copy-start | bytes 786436
  2.2 20.1 %copy-start.16 = (s32[1,64]{1,0:T(1,128)S(1)}, s32[1,64]{1,0:T(1,128)}, u32[]{:S(2)}) copy-start(s32[1,64]{1,0:T(1,128)} %route_ref.5) | copy-start | bytes 772
  3.1 1.4 collective-permute-start
  5.5 31.2 %all-to-all-start = ((bf16[16,40,512]{2,1,0:T(8,128)(2,1)}), bf16[16,40,512]{2,1,0:T(8,128)(2,1)S(1)}, u32[]{:S(2)}, u32[]{:S(2)}) async-start(bf16[16,40,512]{2,1,0:T(8,128)(2,1)} %copies.1.after_ref), calls=%async_computation | async-start | bytes 1310720 | tf_op jit(solution)/shard_map/all_to_all | solution.py:305
  32.6 2.2 %collective-permute-start.1 = (bf16[8,64,512]{2,1,0:T(8,128)(2,1)}, bf16[8,64,512]{2,1,0:T(8,128)(2,1)S(1)}, u32[]{:S(2)}, u32[]{:S(2)}) collective-permute-start(bf16[8,64,512]{2,1,0:T(8,128)(2,1)} %get-tuple-element.39), channel_id=1, source_target_pairs={{0,1},{1,0},{2,3},{3,2},{4,5},{5,4},{6,7},{7,6},{8,9},{9,8},{10,11... | collective-permute-start | bytes 1572872 | tf_op jit(solution)/shard_map/ppermute | solution.py:331
  37.5 17.9 %copy-start.5 = (bf16[2,64,512]{2,1,0:T(8,128)(2,1)S(1)}, bf16[2,64,512]{2,1,0:T(8,128)(2,1)}, u32[]{:S(2)}) copy-start(bf16[2,64,512]{2,1,0:T(8,128)(2,1)} %get-tuple-element.40.after_ref.refs_0_.refs_4_) | copy-start | bytes 393220
  37.5 17.9 %copy-start.6 = (bf16[512,256]{1,0:T(8,128)(2,1)S(1)}, bf16[512,256]{1,0:T(8,128)(2,1)}, u32[]{:S(2)}) copy-start(bf16[512,256]{1,0:T(8,128)(2,1)} %residual_ref.3) | copy-start | bytes 786436
  40.1 19.2 %copy-start = (bf16[8,256,512]{2,1,0:T(8,128)(2,1)S(1)}, bf16[8,256,512]{2,1,0:T(8,128)(2,1)}, u32[]{:S(2)}) copy-start(bf16[8,256,512]{2,1,0:T(8,128)(2,1)} %get-tuple-element.37.refs_0_.refs_1_.refs_2_.refs_3_) | copy-start | bytes 6291460
  40.1 19.2 %collective-permute-start.2 = (bf16[8,256,512]{2,1,0:T(8,128)(2,1)}, bf16[8,256,512]{2,1,0:T(8,128)(2,1)}, u32[]{:S(2)}, u32[]{:S(2)}) collective-permute-start(bf16[8,256,512]{2,1,0:T(8,128)(2,1)} %get-tuple-element.42), channel_id=1, source_target_pairs={{0,1},{1,0},{2,3},{3,2},{4,5},{5,4},{6,7},{7,6},{8,9},{9,8},{10,11... | collective-permute-start | bytes 6291464 | tf_op jit(solution)/shard_map/ppermute | solution.py:331
  40.6 22.6 %all-to-all-start.1 = ((bf16[8,32,1152]{2,1,0:T(8,128)(2,1)}), bf16[8,32,1152]{2,1,0:T(8,128)(2,1)S(1)}, u32[]{:S(2)}, u32[]{:S(2)}) async-start(bf16[8,32,1152]{2,1,0:T(8,128)(2,1)} %get-tuple-element.44), calls=%async_computation.1 | async-start | bytes 1179648 | tf_op jit(solution)/shard_map/all_to_all | solution.py:413
  44.3 7.2 %collective-permute-start.3 = (bf16[2,64,512]{2,1,0:T(8,128)(2,1)}, bf16[2,64,512]{2,1,0:T(8,128)(2,1)S(1)}, u32[]{:S(2)}, u32[]{:S(2)}) collective-permute-start(bf16[2,64,512]{2,1,0:T(8,128)(2,1)} %get-tuple-element.45), channel_id=1, source_target_pairs={{0,2},{1,3},{2,4},{3,5},{4,6},{5,7},{6,0},{7,1},{8,10},{9,11},{10,... | collective-permute-start | bytes 393224 | tf_op jit(solution)/shard_map/ppermute | solution.py:331
  46.0 9.4 %collective-permute-start.4 = (bf16[2,64,512]{2,1,0:T(8,128)(2,1)}, bf16[2,64,512]{2,1,0:T(8,128)(2,1)S(1)}, u32[]{:S(2)}, u32[]{:S(2)}) collective-permute-start(bf16[2,64,512]{2,1,0:T(8,128)(2,1)} %get-tuple-element.46), channel_id=1, source_target_pairs={{0,4},{1,5},{2,6},{3,7},{4,0},{5,1},{6,2},{7,3},{8,12},{9,13},{10,... | collective-permute-start | bytes 393224 | tf_op jit(solution)/shard_map/ppermute | solution.py:331
  48.7 6.7 %collective-permute-start.5 = (bf16[2,64,512]{2,1,0:T(8,128)(2,1)}, bf16[2,64,512]{2,1,0:T(8,128)(2,1)S(1)}, u32[]{:S(2)}, u32[]{:S(2)}) collective-permute-start(bf16[2,64,512]{2,1,0:T(8,128)(2,1)} %get-tuple-element.47), channel_id=1, source_target_pairs={{0,6},{1,7},{2,0},{3,1},{4,2},{5,3},{6,4},{7,5},{8,14},{9,15},{10,... | collective-permute-start | bytes 393224 | tf_op jit(solution)/shard_map/ppermute | solution.py:331
  56.3 6.9 %collective-permute-start.6 = (bf16[1,64,512]{2,1,0:T(8,128)(2,1)}, bf16[1,64,512]{2,1,0:T(8,128)(2,1)S(1)}, u32[]{:S(2)}, u32[]{:S(2)}) collective-permute-start(bf16[1,64,512]{2,1,0:T(8,128)(2,1)} %get-tuple-element.49), channel_id=1, source_target_pairs={{0,8},{1,9},{2,10},{3,11},{4,12},{5,13},{6,14},{7,15},{8,0},{9,1},... | collective-permute-start | bytes 196616 | tf_op jit(solution)/shard_map/ppermute | solution.py:331
  64.3 16.0 %all-to-all-start.2 = ((bf16[8,96,512]{2,1,0:T(8,128)(2,1)}), bf16[8,96,512]{2,1,0:T(8,128)(2,1)S(1)}, u32[]{:S(2)}, u32[]{:S(2)}) async-start(bf16[8,96,512]{2,1,0:T(8,128)(2,1)} %get-tuple-element.57), calls=%async_computation.2 | async-start | bytes 1572864 | tf_op jit(solution)/shard_map/all_to_all | solution.py:429
  69.0 19.0 %collective-permute-start.7 = (bf16[2,256,512]{2,1,0:T(8,128)(2,1)}, bf16[2,256,512]{2,1,0:T(8,128)(2,1)S(1)}, u32[]{:S(2)}, u32[]{:S(2)}) collective-permute-start(bf16[2,256,512]{2,1,0:T(8,128)(2,1)} %get-tuple-element.53), channel_id=1, source_target_pairs={{0,2},{1,3},{2,4},{3,5},{4,6},{5,7},{6,0},{7,1},{8,10},{9,11},{10,... | collective-permute-start | bytes 1572872 | tf_op jit(solution)/shard_map/ppermute | solution.py:331
  70.4 25.7 %collective-permute-start.8 = (bf16[2,256,512]{2,1,0:T(8,128)(2,1)}, bf16[2,256,512]{2,1,0:T(8,128)(2,1)S(1)}, u32[]{:S(2)}, u32[]{:S(2)}) collective-permute-start(bf16[2,256,512]{2,1,0:T(8,128)(2,1)} %get-tuple-element.54), channel_id=1, source_target_pairs={{0,4},{1,5},{2,6},{3,7},{4,0},{5,1},{6,2},{7,3},{8,12},{9,13},{10,... | collective-permute-start | bytes 1572872 | tf_op jit(solution)/shard_map/ppermute | solution.py:331
  72.8 23.4 %collective-permute-start.9 = (bf16[2,256,512]{2,1,0:T(8,128)(2,1)}, bf16[2,256,512]{2,1,0:T(8,128)(2,1)S(1)}, u32[]{:S(2)}, u32[]{:S(2)}) collective-permute-start(bf16[2,256,512]{2,1,0:T(8,128)(2,1)} %get-tuple-element.55), channel_id=1, source_target_pairs={{0,6},{1,7},{2,0},{3,1},{4,2},{5,3},{6,4},{7,5},{8,14},{9,15},{10,... | collective-permute-start | bytes 1572872 | tf_op jit(solution)/shard_map/ppermute | solution.py:331
  82.8 16.0 %all-to-all-start.3 = ((bf16[16,16,512]{2,1,0:T(8,128)(2,1)}), bf16[16,16,512]{2,1,0:T(8,128)(2,1)S(1)}, u32[]{:S(2)}, u32[]{:S(2)}) async-start(bf16[16,16,512]{2,1,0:T(8,128)(2,1)} %get-tuple-element.59), calls=%async_computation.3 | async-start | bytes 524288 | tf_op jit(solution)/shard_map/all_to_all | solution.py:447
  99.5 33.9 %copy-start.17 = (bf16[1,256,512]{2,1,0:T(8,128)(2,1)S(1)}, bf16[1,256,512]{2,1,0:T(8,128)(2,1)}, u32[]{:S(2)}) copy-start(bf16[1,256,512]{2,1,0:T(8,128)(2,1)} %get-tuple-element.61) | copy-start | bytes 786436
  99.5 35.5 %copy-start.11 = (bf16[256,512]{1,0:T(8,128)(2,1)S(1)}, bf16[256,512]{1,0:T(8,128)(2,1)}, u32[]{:S(2)}) copy-start(bf16[256,512]{1,0:T(8,128)(2,1)} %get-tuple-element.69.hidden_ref) | copy-start | bytes 786436
  116.2 29.6 %copy-start.7 = (f32[1,256,512]{2,1,0:T(8,128)S(1)}, f32[1,256,512]{2,1,0:T(8,128)}, u32[]{:S(2)}) copy-start(f32[1,256,512]{2,1,0:T(8,128)} %get-tuple-element.56.keep_ref) | copy-start | bytes 1572868
  129.8 16.8 %all-to-all-start.6 = ((bf16[8,32,1024]{2,1,0:T(8,128)(2,1)}), bf16[8,32,1024]{2,1,0:T(8,128)(2,1)S(1)}, u32[]{:S(2)}, u32[]{:S(2)}) async-start(bf16[8,32,1024]{2,1,0:T(8,128)(2,1)} %acts.1), calls=%async_computation.6 | async-start | bytes 1048576 | tf_op jit(solution)/shard_map/all_to_all | solution.py:490
  133.5 12.3 %collective-permute-start.10 = (bf16[1,256,512]{2,1,0:T(8,128)(2,1)S(1)}, bf16[1,256,512]{2,1,0:T(8,128)(2,1)S(1)}, u32[]{:S(2)}, u32[]{:S(2)}) collective-permute-start(bf16[1,256,512]{2,1,0:T(8,128)(2,1)S(1)} %copy-done.17), channel_id=1, source_target_pairs={{0,8},{1,9},{2,10},{3,11},{4,12},{5,13},{6,14},{7,15},{8,0},{9,1},... | collective-permute-start | bytes 786440 | tf_op jit(solution)/shard_map/ppermute | solution.py:331
  (10 other events, 59.2 us)

commit v5 on v4

--- a/solution.py
+++ b/solution.py
@@ -50,27 +50,25 @@
     out_ref[half : half + 8, :] = jnp.broadcast_to(live, (8, 2 * wide)).astype(BF)
 
 
-def teacher_kernel(
-    core_ref, route_ref, attn_ref, mine_ref, other_ref, after_ref,
-    keep_ref, send_ref, keep_routed_ref, send_routed_ref, left_ref,
-):
-    tokens = attn_ref.shape[0]
-
+def routed_kernel(core_ref, route_ref, attn_ref, weight_ref, keep_ref, send_ref, left_ref):
     @pl.when(pl.program_id(0) == 0)
     def _():
-        left_ref[0:tokens, :] = attn_ref[...]
-        left_ref[tokens:, :] = dot(slot_rows(route_ref[...], tokens), attn_ref[...]).astype(BF)
-
-    for weight_ref, out_ref, routed_ref in (
-        (other_ref, send_ref, send_routed_ref),
-        (mine_ref, keep_ref, keep_routed_ref),
-    ):
-        product = dot(left_ref[...], weight_ref[...]).astype(BF)
-        out_ref[0] = product[0:tokens]
-        routed_ref[0] = product[tokens:]
-
-
-def copies_kernel(rows_ref, out_ref, sems):
+        hot = slot_rows(route_ref[...], attn_ref.shape[0])
+        left_ref[...] = dot(hot, attn_ref[...]).astype(BF)
+
+    wide = keep_ref.shape[2]
+    product = dot(left_ref[...], weight_ref[...]).astype(BF)
+    first = core_ref[0] == 0
+    keep_ref[0] = jnp.where(first, product[:, 0:wide], product[:, wide:])
+    send_ref[0] = jnp.where(first, product[:, wide:], product[:, 0:wide])
+
+
+def teacher_kernel(core_ref, attn_ref, mine_ref, other_ref, after_ref, keep_ref, send_ref):
+    for weight_ref, out_ref in ((other_ref, send_ref), (mine_ref, keep_ref)):
+        out_ref[0] = dot(attn_ref[...], weight_ref[...]).astype(BF)
+
+
+def copies_kernel(rows_ref, passed_ref, out_ref, same_ref, sems):
     copies = [
         pltpu.make_async_copy(rows_ref, out_ref.at[s], sems.at[s]) for s in range(out_ref.shape[0])
     ]
@@ -108,7 +106,7 @@
 
 
 def up_kernel(
-    group_ref, got_ref, gain_ref, gate_ref, up_ref, after_ref, passed_ref,
+    group_ref, got_ref, gain_ref, gate_ref, up_ref, passed_ref,
     out_ref, rows_ref, chosen_ref, same_ref, padded_ref, weights_ref, sems,
 ):
     loads = [
@@ -169,8 +167,8 @@
 
 
 def hidden_kernel(
-    features, got_ref, keep_ref, other_ref, s1, s2, s3,
-    out_ref, gate_ref, up_ref, scale_ref, t1, t2, t3,
+    features, got_ref, keep_ref, other_ref, passed_ref,
+    out_ref, gate_ref, up_ref, scale_ref, same_ref,
 ):
     per, wide = gate_ref.shape
     at = got_ref.shape[2]
@@ -192,7 +190,8 @@
 
 
 def down_kernel(
-    group_ref, got_ref, down_ref, chosen_ref, projector_ref, out_ref, hidden_ref, rows_ref
+    group_ref, got_ref, down_ref, chosen_ref, projector_ref, after_ref,
+    out_ref, hidden_ref, rows_ref,
 ):
     groups = got_ref.shape[0]
     per = hidden_ref.shape[0] // groups
@@ -205,7 +204,7 @@
     out_ref[...] = part.astype(BF).reshape(out_ref.shape)
 
 
-def misfit_kernel(scale, got_ref, passed_ref, out_ref, same_ref):
+def misfit_kernel(scale, got_ref, out_ref):
     total = got_ref[0].astype(F32)
     for s in range(1, got_ref.shape[0]):
         total = total + got_ref[s].astype(F32)
@@ -214,13 +213,13 @@
         out_ref[s] = grad
 
 
-def back_kernel(got_ref, down_ref, out_ref):
+def back_kernel(got_ref, down_ref, after_ref, out_ref):
     groups, per, wide = out_ref.shape
     part = dot(got_ref[...].reshape(groups * per, got_ref.shape[2]), down_ref[...])
     out_ref[...] = part.astype(BF).reshape(groups, per, wide)
 
 
-def acts_kernel(got_ref, gate_ref, up_ref, scale_ref, out_ref):
+def acts_kernel(got_ref, gate_ref, up_ref, scale_ref, passed_ref, out_ref, same_ref):
     wide = gate_ref.shape[1]
     grad = got_ref[0].astype(F32)
     for g in range(1, got_ref.shape[0]):
@@ -273,9 +272,12 @@
     shape = jax.ShapeDtypeStruct
     vmem = pl.BlockSpec(memory_space=pltpu.VMEM)
     anywhere = pl.BlockSpec(memory_space=pl.ANY)
-    out_weight, w_gate, w_up, w_down, projector = (
-        pltpu.with_memory_space_constraint(w, pltpu.HBM)
-        for w in (out_weight, w_gate, w_up, w_down, projector)
+
+    def hbm(value):
+        return pltpu.with_memory_space_constraint(value, pltpu.HBM)
+
+    out_weight, w_gate, w_up, w_down, projector, student_input, route_index = (
+        hbm(w) for w in (out_weight, w_gate, w_up, w_down, projector, student_input, route_index)
     )
 
     rows = pl.pallas_call(
@@ -292,40 +294,36 @@
     ]
     rows = lax.ppermute(rows, ("batch", "tensor"), pairs)
 
-    copies = pl.pallas_call(
-        copies_kernel,
-        in_specs=[vmem],
-        out_specs=anywhere,
-        out_shape=pltpu.HBM((parts, *rows.shape), BF),
-        scratch_shapes=[pltpu.SemaphoreType.DMA((parts,))],
-        compiler_params=params(4),
-        cost_estimate=cost(0, MIB // 2),
-        name="copies",
-    )(rows)
-    every = lax.all_to_all(copies, "tensor", 0, 0, tiled=True)
-
-    keep, send, keep_routed, send_routed = pl.pallas_call(
-        teacher_kernel,
+    keep_routed, send_routed = pl.pallas_call(
+        routed_kernel,
         grid_spec=pltpu.PrefetchScalarGridSpec(
             num_scalar_prefetch=1,
             grid=(parts // 2,),
             in_specs=[
                 pl.BlockSpec(route_index.shape, lambda j, core: (0, 0)),
                 pl.BlockSpec(attn_values.shape, lambda j, core: (0, 0)),
-                pl.BlockSpec((wide, wide), lambda j, core: (0, 2 * j + core[0])),
-                pl.BlockSpec((wide, wide), lambda j, core: (0, 2 * j + 1 - core[0])),
-                anywhere,
+                pl.BlockSpec((wide, 2 * wide), lambda j, core: (0, j)),
             ],
-            out_specs=[pl.BlockSpec((1, tokens, wide), lambda j, core: (j, 0, 0))] * 2
-            + [pl.BlockSpec((1, slots, wide), lambda j, core: (j, 0, 0))] * 2,
-            scratch_shapes=[pltpu.VMEM((tokens + slots, wide), BF)],
+            out_specs=[pl.BlockSpec((1, slots, wide), lambda j, core: (j, 0, 0))] * 2,
+            scratch_shapes=[pltpu.VMEM((slots, wide), BF)],
         ),
-        out_shape=[pltpu.HBM((parts // 2, tokens, wide), BF)] * 2
-        + [pltpu.HBM((parts // 2, slots, wide), BF)] * 2,
-        compiler_params=params(16),
-        cost_estimate=cost(2 * (tokens + slots) * wide * wide * parts, 14 * MIB),
-        name="teacher",
-    )(core.reshape(1), route_index, attn_values, out_weight, out_weight, copies)
+        out_shape=[pltpu.HBM((parts // 2, slots, wide), BF)] * 2,
+        compiler_params=params(16),
+        cost_estimate=cost(2 * slots * wide * wide * parts, 10 * MIB),
+        name="routed",
+    )(core.reshape(1), route_index, attn_values, out_weight)
+    copies, send_routed = pl.pallas_call(
+        copies_kernel,
+        in_specs=[vmem, anywhere],
+        out_specs=[anywhere] * 2,
+        out_shape=[pltpu.HBM((parts, *rows.shape), BF), pltpu.HBM(send_routed.shape, BF)],
+        scratch_shapes=[pltpu.SemaphoreType.DMA((parts,))],
+        input_output_aliases={1: 1},
+        compiler_params=params(4),
+        cost_estimate=cost(0, MIB // 2),
+        name="copies",
+    )(rows, send_routed)
+    every = lax.all_to_all(copies, "tensor", 0, 0, tiled=True)
 
     def along(value, move):
         return lax.ppermute(value, "tensor", [(t, move(t // 8, (t // 2) % 4, t % 2)) for t in range(parts)])
@@ -350,7 +348,7 @@
             compiler_params=params(16),
             cost_estimate=cost(MIB, 24 * height * wide * 2),
             name="core_sum",
-        )(x_at.reshape(1), *[keep] * 4, *[got] * 4)
+        )(x_at.reshape(1), *[hbm(keep)] * 4, *[got] * 4)
 
     def along_x(own, moved):
         return [own] + [
@@ -367,8 +365,7 @@
             pl.BlockSpec(block, lambda i, y: (y[0], i, 0))
         ] * 4
 
-    routed_sums = core_sum(keep_routed, send_routed, slots)
-    own, *moved = routed_sums
+    own, *moved = core_sum(keep_routed, send_routed, slots)
     send_routed, keep_routed = pl.pallas_call(
         routed_sum_kernel,
         grid_spec=pltpu.PrefetchScalarGridSpec(
@@ -382,16 +379,14 @@
         cost_estimate=cost(MIB, MIB),
         name="routed_sum",
     )(y_at.reshape(1), route_index, residual_t, *along_x(own, moved) * 2)
-    other_routed = along_y(send_routed)
-
     packed = 2 * wide + 128
-    sent, scaled, chosen, send = pl.pallas_call(
+    sent, scaled, chosen, send_routed = pl.pallas_call(
         up_kernel,
         grid_spec=pltpu.PrefetchScalarGridSpec(
             num_scalar_prefetch=1,
             grid=(1,),
             in_specs=[vmem, pl.BlockSpec((1, wide), lambda i, group: (0, group[0]))]
-            + [anywhere] * 4,
+            + [anywhere] * 3,
             out_specs=[vmem] * 3 + [anywhere],
             scratch_shapes=[
                 pltpu.VMEM((groups * slots, wide), BF),
@@ -403,36 +398,61 @@
             pltpu.HBM((groups, per, packed), BF),
             pltpu.HBM((live, wide), BF),
             pltpu.HBM((live, groups * slots), BF),
+            pltpu.HBM(send_routed.shape, BF),
+        ],
+        input_output_aliases={5: 3},
+        compiler_params=params(16),
+        cost_estimate=cost(800 * MIB, 4 * MIB),
+        name="up",
+    )(group.reshape(1), every, norm_gain[None], w_gate, w_up, send_routed)
+    other_routed = along_y(send_routed)
+    got = lax.all_to_all(sent, "batch", 0, 0, tiled=True)
+
+    keep, send = pl.pallas_call(
+        teacher_kernel,
+        grid_spec=pltpu.PrefetchScalarGridSpec(
+            num_scalar_prefetch=1,
+            grid=(parts // 2,),
+            in_specs=[
+                pl.BlockSpec(attn_values.shape, lambda j, core: (0, 0)),
+                pl.BlockSpec((wide, wide), lambda j, core: (0, 2 * j + core[0])),
+                pl.BlockSpec((wide, wide), lambda j, core: (0, 2 * j + 1 - core[0])),
+                anywhere,
+            ],
+            out_specs=[pl.BlockSpec((1, tokens, wide), lambda j, core: (j, 0, 0))] * 2,
+        ),
+        out_shape=[pltpu.HBM((parts // 2, tokens, wide), BF)] * 2,
+        compiler_params=params(16),
+        cost_estimate=cost(2 * tokens * wide * wide * parts, 12 * MIB),
+        name="teacher",
+    )(core.reshape(1), attn_values, out_weight, out_weight, hbm(sent))
+    strip = tokens // 2
+    flat = shape((per, units), F32)
+    both, gate, up, scale, send = pl.pallas_call(
+        lambda *refs: hidden_kernel(features, *refs),
+        in_specs=[vmem] * 3 + [anywhere],
+        out_specs=[vmem] * 4 + [anywhere],
+        out_shape=[
+            pltpu.HBM((groups, per + slots, units), BF),
+            flat,
+            flat,
+            shape((per, 128), F32),
             pltpu.HBM(send.shape, BF),
         ],
-        input_output_aliases={6: 3},
-        compiler_params=params(16),
-        cost_estimate=cost(800 * MIB, 4 * MIB),
-        name="up",
-    )(group.reshape(1), every, norm_gain[None], w_gate, w_up, routed_sums[0], send)
-    got = lax.all_to_all(sent, "batch", 0, 0, tiled=True)
-
-    strip = tokens // 2
-    own, *moved = core_sum(keep, send, strip)
-    flat = shape((per, units), F32)
-    both, gate, up, scale, *moved = pl.pallas_call(
-        lambda *refs: hidden_kernel(features, *refs),
-        in_specs=[vmem] * 3 + [anywhere] * 3,
-        out_specs=[vmem] * 4 + [anywhere] * 3,
-        out_shape=[pltpu.HBM((groups, per + slots, units), BF), flat, flat, shape((per, 128), F32)]
-        + [pltpu.HBM((2, tokens, wide), BF)] * 3,
-        input_output_aliases={3: 4, 4: 5, 5: 6},
+        input_output_aliases={3: 4},
         compiler_params=params(8),
         cost_estimate=cost(MIB, MIB),
         name="hidden",
-    )(got, keep_routed, other_routed, *moved)
+    )(got, keep_routed, other_routed, send)
+    own, *moved = core_sum(keep, send, strip)
     both = lax.all_to_all(both, "batch", 0, 0, tiled=True)
     misfit, hidden = pl.pallas_call(
         down_kernel,
         grid_spec=pltpu.PrefetchScalarGridSpec(
             num_scalar_prefetch=1,
             grid=(1,),
-            in_specs=[vmem] * 3 + [pl.BlockSpec((wide, wide), lambda i, group: (0, group[0]))],
+            in_specs=[vmem] * 3
+            + [pl.BlockSpec((wide, wide), lambda i, group: (0, group[0])), anywhere],
             out_specs=[vmem] * 2,
             scratch_shapes=[pltpu.VMEM((groups * slots, wide), BF)],
         ),
@@ -443,7 +463,7 @@
         compiler_params=params(16),
         cost_estimate=cost(768 * MIB, 4 * MIB),
         name="down",
-    )(group.reshape(1), both, w_down, chosen, projector)
+    )(group.reshape(1), both, w_down, hbm(chosen), projector, hbm(own))
     misfit = lax.all_to_all(misfit, "tensor", 0, 0, tiled=True)
     loss_scale = 1.0 / math.sqrt(live)
     send, keep = pl.pallas_call(
@@ -459,42 +479,46 @@
         cost_estimate=cost(MIB, 3 * MIB),
         name="x_sum",
     )(y_at.reshape(1), *along_x(own, moved) * 2)
-    grad_out, send = pl.pallas_call(
+    grad_out = pl.pallas_call(
         lambda *refs: misfit_kernel(loss_scale, *refs),
-        in_specs=[vmem, anywhere],
-        out_specs=[vmem, anywhere],
-        out_shape=[pltpu.HBM(misfit.shape, BF), pltpu.HBM(send.shape, BF)],
-        input_output_aliases={1: 1},
+        out_shape=pltpu.HBM(misfit.shape, BF),
         compiler_params=params(8),
         cost_estimate=cost(MIB, MIB),
         name="misfit",
-    )(misfit, send)
+    )(misfit)
     other = along_y(send)
     grad_out = lax.all_to_all(grad_out, "tensor", 0, 0, tiled=True)
 
     back = pl.pallas_call(
         back_kernel,
+        in_specs=[vmem] * 2 + [anywhere],
         out_shape=pltpu.HBM((groups, per, units), BF),
         compiler_params=params(16),
         cost_estimate=cost(256 * MIB, MIB),
         name="back",
-    )(grad_out, w_down)
+    )(grad_out, w_down, hbm(send))
     back = lax.all_to_all(back, "batch", 0, 0, tiled=True)
-    acts = pl.pallas_call(
-        acts_kernel,
-        out_shape=pltpu.HBM((groups, per, 2 * units), BF),
-        compiler_params=params(8),
-        cost_estimate=cost(MIB, MIB),
-        name="acts",
-    )(back, gate, up, scale)
-    acts = lax.all_to_all(acts, "batch", 0, 0, tiled=True)
     teacher_hidden = pl.pallas_call(
         residual_kernel,
-        out_shape=shape(residual_t.shape, BF),
+        out_shape=pltpu.HBM(residual_t.shape, BF),
         compiler_params=params(8),
         cost_estimate=cost(MIB, 2 * MIB),
         name="residual",
     )(residual_t, keep, other)
+    acts, teacher_hidden = pl.pallas_call(
+        acts_kernel,
+        in_specs=[vmem] * 4 + [anywhere],
+        out_specs=[vmem, anywhere],
+        out_shape=[
+            pltpu.HBM((groups, per, 2 * units), BF),
+            pltpu.HBM(residual_t.shape, BF),
+        ],
+        input_output_aliases={4: 1},
+        compiler_params=params(8),
+        cost_estimate=cost(MIB, MIB),
+        name="acts",
+    )(back, gate, up, scale, teacher_hidden)
+    acts = lax.all_to_all(acts, "batch", 0, 0, tiled=True)
     grad_down = pl.pallas_call(
         down_weights_kernel,
         out_shape=shape((wide, units), F32),
@@ -508,7 +532,7 @@
         compiler_params=params(16),
         cost_estimate=cost(512 * MIB, 4 * MIB),
         name="weights",
-    )(scaled, acts)
+    )(hbm(scaled), acts)
     return teacher_hidden, grad_gate, grad_up, grad_down
 
 

time: 150 us -> 151 us (level)
  Pallas kernels: 31.2 us -> 42.4 us
  blocking collectives: 27.3 us -> 19 us
  local copies, waits for them, and re-layouts: 4.7 us -> 1.89 us
    ppermute x10, waiting for transfers between devices: 24.7 us -> 9.3 us  [along(): lax.ppermute(value, 'tensor', [(t, move(t // 8, t // 2 % 4, t % 2)) for t...]
    all_to_all x1 -> x2, waiting for transfers between devices: 1.62 us -> 11.2 us  [the longest x1 6.29 us: on_device(): back = lax.all_to_all(back, 'batch', 0, 0, tiled=True)]
    all_to_all x2 -> x1, blocking collectives: 27.3 us -> 19 us  [on_device(): misfit = lax.all_to_all(misfit, 'tensor', 0, 0, tiled=True)]
    pallas_call x5 -> x6, Pallas kernels: 5.57 us -> 13.6 us  [the longest x1 8 us: on_device(): pl.pallas_call(routed_kernel, grid_spec=pltpu.PrefetchScalarGridSpec(num_...]
    all_to_all x1, waiting for transfers between devices: 0.01 us -> 7.07 us  [on_device(): acts = lax.all_to_all(acts, 'batch', 0, 0, tiled=True)]
    all_to_all x1 -> x2, starting transfers between devices: 5.14 us -> 11.4 us  [the longest x1 5.83 us: on_device(): grad_out = lax.all_to_all(grad_out, 'tensor', 0, 0, tiled=True)]
    all_to_all x1, starting transfers between devices: 16.9 us -> 11.4 us  [on_device(): every = lax.all_to_all(copies, 'tensor', 0, 0, tiled=True)]
    unnamed x36 -> x20, local copies, waits for them, and re-layouts: 4.7 us -> 1.89 us
  transfers between devices with their start and end apart: 16 -> 17, of which waited for: 7 -> 6; matrix products, arithmetic and copies ran while one was open for 0% -> 0% of each run, Pallas kernels for 14% -> 22%
where the time goes in v5:
time: 151 us; the launch traced here: 150 us
  starting transfers between devices  52.9 us (35%)
  Pallas kernels  42.4 us (28%)
  waiting for transfers between devices  32.6 us (22%)
  blocking collectives  19 us (13%)
  local copies, waits for them, and re-layouts  1.89 us (1%)
    all_to_all x1, blocking collectives, on_device(): misfit = lax.all_to_all(misfit, 'tensor', 0, 0, tiled=True)  19 us
    ppermute x10, starting transfers between devices, along(): lax.ppermute(value, 'tensor', [(t, move(t // 8, t // 2 % 4, t % 2)) for t...  16.7 us
    all_to_all x1, starting transfers between devices, on_device(): every = lax.all_to_all(copies, 'tensor', 0, 0, tiled=True)  11.4 us
    ppermute x10, waiting for transfers between devices, along(): lax.ppermute(value, 'tensor', [(t, move(t // 8, t // 2 % 4, t % 2)) for t...  9.3 us
    pallas_call x1, Pallas kernels, on_device(): pl.pallas_call(teacher_kernel, grid_spec=pltpu.PrefetchScalarGridSpec(num...  8.66 us
    pallas_call x1, Pallas kernels, on_device(): pl.pallas_call(routed_kernel, grid_spec=pltpu.PrefetchScalarGridSpec(num_...  8 us
    all_to_all x1, waiting for transfers between devices, on_device(): acts = lax.all_to_all(acts, 'batch', 0, 0, tiled=True)  7.07 us
    all_to_all x1, waiting for transfers between devices, on_device(): back = lax.all_to_all(back, 'batch', 0, 0, tiled=True)  6.29 us
  transfers between devices with their start and end apart: 17, of which 6 were waited for; matrix products, arithmetic and copies ran while one was open for 0% of the time, Pallas kernels for 22%

profile of v5, /device:TPU:0, one launch (start us, length us, event | category | flops | bytes accessed | tf_op | source)
XLA Modules:
  0.0 149.6 jit_solution(8967274454124698681)
XLA Ops:
  4.8 8.0 %routed.1 = (bf16[8,64,512]{2,1,0:T(8,128)(2,1)}, bf16[8,64,512]{2,1,0:T(8,128)(2,1)}) custom-call(s32[1]{0:T(128)} %bitcast.1.core_ref, s32[1,64]{1,0:T(1,128)} %route_ref.5, bf16[256,512]{1,0:T(8,128)(2,1)S(1)} %copy-done.1, bf16[512,8192]{1,0:T(8,128)(2,1)} %other_ref.1), custom_call_target="tpu_custom_call" | custom-call | flops 524288 | bytes 10240 | tf_op jit(solution)/shard_map/routed/pallas_call | solution.py:297
  13.8 11.4 %all-to-all-start = ((bf16[16,40,512]{2,1,0:T(8,128)(2,1)}), bf16[16,40,512]{2,1,0:T(8,128)(2,1)S(1)}, u32[]{:S(2)}, u32[]{:S(2)}) async-start(bf16[16,40,512]{2,1,0:T(8,128)(2,1)} %get-tuple-element.38), calls=%async_computation | async-start | bytes 1310720 | tf_op jit(solution)/shard_map/all_to_all | solution.py:326
  29.1 2.7 %collective-permute-start.3 = (bf16[2,64,512]{2,1,0:T(8,128)(2,1)}, bf16[2,64,512]{2,1,0:T(8,128)(2,1)S(1)}, u32[]{:S(2)}, u32[]{:S(2)}) collective-permute-start(bf16[2,64,512]{2,1,0:T(8,128)(2,1)} %get-tuple-element.43), channel_id=1, source_target_pairs={{0,4},{1,5},{2,6},{3,7},{4,0},{5,1},{6,2},{7,3},{8,12},{9,13},{10,... | collective-permute-start | bytes 393224 | tf_op jit(solution)/shard_map/ppermute | solution.py:329
  33.2 6.4 %collective-permute-done.2.refs_1_.refs_5_ = bf16[2,64,512]{2,1,0:T(8,128)(2,1)S(1)} collective-permute-done((bf16[2,64,512]{2,1,0:T(8,128)(2,1)}, bf16[2,64,512]{2,1,0:T(8,128)(2,1)S(1)}, u32[]{:S(2)}, u32[]{:S(2)}) %collective-permute-start.2) | collective-permute-done | bytes 131104 | tf_op jit(solution)/shard_map/ppermute | solution.py:329
  39.6 2.9 %collective-permute-done.3.refs_2_.refs_6_ = bf16[2,64,512]{2,1,0:T(8,128)(2,1)S(1)} collective-permute-done((bf16[2,64,512]{2,1,0:T(8,128)(2,1)}, bf16[2,64,512]{2,1,0:T(8,128)(2,1)S(1)}, u32[]{:S(2)}, u32[]{:S(2)}) %collective-permute-start.3) | collective-permute-done | bytes 131104 | tf_op jit(solution)/shard_map/ppermute | solution.py:329
  45.0 2.5 %up.1 = (bf16[8,32,1152]{2,1,0:T(8,128)(2,1)}, bf16[256,512]{1,0:T(8,128)(2,1)}, bf16[256,512]{1,0:T(8,128)(2,1)}, bf16[1,64,512]{2,1,0:T(8,128)(2,1)}) custom-call(s32[1]{0:T(128)} %bitcast.group_ref, bf16[16,40,512]{2,1,0:T(8,128)(2,1)S(1)} %all-to-all-done.got_ref, f32[1,4096]{1,0:T(1,128)S(1)} %bitcast.5, ...), custom_call_target="tpu_custom_call", output_to_operand_aliasing={{3}: (5, {})} | custom-call | flops 819200 | bytes 4096 | tf_op jit(solution)/shard_map/up/pallas_call | solution.py:383
  47.5 3.6 %all-to-all-start.1 = ((bf16[8,32,1152]{2,1,0:T(8,128)(2,1)}), bf16[8,32,1152]{2,1,0:T(8,128)(2,1)S(1)}, u32[]{:S(2)}, u32[]{:S(2)}) async-start(bf16[8,32,1152]{2,1,0:T(8,128)(2,1)} %get-tuple-element.46.after_ref), calls=%async_computation.1 | async-start | bytes 1179648 | tf_op jit(solution)/shard_map/all_to_all | solution.py:409
  51.1 3.3 %collective-permute-start.5 = (bf16[1,64,512]{2,1,0:T(8,128)(2,1)}, bf16[1,64,512]{2,1,0:T(8,128)(2,1)S(1)}, u32[]{:S(2)}, u32[]{:S(2)}) collective-permute-start(bf16[1,64,512]{2,1,0:T(8,128)(2,1)} %get-tuple-element.48), channel_id=1, source_target_pairs={{0,8},{1,9},{2,10},{3,11},{4,12},{5,13},{6,14},{7,15},{8,0},{9,1},... | collective-permute-start | bytes 196616 | tf_op jit(solution)/shard_map/ppermute | solution.py:329
  54.4 8.7 %teacher.1 = (bf16[8,256,512]{2,1,0:T(8,128)(2,1)}, bf16[8,256,512]{2,1,0:T(8,128)(2,1)}) custom-call(s32[1]{0:T(128)} %bitcast.1.core_ref, bf16[256,512]{1,0:T(8,128)(2,1)S(1)} %copy-done.2, bf16[512,8192]{1,0:T(8,128)(2,1)} %other_ref.1, bf16[512,8192]{1,0:T(8,128)(2,1)} %other_ref.1, bf16[8,32,1152]{2,1,0:T(8,128)(2,1)} %get-tuple-element.46.after_ref), custom_call_target="tpu_custom_call" | custom-call | flops 2097152 | bytes 12288 | tf_op jit(solution)/shard_map/teacher/pallas_call | solution.py:411
  64.2 5.0 %all-to-all-start.2 = ((bf16[8,96,512]{2,1,0:T(8,128)(2,1)}), bf16[8,96,512]{2,1,0:T(8,128)(2,1)S(1)}, u32[]{:S(2)}, u32[]{:S(2)}) async-start(bf16[8,96,512]{2,1,0:T(8,128)(2,1)} %get-tuple-element.50), calls=%async_computation.2 | async-start | bytes 1572864 | tf_op jit(solution)/shard_map/all_to_all | solution.py:448
  69.2 3.9 %core_sum.3 = (bf16[2,256,512]{2,1,0:T(8,128)(2,1)}, bf16[2,256,512]{2,1,0:T(8,128)(2,1)}, bf16[2,256,512]{2,1,0:T(8,128)(2,1)}, bf16[2,256,512]{2,1,0:T(8,128)(2,1)}) custom-call(s32[1]{0:T(128)} %bitcast.4.x_ref, bf16[8,256,512]{2,1,0:T(8,128)(2,1)} %get-tuple-element.52.refs_0_.refs_1_.refs_2_.refs_3_, ...), custom_call_target="tpu_custom_call" | custom-call | flops 1024 | bytes 6144 | tf_op jit(solution)/shard_map/core_sum/pallas_call | solution.py:335
  74.9 2.0 %collective-permute-start.9 = (bf16[2,256,512]{2,1,0:T(8,128)(2,1)}, bf16[2,256,512]{2,1,0:T(8,128)(2,1)S(1)}, u32[]{:S(2)}, u32[]{:S(2)}) collective-permute-start(bf16[2,256,512]{2,1,0:T(8,128)(2,1)} %get-tuple-element.58), channel_id=1, source_target_pairs={{0,6},{1,7},{2,0},{3,1},{4,2},{5,3},{6,4},{7,5},{8,14},{9,15},{10,... | collective-permute-start | bytes 1572872 | tf_op jit(solution)/shard_map/ppermute | solution.py:329
  76.8 5.0 %all-to-all-done.2.got_ref = bf16[8,96,512]{2,1,0:T(8,128)(2,1)S(1)} async-done(((bf16[8,96,512]{2,1,0:T(8,128)(2,1)}), bf16[8,96,512]{2,1,0:T(8,128)(2,1)S(1)}, u32[]{:S(2)}, u32[]{:S(2)}) %all-to-all-start.2) | async-done | bytes 786464 | tf_op jit(solution)/shard_map/all_to_all | solution.py:448
  81.8 2.6 %down.1 = (bf16[16,16,512]{2,1,0:T(8,128)(2,1)}, bf16[256,512]{1,0:T(8,128)(2,1)}) custom-call(s32[1]{0:T(128)} %bitcast.group_ref, bf16[8,96,512]{2,1,0:T(8,128)(2,1)S(1)} %all-to-all-done.2.got_ref, bf16[512,512]{1,0:T(8,128)(2,1)} %down_ref.3, bf16[256,512]{1,0:T(8,128)(2,1)} %get-tuple-element.51.chosen_ref, bf16[512,4096]{1,0:T(8,128)(2,1)} %projector_ref.1, ...), custom_call_target="tpu_custom_call" | custom-call | flops 786432 | bytes 4096 | tf_op jit(solution)/shard_map/down/pallas_call | solution.py:449
  84.5 19.0 %all_to_all.35.refs_0_ = bf16[16,16,512]{2,1,0:T(8,128)(2,1)S(1)} all-to-all(bf16[16,16,512]{2,1,0:T(8,128)(2,1)} %get-tuple-element.55), channel_id=1, replica_groups=mesh['batch'=8,'tensor'=16] {'tensor'}, dimensions={0} | all-to-all | bytes 524288 | tf_op jit(solution)/shard_map/all_to_all | solution.py:467
  104.2 5.8 %all-to-all-start.4 = ((bf16[16,16,512]{2,1,0:T(8,128)(2,1)}), bf16[16,16,512]{2,1,0:T(8,128)(2,1)S(1)}, u32[]{:S(2)}, u32[]{:S(2)}) async-start(bf16[16,16,512]{2,1,0:T(8,128)(2,1)} %misfit.1), calls=%async_computation.4 | async-start | bytes 524288 | tf_op jit(solution)/shard_map/all_to_all | solution.py:490
  111.1 3.4 %collective-permute-start.10 = (bf16[1,256,512]{2,1,0:T(8,128)(2,1)}, bf16[1,256,512]{2,1,0:T(8,128)(2,1)S(1)}, u32[]{:S(2)}, u32[]{:S(2)}) collective-permute-start(bf16[1,256,512]{2,1,0:T(8,128)(2,1)} %get-tuple-element.59.after_ref), channel_id=1, source_target_pairs={{0,8},{1,9},{2,10},{3,11},{4,12},{5,13},{6,14},{7,15},{8,0},{9,1},... | collective-permute-start | bytes 786440 | tf_op jit(solution)/shard_map/ppermute | solution.py:329
  114.6 4.9 %all-to-all-done.4.got_ref.grad_ref = bf16[16,16,512]{2,1,0:T(8,128)(2,1)S(1)} async-done(((bf16[16,16,512]{2,1,0:T(8,128)(2,1)}), bf16[16,16,512]{2,1,0:T(8,128)(2,1)S(1)}, u32[]{:S(2)}, u32[]{:S(2)}) %all-to-all-start.4) | async-done | bytes 262176 | tf_op jit(solution)/shard_map/all_to_all | solution.py:490
  119.4 2.0 %back.1 = bf16[8,32,512]{2,1,0:T(8,128)(2,1)} custom-call(bf16[16,16,512]{2,1,0:T(8,128)(2,1)S(1)} %all-to-all-done.4.got_ref.grad_ref, bf16[512,512]{1,0:T(8,128)(2,1)} %down_ref.3, bf16[1,256,512]{2,1,0:T(8,128)(2,1)} %get-tuple-element.59.after_ref), custom_call_target="tpu_custom_call" | custom-call | flops 262144 | bytes 1024 | tf_op jit(solution)/shard_map/back/pallas_call | solution.py:492
  121.5 5.5 %all-to-all-start.5 = ((bf16[8,32,512]{2,1,0:T(8,128)(2,1)}), bf16[8,32,512]{2,1,0:T(8,128)(2,1)S(1)}, u32[]{:S(2)}, u32[]{:S(2)}) async-start(bf16[8,32,512]{2,1,0:T(8,128)(2,1)} %back.1), calls=%async_computation.5 | async-start | bytes 524288 | tf_op jit(solution)/shard_map/all_to_all | solution.py:500
  128.0 6.3 %all-to-all-done.5.got_ref = bf16[8,32,512]{2,1,0:T(8,128)(2,1)S(1)} async-done(((bf16[8,32,512]{2,1,0:T(8,128)(2,1)}), bf16[8,32,512]{2,1,0:T(8,128)(2,1)S(1)}, u32[]{:S(2)}, u32[]{:S(2)}) %all-to-all-start.5) | async-done | bytes 262176 | tf_op jit(solution)/shard_map/all_to_all | solution.py:500
  135.2 3.5 %all-to-all-start.6 = ((bf16[8,32,1024]{2,1,0:T(8,128)(2,1)}), bf16[8,32,1024]{2,1,0:T(8,128)(2,1)S(1)}, u32[]{:S(2)}, u32[]{:S(2)}) async-start(bf16[8,32,1024]{2,1,0:T(8,128)(2,1)} %get-tuple-element.66), calls=%async_computation.6 | async-start | bytes 1048576 | tf_op jit(solution)/shard_map/all_to_all | solution.py:521
  140.0 7.1 %all-to-all-done.6.got_ref = bf16[8,32,1024]{2,1,0:T(8,128)(2,1)S(1)} async-done(((bf16[8,32,1024]{2,1,0:T(8,128)(2,1)}), bf16[8,32,1024]{2,1,0:T(8,128)(2,1)S(1)}, u32[]{:S(2)}, u32[]{:S(2)}) %all-to-all-start.6) | async-done | bytes 524320 | tf_op jit(solution)/shard_map/all_to_all | solution.py:521
  147.0 2.6 %weights.1 = (f32[512,512]{1,0:T(8,128)}, f32[512,512]{1,0:T(8,128)}) custom-call(bf16[256,512]{1,0:T(8,128)(2,1)} %get-tuple-element.65.rows_ref, bf16[8,32,1024]{2,1,0:T(8,128)(2,1)S(1)} %all-to-all-done.6.got_ref), custom_call_target="tpu_custom_call" | custom-call | flops 524288 | bytes 4096 | tf_op jit(solution)/shard_map/weights/pallas_call | solution.py:529
  (48 shorter events, 20.8 us)
Async XLA Ops:
  2.4 10.4 %collective-permute-start = (bf16[40,512]{1,0:T(8,128)(2,1)}, bf16[40,512]{1,0:T(8,128)(2,1)S(1)}, u32[]{:S(2)}, u32[]{:S(2)}) collective-permute-start(bf16[40,512]{1,0:T(8,128)(2,1)} %rows.1), channel_id=1, source_target_pairs={{0,0},{1,1},{2,16},{3,17},{4,32},{5,33},{6,48},{7,49},{8,64},{9,65... | collective-permute-start | bytes 122888 | tf_op jit(solution)/shard_map/ppermute | solution.py:295
  13.7 11.5 %collective-permute-start.1 = (bf16[8,64,512]{2,1,0:T(8,128)(2,1)}, bf16[8,64,512]{2,1,0:T(8,128)(2,1)S(1)}, u32[]{:S(2)}, u32[]{:S(2)}) collective-permute-start(bf16[8,64,512]{2,1,0:T(8,128)(2,1)} %get-tuple-element.40), channel_id=1, source_target_pairs={{0,1},{1,0},{2,3},{3,2},{4,5},{5,4},{6,7},{7,6},{8,9},{9,8},{10,11... | collective-permute-start | bytes 1572872 | tf_op jit(solution)/shard_map/ppermute | solution.py:329
  13.8 31.2 %all-to-all-start = ((bf16[16,40,512]{2,1,0:T(8,128)(2,1)}), bf16[16,40,512]{2,1,0:T(8,128)(2,1)S(1)}, u32[]{:S(2)}, u32[]{:S(2)}) async-start(bf16[16,40,512]{2,1,0:T(8,128)(2,1)} %get-tuple-element.38), calls=%async_computation | async-start | bytes 1310720 | tf_op jit(solution)/shard_map/all_to_all | solution.py:326
  25.2 17.3 %copy-start.3 = (bf16[512,256]{1,0:T(8,128)(2,1)S(1)}, bf16[512,256]{1,0:T(8,128)(2,1)}, u32[]{:S(2)}) copy-start(bf16[512,256]{1,0:T(8,128)(2,1)} %residual_ref.3) | copy-start | bytes 786436
  25.3 19.7 %copy-start.9 = (f32[4096]{0:T(1024)S(1)}, f32[4096]{0:T(1024)}, u32[]{:S(2)}) copy-start(f32[4096]{0:T(1024)} %param.15) | copy-start | bytes 49156
  27.1 12.4 %collective-permute-start.2 = (bf16[2,64,512]{2,1,0:T(8,128)(2,1)}, bf16[2,64,512]{2,1,0:T(8,128)(2,1)S(1)}, u32[]{:S(2)}, u32[]{:S(2)}) collective-permute-start(bf16[2,64,512]{2,1,0:T(8,128)(2,1)} %get-tuple-element.42), channel_id=1, source_target_pairs={{0,2},{1,3},{2,4},{3,5},{4,6},{5,7},{6,0},{7,1},{8,10},{9,11},{10,... | collective-permute-start | bytes 393224 | tf_op jit(solution)/shard_map/ppermute | solution.py:329
  29.1 13.4 %collective-permute-start.3 = (bf16[2,64,512]{2,1,0:T(8,128)(2,1)}, bf16[2,64,512]{2,1,0:T(8,128)(2,1)S(1)}, u32[]{:S(2)}, u32[]{:S(2)}) collective-permute-start(bf16[2,64,512]{2,1,0:T(8,128)(2,1)} %get-tuple-element.43), channel_id=1, source_target_pairs={{0,4},{1,5},{2,6},{3,7},{4,0},{5,1},{6,2},{7,3},{8,12},{9,13},{10,... | collective-permute-start | bytes 393224 | tf_op jit(solution)/shard_map/ppermute | solution.py:329
  31.8 10.7 %collective-permute-start.4 = (bf16[2,64,512]{2,1,0:T(8,128)(2,1)}, bf16[2,64,512]{2,1,0:T(8,128)(2,1)S(1)}, u32[]{:S(2)}, u32[]{:S(2)}) collective-permute-start(bf16[2,64,512]{2,1,0:T(8,128)(2,1)} %get-tuple-element.44), channel_id=1, source_target_pairs={{0,6},{1,7},{2,0},{3,1},{4,2},{5,3},{6,4},{7,5},{8,14},{9,15},{10,... | collective-permute-start | bytes 393224 | tf_op jit(solution)/shard_map/ppermute | solution.py:329
  47.5 15.5 %all-to-all-start.1 = ((bf16[8,32,1152]{2,1,0:T(8,128)(2,1)}), bf16[8,32,1152]{2,1,0:T(8,128)(2,1)S(1)}, u32[]{:S(2)}, u32[]{:S(2)}) async-start(bf16[8,32,1152]{2,1,0:T(8,128)(2,1)} %get-tuple-element.46.after_ref), calls=%async_computation.1 | async-start | bytes 1179648 | tf_op jit(solution)/shard_map/all_to_all | solution.py:409
  51.1 12.0 %copy-start.8 = (f32[1,64,512]{2,1,0:T(8,128)S(1)}, f32[1,64,512]{2,1,0:T(8,128)}, u32[]{:S(2)}) copy-start(f32[1,64,512]{2,1,0:T(8,128)} %get-tuple-element.47.refs_1_) | copy-start | bytes 393220
  51.1 11.9 %collective-permute-start.5 = (bf16[1,64,512]{2,1,0:T(8,128)(2,1)}, bf16[1,64,512]{2,1,0:T(8,128)(2,1)S(1)}, u32[]{:S(2)}, u32[]{:S(2)}) collective-permute-start(bf16[1,64,512]{2,1,0:T(8,128)(2,1)} %get-tuple-element.48), channel_id=1, source_target_pairs={{0,8},{1,9},{2,10},{3,11},{4,12},{5,13},{6,14},{7,15},{8,0},{9,1},... | collective-permute-start | bytes 196616 | tf_op jit(solution)/shard_map/ppermute | solution.py:329
  64.2 5.0 %collective-permute-start.6 = (bf16[8,256,512]{2,1,0:T(8,128)(2,1)}, bf16[8,256,512]{2,1,0:T(8,128)(2,1)S(1)}, u32[]{:S(2)}, u32[]{:S(2)}) collective-permute-start(bf16[8,256,512]{2,1,0:T(8,128)(2,1)} %get-tuple-element.53), channel_id=1, source_target_pairs={{0,1},{1,0},{2,3},{3,2},{4,5},{5,4},{6,7},{7,6},{8,9},{9,8},{10,11... | collective-permute-start | bytes 6291464 | tf_op jit(solution)/shard_map/ppermute | solution.py:329
  64.2 17.7 %all-to-all-start.2 = ((bf16[8,96,512]{2,1,0:T(8,128)(2,1)}), bf16[8,96,512]{2,1,0:T(8,128)(2,1)S(1)}, u32[]{:S(2)}, u32[]{:S(2)}) async-start(bf16[8,96,512]{2,1,0:T(8,128)(2,1)} %get-tuple-element.50), calls=%async_computation.2 | async-start | bytes 1572864 | tf_op jit(solution)/shard_map/all_to_all | solution.py:448
  73.0 37.0 %collective-permute-start.7 = (bf16[2,256,512]{2,1,0:T(8,128)(2,1)}, bf16[2,256,512]{2,1,0:T(8,128)(2,1)S(1)}, u32[]{:S(2)}, u32[]{:S(2)}) collective-permute-start(bf16[2,256,512]{2,1,0:T(8,128)(2,1)} %get-tuple-element.56), channel_id=1, source_target_pairs={{0,2},{1,3},{2,4},{3,5},{4,6},{5,7},{6,0},{7,1},{8,10},{9,11},{10,... | collective-permute-start | bytes 1572872 | tf_op jit(solution)/shard_map/ppermute | solution.py:329
  73.0 37.0 %collective-permute-start.8 = (bf16[2,256,512]{2,1,0:T(8,128)(2,1)}, bf16[2,256,512]{2,1,0:T(8,128)(2,1)S(1)}, u32[]{:S(2)}, u32[]{:S(2)}) collective-permute-start(bf16[2,256,512]{2,1,0:T(8,128)(2,1)} %get-tuple-element.57), channel_id=1, source_target_pairs={{0,4},{1,5},{2,6},{3,7},{4,0},{5,1},{6,2},{7,3},{8,12},{9,13},{10,... | collective-permute-start | bytes 1572872 | tf_op jit(solution)/shard_map/ppermute | solution.py:329
  74.9 35.2 %collective-permute-start.9 = (bf16[2,256,512]{2,1,0:T(8,128)(2,1)}, bf16[2,256,512]{2,1,0:T(8,128)(2,1)S(1)}, u32[]{:S(2)}, u32[]{:S(2)}) collective-permute-start(bf16[2,256,512]{2,1,0:T(8,128)(2,1)} %get-tuple-element.58), channel_id=1, source_target_pairs={{0,6},{1,7},{2,0},{3,1},{4,2},{5,3},{6,4},{7,5},{8,14},{9,15},{10,... | collective-permute-start | bytes 1572872 | tf_op jit(solution)/shard_map/ppermute | solution.py:329
  81.8 28.3 %copy-start = (bf16[2,256,512]{2,1,0:T(8,128)(2,1)S(1)}, bf16[2,256,512]{2,1,0:T(8,128)(2,1)}, u32[]{:S(2)}) copy-start(bf16[2,256,512]{2,1,0:T(8,128)(2,1)} %get-tuple-element.54.after_ref.refs_0_.refs_4_) | copy-start | bytes 1572868
  104.2 15.2 %all-to-all-start.4 = ((bf16[16,16,512]{2,1,0:T(8,128)(2,1)}), bf16[16,16,512]{2,1,0:T(8,128)(2,1)S(1)}, u32[]{:S(2)}, u32[]{:S(2)}) async-start(bf16[16,16,512]{2,1,0:T(8,128)(2,1)} %misfit.1), calls=%async_computation.4 | async-start | bytes 524288 | tf_op jit(solution)/shard_map/all_to_all | solution.py:490
  110.1 17.0 %copy-start.4 = (bf16[512,256]{1,0:T(8,128)(2,1)S(1)}, bf16[512,256]{1,0:T(8,128)(2,1)}, u32[]{:S(2)}) copy-start(bf16[512,256]{1,0:T(8,128)(2,1)} %residual_ref.3) | copy-start | bytes 786436
  111.1 15.9 %copy-start.6 = (f32[1,256,512]{2,1,0:T(8,128)S(1)}, f32[1,256,512]{2,1,0:T(8,128)}, u32[]{:S(2)}) copy-start(f32[1,256,512]{2,1,0:T(8,128)} %get-tuple-element.63.keep_ref) | copy-start | bytes 1572868
  111.1 15.9 %collective-permute-start.10 = (bf16[1,256,512]{2,1,0:T(8,128)(2,1)}, bf16[1,256,512]{2,1,0:T(8,128)(2,1)S(1)}, u32[]{:S(2)}, u32[]{:S(2)}) collective-permute-start(bf16[1,256,512]{2,1,0:T(8,128)(2,1)} %get-tuple-element.59.after_ref), channel_id=1, source_target_pairs={{0,8},{1,9},{2,10},{3,11},{4,12},{5,13},{6,14},{7,15},{8,0},{9,1},... | collective-permute-start | bytes 786440 | tf_op jit(solution)/shard_map/ppermute | solution.py:329
  121.5 17.2 %copy-start.7 = (bf16[256,512]{1,0:T(8,128)(2,1)S(1)}, bf16[256,512]{1,0:T(8,128)(2,1)}, u32[]{:S(2)}) copy-start(bf16[256,512]{1,0:T(8,128)(2,1)} %get-tuple-element.69.hidden_ref) | copy-start | bytes 786436
  121.5 12.8 %all-to-all-start.5 = ((bf16[8,32,512]{2,1,0:T(8,128)(2,1)}), bf16[8,32,512]{2,1,0:T(8,128)(2,1)S(1)}, u32[]{:S(2)}, u32[]{:S(2)}) async-start(bf16[8,32,512]{2,1,0:T(8,128)(2,1)} %back.1), calls=%async_computation.5 | async-start | bytes 524288 | tf_op jit(solution)/shard_map/all_to_all | solution.py:500
  135.2 11.9 %all-to-all-start.6 = ((bf16[8,32,1024]{2,1,0:T(8,128)(2,1)}), bf16[8,32,1024]{2,1,0:T(8,128)(2,1)S(1)}, u32[]{:S(2)}, u32[]{:S(2)}) async-start(bf16[8,32,1024]{2,1,0:T(8,128)(2,1)} %get-tuple-element.66), calls=%async_computation.6 | async-start | bytes 1048576 | tf_op jit(solution)/shard_map/all_to_all | solution.py:521
  (3 other events, 12.8 us)

commit v6 on v4

--- a/solution.py
+++ b/solution.py
@@ -51,7 +51,7 @@
 
 
 def teacher_kernel(
-    core_ref, route_ref, attn_ref, mine_ref, other_ref, after_ref,
+    core_ref, route_ref, attn_ref, mine_ref, other_ref,
     keep_ref, send_ref, keep_routed_ref, send_routed_ref, left_ref,
 ):
     tokens = attn_ref.shape[0]
@@ -70,7 +70,7 @@
         routed_ref[0] = product[tokens:]
 
 
-def copies_kernel(rows_ref, out_ref, sems):
+def copies_kernel(rows_ref, p1, p2, out_ref, q1, q2, sems):
     copies = [
         pltpu.make_async_copy(rows_ref, out_ref.at[s], sems.at[s]) for s in range(out_ref.shape[0])
     ]
@@ -87,17 +87,17 @@
         refs[2 * ways + j][...] = total.astype(BF).reshape(refs[2 * ways + j].shape)
 
 
-def x_sum_kernel(y_ref, *refs):
+def x_sum_kernel(*refs):
+    total = refs[0][...].astype(F32)
+    for ref in refs[1:-1]:
+        total = total + ref[...].astype(F32)
+    refs[-1][...] = total.astype(refs[-1].dtype)
+
+
+def routed_sum_kernel(y_ref, route_ref, residual_ref, after_ref, *refs):
     ways = len(refs) // 2 - 1
-    for i, out_ref in enumerate(refs[-2:]):
-        total = refs[i * ways][...].astype(F32)
-        for ref in refs[i * ways + 1 : (i + 1) * ways]:
-            total = total + ref[...].astype(F32)
-        out_ref[...] = total.astype(out_ref.dtype)
-
-
-def routed_sum_kernel(y_ref, route_ref, residual_ref, *refs):
-    x_sum_kernel(y_ref, *refs)
+    x_sum_kernel(*refs[0:ways], refs[-2])
+    x_sum_kernel(*refs[ways : 2 * ways], refs[-1])
     hot = slot_rows(route_ref[...], residual_ref.shape[1])
     refs[-1][0] = refs[-1][0] + dot(hot, residual_ref[...], 1, 1)
 
@@ -108,8 +108,8 @@
 
 
 def up_kernel(
-    group_ref, got_ref, gain_ref, gate_ref, up_ref, after_ref, passed_ref,
-    out_ref, rows_ref, chosen_ref, same_ref, padded_ref, weights_ref, sems,
+    group_ref, got_ref, gain_ref, gate_ref, up_ref, p1, p2, p3, p4,
+    out_ref, rows_ref, chosen_ref, q1, q2, q3, q4, padded_ref, weights_ref, sems,
 ):
     loads = [
         pltpu.make_async_copy(ref, weights_ref.at[i], sems.at[i])
@@ -169,8 +169,8 @@
 
 
 def hidden_kernel(
-    features, got_ref, keep_ref, other_ref, s1, s2, s3,
-    out_ref, gate_ref, up_ref, scale_ref, t1, t2, t3,
+    features, got_ref, keep_ref, other_ref, p1, p2, p3, p4,
+    out_ref, gate_ref, up_ref, scale_ref, q1, q2, q3, q4,
 ):
     per, wide = gate_ref.shape
     at = got_ref.shape[2]
@@ -192,7 +192,8 @@
 
 
 def down_kernel(
-    group_ref, got_ref, down_ref, chosen_ref, projector_ref, out_ref, hidden_ref, rows_ref
+    group_ref, got_ref, down_ref, chosen_ref, projector_ref, after_ref,
+    out_ref, hidden_ref, rows_ref,
 ):
     groups = got_ref.shape[0]
     per = hidden_ref.shape[0] // groups
@@ -205,7 +206,7 @@
     out_ref[...] = part.astype(BF).reshape(out_ref.shape)
 
 
-def misfit_kernel(scale, got_ref, passed_ref, out_ref, same_ref):
+def misfit_kernel(scale, got_ref, out_ref):
     total = got_ref[0].astype(F32)
     for s in range(1, got_ref.shape[0]):
         total = total + got_ref[s].astype(F32)
@@ -214,7 +215,7 @@
         out_ref[s] = grad
 
 
-def back_kernel(got_ref, down_ref, out_ref):
+def back_kernel(got_ref, down_ref, passed_ref, out_ref, same_ref):
     groups, per, wide = out_ref.shape
     part = dot(got_ref[...].reshape(groups * per, got_ref.shape[2]), down_ref[...])
     out_ref[...] = part.astype(BF).reshape(groups, per, wide)
@@ -273,9 +274,12 @@
     shape = jax.ShapeDtypeStruct
     vmem = pl.BlockSpec(memory_space=pltpu.VMEM)
     anywhere = pl.BlockSpec(memory_space=pl.ANY)
-    out_weight, w_gate, w_up, w_down, projector = (
-        pltpu.with_memory_space_constraint(w, pltpu.HBM)
-        for w in (out_weight, w_gate, w_up, w_down, projector)
+
+    def hbm(value):
+        return pltpu.with_memory_space_constraint(value, pltpu.HBM)
+
+    out_weight, w_gate, w_up, projector, student_input, route_index = (
+        hbm(w) for w in (out_weight, w_gate, w_up, projector, student_input, route_index)
     )
 
     rows = pl.pallas_call(
@@ -292,18 +296,6 @@
     ]
     rows = lax.ppermute(rows, ("batch", "tensor"), pairs)
 
-    copies = pl.pallas_call(
-        copies_kernel,
-        in_specs=[vmem],
-        out_specs=anywhere,
-        out_shape=pltpu.HBM((parts, *rows.shape), BF),
-        scratch_shapes=[pltpu.SemaphoreType.DMA((parts,))],
-        compiler_params=params(4),
-        cost_estimate=cost(0, MIB // 2),
-        name="copies",
-    )(rows)
-    every = lax.all_to_all(copies, "tensor", 0, 0, tiled=True)
-
     keep, send, keep_routed, send_routed = pl.pallas_call(
         teacher_kernel,
         grid_spec=pltpu.PrefetchScalarGridSpec(
@@ -314,7 +306,6 @@
                 pl.BlockSpec(attn_values.shape, lambda j, core: (0, 0)),
                 pl.BlockSpec((wide, wide), lambda j, core: (0, 2 * j + core[0])),
                 pl.BlockSpec((wide, wide), lambda j, core: (0, 2 * j + 1 - core[0])),
-                anywhere,
             ],
             out_specs=[pl.BlockSpec((1, tokens, wide), lambda j, core: (j, 0, 0))] * 2
             + [pl.BlockSpec((1, slots, wide), lambda j, core: (j, 0, 0))] * 2,
@@ -325,7 +316,23 @@
         compiler_params=params(16),
         cost_estimate=cost(2 * (tokens + slots) * wide * wide * parts, 14 * MIB),
         name="teacher",
-    )(core.reshape(1), route_index, attn_values, out_weight, out_weight, copies)
+    )(core.reshape(1), route_index, hbm(attn_values), out_weight, out_weight)
+    copies, send_routed, send = pl.pallas_call(
+        copies_kernel,
+        in_specs=[vmem] + [anywhere] * 2,
+        out_specs=[anywhere] * 3,
+        out_shape=[
+            pltpu.HBM((parts, *rows.shape), BF),
+            pltpu.HBM(send_routed.shape, BF),
+            pltpu.HBM(send.shape, BF),
+        ],
+        scratch_shapes=[pltpu.SemaphoreType.DMA((parts,))],
+        input_output_aliases={1: 1, 2: 2},
+        compiler_params=params(4),
+        cost_estimate=cost(0, MIB // 2),
+        name="copies",
+    )(rows, send_routed, send)
+    every = lax.all_to_all(copies, "tensor", 0, 0, tiled=True)
 
     def along(value, move):
         return lax.ppermute(value, "tensor", [(t, move(t // 8, (t // 2) % 4, t % 2)) for t in range(parts)])
@@ -350,7 +357,7 @@
             compiler_params=params(16),
             cost_estimate=cost(MIB, 24 * height * wide * 2),
             name="core_sum",
-        )(x_at.reshape(1), *[keep] * 4, *[got] * 4)
+        )(x_at.reshape(1), *[hbm(keep)] * 4, *[got] * 4)
 
     def along_x(own, moved):
         return [own] + [
@@ -367,32 +374,66 @@
             pl.BlockSpec(block, lambda i, y: (y[0], i, 0))
         ] * 4
 
-    routed_sums = core_sum(keep_routed, send_routed, slots)
-    own, *moved = routed_sums
+    strip = tokens // 4
+    got = along(send, lambda y, x, c: y * 8 + x * 2 + 1 - c)
+    blocks = [
+        pl.BlockSpec(
+            (1, strip, wide), lambda n, x, y, i=i, j=j: (4 * ((y[0] + i) & 1) + ((x[0] + j) & 3), n, 0)
+        )
+        for i in (1, 0)
+        for j in range(4)
+    ]
+    sums = pl.pallas_call(
+        lambda x_ref, *refs: core_sum_kernel(*refs),
+        grid_spec=pltpu.PrefetchScalarGridSpec(
+            num_scalar_prefetch=2,
+            grid=(tokens // strip,),
+            in_specs=blocks * 2,
+            out_specs=[pl.BlockSpec((1, strip, wide), lambda n, x, y: (0, n, 0))] * 8,
+        ),
+        out_shape=[pltpu.HBM((1, tokens, wide), BF)] * 8,
+        compiler_params=params(16),
+        cost_estimate=cost(MIB, 6 * MIB),
+        name="core_sum",
+    )(x_at.reshape(1), y_at.reshape(1), *[hbm(keep)] * 8, *[got] * 8)
+    others, own = sums[:4], sums[4:]
+
+    routed, *moved = core_sum(keep_routed, send_routed, slots)
     send_routed, keep_routed = pl.pallas_call(
         routed_sum_kernel,
         grid_spec=pltpu.PrefetchScalarGridSpec(
             num_scalar_prefetch=1,
             grid=(1,),
-            in_specs=[vmem, vmem] + y_blocks(slots),
+            in_specs=[vmem, vmem, anywhere] + y_blocks(slots),
             out_specs=[pl.BlockSpec((1, slots, wide), lambda i, y: (0, 0, 0))] * 2,
         ),
         out_shape=[pltpu.HBM((1, slots, wide), BF), pltpu.HBM((1, slots, wide), F32)],
         compiler_params=params(8),
         cost_estimate=cost(MIB, MIB),
         name="routed_sum",
-    )(y_at.reshape(1), route_index, residual_t, *along_x(own, moved) * 2)
-    other_routed = along_y(send_routed)
+    )(y_at.reshape(1), route_index, residual_t, hbm(own[0]), *along_x(routed, moved) * 2)
+
+    def x_sum(own, moved, kind):
+        return pl.pallas_call(
+            x_sum_kernel,
+            grid=(2,),
+            in_specs=[pl.BlockSpec((1, tokens // 2, wide), lambda n: (0, n, 0))] * 4,
+            out_specs=pl.BlockSpec((1, tokens // 2, wide), lambda n: (0, n, 0)),
+            out_shape=pltpu.HBM((1, tokens, wide), kind),
+            compiler_params=params(8),
+            cost_estimate=cost(MIB, 2 * MIB),
+            name="x_sum",
+        )(*along_x(own, moved))
 
     packed = 2 * wide + 128
-    sent, scaled, chosen, send = pl.pallas_call(
+    sent, scaled, chosen, send_routed, *moved = pl.pallas_call(
         up_kernel,
         grid_spec=pltpu.PrefetchScalarGridSpec(
             num_scalar_prefetch=1,
             grid=(1,),
             in_specs=[vmem, pl.BlockSpec((1, wide), lambda i, group: (0, group[0]))]
-            + [anywhere] * 4,
-            out_specs=[vmem] * 3 + [anywhere],
+            + [anywhere] * 6,
+            out_specs=[vmem] * 3 + [anywhere] * 4,
             scratch_shapes=[
                 pltpu.VMEM((groups * slots, wide), BF),
                 pltpu.VMEM((2, wide, units), BF),
@@ -403,36 +444,45 @@
             pltpu.HBM((groups, per, packed), BF),
             pltpu.HBM((live, wide), BF),
             pltpu.HBM((live, groups * slots), BF),
-            pltpu.HBM(send.shape, BF),
-        ],
-        input_output_aliases={6: 3},
+            pltpu.HBM(send_routed.shape, BF),
+        ]
+        + [pltpu.HBM((1, tokens, wide), BF)] * 3,
+        input_output_aliases={5: 3, 6: 4, 7: 5, 8: 6},
         compiler_params=params(16),
         cost_estimate=cost(800 * MIB, 4 * MIB),
         name="up",
-    )(group.reshape(1), every, norm_gain[None], w_gate, w_up, routed_sums[0], send)
+    )(group.reshape(1), every, norm_gain[None], w_gate, w_up, send_routed, *others[1:])
+    other_routed = along_y(send_routed)
     got = lax.all_to_all(sent, "batch", 0, 0, tiled=True)
 
-    strip = tokens // 2
-    own, *moved = core_sum(keep, send, strip)
     flat = shape((per, units), F32)
-    both, gate, up, scale, *moved = pl.pallas_call(
+    send = x_sum(others[0], moved, BF)
+    both, gate, up, scale, send, *moved = pl.pallas_call(
         lambda *refs: hidden_kernel(features, *refs),
-        in_specs=[vmem] * 3 + [anywhere] * 3,
-        out_specs=[vmem] * 4 + [anywhere] * 3,
-        out_shape=[pltpu.HBM((groups, per + slots, units), BF), flat, flat, shape((per, 128), F32)]
-        + [pltpu.HBM((2, tokens, wide), BF)] * 3,
-        input_output_aliases={3: 4, 4: 5, 5: 6},
+        in_specs=[vmem] * 3 + [anywhere] * 4,
+        out_specs=[vmem] * 4 + [anywhere] * 4,
+        out_shape=[
+            pltpu.HBM((groups, per + slots, units), BF),
+            flat,
+            flat,
+            shape((per, 128), F32),
+        ]
+        + [pltpu.HBM((1, tokens, wide), BF)] * 4,
+        input_output_aliases={3: 4, 4: 5, 5: 6, 6: 7},
         compiler_params=params(8),
         cost_estimate=cost(MIB, MIB),
         name="hidden",
-    )(got, keep_routed, other_routed, *moved)
+    )(got, keep_routed, other_routed, send, *own[1:])
+    other = along_y(send)
+    keep = x_sum(own[0], moved, F32)
     both = lax.all_to_all(both, "batch", 0, 0, tiled=True)
     misfit, hidden = pl.pallas_call(
         down_kernel,
         grid_spec=pltpu.PrefetchScalarGridSpec(
             num_scalar_prefetch=1,
             grid=(1,),
-            in_specs=[vmem] * 3 + [pl.BlockSpec((wide, wide), lambda i, group: (0, group[0]))],
+            in_specs=[vmem] * 3
+            + [pl.BlockSpec((wide, wide), lambda i, group: (0, group[0])), anywhere],
             out_specs=[vmem] * 2,
             scratch_shapes=[pltpu.VMEM((groups * slots, wide), BF)],
         ),
@@ -443,42 +493,35 @@
         compiler_params=params(16),
         cost_estimate=cost(768 * MIB, 4 * MIB),
         name="down",
-    )(group.reshape(1), both, w_down, chosen, projector)
+    )(group.reshape(1), both, w_down, chosen, projector, hbm(keep))
     misfit = lax.all_to_all(misfit, "tensor", 0, 0, tiled=True)
     loss_scale = 1.0 / math.sqrt(live)
-    send, keep = pl.pallas_call(
-        x_sum_kernel,
-        grid_spec=pltpu.PrefetchScalarGridSpec(
-            num_scalar_prefetch=1,
-            grid=(tokens // strip,),
-            in_specs=y_blocks(strip),
-            out_specs=[pl.BlockSpec((1, strip, wide), lambda i, y: (0, i, 0))] * 2,
-        ),
-        out_shape=[pltpu.HBM((1, tokens, wide), BF), pltpu.HBM((1, tokens, wide), F32)],
-        compiler_params=params(16),
-        cost_estimate=cost(MIB, 3 * MIB),
-        name="x_sum",
-    )(y_at.reshape(1), *along_x(own, moved) * 2)
-    grad_out, send = pl.pallas_call(
+    grad_out = pl.pallas_call(
         lambda *refs: misfit_kernel(loss_scale, *refs),
-        in_specs=[vmem, anywhere],
-        out_specs=[vmem, anywhere],
-        out_shape=[pltpu.HBM(misfit.shape, BF), pltpu.HBM(send.shape, BF)],
-        input_output_aliases={1: 1},
+        out_shape=pltpu.HBM(misfit.shape, BF),
         compiler_params=params(8),
         cost_estimate=cost(MIB, MIB),
         name="misfit",
-    )(misfit, send)
-    other = along_y(send)
+    )(misfit)
     grad_out = lax.all_to_all(grad_out, "tensor", 0, 0, tiled=True)
 
-    back = pl.pallas_call(
+    teacher_hidden = pl.pallas_call(
+        residual_kernel,
+        out_shape=pltpu.HBM(residual_t.shape, BF),
+        compiler_params=params(8),
+        cost_estimate=cost(MIB, 2 * MIB),
+        name="residual",
+    )(residual_t, keep, other)
+    back, teacher_hidden = pl.pallas_call(
         back_kernel,
-        out_shape=pltpu.HBM((groups, per, units), BF),
+        in_specs=[vmem] * 2 + [anywhere],
+        out_specs=[vmem, anywhere],
+        out_shape=[shape((groups, per, units), BF), pltpu.HBM(residual_t.shape, BF)],
+        input_output_aliases={2: 1},
         compiler_params=params(16),
         cost_estimate=cost(256 * MIB, MIB),
         name="back",
-    )(grad_out, w_down)
+    )(grad_out, w_down, teacher_hidden)
     back = lax.all_to_all(back, "batch", 0, 0, tiled=True)
     acts = pl.pallas_call(
         acts_kernel,
@@ -488,13 +531,6 @@
         name="acts",
     )(back, gate, up, scale)
     acts = lax.all_to_all(acts, "batch", 0, 0, tiled=True)
-    teacher_hidden = pl.pallas_call(
-        residual_kernel,
-        out_shape=shape(residual_t.shape, BF),
-        compiler_params=params(8),
-        cost_estimate=cost(MIB, 2 * MIB),
-        name="residual",
-    )(residual_t, keep, other)
     grad_down = pl.pallas_call(
         down_weights_kernel,
         out_shape=shape((wide, units), F32),

time: 150 us -> 150 us (level)
  blocking collectives: 27.3 us -> 11.9 us
  waiting for transfers between devices: 32.3 us -> 47.1 us
  local copies, waits for them, and re-layouts: 4.7 us -> 0.05 us
  starting transfers between devices: 52 us -> 55.9 us
    all_to_all x1 -> x0, blocking collectives: 14.6 us -> none  [on_device(): grad_out = lax.all_to_all(grad_out, 'tensor', 0, 0, tiled=True)]
    all_to_all x0 -> x1, waiting for transfers between devices: none -> 8.41 us  [on_device(): grad_out = lax.all_to_all(grad_out, 'tensor', 0, 0, tiled=True)]
    all_to_all x1, waiting for transfers between devices: 0.01 us -> 7.06 us  [on_device(): acts = lax.all_to_all(acts, 'batch', 0, 0, tiled=True)]
    all_to_all x1, waiting for transfers between devices: 5.97 us -> 0.01 us  [on_device(): both = lax.all_to_all(both, 'batch', 0, 0, tiled=True)]
    all_to_all x1, starting transfers between devices: 16.9 us -> 11.3 us  [on_device(): every = lax.all_to_all(copies, 'tensor', 0, 0, tiled=True)]
    ppermute x10 -> x13, starting transfers between devices: 16.6 us -> 21.2 us  [along(): lax.ppermute(value, 'tensor', [(t, move(t // 8, t // 2 % 4, t % 2)) for t...]
    unnamed x36 -> x24, local copies, waits for them, and re-layouts: 4.7 us -> 0.05 us
    all_to_all x1, waiting for transfers between devices: 1.62 us -> 5.87 us  [on_device(): misfit = lax.all_to_all(misfit, 'tensor', 0, 0, tiled=True)]
  transfers between devices with their start and end apart: 16 -> 20, of which waited for: 7 -> 9; matrix products, arithmetic and copies ran while one was open for 0% -> 0% of each run, Pallas kernels for 14% -> 14%
where the time goes in v6:
time: 150 us; the launch traced here: 148 us
  starting transfers between devices  55.9 us (37%)
  waiting for transfers between devices  47.1 us (31%)
  Pallas kernels  32.6 us (22%)
  blocking collectives  11.9 us (8%)
    ppermute x13, waiting for transfers between devices, along(): lax.ppermute(value, 'tensor', [(t, move(t // 8, t // 2 % 4, t % 2)) for t...  25.8 us
    ppermute x13, starting transfers between devices, along(): lax.ppermute(value, 'tensor', [(t, move(t // 8, t // 2 % 4, t % 2)) for t...  21.2 us
    all_to_all x1, blocking collectives, on_device(): back = lax.all_to_all(back, 'batch', 0, 0, tiled=True)  11.9 us
    all_to_all x1, starting transfers between devices, on_device(): every = lax.all_to_all(copies, 'tensor', 0, 0, tiled=True)  11.3 us
    pallas_call x1, Pallas kernels, on_device(): pl.pallas_call(teacher_kernel, grid_spec=pltpu.PrefetchScalarGridSpec(num...  9.12 us
    all_to_all x1, waiting for transfers between devices, on_device(): grad_out = lax.all_to_all(grad_out, 'tensor', 0, 0, tiled=True)  8.41 us
    all_to_all x1, waiting for transfers between devices, on_device(): acts = lax.all_to_all(acts, 'batch', 0, 0, tiled=True)  7.06 us
    all_to_all x1, starting transfers between devices, on_device(): misfit = lax.all_to_all(misfit, 'tensor', 0, 0, tiled=True)  5.98 us
  transfers between devices with their start and end apart: 20, of which 9 were waited for; matrix products, arithmetic and copies ran while one was open for 0% of the time, Pallas kernels for 14%

profile of v6, /device:TPU:0, one launch (start us, length us, event | category | flops | bytes accessed | tf_op | source)
XLA Modules:
  0.0 148.3 jit_solution(12840462509659867199)
XLA Ops:
  3.8 9.1 %teacher.1 = (bf16[8,256,512]{2,1,0:T(8,128)(2,1)}, bf16[8,256,512]{2,1,0:T(8,128)(2,1)}, bf16[8,64,512]{2,1,0:T(8,128)(2,1)}, bf16[8,64,512]{2,1,0:T(8,128)(2,1)}) custom-call(s32[1]{0:T(128)} %bitcast.1.core_ref, s32[1,64]{1,0:T(1,128)} %route_ref.5, bf16[256,512]{1,0:T(8,128)(2,1)} %attn_ref.1, bf16[512,8192]{1,0:T(8,128)(2,1)} %other_ref.1, ...), custom_call_target="tpu_custom_call" | custom-call | flops 2621440 | bytes 14336 | tf_op jit(solution)/shard_map/teacher/pallas_call | solution.py:299
  14.5 11.3 %all-to-all-start = ((bf16[16,40,512]{2,1,0:T(8,128)(2,1)}), bf16[16,40,512]{2,1,0:T(8,128)(2,1)S(1)}, u32[]{:S(2)}, u32[]{:S(2)}) async-start(bf16[16,40,512]{2,1,0:T(8,128)(2,1)} %get-tuple-element.48), calls=%async_computation | async-start | bytes 1310720 | tf_op jit(solution)/shard_map/all_to_all | solution.py:335
  29.6 2.7 %collective-permute-start.4 = (bf16[2,64,512]{2,1,0:T(8,128)(2,1)}, bf16[2,64,512]{2,1,0:T(8,128)(2,1)S(1)}, u32[]{:S(2)}, u32[]{:S(2)}) collective-permute-start(bf16[2,64,512]{2,1,0:T(8,128)(2,1)} %get-tuple-element.56), channel_id=1, source_target_pairs={{0,4},{1,5},{2,6},{3,7},{4,0},{5,1},{6,2},{7,3},{8,12},{9,13},{10,... | collective-permute-start | bytes 393224 | tf_op jit(solution)/shard_map/ppermute | solution.py:338
  33.8 3.9 %core_sum.2 = (bf16[1,256,512]{2,1,0:T(8,128)(2,1)}, bf16[1,256,512]{2,1,0:T(8,128)(2,1)}, bf16[1,256,512]{2,1,0:T(8,128)(2,1)}, bf16[1,256,512]{2,1,0:T(8,128)(...) custom-call(s32[1]{0:T(128)} %bitcast.4.x_ref, ...), custom_call_target="tpu_custom_call" | custom-call | flops 1024 | bytes 6144 | tf_op jit(solution)/shard_map/core_sum/pallas_call | solution.py:386
  37.7 2.5 %collective-permute-done.3.refs_1_.refs_5_ = bf16[2,64,512]{2,1,0:T(8,128)(2,1)S(1)} collective-permute-done((bf16[2,64,512]{2,1,0:T(8,128)(2,1)}, bf16[2,64,512]{2,1,0:T(8,128)(2,1)S(1)}, u32[]{:S(2)}, u32[]{:S(2)}) %collective-permute-start.3) | collective-permute-done | bytes 131104 | tf_op jit(solution)/shard_map/ppermute | solution.py:338
  40.2 2.9 %collective-permute-done.4.refs_2_.refs_6_ = bf16[2,64,512]{2,1,0:T(8,128)(2,1)S(1)} collective-permute-done((bf16[2,64,512]{2,1,0:T(8,128)(2,1)}, bf16[2,64,512]{2,1,0:T(8,128)(2,1)S(1)}, u32[]{:S(2)}, u32[]{:S(2)}) %collective-permute-start.4) | collective-permute-done | bytes 131104 | tf_op jit(solution)/shard_map/ppermute | solution.py:338
  44.7 2.6 %up.1 = (bf16[8,32,1152]{2,1,0:T(8,128)(2,1)}, bf16[256,512]{1,0:T(8,128)(2,1)}, bf16[256,512]{1,0:T(8,128)(2,1)}, bf16[1,64,512]{2,1,0:T(8,128)(2,1)}, bf16[1,2...) custom-call(s32[1]{0:T(128)} %bitcast.group_ref, ...), custom_call_target="tpu_custom_call", output_to_operand_aliasing={{3}: (5, {}), {4}: (6, {}), {5}: (7, {}), {6}: (8, {})} | custom-call | flops 819200 | bytes 4096 | tf_op jit(solution)/shard_map/up/pallas_call | solution.py:429
  47.3 3.6 %all-to-all-start.1 = ((bf16[8,32,1152]{2,1,0:T(8,128)(2,1)}), bf16[8,32,1152]{2,1,0:T(8,128)(2,1)S(1)}, u32[]{:S(2)}, u32[]{:S(2)}) async-start(bf16[8,32,1152]{2,1,0:T(8,128)(2,1)} %get-tuple-element.62), calls=%async_computation.1 | async-start | bytes 1179648 | tf_op jit(solution)/shard_map/all_to_all | solution.py:456
  52.7 2.0 %collective-permute-start.9 = (bf16[1,256,512]{2,1,0:T(8,128)(2,1)}, bf16[1,256,512]{2,1,0:T(8,128)(2,1)S(1)}, u32[]{:S(2)}, u32[]{:S(2)}) collective-permute-start(bf16[1,256,512]{2,1,0:T(8,128)(2,1)} %get-tuple-element.68), channel_id=1, source_target_pairs={{0,6},{1,7},{2,0},{3,1},{4,2},{5,3},{6,4},{7,5},{8,14},{9,15},{10,... | collective-permute-start | bytes 786440 | tf_op jit(solution)/shard_map/ppermute | solution.py:338
  54.7 3.1 %collective-permute-start.6 = (bf16[1,64,512]{2,1,0:T(8,128)(2,1)}, bf16[1,64,512]{2,1,0:T(8,128)(2,1)S(1)}, u32[]{:S(2)}, u32[]{:S(2)}) collective-permute-start(bf16[1,64,512]{2,1,0:T(8,128)(2,1)} %get-tuple-element.64), channel_id=1, source_target_pairs={{0,8},{1,9},{2,10},{3,11},{4,12},{5,13},{6,14},{7,15},{8,0},{9,1},... | collective-permute-start | bytes 196616 | tf_op jit(solution)/shard_map/ppermute | solution.py:338
  57.8 7.9 %collective-permute-done.7.refs_1_ = bf16[1,256,512]{2,1,0:T(8,128)(2,1)S(1)} collective-permute-done((bf16[1,256,512]{2,1,0:T(8,128)(2,1)}, bf16[1,256,512]{2,1,0:T(8,128)(2,1)S(1)}, u32[]{:S(2)}, u32[]{:S(2)}) %collective-permute-start.7) | collective-permute-done | bytes 262176 | tf_op jit(solution)/shard_map/ppermute | solution.py:338
  68.3 5.3 %all-to-all-start.2 = ((bf16[8,96,512]{2,1,0:T(8,128)(2,1)}), bf16[8,96,512]{2,1,0:T(8,128)(2,1)S(1)}, u32[]{:S(2)}, u32[]{:S(2)}) async-start(bf16[8,96,512]{2,1,0:T(8,128)(2,1)} %get-tuple-element.72), calls=%async_computation.2 | async-start | bytes 1572864 | tf_op jit(solution)/shard_map/all_to_all | solution.py:478
  74.1 3.6 %collective-permute-start.11 = (bf16[1,256,512]{2,1,0:T(8,128)(2,1)}, bf16[1,256,512]{2,1,0:T(8,128)(2,1)S(1)}, u32[]{:S(2)}, u32[]{:S(2)}) collective-permute-start(bf16[1,256,512]{2,1,0:T(8,128)(2,1)} %get-tuple-element.75), channel_id=1, source_target_pairs={{0,4},{1,5},{2,6},{3,7},{4,0},{5,1},{6,2},{7,3},{8,12},{9,13},{10,... | collective-permute-start | bytes 786440 | tf_op jit(solution)/shard_map/ppermute | solution.py:338
  77.7 5.0 %collective-permute-done.10.refs_1_ = bf16[1,256,512]{2,1,0:T(8,128)(2,1)S(1)} collective-permute-done((bf16[1,256,512]{2,1,0:T(8,128)(2,1)}, bf16[1,256,512]{2,1,0:T(8,128)(2,1)S(1)}, u32[]{:S(2)}, u32[]{:S(2)}) %collective-permute-start.10) | collective-permute-done | bytes 262176 | tf_op jit(solution)/shard_map/ppermute | solution.py:338
  82.7 6.7 %collective-permute-done.11.refs_2_ = bf16[1,256,512]{2,1,0:T(8,128)(2,1)S(1)} collective-permute-done((bf16[1,256,512]{2,1,0:T(8,128)(2,1)}, bf16[1,256,512]{2,1,0:T(8,128)(2,1)S(1)}, u32[]{:S(2)}, u32[]{:S(2)}) %collective-permute-start.11) | collective-permute-done | bytes 262176 | tf_op jit(solution)/shard_map/ppermute | solution.py:338
  90.3 2.4 %down.1 = (bf16[16,16,512]{2,1,0:T(8,128)(2,1)}, bf16[256,512]{1,0:T(8,128)(2,1)}) custom-call(s32[1]{0:T(128)} %bitcast.group_ref, bf16[8,96,512]{2,1,0:T(8,128)(2,1)S(1)} %all-to-all-done.2.got_ref, bf16[512,512]{1,0:T(8,128)(2,1)S(1)} %copy-done.1, bf16[256,512]{1,0:T(8,128)(2,1)S(1)} %copy-done.6, bf16[512,4096]{1,0:T(8,128)(2,1)} %projector_ref.1, ...), custom_call_target="tpu_custom_call" | custom-call | flops 786432 | bytes 4096 | tf_op jit(solution)/shard_map/down/pallas_call | solution.py:479
  92.7 6.0 %all-to-all-start.3 = ((bf16[16,16,512]{2,1,0:T(8,128)(2,1)}), bf16[16,16,512]{2,1,0:T(8,128)(2,1)S(1)}, u32[]{:S(2)}, u32[]{:S(2)}) async-start(bf16[16,16,512]{2,1,0:T(8,128)(2,1)} %get-tuple-element.77), calls=%async_computation.3 | async-start | bytes 524288 | tf_op jit(solution)/shard_map/all_to_all | solution.py:497
  98.7 3.5 %collective-permute-start.13 = (bf16[1,256,512]{2,1,0:T(8,128)(2,1)S(1)}, bf16[1,256,512]{2,1,0:T(8,128)(2,1)S(1)}, u32[]{:S(2)}, u32[]{:S(2)}) collective-permute-start(bf16[1,256,512]{2,1,0:T(8,128)(2,1)S(1)} %copy-done.11), channel_id=1, source_target_pairs={{0,8},{1,9},{2,10},{3,11},{4,12},{5,13},{6,14},{7,15},{8,0},{9,1},... | collective-permute-start | bytes 786440 | tf_op jit(solution)/shard_map/ppermute | solution.py:338
  102.2 5.9 %all-to-all-done.3.refs_0_ = bf16[16,16,512]{2,1,0:T(8,128)(2,1)S(1)} async-done(((bf16[16,16,512]{2,1,0:T(8,128)(2,1)}), bf16[16,16,512]{2,1,0:T(8,128)(2,1)S(1)}, u32[]{:S(2)}, u32[]{:S(2)}) %all-to-all-start.3) | async-done | bytes 262176 | tf_op jit(solution)/shard_map/all_to_all | solution.py:497
  108.8 3.5 %all-to-all-start.4 = ((bf16[16,16,512]{2,1,0:T(8,128)(2,1)}), bf16[16,16,512]{2,1,0:T(8,128)(2,1)S(1)}, u32[]{:S(2)}, u32[]{:S(2)}) async-start(bf16[16,16,512]{2,1,0:T(8,128)(2,1)} %misfit.1), calls=%async_computation.4 | async-start | bytes 524288 | tf_op jit(solution)/shard_map/all_to_all | solution.py:506
  113.3 8.4 %all-to-all-done.4.got_ref.grad_ref = bf16[16,16,512]{2,1,0:T(8,128)(2,1)S(1)} async-done(((bf16[16,16,512]{2,1,0:T(8,128)(2,1)}), bf16[16,16,512]{2,1,0:T(8,128)(2,1)S(1)}, u32[]{:S(2)}, u32[]{:S(2)}) %all-to-all-start.4) | async-done | bytes 262176 | tf_op jit(solution)/shard_map/all_to_all | solution.py:506
  122.0 11.9 %all_to_all.35.got_ref = bf16[8,32,512]{2,1,0:T(8,128)(2,1)S(1)} all-to-all(bf16[8,32,512]{2,1,0:T(8,128)(2,1)S(1)} %get-tuple-element.81), channel_id=1, replica_groups=mesh['batch'=8,'tensor'=16] {'batch'}, dimensions={0} | all-to-all | bytes 524288 | tf_op jit(solution)/shard_map/all_to_all | solution.py:525
  134.8 3.5 %all-to-all-start.6 = ((bf16[8,32,1024]{2,1,0:T(8,128)(2,1)}), bf16[8,32,1024]{2,1,0:T(8,128)(2,1)S(1)}, u32[]{:S(2)}, u32[]{:S(2)}) async-start(bf16[8,32,1024]{2,1,0:T(8,128)(2,1)} %acts.1), calls=%async_computation.6 | async-start | bytes 1048576 | tf_op jit(solution)/shard_map/all_to_all | solution.py:533
  139.6 7.1 %all-to-all-done.6.got_ref = bf16[8,32,1024]{2,1,0:T(8,128)(2,1)S(1)} async-done(((bf16[8,32,1024]{2,1,0:T(8,128)(2,1)}), bf16[8,32,1024]{2,1,0:T(8,128)(2,1)S(1)}, u32[]{:S(2)}, u32[]{:S(2)}) %all-to-all-start.6) | async-done | bytes 524320 | tf_op jit(solution)/shard_map/all_to_all | solution.py:533
  (58 shorter events, 23.1 us)
Async XLA Ops:
  2.4 10.5 %collective-permute-start = (bf16[40,512]{1,0:T(8,128)(2,1)}, bf16[40,512]{1,0:T(8,128)(2,1)S(1)}, u32[]{:S(2)}, u32[]{:S(2)}) collective-permute-start(bf16[40,512]{1,0:T(8,128)(2,1)} %rows.1), channel_id=1, source_target_pairs={{0,0},{1,1},{2,16},{3,17},{4,32},{5,33},{6,48},{7,49},{8,64},{9,65... | collective-permute-start | bytes 122888 | tf_op jit(solution)/shard_map/ppermute | solution.py:297
  13.9 19.9 %collective-permute-start.1 = (bf16[8,256,512]{2,1,0:T(8,128)(2,1)}, bf16[8,256,512]{2,1,0:T(8,128)(2,1)S(1)}, u32[]{:S(2)}, u32[]{:S(2)}) collective-permute-start(bf16[8,256,512]{2,1,0:T(8,128)(2,1)} %get-tuple-element.50), channel_id=1, source_target_pairs={{0,1},{1,0},{2,3},{3,2},{4,5},{5,4},{6,7},{7,6},{8,9},{9,8},{10,11... | collective-permute-start | bytes 6291464 | tf_op jit(solution)/shard_map/ppermute | solution.py:338
  14.0 11.9 %collective-permute-start.2 = (bf16[8,64,512]{2,1,0:T(8,128)(2,1)}, bf16[8,64,512]{2,1,0:T(8,128)(2,1)S(1)}, u32[]{:S(2)}, u32[]{:S(2)}) collective-permute-start(bf16[8,64,512]{2,1,0:T(8,128)(2,1)} %get-tuple-element.53), channel_id=1, source_target_pairs={{0,1},{1,0},{2,3},{3,2},{4,5},{5,4},{6,7},{7,6},{8,9},{9,8},{10,11... | collective-permute-start | bytes 1572872 | tf_op jit(solution)/shard_map/ppermute | solution.py:338
  14.5 30.2 %all-to-all-start = ((bf16[16,40,512]{2,1,0:T(8,128)(2,1)}), bf16[16,40,512]{2,1,0:T(8,128)(2,1)S(1)}, u32[]{:S(2)}, u32[]{:S(2)}) async-start(bf16[16,40,512]{2,1,0:T(8,128)(2,1)} %get-tuple-element.48), calls=%async_computation | async-start | bytes 1310720 | tf_op jit(solution)/shard_map/all_to_all | solution.py:335
  27.7 12.5 %collective-permute-start.3 = (bf16[2,64,512]{2,1,0:T(8,128)(2,1)}, bf16[2,64,512]{2,1,0:T(8,128)(2,1)S(1)}, u32[]{:S(2)}, u32[]{:S(2)}) collective-permute-start(bf16[2,64,512]{2,1,0:T(8,128)(2,1)} %get-tuple-element.55), channel_id=1, source_target_pairs={{0,2},{1,3},{2,4},{3,5},{4,6},{5,7},{6,0},{7,1},{8,10},{9,11},{10,... | collective-permute-start | bytes 393224 | tf_op jit(solution)/shard_map/ppermute | solution.py:338
  29.6 13.5 %collective-permute-start.4 = (bf16[2,64,512]{2,1,0:T(8,128)(2,1)}, bf16[2,64,512]{2,1,0:T(8,128)(2,1)S(1)}, u32[]{:S(2)}, u32[]{:S(2)}) collective-permute-start(bf16[2,64,512]{2,1,0:T(8,128)(2,1)} %get-tuple-element.56), channel_id=1, source_target_pairs={{0,4},{1,5},{2,6},{3,7},{4,0},{5,1},{6,2},{7,3},{8,12},{9,13},{10,... | collective-permute-start | bytes 393224 | tf_op jit(solution)/shard_map/ppermute | solution.py:338
  32.3 10.8 %collective-permute-start.5 = (bf16[2,64,512]{2,1,0:T(8,128)(2,1)}, bf16[2,64,512]{2,1,0:T(8,128)(2,1)S(1)}, u32[]{:S(2)}, u32[]{:S(2)}) collective-permute-start(bf16[2,64,512]{2,1,0:T(8,128)(2,1)} %get-tuple-element.57), channel_id=1, source_target_pairs={{0,6},{1,7},{2,0},{3,1},{4,2},{5,3},{6,4},{7,5},{8,14},{9,15},{10,... | collective-permute-start | bytes 393224 | tf_op jit(solution)/shard_map/ppermute | solution.py:338
  47.3 19.9 %all-to-all-start.1 = ((bf16[8,32,1152]{2,1,0:T(8,128)(2,1)}), bf16[8,32,1152]{2,1,0:T(8,128)(2,1)S(1)}, u32[]{:S(2)}, u32[]{:S(2)}) async-start(bf16[8,32,1152]{2,1,0:T(8,128)(2,1)} %get-tuple-element.62), calls=%async_computation.1 | async-start | bytes 1179648 | tf_op jit(solution)/shard_map/all_to_all | solution.py:456
  50.8 15.0 %collective-permute-start.7 = (bf16[1,256,512]{2,1,0:T(8,128)(2,1)}, bf16[1,256,512]{2,1,0:T(8,128)(2,1)S(1)}, u32[]{:S(2)}, u32[]{:S(2)}) collective-permute-start(bf16[1,256,512]{2,1,0:T(8,128)(2,1)} %get-tuple-element.66), channel_id=1, source_target_pairs={{0,2},{1,3},{2,4},{3,5},{4,6},{5,7},{6,0},{7,1},{8,10},{9,11},{10,... | collective-permute-start | bytes 786440 | tf_op jit(solution)/shard_map/ppermute | solution.py:338
  50.9 14.9 %collective-permute-start.8 = (bf16[1,256,512]{2,1,0:T(8,128)(2,1)}, bf16[1,256,512]{2,1,0:T(8,128)(2,1)S(1)}, u32[]{:S(2)}, u32[]{:S(2)}) collective-permute-start(bf16[1,256,512]{2,1,0:T(8,128)(2,1)} %get-tuple-element.67), channel_id=1, source_target_pairs={{0,4},{1,5},{2,6},{3,7},{4,0},{5,1},{6,2},{7,3},{8,12},{9,13},{10,... | collective-permute-start | bytes 786440 | tf_op jit(solution)/shard_map/ppermute | solution.py:338
  52.7 13.7 %collective-permute-start.9 = (bf16[1,256,512]{2,1,0:T(8,128)(2,1)}, bf16[1,256,512]{2,1,0:T(8,128)(2,1)S(1)}, u32[]{:S(2)}, u32[]{:S(2)}) collective-permute-start(bf16[1,256,512]{2,1,0:T(8,128)(2,1)} %get-tuple-element.68), channel_id=1, source_target_pairs={{0,6},{1,7},{2,0},{3,1},{4,2},{5,3},{6,4},{7,5},{8,14},{9,15},{10,... | collective-permute-start | bytes 786440 | tf_op jit(solution)/shard_map/ppermute | solution.py:338
  54.7 12.5 %collective-permute-start.6 = (bf16[1,64,512]{2,1,0:T(8,128)(2,1)}, bf16[1,64,512]{2,1,0:T(8,128)(2,1)S(1)}, u32[]{:S(2)}, u32[]{:S(2)}) collective-permute-start(bf16[1,64,512]{2,1,0:T(8,128)(2,1)} %get-tuple-element.64), channel_id=1, source_target_pairs={{0,8},{1,9},{2,10},{3,11},{4,12},{5,13},{6,14},{7,15},{8,0},{9,1},... | collective-permute-start | bytes 196616 | tf_op jit(solution)/shard_map/ppermute | solution.py:338
  67.2 23.1 %copy-start.1 = (bf16[512,512]{1,0:T(8,128)(2,1)S(1)}, bf16[512,512]{1,0:T(8,128)(2,1)}, u32[]{:S(2)}) copy-start(bf16[512,512]{1,0:T(8,128)(2,1)} %down_ref.3) | copy-start | bytes 1572868
  67.2 23.1 %copy-start.6 = (bf16[256,512]{1,0:T(8,128)(2,1)S(1)}, bf16[256,512]{1,0:T(8,128)(2,1)}, u32[]{:S(2)}) copy-start(bf16[256,512]{1,0:T(8,128)(2,1)} %get-tuple-element.73.chosen_ref) | copy-start | bytes 786436
  68.3 21.9 %all-to-all-start.2 = ((bf16[8,96,512]{2,1,0:T(8,128)(2,1)}), bf16[8,96,512]{2,1,0:T(8,128)(2,1)S(1)}, u32[]{:S(2)}, u32[]{:S(2)}) async-start(bf16[8,96,512]{2,1,0:T(8,128)(2,1)} %get-tuple-element.72), calls=%async_computation.2 | async-start | bytes 1572864 | tf_op jit(solution)/shard_map/all_to_all | solution.py:478
  73.6 9.1 %collective-permute-start.10 = (bf16[1,256,512]{2,1,0:T(8,128)(2,1)}, bf16[1,256,512]{2,1,0:T(8,128)(2,1)S(1)}, u32[]{:S(2)}, u32[]{:S(2)}) collective-permute-start(bf16[1,256,512]{2,1,0:T(8,128)(2,1)} %get-tuple-element.74), channel_id=1, source_target_pairs={{0,2},{1,3},{2,4},{3,5},{4,6},{5,7},{6,0},{7,1},{8,10},{9,11},{10,... | collective-permute-start | bytes 786440 | tf_op jit(solution)/shard_map/ppermute | solution.py:338
  74.1 15.3 %collective-permute-start.11 = (bf16[1,256,512]{2,1,0:T(8,128)(2,1)}, bf16[1,256,512]{2,1,0:T(8,128)(2,1)S(1)}, u32[]{:S(2)}, u32[]{:S(2)}) collective-permute-start(bf16[1,256,512]{2,1,0:T(8,128)(2,1)} %get-tuple-element.75), channel_id=1, source_target_pairs={{0,4},{1,5},{2,6},{3,7},{4,0},{5,1},{6,2},{7,3},{8,12},{9,13},{10,... | collective-permute-start | bytes 786440 | tf_op jit(solution)/shard_map/ppermute | solution.py:338
  77.7 11.7 %collective-permute-start.12 = (bf16[1,256,512]{2,1,0:T(8,128)(2,1)}, bf16[1,256,512]{2,1,0:T(8,128)(2,1)S(1)}, u32[]{:S(2)}, u32[]{:S(2)}) collective-permute-start(bf16[1,256,512]{2,1,0:T(8,128)(2,1)} %get-tuple-element.76), channel_id=1, source_target_pairs={{0,6},{1,7},{2,0},{3,1},{4,2},{5,3},{6,4},{7,5},{8,14},{9,15},{10,... | collective-permute-start | bytes 786440 | tf_op jit(solution)/shard_map/ppermute | solution.py:338
  92.7 15.4 %all-to-all-start.3 = ((bf16[16,16,512]{2,1,0:T(8,128)(2,1)}), bf16[16,16,512]{2,1,0:T(8,128)(2,1)S(1)}, u32[]{:S(2)}, u32[]{:S(2)}) async-start(bf16[16,16,512]{2,1,0:T(8,128)(2,1)} %get-tuple-element.77), calls=%async_computation.3 | async-start | bytes 524288 | tf_op jit(solution)/shard_map/all_to_all | solution.py:497
  98.7 13.7 %collective-permute-start.13 = (bf16[1,256,512]{2,1,0:T(8,128)(2,1)S(1)}, bf16[1,256,512]{2,1,0:T(8,128)(2,1)S(1)}, u32[]{:S(2)}, u32[]{:S(2)}) collective-permute-start(bf16[1,256,512]{2,1,0:T(8,128)(2,1)S(1)} %copy-done.11), channel_id=1, source_target_pairs={{0,8},{1,9},{2,10},{3,11},{4,12},{5,13},{6,14},{7,15},{8,0},{9,1},... | collective-permute-start | bytes 786440 | tf_op jit(solution)/shard_map/ppermute | solution.py:338
  108.8 12.9 %all-to-all-start.4 = ((bf16[16,16,512]{2,1,0:T(8,128)(2,1)}), bf16[16,16,512]{2,1,0:T(8,128)(2,1)S(1)}, u32[]{:S(2)}, u32[]{:S(2)}) async-start(bf16[16,16,512]{2,1,0:T(8,128)(2,1)} %misfit.1), calls=%async_computation.4 | async-start | bytes 524288 | tf_op jit(solution)/shard_map/all_to_all | solution.py:506
  113.3 25.0 %copy-start.8 = (bf16[256,512]{1,0:T(8,128)(2,1)S(1)}, bf16[256,512]{1,0:T(8,128)(2,1)}, u32[]{:S(2)}) copy-start(bf16[256,512]{1,0:T(8,128)(2,1)} %get-tuple-element.87.hidden_ref) | copy-start | bytes 786436
  122.0 24.7 %copy-start.5 = (bf16[256,512]{1,0:T(8,128)(2,1)S(1)}, bf16[256,512]{1,0:T(8,128)(2,1)}, u32[]{:S(2)}) copy-start(bf16[256,512]{1,0:T(8,128)(2,1)} %get-tuple-element.80.rows_ref) | copy-start | bytes 786436
  134.8 11.9 %all-to-all-start.6 = ((bf16[8,32,1024]{2,1,0:T(8,128)(2,1)}), bf16[8,32,1024]{2,1,0:T(8,128)(2,1)S(1)}, u32[]{:S(2)}, u32[]{:S(2)}) async-start(bf16[8,32,1024]{2,1,0:T(8,128)(2,1)} %acts.1), calls=%async_computation.6 | async-start | bytes 1048576 | tf_op jit(solution)/shard_map/all_to_all | solution.py:533
  (8 other events, 127.4 us)

commit v7 on v6

--- a/solution.py
+++ b/solution.py
@@ -102,14 +102,36 @@
     refs[-1][0] = refs[-1][0] + dot(hot, residual_ref[...], 1, 1)
 
 
+def halves_kernel(x_ref, *refs):
+    ins, (keep_a, send_a, keep_b, send_b) = refs[:8], refs[8:]
+    sums = [(ins[m][0].astype(F32) + ins[4 + m][0].astype(F32)).astype(BF) for m in range(4)]
+    for half, ref, order in ((0, keep_a, (0, 3)), (0, send_a, (1, 2)), (1, keep_b, (0, 1)), (1, send_b, (3, 2))):
+        for i, m in enumerate(order):
+            ref[i, 0] = sums[m][half]
+
+
+def first_sum_kernel(keep_a, got_a, keep_b, got_b, own_a, on_a, own_b, on_b):
+    for keep, got, own, on in ((keep_a, got_a, own_a, on_a), (keep_b, got_b, own_b, on_b)):
+        own[...] = keep[0].astype(F32) + got[0].astype(F32)
+        on[...] = (keep[1].astype(F32) + got[1].astype(F32)).astype(BF)
+
+
+def second_sum_kernel(y_ref, *refs):
+    ins, (send_ref, keep_ref) = refs[:8], refs[8:]
+    for half in range(2):
+        own, got, other_own, other_got = ins[4 * half : 4 * half + 4]
+        send_ref[half] = (other_own[0] + other_got[0].astype(F32)).astype(BF)
+        keep_ref[half] = own[0] + got[0].astype(F32)
+
+
 def residual_kernel(residual_ref, keep_ref, got_ref, out_ref):
-    summed = keep_ref[0] + got_ref[0].astype(F32)
+    summed = (keep_ref[...] + got_ref[...].astype(F32)).reshape(-1, keep_ref.shape[2])
     out_ref[...] = (residual_ref[...].astype(F32) + summed.T).astype(BF)
 
 
 def up_kernel(
-    group_ref, got_ref, gain_ref, gate_ref, up_ref, p1, p2, p3, p4,
-    out_ref, rows_ref, chosen_ref, q1, q2, q3, q4, padded_ref, weights_ref, sems,
+    group_ref, got_ref, gain_ref, gate_ref, up_ref, p1, p2, p3,
+    out_ref, rows_ref, chosen_ref, q1, q2, q3, padded_ref, weights_ref, sems,
 ):
     loads = [
         pltpu.make_async_copy(ref, weights_ref.at[i], sems.at[i])
@@ -169,8 +191,8 @@
 
 
 def hidden_kernel(
-    features, got_ref, keep_ref, other_ref, p1, p2, p3, p4,
-    out_ref, gate_ref, up_ref, scale_ref, q1, q2, q3, q4,
+    features, got_ref, keep_ref, other_ref, p1, p2,
+    out_ref, gate_ref, up_ref, scale_ref, q1, q2,
 ):
     per, wide = gate_ref.shape
     at = got_ref.shape[2]
@@ -374,29 +396,30 @@
             pl.BlockSpec(block, lambda i, y: (y[0], i, 0))
         ] * 4
 
-    strip = tokens // 4
+    half, strip = tokens // 2, tokens // 4
     got = along(send, lambda y, x, c: y * 8 + x * 2 + 1 - c)
-    blocks = [
-        pl.BlockSpec(
-            (1, strip, wide), lambda n, x, y, i=i, j=j: (4 * ((y[0] + i) & 1) + ((x[0] + j) & 3), n, 0)
-        )
-        for i in (1, 0)
-        for j in range(4)
-    ]
-    sums = pl.pallas_call(
-        lambda x_ref, *refs: core_sum_kernel(*refs),
+    halves = (parts // 2, 2, half, wide)
+    pair = pltpu.HBM((2, 2, half, wide), BF)
+    keep_a, send_a, keep_b, send_b = pl.pallas_call(
+        halves_kernel,
         grid_spec=pltpu.PrefetchScalarGridSpec(
-            num_scalar_prefetch=2,
-            grid=(tokens // strip,),
-            in_specs=blocks * 2,
-            out_specs=[pl.BlockSpec((1, strip, wide), lambda n, x, y: (0, n, 0))] * 8,
+            num_scalar_prefetch=1,
+            grid=(2, half // strip),
+            in_specs=[
+                pl.BlockSpec(
+                    (1, 2, strip, wide),
+                    lambda y, n, x, m=m: (4 * y + lax.bitwise_xor(x[0], jnp.int32(m)), 0, n, 0),
+                )
+                for m in range(4)
+            ]
+            * 2,
+            out_specs=[pl.BlockSpec((2, 1, strip, wide), lambda y, n, x: (0, y, n, 0))] * 4,
         ),
-        out_shape=[pltpu.HBM((1, tokens, wide), BF)] * 8,
+        out_shape=[pair] * 4,
         compiler_params=params(16),
         cost_estimate=cost(MIB, 6 * MIB),
-        name="core_sum",
-    )(x_at.reshape(1), y_at.reshape(1), *[hbm(keep)] * 8, *[got] * 8)
-    others, own = sums[:4], sums[4:]
+        name="halves",
+    )(x_at.reshape(1), *[hbm(keep.reshape(halves))] * 4, *[got.reshape(halves)] * 4)
 
     routed, *moved = core_sum(keep_routed, send_routed, slots)
     send_routed, keep_routed = pl.pallas_call(
@@ -411,29 +434,20 @@
         compiler_params=params(8),
         cost_estimate=cost(MIB, MIB),
         name="routed_sum",
-    )(y_at.reshape(1), route_index, residual_t, hbm(own[0]), *along_x(routed, moved) * 2)
-
-    def x_sum(own, moved, kind):
-        return pl.pallas_call(
-            x_sum_kernel,
-            grid=(2,),
-            in_specs=[pl.BlockSpec((1, tokens // 2, wide), lambda n: (0, n, 0))] * 4,
-            out_specs=pl.BlockSpec((1, tokens // 2, wide), lambda n: (0, n, 0)),
-            out_shape=pltpu.HBM((1, tokens, wide), kind),
-            compiler_params=params(8),
-            cost_estimate=cost(MIB, 2 * MIB),
-            name="x_sum",
-        )(*along_x(own, moved))
+    )(y_at.reshape(1), route_index, residual_t, hbm(keep_a), *along_x(routed, moved) * 2)
+
+    def along_x_by(value, mask):
+        return along(value, lambda y, x, c: y * 8 + (x ^ mask) * 2 + c)
 
     packed = 2 * wide + 128
-    sent, scaled, chosen, send_routed, *moved = pl.pallas_call(
+    sent, scaled, chosen, send_routed, send_a, send_b = pl.pallas_call(
         up_kernel,
         grid_spec=pltpu.PrefetchScalarGridSpec(
             num_scalar_prefetch=1,
             grid=(1,),
             in_specs=[vmem, pl.BlockSpec((1, wide), lambda i, group: (0, group[0]))]
-            + [anywhere] * 6,
-            out_specs=[vmem] * 3 + [anywhere] * 4,
+            + [anywhere] * 5,
+            out_specs=[vmem] * 3 + [anywhere] * 3,
             scratch_shapes=[
                 pltpu.VMEM((groups * slots, wide), BF),
                 pltpu.VMEM((2, wide, units), BF),
@@ -446,35 +460,61 @@
             pltpu.HBM((live, groups * slots), BF),
             pltpu.HBM(send_routed.shape, BF),
         ]
-        + [pltpu.HBM((1, tokens, wide), BF)] * 3,
-        input_output_aliases={5: 3, 6: 4, 7: 5, 8: 6},
+        + [pair] * 2,
+        input_output_aliases={5: 3, 6: 4, 7: 5},
         compiler_params=params(16),
         cost_estimate=cost(800 * MIB, 4 * MIB),
         name="up",
-    )(group.reshape(1), every, norm_gain[None], w_gate, w_up, send_routed, *others[1:])
+    )(group.reshape(1), every, norm_gain[None], w_gate, w_up, send_routed, send_a, send_b)
     other_routed = along_y(send_routed)
     got = lax.all_to_all(sent, "batch", 0, 0, tiled=True)
 
     flat = shape((per, units), F32)
-    send = x_sum(others[0], moved, BF)
-    both, gate, up, scale, send, *moved = pl.pallas_call(
+    block = pl.BlockSpec((2, 2, strip, wide), lambda n: (0, 0, n, 0))
+    line = pl.BlockSpec((2, strip, wide), lambda n: (0, n, 0))
+    own_a, on_a, own_b, on_b = pl.pallas_call(
+        first_sum_kernel,
+        grid=(half // strip,),
+        in_specs=[block] * 4,
+        out_specs=[line] * 4,
+        out_shape=[pltpu.HBM((2, half, wide), F32), pltpu.HBM((2, half, wide), BF)] * 2,
+        compiler_params=params(16),
+        cost_estimate=cost(MIB, 3 * MIB),
+        name="first_sum",
+    )(keep_a, along_x_by(send_a, 1), keep_b, along_x_by(send_b, 3))
+    both, gate, up, scale, on_a, on_b = pl.pallas_call(
         lambda *refs: hidden_kernel(features, *refs),
-        in_specs=[vmem] * 3 + [anywhere] * 4,
-        out_specs=[vmem] * 4 + [anywhere] * 4,
+        in_specs=[vmem] * 3 + [anywhere] * 2,
+        out_specs=[vmem] * 4 + [anywhere] * 2,
         out_shape=[
             pltpu.HBM((groups, per + slots, units), BF),
             flat,
             flat,
             shape((per, 128), F32),
         ]
-        + [pltpu.HBM((1, tokens, wide), BF)] * 4,
-        input_output_aliases={3: 4, 4: 5, 5: 6, 6: 7},
+        + [pltpu.HBM((2, half, wide), BF)] * 2,
+        input_output_aliases={3: 4, 4: 5},
         compiler_params=params(8),
         cost_estimate=cost(MIB, MIB),
         name="hidden",
-    )(got, keep_routed, other_routed, send, *own[1:])
+    )(got, keep_routed, other_routed, on_a, on_b)
+    got_a, got_b = along_x_by(on_a, 3), along_x_by(on_b, 1)
+    here = pl.BlockSpec((1, strip, wide), lambda n, y: (y[0], n, 0))
+    there = pl.BlockSpec((1, strip, wide), lambda n, y: (1 - y[0], n, 0))
+    send, keep = pl.pallas_call(
+        second_sum_kernel,
+        grid_spec=pltpu.PrefetchScalarGridSpec(
+            num_scalar_prefetch=1,
+            grid=(half // strip,),
+            in_specs=[here, here, there, there] * 2,
+            out_specs=[pl.BlockSpec((2, strip, wide), lambda n, y: (0, n, 0))] * 2,
+        ),
+        out_shape=[pltpu.HBM((2, half, wide), BF), pltpu.HBM((2, half, wide), F32)],
+        compiler_params=params(16),
+        cost_estimate=cost(MIB, 3 * MIB),
+        name="second_sum",
+    )(y_at.reshape(1), *[own_a, got_a] * 2, *[own_b, got_b] * 2)
     other = along_y(send)
-    keep = x_sum(own[0], moved, F32)
     both = lax.all_to_all(both, "batch", 0, 0, tiled=True)
     misfit, hidden = pl.pallas_call(
         down_kernel,

time: 150 us -> 137 us (0.913)
  waiting for transfers between devices: 47.1 us -> 39.7 us
  starting transfers between devices: 55.9 us -> 51 us
    ppermute x13 -> x11, waiting for transfers between devices: 25.8 us -> 17.1 us  [along(): lax.ppermute(value, 'tensor', [(t, move(t // 8, t // 2 % 4, t % 2)) for t...]
    ppermute x13 -> x11, starting transfers between devices: 21.2 us -> 18.1 us  [along(): lax.ppermute(value, 'tensor', [(t, move(t // 8, t // 2 % 4, t % 2)) for t...]
  transfers between devices with their start and end apart: 20 -> 18, of which waited for: 9 -> 10; matrix products, arithmetic and copies ran while one was open for 0% -> 0% of each run, Pallas kernels for 14% -> 16%
where the time goes in v7:
time: 137 us; the launch traced here: 136 us
  starting transfers between devices  51 us (37%)
  waiting for transfers between devices  39.7 us (29%)
  Pallas kernels  33.6 us (25%)
  blocking collectives  11 us (8%)
    ppermute x11, starting transfers between devices, along(): lax.ppermute(value, 'tensor', [(t, move(t // 8, t // 2 % 4, t % 2)) for t...  18.1 us
    ppermute x11, waiting for transfers between devices, along(): lax.ppermute(value, 'tensor', [(t, move(t // 8, t // 2 % 4, t % 2)) for t...  17.1 us
    all_to_all x1, starting transfers between devices, on_device(): every = lax.all_to_all(copies, 'tensor', 0, 0, tiled=True)  11.3 us
    all_to_all x1, blocking collectives, on_device(): back = lax.all_to_all(back, 'batch', 0, 0, tiled=True)  11 us
    pallas_call x1, Pallas kernels, on_device(): pl.pallas_call(teacher_kernel, grid_spec=pltpu.PrefetchScalarGridSpec(num...  9.12 us
    all_to_all x1, waiting for transfers between devices, on_device(): grad_out = lax.all_to_all(grad_out, 'tensor', 0, 0, tiled=True)  8.41 us
    all_to_all x1, waiting for transfers between devices, on_device(): acts = lax.all_to_all(acts, 'batch', 0, 0, tiled=True)  7.06 us
    all_to_all x1, waiting for transfers between devices, on_device(): misfit = lax.all_to_all(misfit, 'tensor', 0, 0, tiled=True)  5.87 us
  transfers between devices with their start and end apart: 18, of which 10 were waited for; matrix products, arithmetic and copies ran while one was open for 0% of the time, Pallas kernels for 16%

profile of v7, /device:TPU:0, one launch (start us, length us, event | category | flops | bytes accessed | tf_op | source)
XLA Modules:
  0.0 136.2 jit_solution(5236127371224572926)
XLA Ops:
  3.8 9.1 %teacher.1 = (bf16[8,256,512]{2,1,0:T(8,128)(2,1)}, bf16[8,256,512]{2,1,0:T(8,128)(2,1)}, bf16[8,64,512]{2,1,0:T(8,128)(2,1)}, bf16[8,64,512]{2,1,0:T(8,128)(2,1)}) custom-call(s32[1]{0:T(128)} %bitcast.1.core_ref, s32[1,64]{1,0:T(1,128)} %route_ref.5, bf16[256,512]{1,0:T(8,128)(2,1)} %attn_ref.1, bf16[512,8192]{1,0:T(8,128)(2,1)} %other_ref.1, ...), custom_call_target="tpu_custom_call" | custom-call | flops 2621440 | bytes 14336 | tf_op jit(solution)/shard_map/teacher/pallas_call | solution.py:321
  14.5 11.3 %all-to-all-start = ((bf16[16,40,512]{2,1,0:T(8,128)(2,1)}), bf16[16,40,512]{2,1,0:T(8,128)(2,1)S(1)}, u32[]{:S(2)}, u32[]{:S(2)}) async-start(bf16[16,40,512]{2,1,0:T(8,128)(2,1)} %get-tuple-element.47), calls=%async_computation | async-start | bytes 1310720 | tf_op jit(solution)/shard_map/all_to_all | solution.py:357
  25.9 1.8 %core_sum.1 = (bf16[2,64,512]{2,1,0:T(8,128)(2,1)}, bf16[2,64,512]{2,1,0:T(8,128)(2,1)}, bf16[2,64,512]{2,1,0:T(8,128)(2,1)}, bf16[2,64,512]{2,1,0:T(8,128)(2,1)}) custom-call(s32[1]{0:T(128)} %bitcast.4.x_ref, bf16[8,64,512]{2,1,0:T(8,128)(2,1)} %get-tuple-element.51.refs_0_.refs_1_.refs_2_.refs_3_, ...), custom_call_target="tpu_custom_call" | custom-call | flops 1024 | bytes 1536 | tf_op jit(solution)/shard_map/core_sum/pallas_call | solution.py:366
  27.7 2.0 %collective-permute-start.3 = (bf16[2,64,512]{2,1,0:T(8,128)(2,1)}, bf16[2,64,512]{2,1,0:T(8,128)(2,1)S(1)}, u32[]{:S(2)}, u32[]{:S(2)}) collective-permute-start(bf16[2,64,512]{2,1,0:T(8,128)(2,1)} %get-tuple-element.54), channel_id=1, source_target_pairs={{0,2},{1,3},{2,4},{3,5},{4,6},{5,7},{6,0},{7,1},{8,10},{9,11},{10,... | collective-permute-start | bytes 393224 | tf_op jit(solution)/shard_map/ppermute | solution.py:360
  29.6 2.7 %collective-permute-start.4 = (bf16[2,64,512]{2,1,0:T(8,128)(2,1)}, bf16[2,64,512]{2,1,0:T(8,128)(2,1)S(1)}, u32[]{:S(2)}, u32[]{:S(2)}) collective-permute-start(bf16[2,64,512]{2,1,0:T(8,128)(2,1)} %get-tuple-element.55), channel_id=1, source_target_pairs={{0,4},{1,5},{2,6},{3,7},{4,0},{5,1},{6,2},{7,3},{8,12},{9,13},{10,... | collective-permute-start | bytes 393224 | tf_op jit(solution)/shard_map/ppermute | solution.py:360
  33.8 4.1 %halves.1 = (bf16[2,2,128,512]{3,2,1,0:T(8,128)(2,1)}, bf16[2,2,128,512]{3,2,1,0:T(8,128)(2,1)}, bf16[2,2,128,512]{3,2,1,0:T(8,128)(2,1)}, bf16[2,2,128,512]{3,2,1,0:T(8,128)(2,1)}) custom-call(s32[1]{0:T(128)} %bitcast.4.x_ref, bf16[8,2,128,512]{3,2,1,0:T(8,128)(2,1)} %bitcast.12, bf16[8,2,128,512]{3,2,1,0:T(8,128)(2,1)} %bitcast.13, ...), custom_call_target="tpu_custom_call" | custom-call | flops 1024 | bytes 6144 | tf_op jit(solution)/shard_map/halves/pallas_call | solution.py:403
  37.9 2.3 %collective-permute-done.3.refs_1_.refs_5_ = bf16[2,64,512]{2,1,0:T(8,128)(2,1)S(1)} collective-permute-done((bf16[2,64,512]{2,1,0:T(8,128)(2,1)}, bf16[2,64,512]{2,1,0:T(8,128)(2,1)S(1)}, u32[]{:S(2)}, u32[]{:S(2)}) %collective-permute-start.3) | collective-permute-done | bytes 131104 | tf_op jit(solution)/shard_map/ppermute | solution.py:360
  40.2 2.9 %collective-permute-done.4.refs_2_.refs_6_ = bf16[2,64,512]{2,1,0:T(8,128)(2,1)S(1)} collective-permute-done((bf16[2,64,512]{2,1,0:T(8,128)(2,1)}, bf16[2,64,512]{2,1,0:T(8,128)(2,1)S(1)}, u32[]{:S(2)}, u32[]{:S(2)}) %collective-permute-start.4) | collective-permute-done | bytes 131104 | tf_op jit(solution)/shard_map/ppermute | solution.py:360
  44.7 2.6 %up.1 = (bf16[8,32,1152]{2,1,0:T(8,128)(2,1)}, bf16[256,512]{1,0:T(8,128)(2,1)}, bf16[256,512]{1,0:T(8,128)(2,1)}, bf16[1,64,512]{2,1,0:T(8,128)(2,1)}, bf16[2,2...) custom-call(s32[1]{0:T(128)} %bitcast.group_ref, ...), custom_call_target="tpu_custom_call", output_to_operand_aliasing={{3}: (5, {}), {4}: (6, {}), {5}: (7, {})} | custom-call | flops 819200 | bytes 4096 | tf_op jit(solution)/shard_map/up/pallas_call | solution.py:443
  49.1 3.5 %all-to-all-start.1 = ((bf16[8,32,1152]{2,1,0:T(8,128)(2,1)}), bf16[8,32,1152]{2,1,0:T(8,128)(2,1)S(1)}, u32[]{:S(2)}, u32[]{:S(2)}) async-start(bf16[8,32,1152]{2,1,0:T(8,128)(2,1)} %get-tuple-element.60), calls=%async_computation.1 | async-start | bytes 1179648 | tf_op jit(solution)/shard_map/all_to_all | solution.py:470
  52.6 3.2 %collective-permute-start.6 = (bf16[1,64,512]{2,1,0:T(8,128)(2,1)}, bf16[1,64,512]{2,1,0:T(8,128)(2,1)S(1)}, u32[]{:S(2)}, u32[]{:S(2)}) collective-permute-start(bf16[1,64,512]{2,1,0:T(8,128)(2,1)} %get-tuple-element.62), channel_id=1, source_target_pairs={{0,8},{1,9},{2,10},{3,11},{4,12},{5,13},{6,14},{7,15},{8,0},{9,1},... | collective-permute-start | bytes 196616 | tf_op jit(solution)/shard_map/ppermute | solution.py:360
  55.9 5.2 %collective-permute-done.7.got_a = bf16[2,2,128,512]{3,2,1,0:T(8,128)(2,1)S(1)} collective-permute-done((bf16[2,2,128,512]{3,2,1,0:T(8,128)(2,1)}, bf16[2,2,128,512]{3,2,1,0:T(8,128)(2,1)S(1)}, u32[]{:S(2)}, u32[]{:S(2)}) %collective-permute-start.7) | collective-permute-done | bytes 524320 | tf_op jit(solution)/shard_map/ppermute | solution.py:360
  64.9 4.6 %all-to-all-start.2 = ((bf16[8,96,512]{2,1,0:T(8,128)(2,1)}), bf16[8,96,512]{2,1,0:T(8,128)(2,1)S(1)}, u32[]{:S(2)}, u32[]{:S(2)}) async-start(bf16[8,96,512]{2,1,0:T(8,128)(2,1)} %get-tuple-element.68), calls=%async_computation.2 | async-start | bytes 1572864 | tf_op jit(solution)/shard_map/all_to_all | solution.py:518
  70.1 2.3 %collective-permute-start.9 = (bf16[2,128,512]{2,1,0:T(8,128)(2,1)}, bf16[2,128,512]{2,1,0:T(8,128)(2,1)S(1)}, u32[]{:S(2)}, u32[]{:S(2)}) collective-permute-start(bf16[2,128,512]{2,1,0:T(8,128)(2,1)} %get-tuple-element.71), channel_id=1, source_target_pairs={{0,6},{1,7},{2,4},{3,5},{4,2},{5,3},{6,0},{7,1},{8,14},{9,15},{10,... | collective-permute-start | bytes 786440 | tf_op jit(solution)/shard_map/ppermute | solution.py:360
  72.4 3.6 %collective-permute-done.10.refs_5_.refs_7_ = bf16[2,128,512]{2,1,0:T(8,128)(2,1)S(1)} collective-permute-done((bf16[2,128,512]{2,1,0:T(8,128)(2,1)}, bf16[2,128,512]{2,1,0:T(8,128)(2,1)S(1)}, u32[]{:S(2)}, u32[]{:S(2)}) %collective-permute-start.10) | collective-permute-done | bytes 262176 | tf_op jit(solution)/shard_map/ppermute | solution.py:360
  80.0 2.4 %down.1 = (bf16[16,16,512]{2,1,0:T(8,128)(2,1)}, bf16[256,512]{1,0:T(8,128)(2,1)}) custom-call(s32[1]{0:T(128)} %bitcast.group_ref, bf16[8,96,512]{2,1,0:T(8,128)(2,1)S(1)} %all-to-all-done.2.got_ref, bf16[512,512]{1,0:T(8,128)(2,1)S(1)} %copy-done, bf16[256,512]{1,0:T(8,128)(2,1)S(1)} %copy-done.9, bf16[512,4096]{1,0:T(8,128)(2,1)} %projector_ref.1, ...), custom_call_target="tpu_custom_call" | custom-call | flops 786432 | bytes 4096 | tf_op jit(solution)/shard_map/down/pallas_call | solution.py:519
  82.4 5.0 %all-to-all-start.3 = ((bf16[16,16,512]{2,1,0:T(8,128)(2,1)}), bf16[16,16,512]{2,1,0:T(8,128)(2,1)S(1)}, u32[]{:S(2)}, u32[]{:S(2)}) async-start(bf16[16,16,512]{2,1,0:T(8,128)(2,1)} %get-tuple-element.75), calls=%async_computation.3 | async-start | bytes 524288 | tf_op jit(solution)/shard_map/all_to_all | solution.py:537
  87.4 3.5 %collective-permute-start.11 = (bf16[2,128,512]{2,1,0:T(8,128)(2,1)S(1)}, bf16[2,128,512]{2,1,0:T(8,128)(2,1)S(1)}, u32[]{:S(2)}, u32[]{:S(2)}) collective-permute-start(bf16[2,128,512]{2,1,0:T(8,128)(2,1)S(1)} %copy-done.13), channel_id=1, source_target_pairs={{0,8},{1,9},{2,10},{3,11},{4,12},{5,13},{6,14},{7,15},{8,0},{9,1},... | collective-permute-start | bytes 786440 | tf_op jit(solution)/shard_map/ppermute | solution.py:360
  90.9 5.9 %all-to-all-done.3.refs_0_ = bf16[16,16,512]{2,1,0:T(8,128)(2,1)S(1)} async-done(((bf16[16,16,512]{2,1,0:T(8,128)(2,1)}), bf16[16,16,512]{2,1,0:T(8,128)(2,1)S(1)}, u32[]{:S(2)}, u32[]{:S(2)}) %all-to-all-start.3) | async-done | bytes 262176 | tf_op jit(solution)/shard_map/all_to_all | solution.py:537
  97.5 3.5 %all-to-all-start.4 = ((bf16[16,16,512]{2,1,0:T(8,128)(2,1)}), bf16[16,16,512]{2,1,0:T(8,128)(2,1)S(1)}, u32[]{:S(2)}, u32[]{:S(2)}) async-start(bf16[16,16,512]{2,1,0:T(8,128)(2,1)} %misfit.1), calls=%async_computation.4 | async-start | bytes 524288 | tf_op jit(solution)/shard_map/all_to_all | solution.py:546
  102.0 8.4 %all-to-all-done.4.got_ref.grad_ref = bf16[16,16,512]{2,1,0:T(8,128)(2,1)S(1)} async-done(((bf16[16,16,512]{2,1,0:T(8,128)(2,1)}), bf16[16,16,512]{2,1,0:T(8,128)(2,1)S(1)}, u32[]{:S(2)}, u32[]{:S(2)}) %all-to-all-start.4) | async-done | bytes 262176 | tf_op jit(solution)/shard_map/all_to_all | solution.py:546
  110.7 11.0 %all_to_all.35.got_ref = bf16[8,32,512]{2,1,0:T(8,128)(2,1)S(1)} all-to-all(bf16[8,32,512]{2,1,0:T(8,128)(2,1)S(1)} %get-tuple-element.79), channel_id=1, replica_groups=mesh['batch'=8,'tensor'=16] {'batch'}, dimensions={0} | all-to-all | bytes 524288 | tf_op jit(solution)/shard_map/all_to_all | solution.py:565
  122.7 3.5 %all-to-all-start.6 = ((bf16[8,32,1024]{2,1,0:T(8,128)(2,1)}), bf16[8,32,1024]{2,1,0:T(8,128)(2,1)S(1)}, u32[]{:S(2)}, u32[]{:S(2)}) async-start(bf16[8,32,1024]{2,1,0:T(8,128)(2,1)} %acts.1), calls=%async_computation.6 | async-start | bytes 1048576 | tf_op jit(solution)/shard_map/all_to_all | solution.py:573
  127.5 7.1 %all-to-all-done.6.got_ref = bf16[8,32,1024]{2,1,0:T(8,128)(2,1)S(1)} async-done(((bf16[8,32,1024]{2,1,0:T(8,128)(2,1)}), bf16[8,32,1024]{2,1,0:T(8,128)(2,1)S(1)}, u32[]{:S(2)}, u32[]{:S(2)}) %all-to-all-start.6) | async-done | bytes 524320 | tf_op jit(solution)/shard_map/all_to_all | solution.py:573
  (58 shorter events, 23.7 us)
Async XLA Ops:
  2.4 10.6 %collective-permute-start = (bf16[40,512]{1,0:T(8,128)(2,1)}, bf16[40,512]{1,0:T(8,128)(2,1)S(1)}, u32[]{:S(2)}, u32[]{:S(2)}) collective-permute-start(bf16[40,512]{1,0:T(8,128)(2,1)} %rows.1), channel_id=1, source_target_pairs={{0,0},{1,1},{2,16},{3,17},{4,32},{5,33},{6,48},{7,49},{8,64},{9,65... | collective-permute-start | bytes 122888 | tf_op jit(solution)/shard_map/ppermute | solution.py:319
  13.9 19.9 %collective-permute-start.1 = (bf16[8,256,512]{2,1,0:T(8,128)(2,1)}, bf16[8,256,512]{2,1,0:T(8,128)(2,1)S(1)}, u32[]{:S(2)}, u32[]{:S(2)}) collective-permute-start(bf16[8,256,512]{2,1,0:T(8,128)(2,1)} %get-tuple-element.49), channel_id=1, source_target_pairs={{0,1},{1,0},{2,3},{3,2},{4,5},{5,4},{6,7},{7,6},{8,9},{9,8},{10,11... | collective-permute-start | bytes 6291464 | tf_op jit(solution)/shard_map/ppermute | solution.py:360
  14.0 11.9 %collective-permute-start.2 = (bf16[8,64,512]{2,1,0:T(8,128)(2,1)}, bf16[8,64,512]{2,1,0:T(8,128)(2,1)S(1)}, u32[]{:S(2)}, u32[]{:S(2)}) collective-permute-start(bf16[8,64,512]{2,1,0:T(8,128)(2,1)} %get-tuple-element.52), channel_id=1, source_target_pairs={{0,1},{1,0},{2,3},{3,2},{4,5},{5,4},{6,7},{7,6},{8,9},{9,8},{10,11... | collective-permute-start | bytes 1572872 | tf_op jit(solution)/shard_map/ppermute | solution.py:360
  14.5 30.2 %all-to-all-start = ((bf16[16,40,512]{2,1,0:T(8,128)(2,1)}), bf16[16,40,512]{2,1,0:T(8,128)(2,1)S(1)}, u32[]{:S(2)}, u32[]{:S(2)}) async-start(bf16[16,40,512]{2,1,0:T(8,128)(2,1)} %get-tuple-element.47), calls=%async_computation | async-start | bytes 1310720 | tf_op jit(solution)/shard_map/all_to_all | solution.py:357
  27.7 12.5 %collective-permute-start.3 = (bf16[2,64,512]{2,1,0:T(8,128)(2,1)}, bf16[2,64,512]{2,1,0:T(8,128)(2,1)S(1)}, u32[]{:S(2)}, u32[]{:S(2)}) collective-permute-start(bf16[2,64,512]{2,1,0:T(8,128)(2,1)} %get-tuple-element.54), channel_id=1, source_target_pairs={{0,2},{1,3},{2,4},{3,5},{4,6},{5,7},{6,0},{7,1},{8,10},{9,11},{10,... | collective-permute-start | bytes 393224 | tf_op jit(solution)/shard_map/ppermute | solution.py:360
  29.6 13.5 %collective-permute-start.4 = (bf16[2,64,512]{2,1,0:T(8,128)(2,1)}, bf16[2,64,512]{2,1,0:T(8,128)(2,1)S(1)}, u32[]{:S(2)}, u32[]{:S(2)}) collective-permute-start(bf16[2,64,512]{2,1,0:T(8,128)(2,1)} %get-tuple-element.55), channel_id=1, source_target_pairs={{0,4},{1,5},{2,6},{3,7},{4,0},{5,1},{6,2},{7,3},{8,12},{9,13},{10,... | collective-permute-start | bytes 393224 | tf_op jit(solution)/shard_map/ppermute | solution.py:360
  32.3 10.8 %collective-permute-start.5 = (bf16[2,64,512]{2,1,0:T(8,128)(2,1)}, bf16[2,64,512]{2,1,0:T(8,128)(2,1)S(1)}, u32[]{:S(2)}, u32[]{:S(2)}) collective-permute-start(bf16[2,64,512]{2,1,0:T(8,128)(2,1)} %get-tuple-element.56), channel_id=1, source_target_pairs={{0,6},{1,7},{2,0},{3,1},{4,2},{5,3},{6,4},{7,5},{8,14},{9,15},{10,... | collective-permute-start | bytes 393224 | tf_op jit(solution)/shard_map/ppermute | solution.py:360
  44.7 17.7 %copy-start.2 = (bf16[2,2,128,512]{3,2,1,0:T(8,128)(2,1)S(1)}, bf16[2,2,128,512]{3,2,1,0:T(8,128)(2,1)}, u32[]{:S(2)}) copy-start(bf16[2,2,128,512]{3,2,1,0:T(8,128)(2,1)} %get-tuple-element.50.after_ref.keep_a) | copy-start | bytes 1572868
  44.7 17.7 %copy-start.7 = (bf16[2,2,128,512]{3,2,1,0:T(8,128)(2,1)S(1)}, bf16[2,2,128,512]{3,2,1,0:T(8,128)(2,1)}, u32[]{:S(2)}) copy-start(bf16[2,2,128,512]{3,2,1,0:T(8,128)(2,1)} %get-tuple-element.64.keep_b) | copy-start | bytes 1572868
  47.3 16.5 %copy-start.11 = (f32[1,64,512]{2,1,0:T(8,128)S(1)}, f32[1,64,512]{2,1,0:T(8,128)}, u32[]{:S(2)}) copy-start(f32[1,64,512]{2,1,0:T(8,128)} %get-tuple-element.61.refs_1_) | copy-start | bytes 393220
  47.3 13.8 %collective-permute-start.7 = (bf16[2,2,128,512]{3,2,1,0:T(8,128)(2,1)}, bf16[2,2,128,512]{3,2,1,0:T(8,128)(2,1)S(1)}, u32[]{:S(2)}, u32[]{:S(2)}) collective-permute-start(bf16[2,2,128,512]{3,2,1,0:T(8,128)(2,1)} %get-tuple-element.63), channel_id=1, source_target_pairs={{0,2},{1,3},{2,0},{3,1},{4,6},{5,7},{6,4},{7,5},{8,10},{9,11},{10,... | collective-permute-start | bytes 1572872 | tf_op jit(solution)/shard_map/ppermute | solution.py:360
  47.4 15.0 %collective-permute-start.8 = (bf16[2,2,128,512]{3,2,1,0:T(8,128)(2,1)}, bf16[2,2,128,512]{3,2,1,0:T(8,128)(2,1)S(1)}, u32[]{:S(2)}, u32[]{:S(2)}) collective-permute-start(bf16[2,2,128,512]{3,2,1,0:T(8,128)(2,1)} %get-tuple-element.65), channel_id=1, source_target_pairs={{0,6},{1,7},{2,4},{3,5},{4,2},{5,3},{6,0},{7,1},{8,14},{9,15},{10,... | collective-permute-start | bytes 1572872 | tf_op jit(solution)/shard_map/ppermute | solution.py:360
  49.1 14.7 %all-to-all-start.1 = ((bf16[8,32,1152]{2,1,0:T(8,128)(2,1)}), bf16[8,32,1152]{2,1,0:T(8,128)(2,1)S(1)}, u32[]{:S(2)}, u32[]{:S(2)}) async-start(bf16[8,32,1152]{2,1,0:T(8,128)(2,1)} %get-tuple-element.60), calls=%async_computation.1 | async-start | bytes 1179648 | tf_op jit(solution)/shard_map/all_to_all | solution.py:470
  52.6 11.2 %collective-permute-start.6 = (bf16[1,64,512]{2,1,0:T(8,128)(2,1)}, bf16[1,64,512]{2,1,0:T(8,128)(2,1)S(1)}, u32[]{:S(2)}, u32[]{:S(2)}) collective-permute-start(bf16[1,64,512]{2,1,0:T(8,128)(2,1)} %get-tuple-element.62), channel_id=1, source_target_pairs={{0,8},{1,9},{2,10},{3,11},{4,12},{5,13},{6,14},{7,15},{8,0},{9,1},... | collective-permute-start | bytes 196616 | tf_op jit(solution)/shard_map/ppermute | solution.py:360
  64.9 15.1 %all-to-all-start.2 = ((bf16[8,96,512]{2,1,0:T(8,128)(2,1)}), bf16[8,96,512]{2,1,0:T(8,128)(2,1)S(1)}, u32[]{:S(2)}, u32[]{:S(2)}) async-start(bf16[8,96,512]{2,1,0:T(8,128)(2,1)} %get-tuple-element.68), calls=%async_computation.2 | async-start | bytes 1572864 | tf_op jit(solution)/shard_map/all_to_all | solution.py:518
  69.5 6.6 %collective-permute-start.10 = (bf16[2,128,512]{2,1,0:T(8,128)(2,1)}, bf16[2,128,512]{2,1,0:T(8,128)(2,1)S(1)}, u32[]{:S(2)}, u32[]{:S(2)}) collective-permute-start(bf16[2,128,512]{2,1,0:T(8,128)(2,1)} %get-tuple-element.73), channel_id=1, source_target_pairs={{0,2},{1,3},{2,0},{3,1},{4,6},{5,7},{6,4},{7,5},{8,10},{9,11},{10,... | collective-permute-start | bytes 786440 | tf_op jit(solution)/shard_map/ppermute | solution.py:360
  70.1 7.8 %collective-permute-start.9 = (bf16[2,128,512]{2,1,0:T(8,128)(2,1)}, bf16[2,128,512]{2,1,0:T(8,128)(2,1)S(1)}, u32[]{:S(2)}, u32[]{:S(2)}) collective-permute-start(bf16[2,128,512]{2,1,0:T(8,128)(2,1)} %get-tuple-element.71), channel_id=1, source_target_pairs={{0,6},{1,7},{2,4},{3,5},{4,2},{5,3},{6,0},{7,1},{8,14},{9,15},{10,... | collective-permute-start | bytes 786440 | tf_op jit(solution)/shard_map/ppermute | solution.py:360
  80.0 21.1 %copy-start.1 = (f32[2,128,512]{2,1,0:T(8,128)S(1)}, f32[2,128,512]{2,1,0:T(8,128)}, u32[]{:S(2)}) copy-start(f32[2,128,512]{2,1,0:T(8,128)} %get-tuple-element.74.after_ref.keep_ref) | copy-start | bytes 1572868
  82.4 14.3 %all-to-all-start.3 = ((bf16[16,16,512]{2,1,0:T(8,128)(2,1)}), bf16[16,16,512]{2,1,0:T(8,128)(2,1)S(1)}, u32[]{:S(2)}, u32[]{:S(2)}) async-start(bf16[16,16,512]{2,1,0:T(8,128)(2,1)} %get-tuple-element.75), calls=%async_computation.3 | async-start | bytes 524288 | tf_op jit(solution)/shard_map/all_to_all | solution.py:537
  87.4 13.7 %collective-permute-start.11 = (bf16[2,128,512]{2,1,0:T(8,128)(2,1)S(1)}, bf16[2,128,512]{2,1,0:T(8,128)(2,1)S(1)}, u32[]{:S(2)}, u32[]{:S(2)}) collective-permute-start(bf16[2,128,512]{2,1,0:T(8,128)(2,1)S(1)} %copy-done.13), channel_id=1, source_target_pairs={{0,8},{1,9},{2,10},{3,11},{4,12},{5,13},{6,14},{7,15},{8,0},{9,1},... | collective-permute-start | bytes 786440 | tf_op jit(solution)/shard_map/ppermute | solution.py:360
  97.5 12.9 %all-to-all-start.4 = ((bf16[16,16,512]{2,1,0:T(8,128)(2,1)}), bf16[16,16,512]{2,1,0:T(8,128)(2,1)S(1)}, u32[]{:S(2)}, u32[]{:S(2)}) async-start(bf16[16,16,512]{2,1,0:T(8,128)(2,1)} %misfit.1), calls=%async_computation.4 | async-start | bytes 524288 | tf_op jit(solution)/shard_map/all_to_all | solution.py:546
  102.0 24.2 %copy-start.10 = (bf16[256,512]{1,0:T(8,128)(2,1)S(1)}, bf16[256,512]{1,0:T(8,128)(2,1)}, u32[]{:S(2)}) copy-start(bf16[256,512]{1,0:T(8,128)(2,1)} %get-tuple-element.85.hidden_ref) | copy-start | bytes 786436
  110.7 23.8 %copy-start.8 = (bf16[256,512]{1,0:T(8,128)(2,1)S(1)}, bf16[256,512]{1,0:T(8,128)(2,1)}, u32[]{:S(2)}) copy-start(bf16[256,512]{1,0:T(8,128)(2,1)} %get-tuple-element.78.rows_ref) | copy-start | bytes 786436
  122.7 11.9 %all-to-all-start.6 = ((bf16[8,32,1024]{2,1,0:T(8,128)(2,1)}), bf16[8,32,1024]{2,1,0:T(8,128)(2,1)S(1)}, u32[]{:S(2)}, u32[]{:S(2)}) async-start(bf16[8,32,1024]{2,1,0:T(8,128)(2,1)} %acts.1), calls=%async_computation.6 | async-start | bytes 1048576 | tf_op jit(solution)/shard_map/all_to_all | solution.py:573
  (8 other events, 95.3 us)

commit v8 on v7

--- a/solution.py
+++ b/solution.py
@@ -94,12 +94,12 @@
     refs[-1][...] = total.astype(refs[-1].dtype)
 
 
-def routed_sum_kernel(y_ref, route_ref, residual_ref, after_ref, *refs):
-    ways = len(refs) // 2 - 1
-    x_sum_kernel(*refs[0:ways], refs[-2])
-    x_sum_kernel(*refs[ways : 2 * ways], refs[-1])
+def routed_sum_kernel(y_ref, route_ref, residual_ref, p1, p2, p3, *refs):
+    ins, (send_ref, keep_ref) = refs[:8], refs[8:10]
+    x_sum_kernel(*ins[:4], send_ref)
+    x_sum_kernel(*ins[4:], keep_ref)
     hot = slot_rows(route_ref[...], residual_ref.shape[1])
-    refs[-1][0] = refs[-1][0] + dot(hot, residual_ref[...], 1, 1)
+    keep_ref[0] = keep_ref[0] + dot(hot, residual_ref[...], 1, 1)
 
 
 def halves_kernel(x_ref, *refs):
@@ -130,8 +130,8 @@
 
 
 def up_kernel(
-    group_ref, got_ref, gain_ref, gate_ref, up_ref, p1, p2, p3,
-    out_ref, rows_ref, chosen_ref, q1, q2, q3, padded_ref, weights_ref, sems,
+    group_ref, got_ref, gain_ref, gate_ref, up_ref, after_ref,
+    out_ref, rows_ref, chosen_ref, padded_ref, weights_ref, sems,
 ):
     loads = [
         pltpu.make_async_copy(ref, weights_ref.at[i], sems.at[i])
@@ -421,33 +421,18 @@
         name="halves",
     )(x_at.reshape(1), *[hbm(keep.reshape(halves))] * 4, *[got.reshape(halves)] * 4)
 
-    routed, *moved = core_sum(keep_routed, send_routed, slots)
-    send_routed, keep_routed = pl.pallas_call(
-        routed_sum_kernel,
-        grid_spec=pltpu.PrefetchScalarGridSpec(
-            num_scalar_prefetch=1,
-            grid=(1,),
-            in_specs=[vmem, vmem, anywhere] + y_blocks(slots),
-            out_specs=[pl.BlockSpec((1, slots, wide), lambda i, y: (0, 0, 0))] * 2,
-        ),
-        out_shape=[pltpu.HBM((1, slots, wide), BF), pltpu.HBM((1, slots, wide), F32)],
-        compiler_params=params(8),
-        cost_estimate=cost(MIB, MIB),
-        name="routed_sum",
-    )(y_at.reshape(1), route_index, residual_t, hbm(keep_a), *along_x(routed, moved) * 2)
-
     def along_x_by(value, mask):
         return along(value, lambda y, x, c: y * 8 + (x ^ mask) * 2 + c)
 
     packed = 2 * wide + 128
-    sent, scaled, chosen, send_routed, send_a, send_b = pl.pallas_call(
+    sent, scaled, chosen = pl.pallas_call(
         up_kernel,
         grid_spec=pltpu.PrefetchScalarGridSpec(
             num_scalar_prefetch=1,
             grid=(1,),
             in_specs=[vmem, pl.BlockSpec((1, wide), lambda i, group: (0, group[0]))]
-            + [anywhere] * 5,
-            out_specs=[vmem] * 3 + [anywhere] * 3,
+            + [anywhere] * 3,
+            out_specs=[vmem] * 3,
             scratch_shapes=[
                 pltpu.VMEM((groups * slots, wide), BF),
                 pltpu.VMEM((2, wide, units), BF),
@@ -458,15 +443,35 @@
             pltpu.HBM((groups, per, packed), BF),
             pltpu.HBM((live, wide), BF),
             pltpu.HBM((live, groups * slots), BF),
-            pltpu.HBM(send_routed.shape, BF),
+        ],
+        compiler_params=params(16),
+        cost_estimate=cost(800 * MIB, 4 * MIB),
+        name="up",
+    )(group.reshape(1), every, norm_gain[None], w_gate, w_up, hbm(keep_a))
+
+    routed, *moved = core_sum(keep_routed, send_routed, slots)
+    send_routed, keep_routed, sent, send_a, send_b = pl.pallas_call(
+        routed_sum_kernel,
+        grid_spec=pltpu.PrefetchScalarGridSpec(
+            num_scalar_prefetch=1,
+            grid=(1,),
+            in_specs=[vmem] * 2 + [anywhere] * 3 + y_blocks(slots),
+            out_specs=[pl.BlockSpec((1, slots, wide), lambda i, y: (0, 0, 0))] * 2
+            + [anywhere] * 3,
+        ),
+        out_shape=[
+            pltpu.HBM((1, slots, wide), BF),
+            pltpu.HBM((1, slots, wide), F32),
+            pltpu.HBM(sent.shape, BF),
         ]
         + [pair] * 2,
-        input_output_aliases={5: 3, 6: 4, 7: 5},
-        compiler_params=params(16),
-        cost_estimate=cost(800 * MIB, 4 * MIB),
-        name="up",
-    )(group.reshape(1), every, norm_gain[None], w_gate, w_up, send_routed, send_a, send_b)
+        input_output_aliases={3: 2, 4: 3, 5: 4},
+        compiler_params=params(8),
+        cost_estimate=cost(MIB, MIB),
+        name="routed_sum",
+    )(y_at.reshape(1), route_index, residual_t, sent, send_a, send_b, *along_x(routed, moved) * 2)
     other_routed = along_y(send_routed)
+
     got = lax.all_to_all(sent, "batch", 0, 0, tiled=True)
 
     flat = shape((per, units), F32)

time: 137 us -> 135 us (0.985)
  waiting for transfers between devices: 39.7 us -> 37 us
    ppermute x11, waiting for transfers between devices: 17.1 us -> 12.5 us  [along(): lax.ppermute(value, 'tensor', [(t, move(t // 8, t // 2 % 4, t % 2)) for t...]
    all_to_all x1, waiting for transfers between devices: 0.01 us -> 2.09 us  [on_device(): every = lax.all_to_all(copies, 'tensor', 0, 0, tiled=True)]
  transfers between devices with their start and end apart: 18 -> 18, of which waited for: 10 -> 10; matrix products, arithmetic and copies ran while one was open for 0% -> 0% of each run, Pallas kernels for 16% -> 17%
where the time goes in v8:
time: 135 us; the launch traced here: 133 us
  starting transfers between devices  51.1 us (38%)
  waiting for transfers between devices  37 us (27%)
  Pallas kernels  33.5 us (25%)
  blocking collectives  11 us (8%)
    ppermute x11, starting transfers between devices, along(): lax.ppermute(value, 'tensor', [(t, move(t // 8, t // 2 % 4, t % 2)) for t...  18.1 us
    ppermute x11, waiting for transfers between devices, along(): lax.ppermute(value, 'tensor', [(t, move(t // 8, t // 2 % 4, t % 2)) for t...  12.5 us
    all_to_all x1, starting transfers between devices, on_device(): every = lax.all_to_all(copies, 'tensor', 0, 0, tiled=True)  11.3 us
    all_to_all x1, blocking collectives, on_device(): back = lax.all_to_all(back, 'batch', 0, 0, tiled=True)  11 us
    pallas_call x1, Pallas kernels, on_device(): pl.pallas_call(teacher_kernel, grid_spec=pltpu.PrefetchScalarGridSpec(num...  9.12 us
    all_to_all x1, waiting for transfers between devices, on_device(): grad_out = lax.all_to_all(grad_out, 'tensor', 0, 0, tiled=True)  8.41 us
    all_to_all x1, waiting for transfers between devices, on_device(): acts = lax.all_to_all(acts, 'batch', 0, 0, tiled=True)  7.06 us
    all_to_all x1, waiting for transfers between devices, on_device(): misfit = lax.all_to_all(misfit, 'tensor', 0, 0, tiled=True)  5.87 us
  transfers between devices with their start and end apart: 18, of which 10 were waited for; matrix products, arithmetic and copies ran while one was open for 0% of the time, Pallas kernels for 17%

profile of v8, /device:TPU:0, one launch (start us, length us, event | category | flops | bytes accessed | tf_op | source)
XLA Modules:
  0.0 133.5 jit_solution(10441778792775485943)
XLA Ops:
  3.8 9.1 %teacher.1 = (bf16[8,256,512]{2,1,0:T(8,128)(2,1)}, bf16[8,256,512]{2,1,0:T(8,128)(2,1)}, bf16[8,64,512]{2,1,0:T(8,128)(2,1)}, bf16[8,64,512]{2,1,0:T(8,128)(2,1)}) custom-call(s32[1]{0:T(128)} %bitcast.2.core_ref, s32[1,64]{1,0:T(1,128)} %route_ref.5, bf16[256,512]{1,0:T(8,128)(2,1)} %attn_ref.1, bf16[512,8192]{1,0:T(8,128)(2,1)} %other_ref.1, ...), custom_call_target="tpu_custom_call" | custom-call | flops 2621440 | bytes 14336 | tf_op jit(solution)/shard_map/teacher/pallas_call | solution.py:321
  14.5 11.3 %all-to-all-start = ((bf16[16,40,512]{2,1,0:T(8,128)(2,1)}), bf16[16,40,512]{2,1,0:T(8,128)(2,1)S(1)}, u32[]{:S(2)}, u32[]{:S(2)}) async-start(bf16[16,40,512]{2,1,0:T(8,128)(2,1)} %get-tuple-element.47), calls=%async_computation | async-start | bytes 1310720 | tf_op jit(solution)/shard_map/all_to_all | solution.py:357
  25.9 1.8 %core_sum.1 = (bf16[2,64,512]{2,1,0:T(8,128)(2,1)}, bf16[2,64,512]{2,1,0:T(8,128)(2,1)}, bf16[2,64,512]{2,1,0:T(8,128)(2,1)}, bf16[2,64,512]{2,1,0:T(8,128)(2,1)}) custom-call(s32[1]{0:T(128)} %bitcast.4.x_ref, bf16[8,64,512]{2,1,0:T(8,128)(2,1)} %get-tuple-element.54.refs_0_.refs_1_.refs_2_.refs_3_, ...), custom_call_target="tpu_custom_call" | custom-call | flops 1024 | bytes 1536 | tf_op jit(solution)/shard_map/core_sum/pallas_call | solution.py:366
  27.7 1.9 %collective-permute-start.3 = (bf16[2,64,512]{2,1,0:T(8,128)(2,1)}, bf16[2,64,512]{2,1,0:T(8,128)(2,1)S(1)}, u32[]{:S(2)}, u32[]{:S(2)}) collective-permute-start(bf16[2,64,512]{2,1,0:T(8,128)(2,1)} %get-tuple-element.57), channel_id=1, source_target_pairs={{0,2},{1,3},{2,4},{3,5},{4,6},{5,7},{6,0},{7,1},{8,10},{9,11},{10,... | collective-permute-start | bytes 393224 | tf_op jit(solution)/shard_map/ppermute | solution.py:360
  29.6 2.7 %collective-permute-start.4 = (bf16[2,64,512]{2,1,0:T(8,128)(2,1)}, bf16[2,64,512]{2,1,0:T(8,128)(2,1)S(1)}, u32[]{:S(2)}, u32[]{:S(2)}) collective-permute-start(bf16[2,64,512]{2,1,0:T(8,128)(2,1)} %get-tuple-element.58), channel_id=1, source_target_pairs={{0,4},{1,5},{2,6},{3,7},{4,0},{5,1},{6,2},{7,3},{8,12},{9,13},{10,... | collective-permute-start | bytes 393224 | tf_op jit(solution)/shard_map/ppermute | solution.py:360
  33.8 4.1 %halves.1 = (bf16[2,2,128,512]{3,2,1,0:T(8,128)(2,1)}, bf16[2,2,128,512]{3,2,1,0:T(8,128)(2,1)}, bf16[2,2,128,512]{3,2,1,0:T(8,128)(2,1)}, bf16[2,2,128,512]{3,2,1,0:T(8,128)(2,1)}) custom-call(s32[1]{0:T(128)} %bitcast.4.x_ref, bf16[8,2,128,512]{3,2,1,0:T(8,128)(2,1)} %bitcast.12, bf16[8,2,128,512]{3,2,1,0:T(8,128)(2,1)} %bitcast.13, ...), custom_call_target="tpu_custom_call" | custom-call | flops 1024 | bytes 6144 | tf_op jit(solution)/shard_map/halves/pallas_call | solution.py:403
  37.9 2.1 %all-to-all-done.got_ref = bf16[16,40,512]{2,1,0:T(8,128)(2,1)S(1)} async-done(((bf16[16,40,512]{2,1,0:T(8,128)(2,1)}), bf16[16,40,512]{2,1,0:T(8,128)(2,1)S(1)}, u32[]{:S(2)}, u32[]{:S(2)}) %all-to-all-start) | async-done | bytes 655392 | tf_op jit(solution)/shard_map/all_to_all | solution.py:357
  39.9 2.5 %up.1 = (bf16[8,32,1152]{2,1,0:T(8,128)(2,1)}, bf16[256,512]{1,0:T(8,128)(2,1)}, bf16[256,512]{1,0:T(8,128)(2,1)}) custom-call(s32[1]{0:T(128)} %bitcast.group_ref, bf16[16,40,512]{2,1,0:T(8,128)(2,1)S(1)} %all-to-all-done.got_ref, f32[1,4096]{1,0:T(1,128)S(1)} %bitcast.11, bf16[512,512]{1,0:T(8,128)(2,1)} %gate_ref.1, bf16[512,512]{1,0:T(8,128)(2,1)} %up_ref.1, ...), custom_call_target="tpu_custom_call" | custom-call | flops 819200 | bytes 4096 | tf_op jit(solution)/shard_map/up/pallas_call | solution.py:428
  46.4 3.5 %all-to-all-start.1 = ((bf16[8,32,1152]{2,1,0:T(8,128)(2,1)}), bf16[8,32,1152]{2,1,0:T(8,128)(2,1)S(1)}, u32[]{:S(2)}, u32[]{:S(2)}) async-start(bf16[8,32,1152]{2,1,0:T(8,128)(2,1)} %get-tuple-element.60), calls=%async_computation.1 | async-start | bytes 1179648 | tf_op jit(solution)/shard_map/all_to_all | solution.py:475
  49.9 3.2 %collective-permute-start.6 = (bf16[1,64,512]{2,1,0:T(8,128)(2,1)}, bf16[1,64,512]{2,1,0:T(8,128)(2,1)S(1)}, u32[]{:S(2)}, u32[]{:S(2)}) collective-permute-start(bf16[1,64,512]{2,1,0:T(8,128)(2,1)} %get-tuple-element.62), channel_id=1, source_target_pairs={{0,8},{1,9},{2,10},{3,11},{4,12},{5,13},{6,14},{7,15},{8,0},{9,1},... | collective-permute-start | bytes 196616 | tf_op jit(solution)/shard_map/ppermute | solution.py:360
  53.2 5.2 %collective-permute-done.7.got_a = bf16[2,2,128,512]{3,2,1,0:T(8,128)(2,1)S(1)} collective-permute-done((bf16[2,2,128,512]{3,2,1,0:T(8,128)(2,1)}, bf16[2,2,128,512]{3,2,1,0:T(8,128)(2,1)S(1)}, u32[]{:S(2)}, u32[]{:S(2)}) %collective-permute-start.7) | collective-permute-done | bytes 524320 | tf_op jit(solution)/shard_map/ppermute | solution.py:360
  62.1 4.7 %all-to-all-start.2 = ((bf16[8,96,512]{2,1,0:T(8,128)(2,1)}), bf16[8,96,512]{2,1,0:T(8,128)(2,1)S(1)}, u32[]{:S(2)}, u32[]{:S(2)}) async-start(bf16[8,96,512]{2,1,0:T(8,128)(2,1)} %get-tuple-element.68), calls=%async_computation.2 | async-start | bytes 1572864 | tf_op jit(solution)/shard_map/all_to_all | solution.py:523
  67.4 2.3 %collective-permute-start.9 = (bf16[2,128,512]{2,1,0:T(8,128)(2,1)}, bf16[2,128,512]{2,1,0:T(8,128)(2,1)S(1)}, u32[]{:S(2)}, u32[]{:S(2)}) collective-permute-start(bf16[2,128,512]{2,1,0:T(8,128)(2,1)} %get-tuple-element.71), channel_id=1, source_target_pairs={{0,6},{1,7},{2,4},{3,5},{4,2},{5,3},{6,0},{7,1},{8,14},{9,15},{10,... | collective-permute-start | bytes 786440 | tf_op jit(solution)/shard_map/ppermute | solution.py:360
  69.7 3.6 %collective-permute-done.10.refs_5_.refs_7_ = bf16[2,128,512]{2,1,0:T(8,128)(2,1)S(1)} collective-permute-done((bf16[2,128,512]{2,1,0:T(8,128)(2,1)}, bf16[2,128,512]{2,1,0:T(8,128)(2,1)S(1)}, u32[]{:S(2)}, u32[]{:S(2)}) %collective-permute-start.10) | collective-permute-done | bytes 262176 | tf_op jit(solution)/shard_map/ppermute | solution.py:360
  73.4 1.8 %collective-permute-done.9.refs_1_.refs_3_ = bf16[2,128,512]{2,1,0:T(8,128)(2,1)S(1)} collective-permute-done((bf16[2,128,512]{2,1,0:T(8,128)(2,1)}, bf16[2,128,512]{2,1,0:T(8,128)(2,1)S(1)}, u32[]{:S(2)}, u32[]{:S(2)}) %collective-permute-start.9) | collective-permute-done | bytes 262176 | tf_op jit(solution)/shard_map/ppermute | solution.py:360
  77.2 2.4 %down.1 = (bf16[16,16,512]{2,1,0:T(8,128)(2,1)}, bf16[256,512]{1,0:T(8,128)(2,1)}) custom-call(s32[1]{0:T(128)} %bitcast.group_ref, bf16[8,96,512]{2,1,0:T(8,128)(2,1)S(1)} %all-to-all-done.2.got_ref, bf16[512,512]{1,0:T(8,128)(2,1)S(1)} %copy-done, bf16[256,512]{1,0:T(8,128)(2,1)S(1)} %copy-done.9, bf16[512,4096]{1,0:T(8,128)(2,1)} %projector_ref.1, ...), custom_call_target="tpu_custom_call" | custom-call | flops 786432 | bytes 4096 | tf_op jit(solution)/shard_map/down/pallas_call | solution.py:524
  79.6 5.1 %all-to-all-start.3 = ((bf16[16,16,512]{2,1,0:T(8,128)(2,1)}), bf16[16,16,512]{2,1,0:T(8,128)(2,1)S(1)}, u32[]{:S(2)}, u32[]{:S(2)}) async-start(bf16[16,16,512]{2,1,0:T(8,128)(2,1)} %get-tuple-element.75), calls=%async_computation.3 | async-start | bytes 524288 | tf_op jit(solution)/shard_map/all_to_all | solution.py:542
  84.7 3.5 %collective-permute-start.11 = (bf16[2,128,512]{2,1,0:T(8,128)(2,1)S(1)}, bf16[2,128,512]{2,1,0:T(8,128)(2,1)S(1)}, u32[]{:S(2)}, u32[]{:S(2)}) collective-permute-start(bf16[2,128,512]{2,1,0:T(8,128)(2,1)S(1)} %copy-done.13), channel_id=1, source_target_pairs={{0,8},{1,9},{2,10},{3,11},{4,12},{5,13},{6,14},{7,15},{8,0},{9,1},... | collective-permute-start | bytes 786440 | tf_op jit(solution)/shard_map/ppermute | solution.py:360
  88.2 5.9 %all-to-all-done.3.refs_0_ = bf16[16,16,512]{2,1,0:T(8,128)(2,1)S(1)} async-done(((bf16[16,16,512]{2,1,0:T(8,128)(2,1)}), bf16[16,16,512]{2,1,0:T(8,128)(2,1)S(1)}, u32[]{:S(2)}, u32[]{:S(2)}) %all-to-all-start.3) | async-done | bytes 262176 | tf_op jit(solution)/shard_map/all_to_all | solution.py:542
  94.8 3.5 %all-to-all-start.4 = ((bf16[16,16,512]{2,1,0:T(8,128)(2,1)}), bf16[16,16,512]{2,1,0:T(8,128)(2,1)S(1)}, u32[]{:S(2)}, u32[]{:S(2)}) async-start(bf16[16,16,512]{2,1,0:T(8,128)(2,1)} %misfit.1), calls=%async_computation.4 | async-start | bytes 524288 | tf_op jit(solution)/shard_map/all_to_all | solution.py:551
  99.3 8.4 %all-to-all-done.4.got_ref.grad_ref = bf16[16,16,512]{2,1,0:T(8,128)(2,1)S(1)} async-done(((bf16[16,16,512]{2,1,0:T(8,128)(2,1)}), bf16[16,16,512]{2,1,0:T(8,128)(2,1)S(1)}, u32[]{:S(2)}, u32[]{:S(2)}) %all-to-all-start.4) | async-done | bytes 262176 | tf_op jit(solution)/shard_map/all_to_all | solution.py:551
  108.0 11.0 %all_to_all.35.got_ref = bf16[8,32,512]{2,1,0:T(8,128)(2,1)S(1)} all-to-all(bf16[8,32,512]{2,1,0:T(8,128)(2,1)S(1)} %get-tuple-element.79), channel_id=1, replica_groups=mesh['batch'=8,'tensor'=16] {'batch'}, dimensions={0} | all-to-all | bytes 524288 | tf_op jit(solution)/shard_map/all_to_all | solution.py:570
  119.9 3.5 %all-to-all-start.6 = ((bf16[8,32,1024]{2,1,0:T(8,128)(2,1)}), bf16[8,32,1024]{2,1,0:T(8,128)(2,1)S(1)}, u32[]{:S(2)}, u32[]{:S(2)}) async-start(bf16[8,32,1024]{2,1,0:T(8,128)(2,1)} %acts.1), calls=%async_computation.6 | async-start | bytes 1048576 | tf_op jit(solution)/shard_map/all_to_all | solution.py:578
  124.8 7.1 %all-to-all-done.6.got_ref = bf16[8,32,1024]{2,1,0:T(8,128)(2,1)S(1)} async-done(((bf16[8,32,1024]{2,1,0:T(8,128)(2,1)}), bf16[8,32,1024]{2,1,0:T(8,128)(2,1)S(1)}, u32[]{:S(2)}, u32[]{:S(2)}) %all-to-all-start.6) | async-done | bytes 524320 | tf_op jit(solution)/shard_map/all_to_all | solution.py:578
  (58 shorter events, 22.3 us)
Async XLA Ops:
  2.4 10.6 %collective-permute-start = (bf16[40,512]{1,0:T(8,128)(2,1)}, bf16[40,512]{1,0:T(8,128)(2,1)S(1)}, u32[]{:S(2)}, u32[]{:S(2)}) collective-permute-start(bf16[40,512]{1,0:T(8,128)(2,1)} %rows.1), channel_id=1, source_target_pairs={{0,0},{1,1},{2,16},{3,17},{4,32},{5,33},{6,48},{7,49},{8,64},{9,65... | collective-permute-start | bytes 122888 | tf_op jit(solution)/shard_map/ppermute | solution.py:319
  13.9 19.9 %collective-permute-start.1 = (bf16[8,256,512]{2,1,0:T(8,128)(2,1)}, bf16[8,256,512]{2,1,0:T(8,128)(2,1)S(1)}, u32[]{:S(2)}, u32[]{:S(2)}) collective-permute-start(bf16[8,256,512]{2,1,0:T(8,128)(2,1)} %get-tuple-element.49), channel_id=1, source_target_pairs={{0,1},{1,0},{2,3},{3,2},{4,5},{5,4},{6,7},{7,6},{8,9},{9,8},{10,11... | collective-permute-start | bytes 6291464 | tf_op jit(solution)/shard_map/ppermute | solution.py:360
  14.0 11.9 %collective-permute-start.2 = (bf16[8,64,512]{2,1,0:T(8,128)(2,1)}, bf16[8,64,512]{2,1,0:T(8,128)(2,1)S(1)}, u32[]{:S(2)}, u32[]{:S(2)}) collective-permute-start(bf16[8,64,512]{2,1,0:T(8,128)(2,1)} %get-tuple-element.55), channel_id=1, source_target_pairs={{0,1},{1,0},{2,3},{3,2},{4,5},{5,4},{6,7},{7,6},{8,9},{9,8},{10,11... | collective-permute-start | bytes 1572872 | tf_op jit(solution)/shard_map/ppermute | solution.py:360
  14.5 25.4 %all-to-all-start = ((bf16[16,40,512]{2,1,0:T(8,128)(2,1)}), bf16[16,40,512]{2,1,0:T(8,128)(2,1)S(1)}, u32[]{:S(2)}, u32[]{:S(2)}) async-start(bf16[16,40,512]{2,1,0:T(8,128)(2,1)} %get-tuple-element.47), calls=%async_computation | async-start | bytes 1310720 | tf_op jit(solution)/shard_map/all_to_all | solution.py:357
  27.7 14.8 %collective-permute-start.3 = (bf16[2,64,512]{2,1,0:T(8,128)(2,1)}, bf16[2,64,512]{2,1,0:T(8,128)(2,1)S(1)}, u32[]{:S(2)}, u32[]{:S(2)}) collective-permute-start(bf16[2,64,512]{2,1,0:T(8,128)(2,1)} %get-tuple-element.57), channel_id=1, source_target_pairs={{0,2},{1,3},{2,4},{3,5},{4,6},{5,7},{6,0},{7,1},{8,10},{9,11},{10,... | collective-permute-start | bytes 393224 | tf_op jit(solution)/shard_map/ppermute | solution.py:360
  29.6 13.5 %collective-permute-start.4 = (bf16[2,64,512]{2,1,0:T(8,128)(2,1)}, bf16[2,64,512]{2,1,0:T(8,128)(2,1)S(1)}, u32[]{:S(2)}, u32[]{:S(2)}) collective-permute-start(bf16[2,64,512]{2,1,0:T(8,128)(2,1)} %get-tuple-element.58), channel_id=1, source_target_pairs={{0,4},{1,5},{2,6},{3,7},{4,0},{5,1},{6,2},{7,3},{8,12},{9,13},{10,... | collective-permute-start | bytes 393224 | tf_op jit(solution)/shard_map/ppermute | solution.py:360
  32.3 10.8 %collective-permute-start.5 = (bf16[2,64,512]{2,1,0:T(8,128)(2,1)}, bf16[2,64,512]{2,1,0:T(8,128)(2,1)S(1)}, u32[]{:S(2)}, u32[]{:S(2)}) collective-permute-start(bf16[2,64,512]{2,1,0:T(8,128)(2,1)} %get-tuple-element.59), channel_id=1, source_target_pairs={{0,6},{1,7},{2,0},{3,1},{4,2},{5,3},{6,4},{7,5},{8,14},{9,15},{10,... | collective-permute-start | bytes 393224 | tf_op jit(solution)/shard_map/ppermute | solution.py:360
  42.5 17.1 %copy-start.2 = (bf16[2,2,128,512]{3,2,1,0:T(8,128)(2,1)S(1)}, bf16[2,2,128,512]{3,2,1,0:T(8,128)(2,1)}, u32[]{:S(2)}) copy-start(bf16[2,2,128,512]{3,2,1,0:T(8,128)(2,1)} %get-tuple-element.50.after_ref.keep_a) | copy-start | bytes 1572868
  42.5 17.1 %copy-start.6 = (bf16[2,2,128,512]{3,2,1,0:T(8,128)(2,1)S(1)}, bf16[2,2,128,512]{3,2,1,0:T(8,128)(2,1)}, u32[]{:S(2)}) copy-start(bf16[2,2,128,512]{3,2,1,0:T(8,128)(2,1)} %get-tuple-element.64.keep_b) | copy-start | bytes 1572868
  44.7 16.3 %copy-start.11 = (f32[1,64,512]{2,1,0:T(8,128)S(1)}, f32[1,64,512]{2,1,0:T(8,128)}, u32[]{:S(2)}) copy-start(f32[1,64,512]{2,1,0:T(8,128)} %get-tuple-element.61.refs_1_) | copy-start | bytes 393220
  44.7 13.7 %collective-permute-start.7 = (bf16[2,2,128,512]{3,2,1,0:T(8,128)(2,1)}, bf16[2,2,128,512]{3,2,1,0:T(8,128)(2,1)S(1)}, u32[]{:S(2)}, u32[]{:S(2)}) collective-permute-start(bf16[2,2,128,512]{3,2,1,0:T(8,128)(2,1)} %get-tuple-element.63), channel_id=1, source_target_pairs={{0,2},{1,3},{2,0},{3,1},{4,6},{5,7},{6,4},{7,5},{8,10},{9,11},{10,... | collective-permute-start | bytes 1572872 | tf_op jit(solution)/shard_map/ppermute | solution.py:360
  44.7 14.9 %collective-permute-start.8 = (bf16[2,2,128,512]{3,2,1,0:T(8,128)(2,1)}, bf16[2,2,128,512]{3,2,1,0:T(8,128)(2,1)S(1)}, u32[]{:S(2)}, u32[]{:S(2)}) collective-permute-start(bf16[2,2,128,512]{3,2,1,0:T(8,128)(2,1)} %get-tuple-element.65), channel_id=1, source_target_pairs={{0,6},{1,7},{2,4},{3,5},{4,2},{5,3},{6,0},{7,1},{8,14},{9,15},{10,... | collective-permute-start | bytes 1572872 | tf_op jit(solution)/shard_map/ppermute | solution.py:360
  46.4 14.6 %all-to-all-start.1 = ((bf16[8,32,1152]{2,1,0:T(8,128)(2,1)}), bf16[8,32,1152]{2,1,0:T(8,128)(2,1)S(1)}, u32[]{:S(2)}, u32[]{:S(2)}) async-start(bf16[8,32,1152]{2,1,0:T(8,128)(2,1)} %get-tuple-element.60), calls=%async_computation.1 | async-start | bytes 1179648 | tf_op jit(solution)/shard_map/all_to_all | solution.py:475
  49.9 11.1 %collective-permute-start.6 = (bf16[1,64,512]{2,1,0:T(8,128)(2,1)}, bf16[1,64,512]{2,1,0:T(8,128)(2,1)S(1)}, u32[]{:S(2)}, u32[]{:S(2)}) collective-permute-start(bf16[1,64,512]{2,1,0:T(8,128)(2,1)} %get-tuple-element.62), channel_id=1, source_target_pairs={{0,8},{1,9},{2,10},{3,11},{4,12},{5,13},{6,14},{7,15},{8,0},{9,1},... | collective-permute-start | bytes 196616 | tf_op jit(solution)/shard_map/ppermute | solution.py:360
  62.1 15.1 %all-to-all-start.2 = ((bf16[8,96,512]{2,1,0:T(8,128)(2,1)}), bf16[8,96,512]{2,1,0:T(8,128)(2,1)S(1)}, u32[]{:S(2)}, u32[]{:S(2)}) async-start(bf16[8,96,512]{2,1,0:T(8,128)(2,1)} %get-tuple-element.68), calls=%async_computation.2 | async-start | bytes 1572864 | tf_op jit(solution)/shard_map/all_to_all | solution.py:523
  66.8 6.6 %collective-permute-start.10 = (bf16[2,128,512]{2,1,0:T(8,128)(2,1)}, bf16[2,128,512]{2,1,0:T(8,128)(2,1)S(1)}, u32[]{:S(2)}, u32[]{:S(2)}) collective-permute-start(bf16[2,128,512]{2,1,0:T(8,128)(2,1)} %get-tuple-element.73), channel_id=1, source_target_pairs={{0,2},{1,3},{2,0},{3,1},{4,6},{5,7},{6,4},{7,5},{8,10},{9,11},{10,... | collective-permute-start | bytes 786440 | tf_op jit(solution)/shard_map/ppermute | solution.py:360
  67.4 7.8 %collective-permute-start.9 = (bf16[2,128,512]{2,1,0:T(8,128)(2,1)}, bf16[2,128,512]{2,1,0:T(8,128)(2,1)S(1)}, u32[]{:S(2)}, u32[]{:S(2)}) collective-permute-start(bf16[2,128,512]{2,1,0:T(8,128)(2,1)} %get-tuple-element.71), channel_id=1, source_target_pairs={{0,6},{1,7},{2,4},{3,5},{4,2},{5,3},{6,0},{7,1},{8,14},{9,15},{10,... | collective-permute-start | bytes 786440 | tf_op jit(solution)/shard_map/ppermute | solution.py:360
  77.2 21.2 %copy-start.1 = (f32[2,128,512]{2,1,0:T(8,128)S(1)}, f32[2,128,512]{2,1,0:T(8,128)}, u32[]{:S(2)}) copy-start(f32[2,128,512]{2,1,0:T(8,128)} %get-tuple-element.74.after_ref.keep_ref) | copy-start | bytes 1572868
  79.6 14.5 %all-to-all-start.3 = ((bf16[16,16,512]{2,1,0:T(8,128)(2,1)}), bf16[16,16,512]{2,1,0:T(8,128)(2,1)S(1)}, u32[]{:S(2)}, u32[]{:S(2)}) async-start(bf16[16,16,512]{2,1,0:T(8,128)(2,1)} %get-tuple-element.75), calls=%async_computation.3 | async-start | bytes 524288 | tf_op jit(solution)/shard_map/all_to_all | solution.py:542
  84.7 13.7 %collective-permute-start.11 = (bf16[2,128,512]{2,1,0:T(8,128)(2,1)S(1)}, bf16[2,128,512]{2,1,0:T(8,128)(2,1)S(1)}, u32[]{:S(2)}, u32[]{:S(2)}) collective-permute-start(bf16[2,128,512]{2,1,0:T(8,128)(2,1)S(1)} %copy-done.13), channel_id=1, source_target_pairs={{0,8},{1,9},{2,10},{3,11},{4,12},{5,13},{6,14},{7,15},{8,0},{9,1},... | collective-permute-start | bytes 786440 | tf_op jit(solution)/shard_map/ppermute | solution.py:360
  94.8 12.9 %all-to-all-start.4 = ((bf16[16,16,512]{2,1,0:T(8,128)(2,1)}), bf16[16,16,512]{2,1,0:T(8,128)(2,1)S(1)}, u32[]{:S(2)}, u32[]{:S(2)}) async-start(bf16[16,16,512]{2,1,0:T(8,128)(2,1)} %misfit.1), calls=%async_computation.4 | async-start | bytes 524288 | tf_op jit(solution)/shard_map/all_to_all | solution.py:551
  99.3 24.1 %copy-start.10 = (bf16[256,512]{1,0:T(8,128)(2,1)S(1)}, bf16[256,512]{1,0:T(8,128)(2,1)}, u32[]{:S(2)}) copy-start(bf16[256,512]{1,0:T(8,128)(2,1)} %get-tuple-element.85.hidden_ref) | copy-start | bytes 786436
  108.0 23.8 %copy-start.8 = (bf16[256,512]{1,0:T(8,128)(2,1)S(1)}, bf16[256,512]{1,0:T(8,128)(2,1)}, u32[]{:S(2)}) copy-start(bf16[256,512]{1,0:T(8,128)(2,1)} %get-tuple-element.78.rows_ref) | copy-start | bytes 786436
  119.9 11.9 %all-to-all-start.6 = ((bf16[8,32,1024]{2,1,0:T(8,128)(2,1)}), bf16[8,32,1024]{2,1,0:T(8,128)(2,1)S(1)}, u32[]{:S(2)}, u32[]{:S(2)}) async-start(bf16[8,32,1024]{2,1,0:T(8,128)(2,1)} %acts.1), calls=%async_computation.6 | async-start | bytes 1048576 | tf_op jit(solution)/shard_map/all_to_all | solution.py:578
  (8 other events, 82.8 us)

commit v9 on v8

--- a/solution.py
+++ b/solution.py
@@ -51,21 +51,31 @@
 
 
 def teacher_kernel(
-    core_ref, route_ref, attn_ref, mine_ref, other_ref,
-    keep_ref, send_ref, keep_routed_ref, send_routed_ref, left_ref,
+    core_ref, route_ref, attn_ref, weight_ref,
+    keep_ref, send_ref, keep_routed_ref, send_routed_ref, left_ref, blocks_ref, sems,
 ):
-    tokens = attn_ref.shape[0]
-
-    @pl.when(pl.program_id(0) == 0)
+    step = pl.program_id(0)
+    tokens, wide = attn_ref.shape
+
+    def load(i, first):
+        source = weight_ref.at[:, pl.ds(first, wide)]
+        return pltpu.make_async_copy(source, blocks_ref.at[i], sems.at[i])
+
+    @pl.when(step == 0)
     def _():
+        for i in range(blocks_ref.shape[0]):
+            load(i, i * wide).start()
         left_ref[0:tokens, :] = attn_ref[...]
         left_ref[tokens:, :] = dot(slot_rows(route_ref[...], tokens), attn_ref[...]).astype(BF)
 
-    for weight_ref, out_ref, routed_ref in (
-        (other_ref, send_ref, send_routed_ref),
-        (mine_ref, keep_ref, keep_routed_ref),
+    for i in (2 * step, 2 * step + 1):
+        load(i, pl.multiple_of(i * wide, wide)).wait()
+    core = core_ref[0]
+    for place, out_ref, routed_ref in (
+        (1 - core, send_ref, send_routed_ref),
+        (core, keep_ref, keep_routed_ref),
     ):
-        product = dot(left_ref[...], weight_ref[...]).astype(BF)
+        product = dot(left_ref[...], blocks_ref[2 * step + place]).astype(BF)
         out_ref[0] = product[0:tokens]
         routed_ref[0] = product[tokens:]
 
@@ -326,19 +336,22 @@
             in_specs=[
                 pl.BlockSpec(route_index.shape, lambda j, core: (0, 0)),
                 pl.BlockSpec(attn_values.shape, lambda j, core: (0, 0)),
-                pl.BlockSpec((wide, wide), lambda j, core: (0, 2 * j + core[0])),
-                pl.BlockSpec((wide, wide), lambda j, core: (0, 2 * j + 1 - core[0])),
+                anywhere,
             ],
             out_specs=[pl.BlockSpec((1, tokens, wide), lambda j, core: (j, 0, 0))] * 2
             + [pl.BlockSpec((1, slots, wide), lambda j, core: (j, 0, 0))] * 2,
-            scratch_shapes=[pltpu.VMEM((tokens + slots, wide), BF)],
+            scratch_shapes=[
+                pltpu.VMEM((tokens + slots, wide), BF),
+                pltpu.VMEM((parts, wide, wide), BF),
+                pltpu.SemaphoreType.DMA((parts,)),
+            ],
         ),
         out_shape=[pltpu.HBM((parts // 2, tokens, wide), BF)] * 2
         + [pltpu.HBM((parts // 2, slots, wide), BF)] * 2,
-        compiler_params=params(16),
+        compiler_params=params(20),
         cost_estimate=cost(2 * (tokens + slots) * wide * wide * parts, 14 * MIB),
         name="teacher",
-    )(core.reshape(1), route_index, hbm(attn_values), out_weight, out_weight)
+    )(core.reshape(1), route_index, hbm(attn_values), out_weight)
     copies, send_routed, send = pl.pallas_call(
         copies_kernel,
         in_specs=[vmem] + [anywhere] * 2,

time: 135 us -> 133 us (0.985)
  Pallas kernels: 33.5 us -> 32.1 us
    pallas_call x1, Pallas kernels: 9.12 us -> 7.72 us  [on_device(): pl.pallas_call(teacher_kernel, grid_spec=pltpu.PrefetchScalarGridSpec(num...]
  transfers between devices with their start and end apart: 18 -> 18, of which waited for: 10 -> 10; matrix products, arithmetic and copies ran while one was open for 0% -> 0% of each run, Pallas kernels for 17% -> 16%
where the time goes in v9:
time: 133 us; the launch traced here: 132 us
  starting transfers between devices  51.1 us (38%)
  waiting for transfers between devices  37 us (28%)
  Pallas kernels  32.1 us (24%)
  blocking collectives  11 us (8%)
    ppermute x11, starting transfers between devices, along(): lax.ppermute(value, 'tensor', [(t, move(t // 8, t // 2 % 4, t % 2)) for t...  18 us
    ppermute x11, waiting for transfers between devices, along(): lax.ppermute(value, 'tensor', [(t, move(t // 8, t // 2 % 4, t % 2)) for t...  12.5 us
    all_to_all x1, starting transfers between devices, on_device(): every = lax.all_to_all(copies, 'tensor', 0, 0, tiled=True)  11.3 us
    all_to_all x1, blocking collectives, on_device(): back = lax.all_to_all(back, 'batch', 0, 0, tiled=True)  11 us
    all_to_all x1, waiting for transfers between devices, on_device(): grad_out = lax.all_to_all(grad_out, 'tensor', 0, 0, tiled=True)  8.41 us
    pallas_call x1, Pallas kernels, on_device(): pl.pallas_call(teacher_kernel, grid_spec=pltpu.PrefetchScalarGridSpec(num...  7.72 us
    all_to_all x1, waiting for transfers between devices, on_device(): acts = lax.all_to_all(acts, 'batch', 0, 0, tiled=True)  7.06 us
    all_to_all x1, waiting for transfers between devices, on_device(): misfit = lax.all_to_all(misfit, 'tensor', 0, 0, tiled=True)  5.87 us
  transfers between devices with their start and end apart: 18, of which 10 were waited for; matrix products, arithmetic and copies ran while one was open for 0% of the time, Pallas kernels for 16%

profile of v9, /device:TPU:0, one launch (start us, length us, event | category | flops | bytes accessed | tf_op | source)
XLA Modules:
  0.0 132.1 jit_solution(1522251193403655227)
XLA Ops:
  3.8 7.7 %teacher.1 = (bf16[8,256,512]{2,1,0:T(8,128)(2,1)}, bf16[8,256,512]{2,1,0:T(8,128)(2,1)}, bf16[8,64,512]{2,1,0:T(8,128)(2,1)}, bf16[8,64,512]{2,1,0:T(8,128)(2,1)}) custom-call(s32[1]{0:T(128)} %bitcast.2.core_ref, s32[1,64]{1,0:T(1,128)} %route_ref.5, bf16[256,512]{1,0:T(8,128)(2,1)} %attn_ref.1, bf16[512,8192]{1,0:T(8,128)(2,1)} %weight_ref.1), custom_call_target="tpu_custom_call" | custom-call | flops 2621440 | bytes 14336 | tf_op jit(solution)/shard_map/teacher/pallas_call | solution.py:331
  13.1 11.3 %all-to-all-start = ((bf16[16,40,512]{2,1,0:T(8,128)(2,1)}), bf16[16,40,512]{2,1,0:T(8,128)(2,1)S(1)}, u32[]{:S(2)}, u32[]{:S(2)}) async-start(bf16[16,40,512]{2,1,0:T(8,128)(2,1)} %get-tuple-element.47), calls=%async_computation | async-start | bytes 1310720 | tf_op jit(solution)/shard_map/all_to_all | solution.py:370
  24.5 1.8 %core_sum.1 = (bf16[2,64,512]{2,1,0:T(8,128)(2,1)}, bf16[2,64,512]{2,1,0:T(8,128)(2,1)}, bf16[2,64,512]{2,1,0:T(8,128)(2,1)}, bf16[2,64,512]{2,1,0:T(8,128)(2,1)}) custom-call(s32[1]{0:T(128)} %bitcast.4.x_ref, bf16[8,64,512]{2,1,0:T(8,128)(2,1)} %get-tuple-element.54.refs_0_.refs_1_.refs_2_.refs_3_, ...), custom_call_target="tpu_custom_call" | custom-call | flops 1024 | bytes 1536 | tf_op jit(solution)/shard_map/core_sum/pallas_call | solution.py:379
  26.3 1.9 %collective-permute-start.3 = (bf16[2,64,512]{2,1,0:T(8,128)(2,1)}, bf16[2,64,512]{2,1,0:T(8,128)(2,1)S(1)}, u32[]{:S(2)}, u32[]{:S(2)}) collective-permute-start(bf16[2,64,512]{2,1,0:T(8,128)(2,1)} %get-tuple-element.57), channel_id=1, source_target_pairs={{0,2},{1,3},{2,4},{3,5},{4,6},{5,7},{6,0},{7,1},{8,10},{9,11},{10,... | collective-permute-start | bytes 393224 | tf_op jit(solution)/shard_map/ppermute | solution.py:373
  28.3 2.7 %collective-permute-start.4 = (bf16[2,64,512]{2,1,0:T(8,128)(2,1)}, bf16[2,64,512]{2,1,0:T(8,128)(2,1)S(1)}, u32[]{:S(2)}, u32[]{:S(2)}) collective-permute-start(bf16[2,64,512]{2,1,0:T(8,128)(2,1)} %get-tuple-element.58), channel_id=1, source_target_pairs={{0,4},{1,5},{2,6},{3,7},{4,0},{5,1},{6,2},{7,3},{8,12},{9,13},{10,... | collective-permute-start | bytes 393224 | tf_op jit(solution)/shard_map/ppermute | solution.py:373
  32.4 4.1 %halves.1 = (bf16[2,2,128,512]{3,2,1,0:T(8,128)(2,1)}, bf16[2,2,128,512]{3,2,1,0:T(8,128)(2,1)}, bf16[2,2,128,512]{3,2,1,0:T(8,128)(2,1)}, bf16[2,2,128,512]{3,2,1,0:T(8,128)(2,1)}) custom-call(s32[1]{0:T(128)} %bitcast.4.x_ref, bf16[8,2,128,512]{3,2,1,0:T(8,128)(2,1)} %bitcast.12, bf16[8,2,128,512]{3,2,1,0:T(8,128)(2,1)} %bitcast.13, ...), custom_call_target="tpu_custom_call" | custom-call | flops 1024 | bytes 6144 | tf_op jit(solution)/shard_map/halves/pallas_call | solution.py:416
  36.5 2.1 %all-to-all-done.got_ref = bf16[16,40,512]{2,1,0:T(8,128)(2,1)S(1)} async-done(((bf16[16,40,512]{2,1,0:T(8,128)(2,1)}), bf16[16,40,512]{2,1,0:T(8,128)(2,1)S(1)}, u32[]{:S(2)}, u32[]{:S(2)}) %all-to-all-start) | async-done | bytes 655392 | tf_op jit(solution)/shard_map/all_to_all | solution.py:370
  38.6 2.5 %up.1 = (bf16[8,32,1152]{2,1,0:T(8,128)(2,1)}, bf16[256,512]{1,0:T(8,128)(2,1)}, bf16[256,512]{1,0:T(8,128)(2,1)}) custom-call(s32[1]{0:T(128)} %bitcast.group_ref, bf16[16,40,512]{2,1,0:T(8,128)(2,1)S(1)} %all-to-all-done.got_ref, f32[1,4096]{1,0:T(1,128)S(1)} %bitcast.11, bf16[512,512]{1,0:T(8,128)(2,1)} %gate_ref.1, bf16[512,512]{1,0:T(8,128)(2,1)} %up_ref.1, ...), custom_call_target="tpu_custom_call" | custom-call | flops 819200 | bytes 4096 | tf_op jit(solution)/shard_map/up/pallas_call | solution.py:441
  45.0 3.5 %all-to-all-start.1 = ((bf16[8,32,1152]{2,1,0:T(8,128)(2,1)}), bf16[8,32,1152]{2,1,0:T(8,128)(2,1)S(1)}, u32[]{:S(2)}, u32[]{:S(2)}) async-start(bf16[8,32,1152]{2,1,0:T(8,128)(2,1)} %get-tuple-element.60), calls=%async_computation.1 | async-start | bytes 1179648 | tf_op jit(solution)/shard_map/all_to_all | solution.py:488
  48.5 3.2 %collective-permute-start.6 = (bf16[1,64,512]{2,1,0:T(8,128)(2,1)}, bf16[1,64,512]{2,1,0:T(8,128)(2,1)S(1)}, u32[]{:S(2)}, u32[]{:S(2)}) collective-permute-start(bf16[1,64,512]{2,1,0:T(8,128)(2,1)} %get-tuple-element.62), channel_id=1, source_target_pairs={{0,8},{1,9},{2,10},{3,11},{4,12},{5,13},{6,14},{7,15},{8,0},{9,1},... | collective-permute-start | bytes 196616 | tf_op jit(solution)/shard_map/ppermute | solution.py:373
  51.8 5.2 %collective-permute-done.7.got_a = bf16[2,2,128,512]{3,2,1,0:T(8,128)(2,1)S(1)} collective-permute-done((bf16[2,2,128,512]{3,2,1,0:T(8,128)(2,1)}, bf16[2,2,128,512]{3,2,1,0:T(8,128)(2,1)S(1)}, u32[]{:S(2)}, u32[]{:S(2)}) %collective-permute-start.7) | collective-permute-done | bytes 524320 | tf_op jit(solution)/shard_map/ppermute | solution.py:373
  60.7 4.7 %all-to-all-start.2 = ((bf16[8,96,512]{2,1,0:T(8,128)(2,1)}), bf16[8,96,512]{2,1,0:T(8,128)(2,1)S(1)}, u32[]{:S(2)}, u32[]{:S(2)}) async-start(bf16[8,96,512]{2,1,0:T(8,128)(2,1)} %get-tuple-element.68), calls=%async_computation.2 | async-start | bytes 1572864 | tf_op jit(solution)/shard_map/all_to_all | solution.py:536
  66.0 2.3 %collective-permute-start.9 = (bf16[2,128,512]{2,1,0:T(8,128)(2,1)}, bf16[2,128,512]{2,1,0:T(8,128)(2,1)S(1)}, u32[]{:S(2)}, u32[]{:S(2)}) collective-permute-start(bf16[2,128,512]{2,1,0:T(8,128)(2,1)} %get-tuple-element.71), channel_id=1, source_target_pairs={{0,6},{1,7},{2,4},{3,5},{4,2},{5,3},{6,0},{7,1},{8,14},{9,15},{10,... | collective-permute-start | bytes 786440 | tf_op jit(solution)/shard_map/ppermute | solution.py:373
  68.3 3.6 %collective-permute-done.10.refs_5_.refs_7_ = bf16[2,128,512]{2,1,0:T(8,128)(2,1)S(1)} collective-permute-done((bf16[2,128,512]{2,1,0:T(8,128)(2,1)}, bf16[2,128,512]{2,1,0:T(8,128)(2,1)S(1)}, u32[]{:S(2)}, u32[]{:S(2)}) %collective-permute-start.10) | collective-permute-done | bytes 262176 | tf_op jit(solution)/shard_map/ppermute | solution.py:373
  72.0 1.8 %collective-permute-done.9.refs_1_.refs_3_ = bf16[2,128,512]{2,1,0:T(8,128)(2,1)S(1)} collective-permute-done((bf16[2,128,512]{2,1,0:T(8,128)(2,1)}, bf16[2,128,512]{2,1,0:T(8,128)(2,1)S(1)}, u32[]{:S(2)}, u32[]{:S(2)}) %collective-permute-start.9) | collective-permute-done | bytes 262176 | tf_op jit(solution)/shard_map/ppermute | solution.py:373
  75.8 2.4 %down.1 = (bf16[16,16,512]{2,1,0:T(8,128)(2,1)}, bf16[256,512]{1,0:T(8,128)(2,1)}) custom-call(s32[1]{0:T(128)} %bitcast.group_ref, bf16[8,96,512]{2,1,0:T(8,128)(2,1)S(1)} %all-to-all-done.2.got_ref, bf16[512,512]{1,0:T(8,128)(2,1)S(1)} %copy-done, bf16[256,512]{1,0:T(8,128)(2,1)S(1)} %copy-done.9, bf16[512,4096]{1,0:T(8,128)(2,1)} %projector_ref.1, ...), custom_call_target="tpu_custom_call" | custom-call | flops 786432 | bytes 4096 | tf_op jit(solution)/shard_map/down/pallas_call | solution.py:537
  78.2 5.1 %all-to-all-start.3 = ((bf16[16,16,512]{2,1,0:T(8,128)(2,1)}), bf16[16,16,512]{2,1,0:T(8,128)(2,1)S(1)}, u32[]{:S(2)}, u32[]{:S(2)}) async-start(bf16[16,16,512]{2,1,0:T(8,128)(2,1)} %get-tuple-element.75), calls=%async_computation.3 | async-start | bytes 524288 | tf_op jit(solution)/shard_map/all_to_all | solution.py:555
  83.3 3.5 %collective-permute-start.11 = (bf16[2,128,512]{2,1,0:T(8,128)(2,1)S(1)}, bf16[2,128,512]{2,1,0:T(8,128)(2,1)S(1)}, u32[]{:S(2)}, u32[]{:S(2)}) collective-permute-start(bf16[2,128,512]{2,1,0:T(8,128)(2,1)S(1)} %copy-done.13), channel_id=1, source_target_pairs={{0,8},{1,9},{2,10},{3,11},{4,12},{5,13},{6,14},{7,15},{8,0},{9,1},... | collective-permute-start | bytes 786440 | tf_op jit(solution)/shard_map/ppermute | solution.py:373
  86.8 5.9 %all-to-all-done.3.refs_0_ = bf16[16,16,512]{2,1,0:T(8,128)(2,1)S(1)} async-done(((bf16[16,16,512]{2,1,0:T(8,128)(2,1)}), bf16[16,16,512]{2,1,0:T(8,128)(2,1)S(1)}, u32[]{:S(2)}, u32[]{:S(2)}) %all-to-all-start.3) | async-done | bytes 262176 | tf_op jit(solution)/shard_map/all_to_all | solution.py:555
  93.5 3.5 %all-to-all-start.4 = ((bf16[16,16,512]{2,1,0:T(8,128)(2,1)}), bf16[16,16,512]{2,1,0:T(8,128)(2,1)S(1)}, u32[]{:S(2)}, u32[]{:S(2)}) async-start(bf16[16,16,512]{2,1,0:T(8,128)(2,1)} %misfit.1), calls=%async_computation.4 | async-start | bytes 524288 | tf_op jit(solution)/shard_map/all_to_all | solution.py:564
  97.9 8.4 %all-to-all-done.4.got_ref.grad_ref = bf16[16,16,512]{2,1,0:T(8,128)(2,1)S(1)} async-done(((bf16[16,16,512]{2,1,0:T(8,128)(2,1)}), bf16[16,16,512]{2,1,0:T(8,128)(2,1)S(1)}, u32[]{:S(2)}, u32[]{:S(2)}) %all-to-all-start.4) | async-done | bytes 262176 | tf_op jit(solution)/shard_map/all_to_all | solution.py:564
  106.7 11.0 %all_to_all.35.got_ref = bf16[8,32,512]{2,1,0:T(8,128)(2,1)S(1)} all-to-all(bf16[8,32,512]{2,1,0:T(8,128)(2,1)S(1)} %get-tuple-element.79), channel_id=1, replica_groups=mesh['batch'=8,'tensor'=16] {'batch'}, dimensions={0} | all-to-all | bytes 524288 | tf_op jit(solution)/shard_map/all_to_all | solution.py:583
  118.6 3.5 %all-to-all-start.6 = ((bf16[8,32,1024]{2,1,0:T(8,128)(2,1)}), bf16[8,32,1024]{2,1,0:T(8,128)(2,1)S(1)}, u32[]{:S(2)}, u32[]{:S(2)}) async-start(bf16[8,32,1024]{2,1,0:T(8,128)(2,1)} %acts.1), calls=%async_computation.6 | async-start | bytes 1048576 | tf_op jit(solution)/shard_map/all_to_all | solution.py:591
  123.4 7.1 %all-to-all-done.6.got_ref = bf16[8,32,1024]{2,1,0:T(8,128)(2,1)S(1)} async-done(((bf16[8,32,1024]{2,1,0:T(8,128)(2,1)}), bf16[8,32,1024]{2,1,0:T(8,128)(2,1)S(1)}, u32[]{:S(2)}, u32[]{:S(2)}) %all-to-all-start.6) | async-done | bytes 524320 | tf_op jit(solution)/shard_map/all_to_all | solution.py:591
  (58 shorter events, 22.3 us)
Async XLA Ops:
  2.4 9.2 %collective-permute-start = (bf16[40,512]{1,0:T(8,128)(2,1)}, bf16[40,512]{1,0:T(8,128)(2,1)S(1)}, u32[]{:S(2)}, u32[]{:S(2)}) collective-permute-start(bf16[40,512]{1,0:T(8,128)(2,1)} %rows.1), channel_id=1, source_target_pairs={{0,0},{1,1},{2,16},{3,17},{4,32},{5,33},{6,48},{7,49},{8,64},{9,65... | collective-permute-start | bytes 122888 | tf_op jit(solution)/shard_map/ppermute | solution.py:329
  12.5 19.9 %collective-permute-start.1 = (bf16[8,256,512]{2,1,0:T(8,128)(2,1)}, bf16[8,256,512]{2,1,0:T(8,128)(2,1)S(1)}, u32[]{:S(2)}, u32[]{:S(2)}) collective-permute-start(bf16[8,256,512]{2,1,0:T(8,128)(2,1)} %get-tuple-element.49), channel_id=1, source_target_pairs={{0,1},{1,0},{2,3},{3,2},{4,5},{5,4},{6,7},{7,6},{8,9},{9,8},{10,11... | collective-permute-start | bytes 6291464 | tf_op jit(solution)/shard_map/ppermute | solution.py:373
  12.6 11.9 %collective-permute-start.2 = (bf16[8,64,512]{2,1,0:T(8,128)(2,1)}, bf16[8,64,512]{2,1,0:T(8,128)(2,1)S(1)}, u32[]{:S(2)}, u32[]{:S(2)}) collective-permute-start(bf16[8,64,512]{2,1,0:T(8,128)(2,1)} %get-tuple-element.55), channel_id=1, source_target_pairs={{0,1},{1,0},{2,3},{3,2},{4,5},{5,4},{6,7},{7,6},{8,9},{9,8},{10,11... | collective-permute-start | bytes 1572872 | tf_op jit(solution)/shard_map/ppermute | solution.py:373
  13.1 25.5 %all-to-all-start = ((bf16[16,40,512]{2,1,0:T(8,128)(2,1)}), bf16[16,40,512]{2,1,0:T(8,128)(2,1)S(1)}, u32[]{:S(2)}, u32[]{:S(2)}) async-start(bf16[16,40,512]{2,1,0:T(8,128)(2,1)} %get-tuple-element.47), calls=%async_computation | async-start | bytes 1310720 | tf_op jit(solution)/shard_map/all_to_all | solution.py:370
  26.3 14.8 %collective-permute-start.3 = (bf16[2,64,512]{2,1,0:T(8,128)(2,1)}, bf16[2,64,512]{2,1,0:T(8,128)(2,1)S(1)}, u32[]{:S(2)}, u32[]{:S(2)}) collective-permute-start(bf16[2,64,512]{2,1,0:T(8,128)(2,1)} %get-tuple-element.57), channel_id=1, source_target_pairs={{0,2},{1,3},{2,4},{3,5},{4,6},{5,7},{6,0},{7,1},{8,10},{9,11},{10,... | collective-permute-start | bytes 393224 | tf_op jit(solution)/shard_map/ppermute | solution.py:373
  28.3 13.5 %collective-permute-start.4 = (bf16[2,64,512]{2,1,0:T(8,128)(2,1)}, bf16[2,64,512]{2,1,0:T(8,128)(2,1)S(1)}, u32[]{:S(2)}, u32[]{:S(2)}) collective-permute-start(bf16[2,64,512]{2,1,0:T(8,128)(2,1)} %get-tuple-element.58), channel_id=1, source_target_pairs={{0,4},{1,5},{2,6},{3,7},{4,0},{5,1},{6,2},{7,3},{8,12},{9,13},{10,... | collective-permute-start | bytes 393224 | tf_op jit(solution)/shard_map/ppermute | solution.py:373
  30.9 10.8 %collective-permute-start.5 = (bf16[2,64,512]{2,1,0:T(8,128)(2,1)}, bf16[2,64,512]{2,1,0:T(8,128)(2,1)S(1)}, u32[]{:S(2)}, u32[]{:S(2)}) collective-permute-start(bf16[2,64,512]{2,1,0:T(8,128)(2,1)} %get-tuple-element.59), channel_id=1, source_target_pairs={{0,6},{1,7},{2,0},{3,1},{4,2},{5,3},{6,4},{7,5},{8,14},{9,15},{10,... | collective-permute-start | bytes 393224 | tf_op jit(solution)/shard_map/ppermute | solution.py:373
  41.1 17.1 %copy-start.2 = (bf16[2,2,128,512]{3,2,1,0:T(8,128)(2,1)S(1)}, bf16[2,2,128,512]{3,2,1,0:T(8,128)(2,1)}, u32[]{:S(2)}) copy-start(bf16[2,2,128,512]{3,2,1,0:T(8,128)(2,1)} %get-tuple-element.50.after_ref.keep_a) | copy-start | bytes 1572868
  41.1 17.1 %copy-start.6 = (bf16[2,2,128,512]{3,2,1,0:T(8,128)(2,1)S(1)}, bf16[2,2,128,512]{3,2,1,0:T(8,128)(2,1)}, u32[]{:S(2)}) copy-start(bf16[2,2,128,512]{3,2,1,0:T(8,128)(2,1)} %get-tuple-element.64.keep_b) | copy-start | bytes 1572868
  43.3 16.3 %copy-start.11 = (f32[1,64,512]{2,1,0:T(8,128)S(1)}, f32[1,64,512]{2,1,0:T(8,128)}, u32[]{:S(2)}) copy-start(f32[1,64,512]{2,1,0:T(8,128)} %get-tuple-element.61.refs_1_) | copy-start | bytes 393220
  43.3 13.7 %collective-permute-start.7 = (bf16[2,2,128,512]{3,2,1,0:T(8,128)(2,1)}, bf16[2,2,128,512]{3,2,1,0:T(8,128)(2,1)S(1)}, u32[]{:S(2)}, u32[]{:S(2)}) collective-permute-start(bf16[2,2,128,512]{3,2,1,0:T(8,128)(2,1)} %get-tuple-element.63), channel_id=1, source_target_pairs={{0,2},{1,3},{2,0},{3,1},{4,6},{5,7},{6,4},{7,5},{8,10},{9,11},{10,... | collective-permute-start | bytes 1572872 | tf_op jit(solution)/shard_map/ppermute | solution.py:373
  43.3 14.9 %collective-permute-start.8 = (bf16[2,2,128,512]{3,2,1,0:T(8,128)(2,1)}, bf16[2,2,128,512]{3,2,1,0:T(8,128)(2,1)S(1)}, u32[]{:S(2)}, u32[]{:S(2)}) collective-permute-start(bf16[2,2,128,512]{3,2,1,0:T(8,128)(2,1)} %get-tuple-element.65), channel_id=1, source_target_pairs={{0,6},{1,7},{2,4},{3,5},{4,2},{5,3},{6,0},{7,1},{8,14},{9,15},{10,... | collective-permute-start | bytes 1572872 | tf_op jit(solution)/shard_map/ppermute | solution.py:373
  45.0 14.6 %all-to-all-start.1 = ((bf16[8,32,1152]{2,1,0:T(8,128)(2,1)}), bf16[8,32,1152]{2,1,0:T(8,128)(2,1)S(1)}, u32[]{:S(2)}, u32[]{:S(2)}) async-start(bf16[8,32,1152]{2,1,0:T(8,128)(2,1)} %get-tuple-element.60), calls=%async_computation.1 | async-start | bytes 1179648 | tf_op jit(solution)/shard_map/all_to_all | solution.py:488
  48.5 11.1 %collective-permute-start.6 = (bf16[1,64,512]{2,1,0:T(8,128)(2,1)}, bf16[1,64,512]{2,1,0:T(8,128)(2,1)S(1)}, u32[]{:S(2)}, u32[]{:S(2)}) collective-permute-start(bf16[1,64,512]{2,1,0:T(8,128)(2,1)} %get-tuple-element.62), channel_id=1, source_target_pairs={{0,8},{1,9},{2,10},{3,11},{4,12},{5,13},{6,14},{7,15},{8,0},{9,1},... | collective-permute-start | bytes 196616 | tf_op jit(solution)/shard_map/ppermute | solution.py:373
  60.7 15.1 %all-to-all-start.2 = ((bf16[8,96,512]{2,1,0:T(8,128)(2,1)}), bf16[8,96,512]{2,1,0:T(8,128)(2,1)S(1)}, u32[]{:S(2)}, u32[]{:S(2)}) async-start(bf16[8,96,512]{2,1,0:T(8,128)(2,1)} %get-tuple-element.68), calls=%async_computation.2 | async-start | bytes 1572864 | tf_op jit(solution)/shard_map/all_to_all | solution.py:536
  65.4 6.6 %collective-permute-start.10 = (bf16[2,128,512]{2,1,0:T(8,128)(2,1)}, bf16[2,128,512]{2,1,0:T(8,128)(2,1)S(1)}, u32[]{:S(2)}, u32[]{:S(2)}) collective-permute-start(bf16[2,128,512]{2,1,0:T(8,128)(2,1)} %get-tuple-element.73), channel_id=1, source_target_pairs={{0,2},{1,3},{2,0},{3,1},{4,6},{5,7},{6,4},{7,5},{8,10},{9,11},{10,... | collective-permute-start | bytes 786440 | tf_op jit(solution)/shard_map/ppermute | solution.py:373
  66.0 7.8 %collective-permute-start.9 = (bf16[2,128,512]{2,1,0:T(8,128)(2,1)}, bf16[2,128,512]{2,1,0:T(8,128)(2,1)S(1)}, u32[]{:S(2)}, u32[]{:S(2)}) collective-permute-start(bf16[2,128,512]{2,1,0:T(8,128)(2,1)} %get-tuple-element.71), channel_id=1, source_target_pairs={{0,6},{1,7},{2,4},{3,5},{4,2},{5,3},{6,0},{7,1},{8,14},{9,15},{10,... | collective-permute-start | bytes 786440 | tf_op jit(solution)/shard_map/ppermute | solution.py:373
  75.8 21.2 %copy-start.1 = (f32[2,128,512]{2,1,0:T(8,128)S(1)}, f32[2,128,512]{2,1,0:T(8,128)}, u32[]{:S(2)}) copy-start(f32[2,128,512]{2,1,0:T(8,128)} %get-tuple-element.74.after_ref.keep_ref) | copy-start | bytes 1572868
  78.2 14.4 %all-to-all-start.3 = ((bf16[16,16,512]{2,1,0:T(8,128)(2,1)}), bf16[16,16,512]{2,1,0:T(8,128)(2,1)S(1)}, u32[]{:S(2)}, u32[]{:S(2)}) async-start(bf16[16,16,512]{2,1,0:T(8,128)(2,1)} %get-tuple-element.75), calls=%async_computation.3 | async-start | bytes 524288 | tf_op jit(solution)/shard_map/all_to_all | solution.py:555
  83.3 13.7 %collective-permute-start.11 = (bf16[2,128,512]{2,1,0:T(8,128)(2,1)S(1)}, bf16[2,128,512]{2,1,0:T(8,128)(2,1)S(1)}, u32[]{:S(2)}, u32[]{:S(2)}) collective-permute-start(bf16[2,128,512]{2,1,0:T(8,128)(2,1)S(1)} %copy-done.13), channel_id=1, source_target_pairs={{0,8},{1,9},{2,10},{3,11},{4,12},{5,13},{6,14},{7,15},{8,0},{9,1},... | collective-permute-start | bytes 786440 | tf_op jit(solution)/shard_map/ppermute | solution.py:373
  93.5 12.9 %all-to-all-start.4 = ((bf16[16,16,512]{2,1,0:T(8,128)(2,1)}), bf16[16,16,512]{2,1,0:T(8,128)(2,1)S(1)}, u32[]{:S(2)}, u32[]{:S(2)}) async-start(bf16[16,16,512]{2,1,0:T(8,128)(2,1)} %misfit.1), calls=%async_computation.4 | async-start | bytes 524288 | tf_op jit(solution)/shard_map/all_to_all | solution.py:564
  97.9 24.1 %copy-start.10 = (bf16[256,512]{1,0:T(8,128)(2,1)S(1)}, bf16[256,512]{1,0:T(8,128)(2,1)}, u32[]{:S(2)}) copy-start(bf16[256,512]{1,0:T(8,128)(2,1)} %get-tuple-element.85.hidden_ref) | copy-start | bytes 786436
  106.6 23.8 %copy-start.8 = (bf16[256,512]{1,0:T(8,128)(2,1)S(1)}, bf16[256,512]{1,0:T(8,128)(2,1)}, u32[]{:S(2)}) copy-start(bf16[256,512]{1,0:T(8,128)(2,1)} %get-tuple-element.78.rows_ref) | copy-start | bytes 786436
  118.6 11.9 %all-to-all-start.6 = ((bf16[8,32,1024]{2,1,0:T(8,128)(2,1)}), bf16[8,32,1024]{2,1,0:T(8,128)(2,1)S(1)}, u32[]{:S(2)}, u32[]{:S(2)}) async-start(bf16[8,32,1024]{2,1,0:T(8,128)(2,1)} %acts.1), calls=%async_computation.6 | async-start | bytes 1048576 | tf_op jit(solution)/shard_map/all_to_all | solution.py:591
  (8 other events, 82.7 us)

commit v10 on v9

--- a/solution.py
+++ b/solution.py
@@ -56,6 +56,7 @@
 ):
     step = pl.program_id(0)
     tokens, wide = attn_ref.shape
+    parts = blocks_ref.shape[0]
 
     def load(i, first):
         source = weight_ref.at[:, pl.ds(first, wide)]
@@ -63,10 +64,14 @@
 
     @pl.when(step == 0)
     def _():
-        for i in range(blocks_ref.shape[0]):
+        rows = left_ref.at[0:tokens, :]
+        acts = pltpu.make_async_copy(attn_ref, rows, sems.at[parts])
+        acts.start()
+        for i in range(parts):
             load(i, i * wide).start()
-        left_ref[0:tokens, :] = attn_ref[...]
-        left_ref[tokens:, :] = dot(slot_rows(route_ref[...], tokens), attn_ref[...]).astype(BF)
+        hot = slot_rows(route_ref[...], tokens)
+        acts.wait()
+        left_ref[tokens:, :] = dot(hot, left_ref[0:tokens, :]).astype(BF)
 
     for i in (2 * step, 2 * step + 1):
         load(i, pl.multiple_of(i * wide, wide)).wait()
@@ -225,8 +230,12 @@
 
 def down_kernel(
     group_ref, got_ref, down_ref, chosen_ref, projector_ref, after_ref,
-    out_ref, hidden_ref, rows_ref,
+    out_ref, hidden_ref, rows_ref, block_ref, sem,
 ):
+    wide = block_ref.shape[1]
+    first = pl.multiple_of(group_ref[0] * wide, wide)
+    load = pltpu.make_async_copy(projector_ref.at[:, pl.ds(first, wide)], block_ref, sem)
+    load.start()
     groups = got_ref.shape[0]
     per = hidden_ref.shape[0] // groups
     slots = got_ref.shape[1] - per
@@ -234,7 +243,9 @@
         hidden_ref[g * per : (g + 1) * per, :] = got_ref[g, 0:per, :]
         rows_ref[g * slots : (g + 1) * slots, :] = got_ref[g, per:, :]
     rows = dot(chosen_ref[...], rows_ref[...]).astype(BF)
-    part = dot(hidden_ref[...], down_ref[...], 1, 1) - dot(rows, projector_ref[...])
+    part = dot(hidden_ref[...], down_ref[...], 1, 1)
+    load.wait()
+    part = part - dot(rows, block_ref[...])
     out_ref[...] = part.astype(BF).reshape(out_ref.shape)
 
 
@@ -335,7 +346,7 @@
             grid=(parts // 2,),
             in_specs=[
                 pl.BlockSpec(route_index.shape, lambda j, core: (0, 0)),
-                pl.BlockSpec(attn_values.shape, lambda j, core: (0, 0)),
+                anywhere,
                 anywhere,
             ],
             out_specs=[pl.BlockSpec((1, tokens, wide), lambda j, core: (j, 0, 0))] * 2
@@ -343,7 +354,7 @@
             scratch_shapes=[
                 pltpu.VMEM((tokens + slots, wide), BF),
                 pltpu.VMEM((parts, wide, wide), BF),
-                pltpu.SemaphoreType.DMA((parts,)),
+                pltpu.SemaphoreType.DMA((parts + 1,)),
             ],
         ),
         out_shape=[pltpu.HBM((parts // 2, tokens, wide), BF)] * 2
@@ -539,10 +550,13 @@
         grid_spec=pltpu.PrefetchScalarGridSpec(
             num_scalar_prefetch=1,
             grid=(1,),
-            in_specs=[vmem] * 3
-            + [pl.BlockSpec((wide, wide), lambda i, group: (0, group[0])), anywhere],
+            in_specs=[vmem] * 3 + [anywhere] * 2,
             out_specs=[vmem] * 2,
-            scratch_shapes=[pltpu.VMEM((groups * slots, wide), BF)],
+            scratch_shapes=[
+                pltpu.VMEM((groups * slots, wide), BF),
+                pltpu.VMEM((wide, wide), BF),
+                pltpu.SemaphoreType.DMA,
+            ],
         ),
         out_shape=[
             pltpu.HBM((parts, live // parts, wide), BF),

time: 133 us -> 133 us (level)
  no operation moved by 1% of the time
where the time goes in v10:
time: 133 us; the launch traced here: 132 us
  starting transfers between devices  51.1 us (38%)
  waiting for transfers between devices  37 us (28%)
  Pallas kernels  31.7 us (24%)
  blocking collectives  11 us (8%)
    ppermute x11, starting transfers between devices, along(): lax.ppermute(value, 'tensor', [(t, move(t // 8, t // 2 % 4, t % 2)) for t...  18 us
    ppermute x11, waiting for transfers between devices, along(): lax.ppermute(value, 'tensor', [(t, move(t // 8, t // 2 % 4, t % 2)) for t...  12.5 us
    all_to_all x1, starting transfers between devices, on_device(): every = lax.all_to_all(copies, 'tensor', 0, 0, tiled=True)  11.3 us
    all_to_all x1, blocking collectives, on_device(): back = lax.all_to_all(back, 'batch', 0, 0, tiled=True)  11 us
    all_to_all x1, waiting for transfers between devices, on_device(): grad_out = lax.all_to_all(grad_out, 'tensor', 0, 0, tiled=True)  8.41 us
    pallas_call x1, Pallas kernels, on_device(): pl.pallas_call(teacher_kernel, grid_spec=pltpu.PrefetchScalarGridSpec(num...  7.49 us
    all_to_all x1, waiting for transfers between devices, on_device(): acts = lax.all_to_all(acts, 'batch', 0, 0, tiled=True)  7.06 us
    all_to_all x1, waiting for transfers between devices, on_device(): misfit = lax.all_to_all(misfit, 'tensor', 0, 0, tiled=True)  5.87 us
  transfers between devices with their start and end apart: 18, of which 10 were waited for; matrix products, arithmetic and copies ran while one was open for 0% of the time, Pallas kernels for 16%

profile of v10, /device:TPU:0, one launch (start us, length us, event | category | flops | bytes accessed | tf_op | source)
XLA Modules:
  0.0 131.7 jit_solution(8771667446018678257)
XLA Ops:
  3.8 7.5 %teacher.1 = (bf16[8,256,512]{2,1,0:T(8,128)(2,1)}, bf16[8,256,512]{2,1,0:T(8,128)(2,1)}, bf16[8,64,512]{2,1,0:T(8,128)(2,1)}, bf16[8,64,512]{2,1,0:T(8,128)(2,1)}) custom-call(s32[1]{0:T(128)} %bitcast.2.core_ref, s32[1,64]{1,0:T(1,128)} %route_ref.5, bf16[256,512]{1,0:T(8,128)(2,1)} %attn_ref.1, bf16[512,8192]{1,0:T(8,128)(2,1)} %weight_ref.1), custom_call_target="tpu_custom_call" | custom-call | flops 2621440 | bytes 14336 | tf_op jit(solution)/shard_map/teacher/pallas_call | solution.py:342
  12.9 11.3 %all-to-all-start = ((bf16[16,40,512]{2,1,0:T(8,128)(2,1)}), bf16[16,40,512]{2,1,0:T(8,128)(2,1)S(1)}, u32[]{:S(2)}, u32[]{:S(2)}) async-start(bf16[16,40,512]{2,1,0:T(8,128)(2,1)} %get-tuple-element.47), calls=%async_computation | async-start | bytes 1310720 | tf_op jit(solution)/shard_map/all_to_all | solution.py:381
  24.2 1.8 %core_sum.1 = (bf16[2,64,512]{2,1,0:T(8,128)(2,1)}, bf16[2,64,512]{2,1,0:T(8,128)(2,1)}, bf16[2,64,512]{2,1,0:T(8,128)(2,1)}, bf16[2,64,512]{2,1,0:T(8,128)(2,1)}) custom-call(s32[1]{0:T(128)} %bitcast.4.x_ref, bf16[8,64,512]{2,1,0:T(8,128)(2,1)} %get-tuple-element.54.refs_0_.refs_1_.refs_2_.refs_3_, ...), custom_call_target="tpu_custom_call" | custom-call | flops 1024 | bytes 1536 | tf_op jit(solution)/shard_map/core_sum/pallas_call | solution.py:390
  26.1 1.9 %collective-permute-start.3 = (bf16[2,64,512]{2,1,0:T(8,128)(2,1)}, bf16[2,64,512]{2,1,0:T(8,128)(2,1)S(1)}, u32[]{:S(2)}, u32[]{:S(2)}) collective-permute-start(bf16[2,64,512]{2,1,0:T(8,128)(2,1)} %get-tuple-element.57), channel_id=1, source_target_pairs={{0,2},{1,3},{2,4},{3,5},{4,6},{5,7},{6,0},{7,1},{8,10},{9,11},{10,... | collective-permute-start | bytes 393224 | tf_op jit(solution)/shard_map/ppermute | solution.py:384
  28.0 2.7 %collective-permute-start.4 = (bf16[2,64,512]{2,1,0:T(8,128)(2,1)}, bf16[2,64,512]{2,1,0:T(8,128)(2,1)S(1)}, u32[]{:S(2)}, u32[]{:S(2)}) collective-permute-start(bf16[2,64,512]{2,1,0:T(8,128)(2,1)} %get-tuple-element.58), channel_id=1, source_target_pairs={{0,4},{1,5},{2,6},{3,7},{4,0},{5,1},{6,2},{7,3},{8,12},{9,13},{10,... | collective-permute-start | bytes 393224 | tf_op jit(solution)/shard_map/ppermute | solution.py:384
  32.2 4.1 %halves.1 = (bf16[2,2,128,512]{3,2,1,0:T(8,128)(2,1)}, bf16[2,2,128,512]{3,2,1,0:T(8,128)(2,1)}, bf16[2,2,128,512]{3,2,1,0:T(8,128)(2,1)}, bf16[2,2,128,512]{3,2,1,0:T(8,128)(2,1)}) custom-call(s32[1]{0:T(128)} %bitcast.4.x_ref, bf16[8,2,128,512]{3,2,1,0:T(8,128)(2,1)} %bitcast.12, bf16[8,2,128,512]{3,2,1,0:T(8,128)(2,1)} %bitcast.13, ...), custom_call_target="tpu_custom_call" | custom-call | flops 1024 | bytes 6144 | tf_op jit(solution)/shard_map/halves/pallas_call | solution.py:427
  36.2 2.1 %all-to-all-done.got_ref = bf16[16,40,512]{2,1,0:T(8,128)(2,1)S(1)} async-done(((bf16[16,40,512]{2,1,0:T(8,128)(2,1)}), bf16[16,40,512]{2,1,0:T(8,128)(2,1)S(1)}, u32[]{:S(2)}, u32[]{:S(2)}) %all-to-all-start) | async-done | bytes 655392 | tf_op jit(solution)/shard_map/all_to_all | solution.py:381
  38.3 2.5 %up.1 = (bf16[8,32,1152]{2,1,0:T(8,128)(2,1)}, bf16[256,512]{1,0:T(8,128)(2,1)}, bf16[256,512]{1,0:T(8,128)(2,1)}) custom-call(s32[1]{0:T(128)} %bitcast.group_ref, bf16[16,40,512]{2,1,0:T(8,128)(2,1)S(1)} %all-to-all-done.got_ref, f32[1,4096]{1,0:T(1,128)S(1)} %bitcast.11, bf16[512,512]{1,0:T(8,128)(2,1)} %gate_ref.1, bf16[512,512]{1,0:T(8,128)(2,1)} %up_ref.1, ...), custom_call_target="tpu_custom_call" | custom-call | flops 819200 | bytes 4096 | tf_op jit(solution)/shard_map/up/pallas_call | solution.py:452
  44.8 3.5 %all-to-all-start.1 = ((bf16[8,32,1152]{2,1,0:T(8,128)(2,1)}), bf16[8,32,1152]{2,1,0:T(8,128)(2,1)S(1)}, u32[]{:S(2)}, u32[]{:S(2)}) async-start(bf16[8,32,1152]{2,1,0:T(8,128)(2,1)} %get-tuple-element.60), calls=%async_computation.1 | async-start | bytes 1179648 | tf_op jit(solution)/shard_map/all_to_all | solution.py:499
  48.3 3.2 %collective-permute-start.6 = (bf16[1,64,512]{2,1,0:T(8,128)(2,1)}, bf16[1,64,512]{2,1,0:T(8,128)(2,1)S(1)}, u32[]{:S(2)}, u32[]{:S(2)}) collective-permute-start(bf16[1,64,512]{2,1,0:T(8,128)(2,1)} %get-tuple-element.62), channel_id=1, source_target_pairs={{0,8},{1,9},{2,10},{3,11},{4,12},{5,13},{6,14},{7,15},{8,0},{9,1},... | collective-permute-start | bytes 196616 | tf_op jit(solution)/shard_map/ppermute | solution.py:384
  51.5 5.2 %collective-permute-done.7.got_a = bf16[2,2,128,512]{3,2,1,0:T(8,128)(2,1)S(1)} collective-permute-done((bf16[2,2,128,512]{3,2,1,0:T(8,128)(2,1)}, bf16[2,2,128,512]{3,2,1,0:T(8,128)(2,1)S(1)}, u32[]{:S(2)}, u32[]{:S(2)}) %collective-permute-start.7) | collective-permute-done | bytes 524320 | tf_op jit(solution)/shard_map/ppermute | solution.py:384
  60.5 4.7 %all-to-all-start.2 = ((bf16[8,96,512]{2,1,0:T(8,128)(2,1)}), bf16[8,96,512]{2,1,0:T(8,128)(2,1)S(1)}, u32[]{:S(2)}, u32[]{:S(2)}) async-start(bf16[8,96,512]{2,1,0:T(8,128)(2,1)} %get-tuple-element.68), calls=%async_computation.2 | async-start | bytes 1572864 | tf_op jit(solution)/shard_map/all_to_all | solution.py:547
  65.7 2.3 %collective-permute-start.9 = (bf16[2,128,512]{2,1,0:T(8,128)(2,1)}, bf16[2,128,512]{2,1,0:T(8,128)(2,1)S(1)}, u32[]{:S(2)}, u32[]{:S(2)}) collective-permute-start(bf16[2,128,512]{2,1,0:T(8,128)(2,1)} %get-tuple-element.71), channel_id=1, source_target_pairs={{0,6},{1,7},{2,4},{3,5},{4,2},{5,3},{6,0},{7,1},{8,14},{9,15},{10,... | collective-permute-start | bytes 786440 | tf_op jit(solution)/shard_map/ppermute | solution.py:384
  68.1 3.6 %collective-permute-done.10.refs_5_.refs_7_ = bf16[2,128,512]{2,1,0:T(8,128)(2,1)S(1)} collective-permute-done((bf16[2,128,512]{2,1,0:T(8,128)(2,1)}, bf16[2,128,512]{2,1,0:T(8,128)(2,1)S(1)}, u32[]{:S(2)}, u32[]{:S(2)}) %collective-permute-start.10) | collective-permute-done | bytes 262176 | tf_op jit(solution)/shard_map/ppermute | solution.py:384
  71.7 1.8 %collective-permute-done.9.refs_1_.refs_3_ = bf16[2,128,512]{2,1,0:T(8,128)(2,1)S(1)} collective-permute-done((bf16[2,128,512]{2,1,0:T(8,128)(2,1)}, bf16[2,128,512]{2,1,0:T(8,128)(2,1)S(1)}, u32[]{:S(2)}, u32[]{:S(2)}) %collective-permute-start.9) | collective-permute-done | bytes 262176 | tf_op jit(solution)/shard_map/ppermute | solution.py:384
  75.6 2.3 %down.1 = (bf16[16,16,512]{2,1,0:T(8,128)(2,1)}, bf16[256,512]{1,0:T(8,128)(2,1)}) custom-call(s32[1]{0:T(128)} %bitcast.group_ref, bf16[8,96,512]{2,1,0:T(8,128)(2,1)S(1)} %all-to-all-done.2.got_ref, bf16[512,512]{1,0:T(8,128)(2,1)S(1)} %copy-done, bf16[256,512]{1,0:T(8,128)(2,1)S(1)} %copy-done.9, bf16[512,4096]{1,0:T(8,128)(2,1)} %projector_ref.1, ...), custom_call_target="tpu_custom_call" | custom-call | flops 786432 | bytes 4096 | tf_op jit(solution)/shard_map/down/pallas_call | solution.py:548
  77.9 5.0 %all-to-all-start.3 = ((bf16[16,16,512]{2,1,0:T(8,128)(2,1)}), bf16[16,16,512]{2,1,0:T(8,128)(2,1)S(1)}, u32[]{:S(2)}, u32[]{:S(2)}) async-start(bf16[16,16,512]{2,1,0:T(8,128)(2,1)} %get-tuple-element.75), calls=%async_computation.3 | async-start | bytes 524288 | tf_op jit(solution)/shard_map/all_to_all | solution.py:569
  83.0 3.5 %collective-permute-start.11 = (bf16[2,128,512]{2,1,0:T(8,128)(2,1)S(1)}, bf16[2,128,512]{2,1,0:T(8,128)(2,1)S(1)}, u32[]{:S(2)}, u32[]{:S(2)}) collective-permute-start(bf16[2,128,512]{2,1,0:T(8,128)(2,1)S(1)} %copy-done.13), channel_id=1, source_target_pairs={{0,8},{1,9},{2,10},{3,11},{4,12},{5,13},{6,14},{7,15},{8,0},{9,1},... | collective-permute-start | bytes 786440 | tf_op jit(solution)/shard_map/ppermute | solution.py:384
  86.5 5.9 %all-to-all-done.3.refs_0_ = bf16[16,16,512]{2,1,0:T(8,128)(2,1)S(1)} async-done(((bf16[16,16,512]{2,1,0:T(8,128)(2,1)}), bf16[16,16,512]{2,1,0:T(8,128)(2,1)S(1)}, u32[]{:S(2)}, u32[]{:S(2)}) %all-to-all-start.3) | async-done | bytes 262176 | tf_op jit(solution)/shard_map/all_to_all | solution.py:569
  93.1 3.5 %all-to-all-start.4 = ((bf16[16,16,512]{2,1,0:T(8,128)(2,1)}), bf16[16,16,512]{2,1,0:T(8,128)(2,1)S(1)}, u32[]{:S(2)}, u32[]{:S(2)}) async-start(bf16[16,16,512]{2,1,0:T(8,128)(2,1)} %misfit.1), calls=%async_computation.4 | async-start | bytes 524288 | tf_op jit(solution)/shard_map/all_to_all | solution.py:578
  97.6 8.4 %all-to-all-done.4.got_ref.grad_ref = bf16[16,16,512]{2,1,0:T(8,128)(2,1)S(1)} async-done(((bf16[16,16,512]{2,1,0:T(8,128)(2,1)}), bf16[16,16,512]{2,1,0:T(8,128)(2,1)S(1)}, u32[]{:S(2)}, u32[]{:S(2)}) %all-to-all-start.4) | async-done | bytes 262176 | tf_op jit(solution)/shard_map/all_to_all | solution.py:578
  106.3 11.0 %all_to_all.35.got_ref = bf16[8,32,512]{2,1,0:T(8,128)(2,1)S(1)} all-to-all(bf16[8,32,512]{2,1,0:T(8,128)(2,1)S(1)} %get-tuple-element.79), channel_id=1, replica_groups=mesh['batch'=8,'tensor'=16] {'batch'}, dimensions={0} | all-to-all | bytes 524288 | tf_op jit(solution)/shard_map/all_to_all | solution.py:597
  118.2 3.5 %all-to-all-start.6 = ((bf16[8,32,1024]{2,1,0:T(8,128)(2,1)}), bf16[8,32,1024]{2,1,0:T(8,128)(2,1)S(1)}, u32[]{:S(2)}, u32[]{:S(2)}) async-start(bf16[8,32,1024]{2,1,0:T(8,128)(2,1)} %acts.1), calls=%async_computation.6 | async-start | bytes 1048576 | tf_op jit(solution)/shard_map/all_to_all | solution.py:605
  123.0 7.1 %all-to-all-done.6.got_ref = bf16[8,32,1024]{2,1,0:T(8,128)(2,1)S(1)} async-done(((bf16[8,32,1024]{2,1,0:T(8,128)(2,1)}), bf16[8,32,1024]{2,1,0:T(8,128)(2,1)S(1)}, u32[]{:S(2)}, u32[]{:S(2)}) %all-to-all-start.6) | async-done | bytes 524320 | tf_op jit(solution)/shard_map/all_to_all | solution.py:605
  (58 shorter events, 22.3 us)
Async XLA Ops:
  2.4 8.9 %collective-permute-start = (bf16[40,512]{1,0:T(8,128)(2,1)}, bf16[40,512]{1,0:T(8,128)(2,1)S(1)}, u32[]{:S(2)}, u32[]{:S(2)}) collective-permute-start(bf16[40,512]{1,0:T(8,128)(2,1)} %rows.1), channel_id=1, source_target_pairs={{0,0},{1,1},{2,16},{3,17},{4,32},{5,33},{6,48},{7,49},{8,64},{9,65... | collective-permute-start | bytes 122888 | tf_op jit(solution)/shard_map/ppermute | solution.py:340
  12.3 19.9 %collective-permute-start.1 = (bf16[8,256,512]{2,1,0:T(8,128)(2,1)}, bf16[8,256,512]{2,1,0:T(8,128)(2,1)S(1)}, u32[]{:S(2)}, u32[]{:S(2)}) collective-permute-start(bf16[8,256,512]{2,1,0:T(8,128)(2,1)} %get-tuple-element.49), channel_id=1, source_target_pairs={{0,1},{1,0},{2,3},{3,2},{4,5},{5,4},{6,7},{7,6},{8,9},{9,8},{10,11... | collective-permute-start | bytes 6291464 | tf_op jit(solution)/shard_map/ppermute | solution.py:384
  12.4 11.9 %collective-permute-start.2 = (bf16[8,64,512]{2,1,0:T(8,128)(2,1)}, bf16[8,64,512]{2,1,0:T(8,128)(2,1)S(1)}, u32[]{:S(2)}, u32[]{:S(2)}) collective-permute-start(bf16[8,64,512]{2,1,0:T(8,128)(2,1)} %get-tuple-element.55), channel_id=1, source_target_pairs={{0,1},{1,0},{2,3},{3,2},{4,5},{5,4},{6,7},{7,6},{8,9},{9,8},{10,11... | collective-permute-start | bytes 1572872 | tf_op jit(solution)/shard_map/ppermute | solution.py:384
  12.9 25.4 %all-to-all-start = ((bf16[16,40,512]{2,1,0:T(8,128)(2,1)}), bf16[16,40,512]{2,1,0:T(8,128)(2,1)S(1)}, u32[]{:S(2)}, u32[]{:S(2)}) async-start(bf16[16,40,512]{2,1,0:T(8,128)(2,1)} %get-tuple-element.47), calls=%async_computation | async-start | bytes 1310720 | tf_op jit(solution)/shard_map/all_to_all | solution.py:381
  26.1 14.8 %collective-permute-start.3 = (bf16[2,64,512]{2,1,0:T(8,128)(2,1)}, bf16[2,64,512]{2,1,0:T(8,128)(2,1)S(1)}, u32[]{:S(2)}, u32[]{:S(2)}) collective-permute-start(bf16[2,64,512]{2,1,0:T(8,128)(2,1)} %get-tuple-element.57), channel_id=1, source_target_pairs={{0,2},{1,3},{2,4},{3,5},{4,6},{5,7},{6,0},{7,1},{8,10},{9,11},{10,... | collective-permute-start | bytes 393224 | tf_op jit(solution)/shard_map/ppermute | solution.py:384
  28.0 13.5 %collective-permute-start.4 = (bf16[2,64,512]{2,1,0:T(8,128)(2,1)}, bf16[2,64,512]{2,1,0:T(8,128)(2,1)S(1)}, u32[]{:S(2)}, u32[]{:S(2)}) collective-permute-start(bf16[2,64,512]{2,1,0:T(8,128)(2,1)} %get-tuple-element.58), channel_id=1, source_target_pairs={{0,4},{1,5},{2,6},{3,7},{4,0},{5,1},{6,2},{7,3},{8,12},{9,13},{10,... | collective-permute-start | bytes 393224 | tf_op jit(solution)/shard_map/ppermute | solution.py:384
  30.7 10.8 %collective-permute-start.5 = (bf16[2,64,512]{2,1,0:T(8,128)(2,1)}, bf16[2,64,512]{2,1,0:T(8,128)(2,1)S(1)}, u32[]{:S(2)}, u32[]{:S(2)}) collective-permute-start(bf16[2,64,512]{2,1,0:T(8,128)(2,1)} %get-tuple-element.59), channel_id=1, source_target_pairs={{0,6},{1,7},{2,0},{3,1},{4,2},{5,3},{6,4},{7,5},{8,14},{9,15},{10,... | collective-permute-start | bytes 393224 | tf_op jit(solution)/shard_map/ppermute | solution.py:384
  40.9 17.1 %copy-start.2 = (bf16[2,2,128,512]{3,2,1,0:T(8,128)(2,1)S(1)}, bf16[2,2,128,512]{3,2,1,0:T(8,128)(2,1)}, u32[]{:S(2)}) copy-start(bf16[2,2,128,512]{3,2,1,0:T(8,128)(2,1)} %get-tuple-element.50.after_ref.keep_a) | copy-start | bytes 1572868
  40.9 17.1 %copy-start.6 = (bf16[2,2,128,512]{3,2,1,0:T(8,128)(2,1)S(1)}, bf16[2,2,128,512]{3,2,1,0:T(8,128)(2,1)}, u32[]{:S(2)}) copy-start(bf16[2,2,128,512]{3,2,1,0:T(8,128)(2,1)} %get-tuple-element.64.keep_b) | copy-start | bytes 1572868
  43.0 16.4 %copy-start.11 = (f32[1,64,512]{2,1,0:T(8,128)S(1)}, f32[1,64,512]{2,1,0:T(8,128)}, u32[]{:S(2)}) copy-start(f32[1,64,512]{2,1,0:T(8,128)} %get-tuple-element.61.refs_1_) | copy-start | bytes 393220
  43.0 13.7 %collective-permute-start.7 = (bf16[2,2,128,512]{3,2,1,0:T(8,128)(2,1)}, bf16[2,2,128,512]{3,2,1,0:T(8,128)(2,1)S(1)}, u32[]{:S(2)}, u32[]{:S(2)}) collective-permute-start(bf16[2,2,128,512]{3,2,1,0:T(8,128)(2,1)} %get-tuple-element.63), channel_id=1, source_target_pairs={{0,2},{1,3},{2,0},{3,1},{4,6},{5,7},{6,4},{7,5},{8,10},{9,11},{10,... | collective-permute-start | bytes 1572872 | tf_op jit(solution)/shard_map/ppermute | solution.py:384
  43.1 14.9 %collective-permute-start.8 = (bf16[2,2,128,512]{3,2,1,0:T(8,128)(2,1)}, bf16[2,2,128,512]{3,2,1,0:T(8,128)(2,1)S(1)}, u32[]{:S(2)}, u32[]{:S(2)}) collective-permute-start(bf16[2,2,128,512]{3,2,1,0:T(8,128)(2,1)} %get-tuple-element.65), channel_id=1, source_target_pairs={{0,6},{1,7},{2,4},{3,5},{4,2},{5,3},{6,0},{7,1},{8,14},{9,15},{10,... | collective-permute-start | bytes 1572872 | tf_op jit(solution)/shard_map/ppermute | solution.py:384
  44.8 14.6 %all-to-all-start.1 = ((bf16[8,32,1152]{2,1,0:T(8,128)(2,1)}), bf16[8,32,1152]{2,1,0:T(8,128)(2,1)S(1)}, u32[]{:S(2)}, u32[]{:S(2)}) async-start(bf16[8,32,1152]{2,1,0:T(8,128)(2,1)} %get-tuple-element.60), calls=%async_computation.1 | async-start | bytes 1179648 | tf_op jit(solution)/shard_map/all_to_all | solution.py:499
  48.3 11.1 %collective-permute-start.6 = (bf16[1,64,512]{2,1,0:T(8,128)(2,1)}, bf16[1,64,512]{2,1,0:T(8,128)(2,1)S(1)}, u32[]{:S(2)}, u32[]{:S(2)}) collective-permute-start(bf16[1,64,512]{2,1,0:T(8,128)(2,1)} %get-tuple-element.62), channel_id=1, source_target_pairs={{0,8},{1,9},{2,10},{3,11},{4,12},{5,13},{6,14},{7,15},{8,0},{9,1},... | collective-permute-start | bytes 196616 | tf_op jit(solution)/shard_map/ppermute | solution.py:384
  60.5 15.1 %all-to-all-start.2 = ((bf16[8,96,512]{2,1,0:T(8,128)(2,1)}), bf16[8,96,512]{2,1,0:T(8,128)(2,1)S(1)}, u32[]{:S(2)}, u32[]{:S(2)}) async-start(bf16[8,96,512]{2,1,0:T(8,128)(2,1)} %get-tuple-element.68), calls=%async_computation.2 | async-start | bytes 1572864 | tf_op jit(solution)/shard_map/all_to_all | solution.py:547
  65.2 6.6 %collective-permute-start.10 = (bf16[2,128,512]{2,1,0:T(8,128)(2,1)}, bf16[2,128,512]{2,1,0:T(8,128)(2,1)S(1)}, u32[]{:S(2)}, u32[]{:S(2)}) collective-permute-start(bf16[2,128,512]{2,1,0:T(8,128)(2,1)} %get-tuple-element.73), channel_id=1, source_target_pairs={{0,2},{1,3},{2,0},{3,1},{4,6},{5,7},{6,4},{7,5},{8,10},{9,11},{10,... | collective-permute-start | bytes 786440 | tf_op jit(solution)/shard_map/ppermute | solution.py:384
  65.7 7.8 %collective-permute-start.9 = (bf16[2,128,512]{2,1,0:T(8,128)(2,1)}, bf16[2,128,512]{2,1,0:T(8,128)(2,1)S(1)}, u32[]{:S(2)}, u32[]{:S(2)}) collective-permute-start(bf16[2,128,512]{2,1,0:T(8,128)(2,1)} %get-tuple-element.71), channel_id=1, source_target_pairs={{0,6},{1,7},{2,4},{3,5},{4,2},{5,3},{6,0},{7,1},{8,14},{9,15},{10,... | collective-permute-start | bytes 786440 | tf_op jit(solution)/shard_map/ppermute | solution.py:384
  75.6 21.0 %copy-start.1 = (f32[2,128,512]{2,1,0:T(8,128)S(1)}, f32[2,128,512]{2,1,0:T(8,128)}, u32[]{:S(2)}) copy-start(f32[2,128,512]{2,1,0:T(8,128)} %get-tuple-element.74.after_ref.keep_ref) | copy-start | bytes 1572868
  77.9 14.4 %all-to-all-start.3 = ((bf16[16,16,512]{2,1,0:T(8,128)(2,1)}), bf16[16,16,512]{2,1,0:T(8,128)(2,1)S(1)}, u32[]{:S(2)}, u32[]{:S(2)}) async-start(bf16[16,16,512]{2,1,0:T(8,128)(2,1)} %get-tuple-element.75), calls=%async_computation.3 | async-start | bytes 524288 | tf_op jit(solution)/shard_map/all_to_all | solution.py:569
  83.0 13.7 %collective-permute-start.11 = (bf16[2,128,512]{2,1,0:T(8,128)(2,1)S(1)}, bf16[2,128,512]{2,1,0:T(8,128)(2,1)S(1)}, u32[]{:S(2)}, u32[]{:S(2)}) collective-permute-start(bf16[2,128,512]{2,1,0:T(8,128)(2,1)S(1)} %copy-done.13), channel_id=1, source_target_pairs={{0,8},{1,9},{2,10},{3,11},{4,12},{5,13},{6,14},{7,15},{8,0},{9,1},... | collective-permute-start | bytes 786440 | tf_op jit(solution)/shard_map/ppermute | solution.py:384
  93.1 12.9 %all-to-all-start.4 = ((bf16[16,16,512]{2,1,0:T(8,128)(2,1)}), bf16[16,16,512]{2,1,0:T(8,128)(2,1)S(1)}, u32[]{:S(2)}, u32[]{:S(2)}) async-start(bf16[16,16,512]{2,1,0:T(8,128)(2,1)} %misfit.1), calls=%async_computation.4 | async-start | bytes 524288 | tf_op jit(solution)/shard_map/all_to_all | solution.py:578
  97.6 24.1 %copy-start.10 = (bf16[256,512]{1,0:T(8,128)(2,1)S(1)}, bf16[256,512]{1,0:T(8,128)(2,1)}, u32[]{:S(2)}) copy-start(bf16[256,512]{1,0:T(8,128)(2,1)} %get-tuple-element.85.hidden_ref) | copy-start | bytes 786436
  106.3 23.8 %copy-start.8 = (bf16[256,512]{1,0:T(8,128)(2,1)S(1)}, bf16[256,512]{1,0:T(8,128)(2,1)}, u32[]{:S(2)}) copy-start(bf16[256,512]{1,0:T(8,128)(2,1)} %get-tuple-element.78.rows_ref) | copy-start | bytes 786436
  118.2 11.9 %all-to-all-start.6 = ((bf16[8,32,1024]{2,1,0:T(8,128)(2,1)}), bf16[8,32,1024]{2,1,0:T(8,128)(2,1)S(1)}, u32[]{:S(2)}, u32[]{:S(2)}) async-start(bf16[8,32,1024]{2,1,0:T(8,128)(2,1)} %acts.1), calls=%async_computation.6 | async-start | bytes 1048576 | tf_op jit(solution)/shard_map/all_to_all | solution.py:605
  (8 other events, 82.6 us)

commit v11 on v10

--- a/solution.py
+++ b/solution.py
@@ -109,7 +109,7 @@
     refs[-1][...] = total.astype(refs[-1].dtype)
 
 
-def routed_sum_kernel(y_ref, route_ref, residual_ref, p1, p2, p3, *refs):
+def routed_sum_kernel(y_ref, route_ref, residual_ref, passed_ref, *refs):
     ins, (send_ref, keep_ref) = refs[:8], refs[8:10]
     x_sum_kernel(*ins[:4], send_ref)
     x_sum_kernel(*ins[4:], keep_ref)
@@ -474,26 +474,24 @@
     )(group.reshape(1), every, norm_gain[None], w_gate, w_up, hbm(keep_a))
 
     routed, *moved = core_sum(keep_routed, send_routed, slots)
-    send_routed, keep_routed, sent, send_a, send_b = pl.pallas_call(
+    send_routed, keep_routed, sent = pl.pallas_call(
         routed_sum_kernel,
         grid_spec=pltpu.PrefetchScalarGridSpec(
             num_scalar_prefetch=1,
             grid=(1,),
-            in_specs=[vmem] * 2 + [anywhere] * 3 + y_blocks(slots),
-            out_specs=[pl.BlockSpec((1, slots, wide), lambda i, y: (0, 0, 0))] * 2
-            + [anywhere] * 3,
+            in_specs=[vmem] * 2 + [anywhere] + y_blocks(slots),
+            out_specs=[pl.BlockSpec((1, slots, wide), lambda i, y: (0, 0, 0))] * 2 + [anywhere],
         ),
         out_shape=[
             pltpu.HBM((1, slots, wide), BF),
             pltpu.HBM((1, slots, wide), F32),
             pltpu.HBM(sent.shape, BF),
-        ]
-        + [pair] * 2,
-        input_output_aliases={3: 2, 4: 3, 5: 4},
+        ],
+        input_output_aliases={3: 2},
         compiler_params=params(8),
         cost_estimate=cost(MIB, MIB),
         name="routed_sum",
-    )(y_at.reshape(1), route_index, residual_t, sent, send_a, send_b, *along_x(routed, moved) * 2)
+    )(y_at.reshape(1), route_index, residual_t, sent, *along_x(routed, moved) * 2)
     other_routed = along_y(send_routed)
 
     got = lax.all_to_all(sent, "batch", 0, 0, tiled=True)

time: 133 us -> 131 us (0.985)
  starting transfers between devices: 51.1 us -> 48.6 us
    ppermute x11, starting transfers between devices: 18 us -> 15.9 us  [along(): lax.ppermute(value, 'tensor', [(t, move(t // 8, t // 2 % 4, t % 2)) for t...]
  transfers between devices with their start and end apart: 18 -> 18, of which waited for: 10 -> 11; matrix products, arithmetic and copies ran while one was open for 0% -> 0% of each run, Pallas kernels for 16% -> 18%
where the time goes in v11:
time: 131 us; the launch traced here: 130 us
  starting transfers between devices  48.6 us (37%)
  waiting for transfers between devices  36.6 us (28%)
  Pallas kernels  32.6 us (25%)
  blocking collectives  10.9 us (8%)
    ppermute x11, starting transfers between devices, along(): lax.ppermute(value, 'tensor', [(t, move(t // 8, t // 2 % 4, t % 2)) for t...  15.9 us
    ppermute x11, waiting for transfers between devices, along(): lax.ppermute(value, 'tensor', [(t, move(t // 8, t // 2 % 4, t % 2)) for t...  12.6 us
    all_to_all x1, starting transfers between devices, on_device(): every = lax.all_to_all(copies, 'tensor', 0, 0, tiled=True)  11.3 us
    all_to_all x1, blocking collectives, on_device(): back = lax.all_to_all(back, 'batch', 0, 0, tiled=True)  10.9 us
    all_to_all x1, waiting for transfers between devices, on_device(): grad_out = lax.all_to_all(grad_out, 'tensor', 0, 0, tiled=True)  8.41 us
    pallas_call x1, Pallas kernels, on_device(): pl.pallas_call(teacher_kernel, grid_spec=pltpu.PrefetchScalarGridSpec(num...  7.49 us
    all_to_all x1, waiting for transfers between devices, on_device(): acts = lax.all_to_all(acts, 'batch', 0, 0, tiled=True)  7.06 us
    all_to_all x1, waiting for transfers between devices, on_device(): misfit = lax.all_to_all(misfit, 'tensor', 0, 0, tiled=True)  5.87 us
  transfers between devices with their start and end apart: 18, of which 11 were waited for; matrix products, arithmetic and copies ran while one was open for 0% of the time, Pallas kernels for 18%

profile of v11, /device:TPU:0, one launch (start us, length us, event | category | flops | bytes accessed | tf_op | source)
XLA Modules:
  0.0 129.6 jit_solution(17299587401888137282)
XLA Ops:
  0.6 1.7 %rows.1 = bf16[40,512]{1,0:T(8,128)(2,1)} custom-call(s32[1,64]{1,0:T(1,128)} %route_ref.5, bf16[256,256]{1,0:T(8,128)(2,1)} %x_ref.1), custom_call_target="tpu_custom_call" | custom-call | flops 8192 | bytes 256 | tf_op jit(solution)/shard_map/rows/pallas_call | solution.py:328
  3.8 7.5 %teacher.1 = (bf16[8,256,512]{2,1,0:T(8,128)(2,1)}, bf16[8,256,512]{2,1,0:T(8,128)(2,1)}, bf16[8,64,512]{2,1,0:T(8,128)(2,1)}, bf16[8,64,512]{2,1,0:T(8,128)(2,1)}) custom-call(s32[1]{0:T(128)} %bitcast.2.core_ref, s32[1,64]{1,0:T(1,128)} %route_ref.5, bf16[256,512]{1,0:T(8,128)(2,1)} %attn_ref.1, bf16[512,8192]{1,0:T(8,128)(2,1)} %weight_ref.1), custom_call_target="tpu_custom_call" | custom-call | flops 2621440 | bytes 14336 | tf_op jit(solution)/shard_map/teacher/pallas_call | solution.py:342
  12.9 11.3 %all-to-all-start = ((bf16[16,40,512]{2,1,0:T(8,128)(2,1)}), bf16[16,40,512]{2,1,0:T(8,128)(2,1)S(1)}, u32[]{:S(2)}, u32[]{:S(2)}) async-start(bf16[16,40,512]{2,1,0:T(8,128)(2,1)} %get-tuple-element.45), calls=%async_computation | async-start | bytes 1310720 | tf_op jit(solution)/shard_map/all_to_all | solution.py:381
  24.2 1.8 %core_sum.1 = (bf16[2,64,512]{2,1,0:T(8,128)(2,1)}, bf16[2,64,512]{2,1,0:T(8,128)(2,1)}, bf16[2,64,512]{2,1,0:T(8,128)(2,1)}, bf16[2,64,512]{2,1,0:T(8,128)(2,1)}) custom-call(s32[1]{0:T(128)} %bitcast.4.x_ref, bf16[8,64,512]{2,1,0:T(8,128)(2,1)} %get-tuple-element.50.refs_0_.refs_1_.refs_2_.refs_3_, ...), custom_call_target="tpu_custom_call" | custom-call | flops 1024 | bytes 1536 | tf_op jit(solution)/shard_map/core_sum/pallas_call | solution.py:390
  26.1 1.9 %collective-permute-start.3 = (bf16[2,64,512]{2,1,0:T(8,128)(2,1)}, bf16[2,64,512]{2,1,0:T(8,128)(2,1)S(1)}, u32[]{:S(2)}, u32[]{:S(2)}) collective-permute-start(bf16[2,64,512]{2,1,0:T(8,128)(2,1)} %get-tuple-element.53), channel_id=1, source_target_pairs={{0,2},{1,3},{2,4},{3,5},{4,6},{5,7},{6,0},{7,1},{8,10},{9,11},{10,... | collective-permute-start | bytes 393224 | tf_op jit(solution)/shard_map/ppermute | solution.py:384
  28.0 2.7 %collective-permute-start.4 = (bf16[2,64,512]{2,1,0:T(8,128)(2,1)}, bf16[2,64,512]{2,1,0:T(8,128)(2,1)S(1)}, u32[]{:S(2)}, u32[]{:S(2)}) collective-permute-start(bf16[2,64,512]{2,1,0:T(8,128)(2,1)} %get-tuple-element.54), channel_id=1, source_target_pairs={{0,4},{1,5},{2,6},{3,7},{4,0},{5,1},{6,2},{7,3},{8,12},{9,13},{10,... | collective-permute-start | bytes 393224 | tf_op jit(solution)/shard_map/ppermute | solution.py:384
  32.2 4.1 %halves.1 = (bf16[2,2,128,512]{3,2,1,0:T(8,128)(2,1)}, bf16[2,2,128,512]{3,2,1,0:T(8,128)(2,1)}, bf16[2,2,128,512]{3,2,1,0:T(8,128)(2,1)}, bf16[2,2,128,512]{3,2,1,0:T(8,128)(2,1)}) custom-call(s32[1]{0:T(128)} %bitcast.4.x_ref, bf16[8,2,128,512]{3,2,1,0:T(8,128)(2,1)} %bitcast.12, bf16[8,2,128,512]{3,2,1,0:T(8,128)(2,1)} %bitcast.13, ...), custom_call_target="tpu_custom_call" | custom-call | flops 1024 | bytes 6144 | tf_op jit(solution)/shard_map/halves/pallas_call | solution.py:427
  38.3 2.5 %up.1 = (bf16[8,32,1152]{2,1,0:T(8,128)(2,1)}, bf16[256,512]{1,0:T(8,128)(2,1)}, bf16[256,512]{1,0:T(8,128)(2,1)}) custom-call(s32[1]{0:T(128)} %bitcast.group_ref, bf16[16,40,512]{2,1,0:T(8,128)(2,1)S(1)} %all-to-all-done.got_ref, f32[1,4096]{1,0:T(1,128)S(1)} %bitcast.11, bf16[512,512]{1,0:T(8,128)(2,1)} %gate_ref.1, bf16[512,512]{1,0:T(8,128)(2,1)} %up_ref.1, ...), custom_call_target="tpu_custom_call" | custom-call | flops 819200 | bytes 4096 | tf_op jit(solution)/shard_map/up/pallas_call | solution.py:452
  43.5 3.7 %all-to-all-start.1 = ((bf16[8,32,1152]{2,1,0:T(8,128)(2,1)}), bf16[8,32,1152]{2,1,0:T(8,128)(2,1)S(1)}, u32[]{:S(2)}, u32[]{:S(2)}) async-start(bf16[8,32,1152]{2,1,0:T(8,128)(2,1)} %get-tuple-element.56), calls=%async_computation.1 | async-start | bytes 1179648 | tf_op jit(solution)/shard_map/all_to_all | solution.py:497
  47.2 3.2 %collective-permute-start.6 = (bf16[1,64,512]{2,1,0:T(8,128)(2,1)}, bf16[1,64,512]{2,1,0:T(8,128)(2,1)S(1)}, u32[]{:S(2)}, u32[]{:S(2)}) collective-permute-start(bf16[1,64,512]{2,1,0:T(8,128)(2,1)} %get-tuple-element.58), channel_id=1, source_target_pairs={{0,8},{1,9},{2,10},{3,11},{4,12},{5,13},{6,14},{7,15},{8,0},{9,1},... | collective-permute-start | bytes 196616 | tf_op jit(solution)/shard_map/ppermute | solution.py:384
  52.8 2.3 %first_sum.1 = (f32[2,128,512]{2,1,0:T(8,128)}, bf16[2,128,512]{2,1,0:T(8,128)(2,1)}, f32[2,128,512]{2,1,0:T(8,128)}, bf16[2,128,512]{2,1,0:T(8,128)(2,1)}) custom-call(bf16[2,2,128,512]{3,2,1,0:T(8,128)(2,1)S(1)} %copy-done.2, bf16[2,2,128,512]{3,2,1,0:T(8,128)(2,1)S(1)} %collective-permute-done.7.got_a, bf16[2,2,128,512]{3,2,1,0:T(8,128)(2,1)S(1)} %copy-done.7, ...), custom_call_target="tpu_custom_call" | custom-call | flops 1024 | bytes 3072 | tf_op jit(solution)/shard_map/first_sum/pallas_call | solution.py:502
  55.1 3.0 %collective-permute-done.6.refs_2_ = bf16[1,64,512]{2,1,0:T(8,128)(2,1)S(1)} collective-permute-done((bf16[1,64,512]{2,1,0:T(8,128)(2,1)}, bf16[1,64,512]{2,1,0:T(8,128)(2,1)S(1)}, u32[]{:S(2)}, u32[]{:S(2)}) %collective-permute-start.6) | collective-permute-done | bytes 65568 | tf_op jit(solution)/shard_map/ppermute | solution.py:384
  59.2 4.9 %all-to-all-start.2 = ((bf16[8,96,512]{2,1,0:T(8,128)(2,1)}), bf16[8,96,512]{2,1,0:T(8,128)(2,1)S(1)}, u32[]{:S(2)}, u32[]{:S(2)}) async-start(bf16[8,96,512]{2,1,0:T(8,128)(2,1)} %get-tuple-element.64), calls=%async_computation.2 | async-start | bytes 1572864 | tf_op jit(solution)/shard_map/all_to_all | solution.py:545
  64.1 1.8 %collective-permute-start.9 = (bf16[2,128,512]{2,1,0:T(8,128)(2,1)}, bf16[2,128,512]{2,1,0:T(8,128)(2,1)S(1)}, u32[]{:S(2)}, u32[]{:S(2)}) collective-permute-start(bf16[2,128,512]{2,1,0:T(8,128)(2,1)} %get-tuple-element.67), channel_id=1, source_target_pairs={{0,6},{1,7},{2,4},{3,5},{4,2},{5,3},{6,0},{7,1},{8,14},{9,15},{10,... | collective-permute-start | bytes 786440 | tf_op jit(solution)/shard_map/ppermute | solution.py:384
  66.0 4.8 %collective-permute-done.10.refs_5_.refs_7_ = bf16[2,128,512]{2,1,0:T(8,128)(2,1)S(1)} collective-permute-done((bf16[2,128,512]{2,1,0:T(8,128)(2,1)}, bf16[2,128,512]{2,1,0:T(8,128)(2,1)S(1)}, u32[]{:S(2)}, u32[]{:S(2)}) %collective-permute-start.10) | collective-permute-done | bytes 262176 | tf_op jit(solution)/shard_map/ppermute | solution.py:384
  74.3 2.3 %down.1 = (bf16[16,16,512]{2,1,0:T(8,128)(2,1)}, bf16[256,512]{1,0:T(8,128)(2,1)}) custom-call(s32[1]{0:T(128)} %bitcast.group_ref, bf16[8,96,512]{2,1,0:T(8,128)(2,1)S(1)} %all-to-all-done.2.got_ref, bf16[512,512]{1,0:T(8,128)(2,1)S(1)} %copy-done, bf16[256,512]{1,0:T(8,128)(2,1)S(1)} %copy-done.9, bf16[512,4096]{1,0:T(8,128)(2,1)} %projector_ref.1, ...), custom_call_target="tpu_custom_call" | custom-call | flops 786432 | bytes 4096 | tf_op jit(solution)/shard_map/down/pallas_call | solution.py:546
  76.6 4.3 %all-to-all-start.3 = ((bf16[16,16,512]{2,1,0:T(8,128)(2,1)}), bf16[16,16,512]{2,1,0:T(8,128)(2,1)S(1)}, u32[]{:S(2)}, u32[]{:S(2)}) async-start(bf16[16,16,512]{2,1,0:T(8,128)(2,1)} %get-tuple-element.71), calls=%async_computation.3 | async-start | bytes 524288 | tf_op jit(solution)/shard_map/all_to_all | solution.py:567
  80.9 3.5 %collective-permute-start.11 = (bf16[2,128,512]{2,1,0:T(8,128)(2,1)S(1)}, bf16[2,128,512]{2,1,0:T(8,128)(2,1)S(1)}, u32[]{:S(2)}, u32[]{:S(2)}) collective-permute-start(bf16[2,128,512]{2,1,0:T(8,128)(2,1)S(1)} %copy-done.13), channel_id=1, source_target_pairs={{0,8},{1,9},{2,10},{3,11},{4,12},{5,13},{6,14},{7,15},{8,0},{9,1},... | collective-permute-start | bytes 786440 | tf_op jit(solution)/shard_map/ppermute | solution.py:384
  84.5 5.9 %all-to-all-done.3.refs_0_ = bf16[16,16,512]{2,1,0:T(8,128)(2,1)S(1)} async-done(((bf16[16,16,512]{2,1,0:T(8,128)(2,1)}), bf16[16,16,512]{2,1,0:T(8,128)(2,1)S(1)}, u32[]{:S(2)}, u32[]{:S(2)}) %all-to-all-start.3) | async-done | bytes 262176 | tf_op jit(solution)/shard_map/all_to_all | solution.py:567
  91.1 3.5 %all-to-all-start.4 = ((bf16[16,16,512]{2,1,0:T(8,128)(2,1)}), bf16[16,16,512]{2,1,0:T(8,128)(2,1)S(1)}, u32[]{:S(2)}, u32[]{:S(2)}) async-start(bf16[16,16,512]{2,1,0:T(8,128)(2,1)} %misfit.1), calls=%async_computation.4 | async-start | bytes 524288 | tf_op jit(solution)/shard_map/all_to_all | solution.py:576
  95.6 8.4 %all-to-all-done.4.got_ref.grad_ref = bf16[16,16,512]{2,1,0:T(8,128)(2,1)S(1)} async-done(((bf16[16,16,512]{2,1,0:T(8,128)(2,1)}), bf16[16,16,512]{2,1,0:T(8,128)(2,1)S(1)}, u32[]{:S(2)}, u32[]{:S(2)}) %all-to-all-start.4) | async-done | bytes 262176 | tf_op jit(solution)/shard_map/all_to_all | solution.py:576
  104.3 10.9 %all_to_all.35.got_ref = bf16[8,32,512]{2,1,0:T(8,128)(2,1)S(1)} all-to-all(bf16[8,32,512]{2,1,0:T(8,128)(2,1)S(1)} %get-tuple-element.75), channel_id=1, replica_groups=mesh['batch'=8,'tensor'=16] {'batch'}, dimensions={0} | all-to-all | bytes 524288 | tf_op jit(solution)/shard_map/all_to_all | solution.py:595
  116.1 3.5 %all-to-all-start.6 = ((bf16[8,32,1024]{2,1,0:T(8,128)(2,1)}), bf16[8,32,1024]{2,1,0:T(8,128)(2,1)S(1)}, u32[]{:S(2)}, u32[]{:S(2)}) async-start(bf16[8,32,1024]{2,1,0:T(8,128)(2,1)} %acts.1), calls=%async_computation.6 | async-start | bytes 1048576 | tf_op jit(solution)/shard_map/all_to_all | solution.py:603
  120.9 7.1 %all-to-all-done.6.got_ref = bf16[8,32,1024]{2,1,0:T(8,128)(2,1)S(1)} async-done(((bf16[8,32,1024]{2,1,0:T(8,128)(2,1)}), bf16[8,32,1024]{2,1,0:T(8,128)(2,1)S(1)}, u32[]{:S(2)}, u32[]{:S(2)}) %all-to-all-start.6) | async-done | bytes 524320 | tf_op jit(solution)/shard_map/all_to_all | solution.py:603
  (58 shorter events, 22.1 us)
Async XLA Ops:
  2.4 8.9 %collective-permute-start = (bf16[40,512]{1,0:T(8,128)(2,1)}, bf16[40,512]{1,0:T(8,128)(2,1)S(1)}, u32[]{:S(2)}, u32[]{:S(2)}) collective-permute-start(bf16[40,512]{1,0:T(8,128)(2,1)} %rows.1), channel_id=1, source_target_pairs={{0,0},{1,1},{2,16},{3,17},{4,32},{5,33},{6,48},{7,49},{8,64},{9,65... | collective-permute-start | bytes 122888 | tf_op jit(solution)/shard_map/ppermute | solution.py:340
  12.3 19.9 %collective-permute-start.1 = (bf16[8,256,512]{2,1,0:T(8,128)(2,1)}, bf16[8,256,512]{2,1,0:T(8,128)(2,1)S(1)}, u32[]{:S(2)}, u32[]{:S(2)}) collective-permute-start(bf16[8,256,512]{2,1,0:T(8,128)(2,1)} %get-tuple-element.47), channel_id=1, source_target_pairs={{0,1},{1,0},{2,3},{3,2},{4,5},{5,4},{6,7},{7,6},{8,9},{9,8},{10,11... | collective-permute-start | bytes 6291464 | tf_op jit(solution)/shard_map/ppermute | solution.py:384
  12.4 11.9 %collective-permute-start.2 = (bf16[8,64,512]{2,1,0:T(8,128)(2,1)}, bf16[8,64,512]{2,1,0:T(8,128)(2,1)S(1)}, u32[]{:S(2)}, u32[]{:S(2)}) collective-permute-start(bf16[8,64,512]{2,1,0:T(8,128)(2,1)} %get-tuple-element.51), channel_id=1, source_target_pairs={{0,1},{1,0},{2,3},{3,2},{4,5},{5,4},{6,7},{7,6},{8,9},{9,8},{10,11... | collective-permute-start | bytes 1572872 | tf_op jit(solution)/shard_map/ppermute | solution.py:384
  12.9 25.4 %all-to-all-start = ((bf16[16,40,512]{2,1,0:T(8,128)(2,1)}), bf16[16,40,512]{2,1,0:T(8,128)(2,1)S(1)}, u32[]{:S(2)}, u32[]{:S(2)}) async-start(bf16[16,40,512]{2,1,0:T(8,128)(2,1)} %get-tuple-element.45), calls=%async_computation | async-start | bytes 1310720 | tf_op jit(solution)/shard_map/all_to_all | solution.py:381
  26.1 14.8 %collective-permute-start.3 = (bf16[2,64,512]{2,1,0:T(8,128)(2,1)}, bf16[2,64,512]{2,1,0:T(8,128)(2,1)S(1)}, u32[]{:S(2)}, u32[]{:S(2)}) collective-permute-start(bf16[2,64,512]{2,1,0:T(8,128)(2,1)} %get-tuple-element.53), channel_id=1, source_target_pairs={{0,2},{1,3},{2,4},{3,5},{4,6},{5,7},{6,0},{7,1},{8,10},{9,11},{10,... | collective-permute-start | bytes 393224 | tf_op jit(solution)/shard_map/ppermute | solution.py:384
  28.0 13.9 %collective-permute-start.4 = (bf16[2,64,512]{2,1,0:T(8,128)(2,1)}, bf16[2,64,512]{2,1,0:T(8,128)(2,1)S(1)}, u32[]{:S(2)}, u32[]{:S(2)}) collective-permute-start(bf16[2,64,512]{2,1,0:T(8,128)(2,1)} %get-tuple-element.54), channel_id=1, source_target_pairs={{0,4},{1,5},{2,6},{3,7},{4,0},{5,1},{6,2},{7,3},{8,12},{9,13},{10,... | collective-permute-start | bytes 393224 | tf_op jit(solution)/shard_map/ppermute | solution.py:384
  30.7 11.3 %collective-permute-start.5 = (bf16[2,64,512]{2,1,0:T(8,128)(2,1)}, bf16[2,64,512]{2,1,0:T(8,128)(2,1)S(1)}, u32[]{:S(2)}, u32[]{:S(2)}) collective-permute-start(bf16[2,64,512]{2,1,0:T(8,128)(2,1)} %get-tuple-element.55), channel_id=1, source_target_pairs={{0,6},{1,7},{2,0},{3,1},{4,2},{5,3},{6,4},{7,5},{8,14},{9,15},{10,... | collective-permute-start | bytes 393224 | tf_op jit(solution)/shard_map/ppermute | solution.py:384
  36.2 15.0 %collective-permute-start.7 = (bf16[2,2,128,512]{3,2,1,0:T(8,128)(2,1)}, bf16[2,2,128,512]{3,2,1,0:T(8,128)(2,1)S(1)}, u32[]{:S(2)}, u32[]{:S(2)}) collective-permute-start(bf16[2,2,128,512]{3,2,1,0:T(8,128)(2,1)} %get-tuple-element.59), channel_id=1, source_target_pairs={{0,2},{1,3},{2,0},{3,1},{4,6},{5,7},{6,4},{7,5},{8,10},{9,11},{10,... | collective-permute-start | bytes 1572872 | tf_op jit(solution)/shard_map/ppermute | solution.py:384
  36.9 16.0 %collective-permute-start.8 = (bf16[2,2,128,512]{3,2,1,0:T(8,128)(2,1)}, bf16[2,2,128,512]{3,2,1,0:T(8,128)(2,1)}, u32[]{:S(2)}, u32[]{:S(2)}) collective-permute-start(bf16[2,2,128,512]{3,2,1,0:T(8,128)(2,1)} %get-tuple-element.61), channel_id=1, source_target_pairs={{0,6},{1,7},{2,4},{3,5},{4,2},{5,3},{6,0},{7,1},{8,14},{9,15},{10,... | collective-permute-start | bytes 1572872 | tf_op jit(solution)/shard_map/ppermute | solution.py:384
  43.5 14.6 %all-to-all-start.1 = ((bf16[8,32,1152]{2,1,0:T(8,128)(2,1)}), bf16[8,32,1152]{2,1,0:T(8,128)(2,1)S(1)}, u32[]{:S(2)}, u32[]{:S(2)}) async-start(bf16[8,32,1152]{2,1,0:T(8,128)(2,1)} %get-tuple-element.56), calls=%async_computation.1 | async-start | bytes 1179648 | tf_op jit(solution)/shard_map/all_to_all | solution.py:497
  47.2 10.9 %collective-permute-start.6 = (bf16[1,64,512]{2,1,0:T(8,128)(2,1)}, bf16[1,64,512]{2,1,0:T(8,128)(2,1)S(1)}, u32[]{:S(2)}, u32[]{:S(2)}) collective-permute-start(bf16[1,64,512]{2,1,0:T(8,128)(2,1)} %get-tuple-element.58), channel_id=1, source_target_pairs={{0,8},{1,9},{2,10},{3,11},{4,12},{5,13},{6,14},{7,15},{8,0},{9,1},... | collective-permute-start | bytes 196616 | tf_op jit(solution)/shard_map/ppermute | solution.py:384
  55.1 16.9 %copy-start.3 = (f32[2,128,512]{2,1,0:T(8,128)S(1)}, f32[2,128,512]{2,1,0:T(8,128)}, u32[]{:S(2)}) copy-start(f32[2,128,512]{2,1,0:T(8,128)} %get-tuple-element.66.refs_0_.refs_2_) | copy-start | bytes 1572868
  55.1 16.9 %copy-start.4 = (f32[2,128,512]{2,1,0:T(8,128)S(1)}, f32[2,128,512]{2,1,0:T(8,128)}, u32[]{:S(2)}) copy-start(f32[2,128,512]{2,1,0:T(8,128)} %get-tuple-element.68.refs_4_.refs_6_) | copy-start | bytes 1572868
  59.2 15.1 %copy-start.9 = (bf16[256,512]{1,0:T(8,128)(2,1)S(1)}, bf16[256,512]{1,0:T(8,128)(2,1)}, u32[]{:S(2)}) copy-start(bf16[256,512]{1,0:T(8,128)(2,1)} %get-tuple-element.65.chosen_ref) | copy-start | bytes 786436
  59.2 15.1 %all-to-all-start.2 = ((bf16[8,96,512]{2,1,0:T(8,128)(2,1)}), bf16[8,96,512]{2,1,0:T(8,128)(2,1)S(1)}, u32[]{:S(2)}, u32[]{:S(2)}) async-start(bf16[8,96,512]{2,1,0:T(8,128)(2,1)} %get-tuple-element.64), calls=%async_computation.2 | async-start | bytes 1572864 | tf_op jit(solution)/shard_map/all_to_all | solution.py:545
  64.1 6.6 %collective-permute-start.10 = (bf16[2,128,512]{2,1,0:T(8,128)(2,1)}, bf16[2,128,512]{2,1,0:T(8,128)(2,1)S(1)}, u32[]{:S(2)}, u32[]{:S(2)}) collective-permute-start(bf16[2,128,512]{2,1,0:T(8,128)(2,1)} %get-tuple-element.69), channel_id=1, source_target_pairs={{0,2},{1,3},{2,0},{3,1},{4,6},{5,7},{6,4},{7,5},{8,10},{9,11},{10,... | collective-permute-start | bytes 786440 | tf_op jit(solution)/shard_map/ppermute | solution.py:384
  64.1 7.9 %collective-permute-start.9 = (bf16[2,128,512]{2,1,0:T(8,128)(2,1)}, bf16[2,128,512]{2,1,0:T(8,128)(2,1)S(1)}, u32[]{:S(2)}, u32[]{:S(2)}) collective-permute-start(bf16[2,128,512]{2,1,0:T(8,128)(2,1)} %get-tuple-element.67), channel_id=1, source_target_pairs={{0,6},{1,7},{2,4},{3,5},{4,2},{5,3},{6,0},{7,1},{8,14},{9,15},{10,... | collective-permute-start | bytes 786440 | tf_op jit(solution)/shard_map/ppermute | solution.py:384
  74.3 20.3 %copy-start.1 = (f32[2,128,512]{2,1,0:T(8,128)S(1)}, f32[2,128,512]{2,1,0:T(8,128)}, u32[]{:S(2)}) copy-start(f32[2,128,512]{2,1,0:T(8,128)} %get-tuple-element.70.after_ref.keep_ref) | copy-start | bytes 1572868
  76.6 13.7 %all-to-all-start.3 = ((bf16[16,16,512]{2,1,0:T(8,128)(2,1)}), bf16[16,16,512]{2,1,0:T(8,128)(2,1)S(1)}, u32[]{:S(2)}, u32[]{:S(2)}) async-start(bf16[16,16,512]{2,1,0:T(8,128)(2,1)} %get-tuple-element.71), calls=%async_computation.3 | async-start | bytes 524288 | tf_op jit(solution)/shard_map/all_to_all | solution.py:567
  80.9 13.7 %collective-permute-start.11 = (bf16[2,128,512]{2,1,0:T(8,128)(2,1)S(1)}, bf16[2,128,512]{2,1,0:T(8,128)(2,1)S(1)}, u32[]{:S(2)}, u32[]{:S(2)}) collective-permute-start(bf16[2,128,512]{2,1,0:T(8,128)(2,1)S(1)} %copy-done.13), channel_id=1, source_target_pairs={{0,8},{1,9},{2,10},{3,11},{4,12},{5,13},{6,14},{7,15},{8,0},{9,1},... | collective-permute-start | bytes 786440 | tf_op jit(solution)/shard_map/ppermute | solution.py:384
  91.1 12.9 %all-to-all-start.4 = ((bf16[16,16,512]{2,1,0:T(8,128)(2,1)}), bf16[16,16,512]{2,1,0:T(8,128)(2,1)S(1)}, u32[]{:S(2)}, u32[]{:S(2)}) async-start(bf16[16,16,512]{2,1,0:T(8,128)(2,1)} %misfit.1), calls=%async_computation.4 | async-start | bytes 524288 | tf_op jit(solution)/shard_map/all_to_all | solution.py:576
  95.5 24.1 %copy-start.10 = (bf16[256,512]{1,0:T(8,128)(2,1)S(1)}, bf16[256,512]{1,0:T(8,128)(2,1)}, u32[]{:S(2)}) copy-start(bf16[256,512]{1,0:T(8,128)(2,1)} %get-tuple-element.81.hidden_ref) | copy-start | bytes 786436
  104.3 23.7 %copy-start.8 = (bf16[256,512]{1,0:T(8,128)(2,1)S(1)}, bf16[256,512]{1,0:T(8,128)(2,1)}, u32[]{:S(2)}) copy-start(bf16[256,512]{1,0:T(8,128)(2,1)} %get-tuple-element.74.rows_ref) | copy-start | bytes 786436
  116.1 11.9 %all-to-all-start.6 = ((bf16[8,32,1024]{2,1,0:T(8,128)(2,1)}), bf16[8,32,1024]{2,1,0:T(8,128)(2,1)S(1)}, u32[]{:S(2)}, u32[]{:S(2)}) async-start(bf16[8,32,1024]{2,1,0:T(8,128)(2,1)} %acts.1), calls=%async_computation.6 | async-start | bytes 1048576 | tf_op jit(solution)/shard_map/all_to_all | solution.py:603
  (8 other events, 77.9 us)

commit v12 on v11

--- a/solution.py
+++ b/solution.py
@@ -284,11 +284,23 @@
     out_ref[...] = dot(grad_ref[...].reshape(rows, out_ref.shape[0]), hidden_ref[...], 0, 0)
 
 
-def weights_kernel(rows_ref, got_ref, gate_ref, up_ref):
+def weights_kernel(rows_ref, got_ref, gate_ref, up_ref, parts_ref, sems):
     wide = gate_ref.shape[1]
+    tall = parts_ref.shape[1]
     acts = got_ref[...].reshape(got_ref.shape[0] * got_ref.shape[1], 2 * wide)
-    gate_ref[...] = dot(rows_ref[...], acts[:, 0:wide], 0, 0)
-    up_ref[...] = dot(rows_ref[...], acts[:, wide:], 0, 0)
+    copies = []
+    for i, out_ref in enumerate((gate_ref, up_ref)):
+        for first in range(0, gate_ref.shape[0], tall):
+            n = len(copies)
+            rows = rows_ref[:, first : first + tall]
+            parts_ref[n] = dot(rows, acts[:, i * wide : (i + 1) * wide], 0, 0)
+            copy = pltpu.make_async_copy(
+                parts_ref.at[n], out_ref.at[first : first + tall, :], sems.at[n]
+            )
+            copy.start()
+            copies.append(copy)
+    for copy in copies:
+        copy.wait()
 
 
 def on_device(
@@ -383,27 +395,30 @@
     def along(value, move):
         return lax.ppermute(value, "tensor", [(t, move(t // 8, (t // 2) % 4, t % 2)) for t in range(parts)])
 
-    def core_sum(keep, send, strip):
+    def core_sum(keep, send, height):
         got = along(send, lambda y, x, c: y * 8 + x * 2 + 1 - c)
-        height = keep.shape[1]
-        block = (1, strip, wide)
+        block = (2, 1, height, wide)
         return pl.pallas_call(
             core_sum_kernel,
             grid_spec=pltpu.PrefetchScalarGridSpec(
                 num_scalar_prefetch=1,
-                grid=(2, height // strip),
+                grid=(1,),
                 in_specs=[
-                    pl.BlockSpec(block, lambda y, i, x, j=j: (4 * y + ((x[0] + j) & 3), i, 0))
+                    pl.BlockSpec(block, lambda i, x, j=j: (0, (x[0] + j) & 3, 0, 0))
                     for j in range(4)
                 ]
                 * 2,
-                out_specs=[pl.BlockSpec(block, lambda y, i, x: (y, i, 0))] * 4,
+                out_specs=[pl.BlockSpec((2, height, wide), lambda i, x: (0, 0, 0))] * 4,
             ),
             out_shape=[pltpu.HBM((2, height, wide), BF)] * 4,
             compiler_params=params(16),
             cost_estimate=cost(MIB, 24 * height * wide * 2),
             name="core_sum",
-        )(x_at.reshape(1), *[hbm(keep)] * 4, *[got] * 4)
+        )(
+            x_at.reshape(1),
+            *[hbm(keep.reshape(2, 4, height, wide))] * 4,
+            *[got.reshape(2, 4, height, wide)] * 4,
+        )
 
     def along_x(own, moved):
         return [own] + [
@@ -610,7 +625,13 @@
     )(grad_out, hidden)
     grad_gate, grad_up = pl.pallas_call(
         weights_kernel,
-        out_shape=[shape((wide, units), F32)] * 2,
+        in_specs=[vmem] * 2,
+        out_specs=[anywhere] * 2,
+        out_shape=[pltpu.HBM((wide, units), F32)] * 2,
+        scratch_shapes=[
+            pltpu.VMEM((4, wide // 2, units), F32),
+            pltpu.SemaphoreType.DMA((4,)),
+        ],
         compiler_params=params(16),
         cost_estimate=cost(512 * MIB, 4 * MIB),
         name="weights",

time: 131 us -> 130 us (level)
  no operation moved by 1% of the time
where the time goes in v12:
time: 130 us; the launch traced here: 129 us
  starting transfers between devices  48.3 us (37%)
  waiting for transfers between devices  36.6 us (28%)
  Pallas kernels  32.7 us (25%)
  blocking collectives  11 us (8%)
    ppermute x11, starting transfers between devices, along(): lax.ppermute(value, 'tensor', [(t, move(t // 8, t // 2 % 4, t % 2)) for t...  15.8 us
    ppermute x11, waiting for transfers between devices, along(): lax.ppermute(value, 'tensor', [(t, move(t // 8, t // 2 % 4, t % 2)) for t...  12.7 us
    all_to_all x1, starting transfers between devices, on_device(): every = lax.all_to_all(copies, 'tensor', 0, 0, tiled=True)  11.3 us
    all_to_all x1, blocking collectives, on_device(): back = lax.all_to_all(back, 'batch', 0, 0, tiled=True)  11 us
    all_to_all x1, waiting for transfers between devices, on_device(): grad_out = lax.all_to_all(grad_out, 'tensor', 0, 0, tiled=True)  8.41 us
    pallas_call x1, Pallas kernels, on_device(): pl.pallas_call(teacher_kernel, grid_spec=pltpu.PrefetchScalarGridSpec(num...  7.49 us
    all_to_all x1, waiting for transfers between devices, on_device(): acts = lax.all_to_all(acts, 'batch', 0, 0, tiled=True)  7.06 us
    all_to_all x1, waiting for transfers between devices, on_device(): misfit = lax.all_to_all(misfit, 'tensor', 0, 0, tiled=True)  5.87 us
  transfers between devices with their start and end apart: 18, of which 11 were waited for; matrix products, arithmetic and copies ran while one was open for 0% of the time, Pallas kernels for 18%

profile of v12, /device:TPU:0, one launch (start us, length us, event | category | flops | bytes accessed | tf_op | source)
XLA Modules:
  0.0 129.5 jit_solution(4379712491906903031)
XLA Ops:
  0.6 1.7 %rows.1 = bf16[40,512]{1,0:T(8,128)(2,1)} custom-call(s32[1,64]{1,0:T(1,128)} %route_ref.5, bf16[256,256]{1,0:T(8,128)(2,1)} %x_ref.1), custom_call_target="tpu_custom_call" | custom-call | flops 8192 | bytes 256 | tf_op jit(solution)/shard_map/rows/pallas_call | solution.py:340
  3.8 7.5 %teacher.1 = (bf16[8,256,512]{2,1,0:T(8,128)(2,1)}, bf16[8,256,512]{2,1,0:T(8,128)(2,1)}, bf16[8,64,512]{2,1,0:T(8,128)(2,1)}, bf16[8,64,512]{2,1,0:T(8,128)(2,1)}) custom-call(s32[1]{0:T(128)} %bitcast.2.core_ref, s32[1,64]{1,0:T(1,128)} %route_ref.5, bf16[256,512]{1,0:T(8,128)(2,1)} %attn_ref.1, bf16[512,8192]{1,0:T(8,128)(2,1)} %weight_ref.1), custom_call_target="tpu_custom_call" | custom-call | flops 2621440 | bytes 14336 | tf_op jit(solution)/shard_map/teacher/pallas_call | solution.py:354
  12.9 11.3 %all-to-all-start = ((bf16[16,40,512]{2,1,0:T(8,128)(2,1)}), bf16[16,40,512]{2,1,0:T(8,128)(2,1)S(1)}, u32[]{:S(2)}, u32[]{:S(2)}) async-start(bf16[16,40,512]{2,1,0:T(8,128)(2,1)} %get-tuple-element.45), calls=%async_computation | async-start | bytes 1310720 | tf_op jit(solution)/shard_map/all_to_all | solution.py:393
  24.2 2.0 %core_sum.1 = (bf16[2,64,512]{2,1,0:T(8,128)(2,1)}, bf16[2,64,512]{2,1,0:T(8,128)(2,1)}, bf16[2,64,512]{2,1,0:T(8,128)(2,1)}, bf16[2,64,512]{2,1,0:T(8,128)(2,1)}) custom-call(s32[1]{0:T(128)} %bitcast.4.x_ref, bf16[2,4,64,512]{3,2,1,0:T(8,128)(2,1)} %bitcast.22, bf16[2,4,64,512]{3,2,1,0:T(8,128)(2,1)} %bitcast.23, bf16[2,4,64,512]{3,2,1,0:T(8,128)(2,1)} %bitcast.24, ...), custom_call_target="tpu_custom_call" | custom-call | flops 1024 | bytes 1536 | tf_op jit(solution)/shard_map/core_sum/pallas_call | solution.py:401
  26.2 1.9 %collective-permute-start.3 = (bf16[2,64,512]{2,1,0:T(8,128)(2,1)}, bf16[2,64,512]{2,1,0:T(8,128)(2,1)S(1)}, u32[]{:S(2)}, u32[]{:S(2)}) collective-permute-start(bf16[2,64,512]{2,1,0:T(8,128)(2,1)} %get-tuple-element.53), channel_id=1, source_target_pairs={{0,2},{1,3},{2,4},{3,5},{4,6},{5,7},{6,0},{7,1},{8,10},{9,11},{10,... | collective-permute-start | bytes 393224 | tf_op jit(solution)/shard_map/ppermute | solution.py:396
  28.1 2.7 %collective-permute-start.4 = (bf16[2,64,512]{2,1,0:T(8,128)(2,1)}, bf16[2,64,512]{2,1,0:T(8,128)(2,1)S(1)}, u32[]{:S(2)}, u32[]{:S(2)}) collective-permute-start(bf16[2,64,512]{2,1,0:T(8,128)(2,1)} %get-tuple-element.54), channel_id=1, source_target_pairs={{0,4},{1,5},{2,6},{3,7},{4,0},{5,1},{6,2},{7,3},{8,12},{9,13},{10,... | collective-permute-start | bytes 393224 | tf_op jit(solution)/shard_map/ppermute | solution.py:396
  32.3 4.1 %halves.1 = (bf16[2,2,128,512]{3,2,1,0:T(8,128)(2,1)}, bf16[2,2,128,512]{3,2,1,0:T(8,128)(2,1)}, bf16[2,2,128,512]{3,2,1,0:T(8,128)(2,1)}, bf16[2,2,128,512]{3,2,1,0:T(8,128)(2,1)}) custom-call(s32[1]{0:T(128)} %bitcast.4.x_ref, bf16[8,2,128,512]{3,2,1,0:T(8,128)(2,1)} %bitcast.18, bf16[8,2,128,512]{3,2,1,0:T(8,128)(2,1)} %bitcast.19, ...), custom_call_target="tpu_custom_call" | custom-call | flops 1024 | bytes 6144 | tf_op jit(solution)/shard_map/halves/pallas_call | solution.py:442
  38.3 2.5 %up.1 = (bf16[8,32,1152]{2,1,0:T(8,128)(2,1)}, bf16[256,512]{1,0:T(8,128)(2,1)}, bf16[256,512]{1,0:T(8,128)(2,1)}) custom-call(s32[1]{0:T(128)} %bitcast.group_ref, bf16[16,40,512]{2,1,0:T(8,128)(2,1)S(1)} %all-to-all-done.got_ref, f32[1,4096]{1,0:T(1,128)S(1)} %bitcast.17, bf16[512,512]{1,0:T(8,128)(2,1)} %gate_ref.1, bf16[512,512]{1,0:T(8,128)(2,1)} %up_ref.1, ...), custom_call_target="tpu_custom_call" | custom-call | flops 819200 | bytes 4096 | tf_op jit(solution)/shard_map/up/pallas_call | solution.py:467
  43.5 3.7 %all-to-all-start.1 = ((bf16[8,32,1152]{2,1,0:T(8,128)(2,1)}), bf16[8,32,1152]{2,1,0:T(8,128)(2,1)S(1)}, u32[]{:S(2)}, u32[]{:S(2)}) async-start(bf16[8,32,1152]{2,1,0:T(8,128)(2,1)} %get-tuple-element.56), calls=%async_computation.1 | async-start | bytes 1179648 | tf_op jit(solution)/shard_map/all_to_all | solution.py:512
  47.2 3.2 %collective-permute-start.6 = (bf16[1,64,512]{2,1,0:T(8,128)(2,1)}, bf16[1,64,512]{2,1,0:T(8,128)(2,1)S(1)}, u32[]{:S(2)}, u32[]{:S(2)}) collective-permute-start(bf16[1,64,512]{2,1,0:T(8,128)(2,1)} %get-tuple-element.58), channel_id=1, source_target_pairs={{0,8},{1,9},{2,10},{3,11},{4,12},{5,13},{6,14},{7,15},{8,0},{9,1},... | collective-permute-start | bytes 196616 | tf_op jit(solution)/shard_map/ppermute | solution.py:396
  52.8 2.3 %first_sum.1 = (f32[2,128,512]{2,1,0:T(8,128)}, bf16[2,128,512]{2,1,0:T(8,128)(2,1)}, f32[2,128,512]{2,1,0:T(8,128)}, bf16[2,128,512]{2,1,0:T(8,128)(2,1)}) custom-call(bf16[2,2,128,512]{3,2,1,0:T(8,128)(2,1)S(1)} %copy-done.2, bf16[2,2,128,512]{3,2,1,0:T(8,128)(2,1)S(1)} %collective-permute-done.7.got_a, bf16[2,2,128,512]{3,2,1,0:T(8,128)(2,1)S(1)} %copy-done.7, ...), custom_call_target="tpu_custom_call" | custom-call | flops 1024 | bytes 3072 | tf_op jit(solution)/shard_map/first_sum/pallas_call | solution.py:517
  55.1 3.0 %collective-permute-done.6.refs_2_ = bf16[1,64,512]{2,1,0:T(8,128)(2,1)S(1)} collective-permute-done((bf16[1,64,512]{2,1,0:T(8,128)(2,1)}, bf16[1,64,512]{2,1,0:T(8,128)(2,1)S(1)}, u32[]{:S(2)}, u32[]{:S(2)}) %collective-permute-start.6) | collective-permute-done | bytes 65568 | tf_op jit(solution)/shard_map/ppermute | solution.py:396
  59.2 4.9 %all-to-all-start.2 = ((bf16[8,96,512]{2,1,0:T(8,128)(2,1)}), bf16[8,96,512]{2,1,0:T(8,128)(2,1)S(1)}, u32[]{:S(2)}, u32[]{:S(2)}) async-start(bf16[8,96,512]{2,1,0:T(8,128)(2,1)} %get-tuple-element.64), calls=%async_computation.2 | async-start | bytes 1572864 | tf_op jit(solution)/shard_map/all_to_all | solution.py:560
  64.1 1.7 %collective-permute-start.9 = (bf16[2,128,512]{2,1,0:T(8,128)(2,1)}, bf16[2,128,512]{2,1,0:T(8,128)(2,1)S(1)}, u32[]{:S(2)}, u32[]{:S(2)}) collective-permute-start(bf16[2,128,512]{2,1,0:T(8,128)(2,1)} %get-tuple-element.67), channel_id=1, source_target_pairs={{0,6},{1,7},{2,4},{3,5},{4,2},{5,3},{6,0},{7,1},{8,14},{9,15},{10,... | collective-permute-start | bytes 786440 | tf_op jit(solution)/shard_map/ppermute | solution.py:396
  65.9 4.9 %collective-permute-done.10.refs_5_.refs_7_ = bf16[2,128,512]{2,1,0:T(8,128)(2,1)S(1)} collective-permute-done((bf16[2,128,512]{2,1,0:T(8,128)(2,1)}, bf16[2,128,512]{2,1,0:T(8,128)(2,1)S(1)}, u32[]{:S(2)}, u32[]{:S(2)}) %collective-permute-start.10) | collective-permute-done | bytes 262176 | tf_op jit(solution)/shard_map/ppermute | solution.py:396
  74.3 2.3 %down.1 = (bf16[16,16,512]{2,1,0:T(8,128)(2,1)}, bf16[256,512]{1,0:T(8,128)(2,1)}) custom-call(s32[1]{0:T(128)} %bitcast.group_ref, bf16[8,96,512]{2,1,0:T(8,128)(2,1)S(1)} %all-to-all-done.2.got_ref, bf16[512,512]{1,0:T(8,128)(2,1)S(1)} %copy-done, bf16[256,512]{1,0:T(8,128)(2,1)S(1)} %copy-done.9, bf16[512,4096]{1,0:T(8,128)(2,1)} %projector_ref.1, ...), custom_call_target="tpu_custom_call" | custom-call | flops 786432 | bytes 4096 | tf_op jit(solution)/shard_map/down/pallas_call | solution.py:561
  76.6 4.1 %all-to-all-start.3 = ((bf16[16,16,512]{2,1,0:T(8,128)(2,1)}), bf16[16,16,512]{2,1,0:T(8,128)(2,1)S(1)}, u32[]{:S(2)}, u32[]{:S(2)}) async-start(bf16[16,16,512]{2,1,0:T(8,128)(2,1)} %get-tuple-element.71), calls=%async_computation.3 | async-start | bytes 524288 | tf_op jit(solution)/shard_map/all_to_all | solution.py:582
  80.8 3.5 %collective-permute-start.11 = (bf16[2,128,512]{2,1,0:T(8,128)(2,1)S(1)}, bf16[2,128,512]{2,1,0:T(8,128)(2,1)S(1)}, u32[]{:S(2)}, u32[]{:S(2)}) collective-permute-start(bf16[2,128,512]{2,1,0:T(8,128)(2,1)S(1)} %copy-done.13), channel_id=1, source_target_pairs={{0,8},{1,9},{2,10},{3,11},{4,12},{5,13},{6,14},{7,15},{8,0},{9,1},... | collective-permute-start | bytes 786440 | tf_op jit(solution)/shard_map/ppermute | solution.py:396
  84.3 5.9 %all-to-all-done.3.refs_0_ = bf16[16,16,512]{2,1,0:T(8,128)(2,1)S(1)} async-done(((bf16[16,16,512]{2,1,0:T(8,128)(2,1)}), bf16[16,16,512]{2,1,0:T(8,128)(2,1)S(1)}, u32[]{:S(2)}, u32[]{:S(2)}) %all-to-all-start.3) | async-done | bytes 262176 | tf_op jit(solution)/shard_map/all_to_all | solution.py:582
  90.9 3.5 %all-to-all-start.4 = ((bf16[16,16,512]{2,1,0:T(8,128)(2,1)}), bf16[16,16,512]{2,1,0:T(8,128)(2,1)S(1)}, u32[]{:S(2)}, u32[]{:S(2)}) async-start(bf16[16,16,512]{2,1,0:T(8,128)(2,1)} %misfit.1), calls=%async_computation.4 | async-start | bytes 524288 | tf_op jit(solution)/shard_map/all_to_all | solution.py:591
  95.4 8.4 %all-to-all-done.4.got_ref.grad_ref = bf16[16,16,512]{2,1,0:T(8,128)(2,1)S(1)} async-done(((bf16[16,16,512]{2,1,0:T(8,128)(2,1)}), bf16[16,16,512]{2,1,0:T(8,128)(2,1)S(1)}, u32[]{:S(2)}, u32[]{:S(2)}) %all-to-all-start.4) | async-done | bytes 262176 | tf_op jit(solution)/shard_map/all_to_all | solution.py:591
  104.1 11.0 %all_to_all.35.got_ref = bf16[8,32,512]{2,1,0:T(8,128)(2,1)S(1)} all-to-all(bf16[8,32,512]{2,1,0:T(8,128)(2,1)S(1)} %get-tuple-element.75), channel_id=1, replica_groups=mesh['batch'=8,'tensor'=16] {'batch'}, dimensions={0} | all-to-all | bytes 524288 | tf_op jit(solution)/shard_map/all_to_all | solution.py:610
  116.0 3.5 %all-to-all-start.6 = ((bf16[8,32,1024]{2,1,0:T(8,128)(2,1)}), bf16[8,32,1024]{2,1,0:T(8,128)(2,1)S(1)}, u32[]{:S(2)}, u32[]{:S(2)}) async-start(bf16[8,32,1024]{2,1,0:T(8,128)(2,1)} %acts.1), calls=%async_computation.6 | async-start | bytes 1048576 | tf_op jit(solution)/shard_map/all_to_all | solution.py:618
  120.8 7.1 %all-to-all-done.6.got_ref = bf16[8,32,1024]{2,1,0:T(8,128)(2,1)S(1)} async-done(((bf16[8,32,1024]{2,1,0:T(8,128)(2,1)}), bf16[8,32,1024]{2,1,0:T(8,128)(2,1)S(1)}, u32[]{:S(2)}, u32[]{:S(2)}) %all-to-all-start.6) | async-done | bytes 524320 | tf_op jit(solution)/shard_map/all_to_all | solution.py:618
  (58 shorter events, 22.0 us)
Async XLA Ops:
  2.4 8.9 %collective-permute-start = (bf16[40,512]{1,0:T(8,128)(2,1)}, bf16[40,512]{1,0:T(8,128)(2,1)S(1)}, u32[]{:S(2)}, u32[]{:S(2)}) collective-permute-start(bf16[40,512]{1,0:T(8,128)(2,1)} %rows.1), channel_id=1, source_target_pairs={{0,0},{1,1},{2,16},{3,17},{4,32},{5,33},{6,48},{7,49},{8,64},{9,65... | collective-permute-start | bytes 122888 | tf_op jit(solution)/shard_map/ppermute | solution.py:352
  12.3 20.0 %collective-permute-start.1 = (bf16[8,256,512]{2,1,0:T(8,128)(2,1)}, bf16[8,256,512]{2,1,0:T(8,128)(2,1)S(1)}, u32[]{:S(2)}, u32[]{:S(2)}) collective-permute-start(bf16[8,256,512]{2,1,0:T(8,128)(2,1)} %get-tuple-element.47), channel_id=1, source_target_pairs={{0,1},{1,0},{2,3},{3,2},{4,5},{5,4},{6,7},{7,6},{8,9},{9,8},{10,11... | collective-permute-start | bytes 6291464 | tf_op jit(solution)/shard_map/ppermute | solution.py:396
  12.4 11.9 %collective-permute-start.2 = (bf16[8,64,512]{2,1,0:T(8,128)(2,1)}, bf16[8,64,512]{2,1,0:T(8,128)(2,1)S(1)}, u32[]{:S(2)}, u32[]{:S(2)}) collective-permute-start(bf16[8,64,512]{2,1,0:T(8,128)(2,1)} %get-tuple-element.51), channel_id=1, source_target_pairs={{0,1},{1,0},{2,3},{3,2},{4,5},{5,4},{6,7},{7,6},{8,9},{9,8},{10,11... | collective-permute-start | bytes 1572872 | tf_op jit(solution)/shard_map/ppermute | solution.py:396
  12.9 25.4 %all-to-all-start = ((bf16[16,40,512]{2,1,0:T(8,128)(2,1)}), bf16[16,40,512]{2,1,0:T(8,128)(2,1)S(1)}, u32[]{:S(2)}, u32[]{:S(2)}) async-start(bf16[16,40,512]{2,1,0:T(8,128)(2,1)} %get-tuple-element.45), calls=%async_computation | async-start | bytes 1310720 | tf_op jit(solution)/shard_map/all_to_all | solution.py:393
  26.2 14.7 %collective-permute-start.3 = (bf16[2,64,512]{2,1,0:T(8,128)(2,1)}, bf16[2,64,512]{2,1,0:T(8,128)(2,1)S(1)}, u32[]{:S(2)}, u32[]{:S(2)}) collective-permute-start(bf16[2,64,512]{2,1,0:T(8,128)(2,1)} %get-tuple-element.53), channel_id=1, source_target_pairs={{0,2},{1,3},{2,4},{3,5},{4,6},{5,7},{6,0},{7,1},{8,10},{9,11},{10,... | collective-permute-start | bytes 393224 | tf_op jit(solution)/shard_map/ppermute | solution.py:396
  28.1 13.9 %collective-permute-start.4 = (bf16[2,64,512]{2,1,0:T(8,128)(2,1)}, bf16[2,64,512]{2,1,0:T(8,128)(2,1)S(1)}, u32[]{:S(2)}, u32[]{:S(2)}) collective-permute-start(bf16[2,64,512]{2,1,0:T(8,128)(2,1)} %get-tuple-element.54), channel_id=1, source_target_pairs={{0,4},{1,5},{2,6},{3,7},{4,0},{5,1},{6,2},{7,3},{8,12},{9,13},{10,... | collective-permute-start | bytes 393224 | tf_op jit(solution)/shard_map/ppermute | solution.py:396
  30.8 11.2 %collective-permute-start.5 = (bf16[2,64,512]{2,1,0:T(8,128)(2,1)}, bf16[2,64,512]{2,1,0:T(8,128)(2,1)S(1)}, u32[]{:S(2)}, u32[]{:S(2)}) collective-permute-start(bf16[2,64,512]{2,1,0:T(8,128)(2,1)} %get-tuple-element.55), channel_id=1, source_target_pairs={{0,6},{1,7},{2,0},{3,1},{4,2},{5,3},{6,4},{7,5},{8,14},{9,15},{10,... | collective-permute-start | bytes 393224 | tf_op jit(solution)/shard_map/ppermute | solution.py:396
  36.3 14.9 %collective-permute-start.7 = (bf16[2,2,128,512]{3,2,1,0:T(8,128)(2,1)}, bf16[2,2,128,512]{3,2,1,0:T(8,128)(2,1)S(1)}, u32[]{:S(2)}, u32[]{:S(2)}) collective-permute-start(bf16[2,2,128,512]{3,2,1,0:T(8,128)(2,1)} %get-tuple-element.59), channel_id=1, source_target_pairs={{0,2},{1,3},{2,0},{3,1},{4,6},{5,7},{6,4},{7,5},{8,10},{9,11},{10,... | collective-permute-start | bytes 1572872 | tf_op jit(solution)/shard_map/ppermute | solution.py:396
  37.0 15.9 %collective-permute-start.8 = (bf16[2,2,128,512]{3,2,1,0:T(8,128)(2,1)}, bf16[2,2,128,512]{3,2,1,0:T(8,128)(2,1)}, u32[]{:S(2)}, u32[]{:S(2)}) collective-permute-start(bf16[2,2,128,512]{3,2,1,0:T(8,128)(2,1)} %get-tuple-element.61), channel_id=1, source_target_pairs={{0,6},{1,7},{2,4},{3,5},{4,2},{5,3},{6,0},{7,1},{8,14},{9,15},{10,... | collective-permute-start | bytes 1572872 | tf_op jit(solution)/shard_map/ppermute | solution.py:396
  43.5 14.6 %all-to-all-start.1 = ((bf16[8,32,1152]{2,1,0:T(8,128)(2,1)}), bf16[8,32,1152]{2,1,0:T(8,128)(2,1)S(1)}, u32[]{:S(2)}, u32[]{:S(2)}) async-start(bf16[8,32,1152]{2,1,0:T(8,128)(2,1)} %get-tuple-element.56), calls=%async_computation.1 | async-start | bytes 1179648 | tf_op jit(solution)/shard_map/all_to_all | solution.py:512
  47.2 10.9 %collective-permute-start.6 = (bf16[1,64,512]{2,1,0:T(8,128)(2,1)}, bf16[1,64,512]{2,1,0:T(8,128)(2,1)S(1)}, u32[]{:S(2)}, u32[]{:S(2)}) collective-permute-start(bf16[1,64,512]{2,1,0:T(8,128)(2,1)} %get-tuple-element.58), channel_id=1, source_target_pairs={{0,8},{1,9},{2,10},{3,11},{4,12},{5,13},{6,14},{7,15},{8,0},{9,1},... | collective-permute-start | bytes 196616 | tf_op jit(solution)/shard_map/ppermute | solution.py:396
  55.1 16.9 %copy-start.3 = (f32[2,128,512]{2,1,0:T(8,128)S(1)}, f32[2,128,512]{2,1,0:T(8,128)}, u32[]{:S(2)}) copy-start(f32[2,128,512]{2,1,0:T(8,128)} %get-tuple-element.66.refs_0_.refs_2_) | copy-start | bytes 1572868
  55.1 16.9 %copy-start.4 = (f32[2,128,512]{2,1,0:T(8,128)S(1)}, f32[2,128,512]{2,1,0:T(8,128)}, u32[]{:S(2)}) copy-start(f32[2,128,512]{2,1,0:T(8,128)} %get-tuple-element.68.refs_4_.refs_6_) | copy-start | bytes 1572868
  59.2 15.1 %copy-start.9 = (bf16[256,512]{1,0:T(8,128)(2,1)S(1)}, bf16[256,512]{1,0:T(8,128)(2,1)}, u32[]{:S(2)}) copy-start(bf16[256,512]{1,0:T(8,128)(2,1)} %get-tuple-element.65.chosen_ref) | copy-start | bytes 786436
  59.2 15.1 %all-to-all-start.2 = ((bf16[8,96,512]{2,1,0:T(8,128)(2,1)}), bf16[8,96,512]{2,1,0:T(8,128)(2,1)S(1)}, u32[]{:S(2)}, u32[]{:S(2)}) async-start(bf16[8,96,512]{2,1,0:T(8,128)(2,1)} %get-tuple-element.64), calls=%async_computation.2 | async-start | bytes 1572864 | tf_op jit(solution)/shard_map/all_to_all | solution.py:560
  64.1 6.6 %collective-permute-start.10 = (bf16[2,128,512]{2,1,0:T(8,128)(2,1)}, bf16[2,128,512]{2,1,0:T(8,128)(2,1)S(1)}, u32[]{:S(2)}, u32[]{:S(2)}) collective-permute-start(bf16[2,128,512]{2,1,0:T(8,128)(2,1)} %get-tuple-element.69), channel_id=1, source_target_pairs={{0,2},{1,3},{2,0},{3,1},{4,6},{5,7},{6,4},{7,5},{8,10},{9,11},{10,... | collective-permute-start | bytes 786440 | tf_op jit(solution)/shard_map/ppermute | solution.py:396
  64.1 7.9 %collective-permute-start.9 = (bf16[2,128,512]{2,1,0:T(8,128)(2,1)}, bf16[2,128,512]{2,1,0:T(8,128)(2,1)S(1)}, u32[]{:S(2)}, u32[]{:S(2)}) collective-permute-start(bf16[2,128,512]{2,1,0:T(8,128)(2,1)} %get-tuple-element.67), channel_id=1, source_target_pairs={{0,6},{1,7},{2,4},{3,5},{4,2},{5,3},{6,0},{7,1},{8,14},{9,15},{10,... | collective-permute-start | bytes 786440 | tf_op jit(solution)/shard_map/ppermute | solution.py:396
  74.3 20.1 %copy-start.1 = (f32[2,128,512]{2,1,0:T(8,128)S(1)}, f32[2,128,512]{2,1,0:T(8,128)}, u32[]{:S(2)}) copy-start(f32[2,128,512]{2,1,0:T(8,128)} %get-tuple-element.70.after_ref.keep_ref) | copy-start | bytes 1572868
  76.6 13.5 %all-to-all-start.3 = ((bf16[16,16,512]{2,1,0:T(8,128)(2,1)}), bf16[16,16,512]{2,1,0:T(8,128)(2,1)S(1)}, u32[]{:S(2)}, u32[]{:S(2)}) async-start(bf16[16,16,512]{2,1,0:T(8,128)(2,1)} %get-tuple-element.71), calls=%async_computation.3 | async-start | bytes 524288 | tf_op jit(solution)/shard_map/all_to_all | solution.py:582
  80.8 13.7 %collective-permute-start.11 = (bf16[2,128,512]{2,1,0:T(8,128)(2,1)S(1)}, bf16[2,128,512]{2,1,0:T(8,128)(2,1)S(1)}, u32[]{:S(2)}, u32[]{:S(2)}) collective-permute-start(bf16[2,128,512]{2,1,0:T(8,128)(2,1)S(1)} %copy-done.13), channel_id=1, source_target_pairs={{0,8},{1,9},{2,10},{3,11},{4,12},{5,13},{6,14},{7,15},{8,0},{9,1},... | collective-permute-start | bytes 786440 | tf_op jit(solution)/shard_map/ppermute | solution.py:396
  90.9 12.9 %all-to-all-start.4 = ((bf16[16,16,512]{2,1,0:T(8,128)(2,1)}), bf16[16,16,512]{2,1,0:T(8,128)(2,1)S(1)}, u32[]{:S(2)}, u32[]{:S(2)}) async-start(bf16[16,16,512]{2,1,0:T(8,128)(2,1)} %misfit.1), calls=%async_computation.4 | async-start | bytes 524288 | tf_op jit(solution)/shard_map/all_to_all | solution.py:591
  95.4 24.1 %copy-start.10 = (bf16[256,512]{1,0:T(8,128)(2,1)S(1)}, bf16[256,512]{1,0:T(8,128)(2,1)}, u32[]{:S(2)}) copy-start(bf16[256,512]{1,0:T(8,128)(2,1)} %get-tuple-element.81.hidden_ref) | copy-start | bytes 786436
  104.1 23.8 %copy-start.8 = (bf16[256,512]{1,0:T(8,128)(2,1)S(1)}, bf16[256,512]{1,0:T(8,128)(2,1)}, u32[]{:S(2)}) copy-start(bf16[256,512]{1,0:T(8,128)(2,1)} %get-tuple-element.74.rows_ref) | copy-start | bytes 786436
  116.0 11.9 %all-to-all-start.6 = ((bf16[8,32,1024]{2,1,0:T(8,128)(2,1)}), bf16[8,32,1024]{2,1,0:T(8,128)(2,1)S(1)}, u32[]{:S(2)}, u32[]{:S(2)}) async-start(bf16[8,32,1024]{2,1,0:T(8,128)(2,1)} %acts.1), calls=%async_computation.6 | async-start | bytes 1048576 | tf_op jit(solution)/shard_map/all_to_all | solution.py:618
  (8 other events, 77.5 us)
